TPU v7x, 32 devices: a whole 2x2x4 slice. The times are simulated.
32 devices in a mesh: rep: 4 (over x, core), shard: 8 (over z, y).
Axes of the slice: x: 2, y: 2, z: 4, core: 2. Of those that a mesh axis runs over, the one named last changes fastest.
Arguments:
- tokens: bfloat16 [4096, 2304], P(('rep', 'shard')), may hold values from -6 to 6
- doc_lengths: int32 [32, 2], P(('rep', 'shard')), may hold values from 1 to 96, 128 in all within a row
- pic_starts: int32 [32, 2], P(('rep', 'shard')), may hold values from 0 to 64
- attn_gain: float32 [2304], P('shard'), may hold values from 0.5 to 1.5
- w_query: float32 [2304, 2304], P('shard'), may hold values from -0.125 to 0.125
- w_key: float32 [2304, 2304], P('shard'), may hold values from -0.125 to 0.125
- w_value: float32 [2304, 2304], P('shard'), may hold values from -0.125 to 0.125
- w_out: float32 [2304, 2304], P('shard'), may hold values from -3.6 to 3.6
- ffn_gain: float32 [2304], P('shard'), may hold values from 0.5 to 1.5
- w_gate: float32 [2304, 5760], P('shard'), may hold values from -0.125 to 0.125
- w_up: float32 [2304, 5760], P('shard'), may hold values from -0.125 to 0.125
- w_down: float32 [5760, 2304], P('shard'), may hold values from -0.6 to 0.6
- cotangent: bfloat16 [4096, 2304], P(('rep', 'shard')), may hold values from -6 to 6
Outputs:
- out_tokens: bfloat16 [4096, 2304], P(('rep', 'shard'))
- input_grad: float32 [4096, 2304], P(('rep', 'shard'))
- attn_gain_grad: float32 [2304], P('shard')
- query_grad: float32 [2304, 2304], P('shard')
- key_grad: float32 [2304, 2304], P('shard')
- value_grad: float32 [2304, 2304], P('shard')
- out_grad: float32 [2304, 2304], P('shard')
- ffn_gain_grad: float32 [2304], P('shard')
- gate_grad: float32 [2304, 5760], P('shard')
- up_grad: float32 [2304, 5760], P('shard')
- down_grad: float32 [5760, 2304], P('shard')
Inputs may be any that keep to these rules, and one draw needn't show every extreme that they name: `doc_lengths`: each row of 2 lengths sums to 128. `pic_starts`: pieces may intersect each other and cross document ends.
All inputs are finite; a program needn't handle non-finite values.
Results may differ from a plain program's by a relative error of at most 0.02.
Values may be sent and summed in bfloat16 or wider, within the bound.
No kernel may reach another device: no remote copies, remote signals or barrier semaphores. Data moves between devices by JAX's collectives and lax.ppermute only.
A program may use at most 512 MiB of HBM per device.

v0:
```python
import math

import jax
import jax.numpy as jnp
from jax import lax
from jax.sharding import PartitionSpec as P

HD = 64
PIC = 64


EPSILON = 1e-05
BRANCH_SCALE = 1.4 / math.sqrt(40.0)
MASKED = -1e30


def layout(lengths, starts, row_count):
    places = jnp.arange(row_count, dtype=jnp.int32)
    bounds = jnp.cumsum(lengths)
    firsts = bounds - lengths
    member = (places[:, None] >= firsts[None, :]) & (places[:, None] < bounds[None, :])
    doc_of = jnp.sum(
        jnp.where(member, jnp.arange(lengths.shape[0], dtype=jnp.int32)[None, :], 0), axis=1
    )
    starting = jnp.sum(jnp.where(member, firsts[None, :], 0), axis=1)
    inside = (places[None, :] >= starts[:, None]) & (places[None, :] < starts[:, None] + PIC)
    shared = jnp.any(inside[:, :, None] & inside[:, None, :], axis=0)
    causal = places[None, :] <= places[:, None]
    allowed = (doc_of[:, None] == doc_of[None, :]) & (causal | shared)
    return (places - starting, allowed.astype(jnp.int32))


def angles(offsets, head_size):
    half_size = head_size // 2
    freq_table = jnp.exp(
        jnp.arange(half_size, dtype=jnp.float32) * (-2.0 * math.log(10000.0) / head_size)
    )
    turned = offsets.astype(jnp.float32)[:, None] * freq_table[None, :]
    return (jnp.cos(turned)[:, None, :], jnp.sin(turned)[:, None, :])


def rotate(values, cosine, sine):
    half_size = values.shape[-1] // 2
    first_half = values[..., :half_size]
    second_half = values[..., half_size:]
    return jnp.concatenate(
        [first_half * cosine - second_half * sine, second_half * cosine + first_half * sine],
        axis=-1,
    )


def unrotate(values, cosine, sine):
    half_size = values.shape[-1] // 2
    first_half = values[..., :half_size]
    second_half = values[..., half_size:]
    return jnp.concatenate(
        [first_half * cosine + second_half * sine, second_half * cosine - first_half * sine],
        axis=-1,
    )


def score_block(query, keys, allowed):
    scores = jnp.einsum("qhd,khd->hqk", query, keys, preferred_element_type=jnp.float32) * HD ** (
        -0.5
    )
    return jnp.where(allowed[None] != 0, scores, MASKED)


def norm_back(grad_hidden, normed, gain_value, scale_rows):
    grad_normed = grad_hidden * gain_value
    inner_mean = jnp.mean(grad_normed * normed, axis=-1, keepdims=True)
    return scale_rows * (grad_normed - normed * inner_mean)


def local(
    tokens,
    doc_lengths,
    pic_starts,
    attn_gain,
    w_query,
    w_key,
    w_value,
    w_out,
    ffn_gain,
    w_gate,
    w_up,
    w_down,
    cotangent,
):
    row_count = tokens.shape[0]
    width_all = tokens.shape[1]
    head_count = width_all // HD
    offsets, allowed = layout(doc_lengths[0], pic_starts[0], row_count)
    cosine, sine = angles(offsets, HD)
    inputs = tokens.astype(jnp.float32)
    gain_one, query_w, key_w, value_w, out_w = (
        lax.all_gather(attn_gain.astype(jnp.bfloat16), "shard", axis=0, tiled=True),
        lax.all_gather(w_query.astype(jnp.bfloat16), "shard", axis=0, tiled=True),
        lax.all_gather(w_key.astype(jnp.bfloat16), "shard", axis=0, tiled=True),
        lax.all_gather(w_value.astype(jnp.bfloat16), "shard", axis=0, tiled=True),
        lax.all_gather(w_out.astype(jnp.bfloat16), "shard", axis=0, tiled=True),
    )
    scale_one = lax.rsqrt(jnp.mean(inputs * inputs, axis=-1, keepdims=True) + EPSILON)
    normed_one = inputs * scale_one
    hidden_one = (normed_one * gain_one.astype(jnp.float32)).astype(jnp.bfloat16)
    query_raw = jnp.dot(hidden_one, query_w, preferred_element_type=jnp.float32).reshape(
        row_count, head_count, HD
    )
    keys_raw = jnp.dot(hidden_one, key_w, preferred_element_type=jnp.float32).reshape(
        row_count, head_count, HD
    )
    query = rotate(query_raw, cosine, sine).astype(jnp.bfloat16)
    keys = rotate(keys_raw, cosine, sine).astype(jnp.bfloat16)
    values = (
        jnp.dot(hidden_one, value_w, preferred_element_type=jnp.float32)
        .astype(jnp.bfloat16)
        .reshape(row_count, head_count, HD)
    )
    scores = score_block(query, keys, allowed)
    highest = jnp.max(scores, axis=-1, keepdims=True)
    expo = jnp.exp(scores - highest)
    totals = jnp.sum(expo, axis=-1, keepdims=True)
    log_total = highest + jnp.log(totals)
    probs = (expo / totals).astype(jnp.bfloat16)
    mixed = (
        jnp.einsum("hqk,khd->qhd", probs, values, preferred_element_type=jnp.float32)
        .reshape(row_count, width_all)
        .astype(jnp.bfloat16)
    )
    middle = inputs + BRANCH_SCALE * jnp.dot(mixed, out_w, preferred_element_type=jnp.float32)
    gain_two, gate_w, up_w, down_w = (
        lax.all_gather(ffn_gain.astype(jnp.bfloat16), "shard", axis=0, tiled=True),
        lax.all_gather(w_gate.astype(jnp.bfloat16), "shard", axis=0, tiled=True),
        lax.all_gather(w_up.astype(jnp.bfloat16), "shard", axis=0, tiled=True),
        lax.all_gather(w_down.astype(jnp.bfloat16), "shard", axis=0, tiled=True),
    )
    scale_two = lax.rsqrt(jnp.mean(middle * middle, axis=-1, keepdims=True) + EPSILON)
    normed_two = middle * scale_two
    hidden_two = (normed_two * gain_two.astype(jnp.float32)).astype(jnp.bfloat16)
    gate_act = jnp.dot(hidden_two, gate_w, preferred_element_type=jnp.float32)
    up_act = jnp.dot(hidden_two, up_w, preferred_element_type=jnp.float32)
    sigmoid_gate = jax.nn.sigmoid(gate_act)
    silu_gate = gate_act * sigmoid_gate
    inner = (silu_gate * up_act).astype(jnp.bfloat16)
    result = middle + BRANCH_SCALE * jnp.dot(inner, down_w, preferred_element_type=jnp.float32)
    out_tokens = result.astype(jnp.bfloat16)
    grad_result = cotangent.astype(jnp.float32)
    gain_two, gate_w, up_w, down_w = (
        lax.all_gather(ffn_gain.astype(jnp.bfloat16), "shard", axis=0, tiled=True),
        lax.all_gather(w_gate.astype(jnp.bfloat16), "shard", axis=0, tiled=True),
        lax.all_gather(w_up.astype(jnp.bfloat16), "shard", axis=0, tiled=True),
        lax.all_gather(w_down.astype(jnp.bfloat16), "shard", axis=0, tiled=True),
    )
    grad_branch = (BRANCH_SCALE * grad_result).astype(jnp.bfloat16)
    grad_down = jnp.einsum("tf,td->fd", inner, grad_branch, preferred_element_type=jnp.float32)
    grad_inner = jnp.einsum("td,fd->tf", grad_branch, down_w, preferred_element_type=jnp.float32)
    grad_gate_act = (
        grad_inner * up_act * sigmoid_gate * (1.0 + gate_act * (1.0 - sigmoid_gate))
    ).astype(jnp.bfloat16)
    grad_up_act = (grad_inner * silu_gate).astype(jnp.bfloat16)
    grad_gate = jnp.einsum(
        "td,tf->df", hidden_two, grad_gate_act, preferred_element_type=jnp.float32
    )
    grad_up = jnp.einsum("td,tf->df", hidden_two, grad_up_act, preferred_element_type=jnp.float32)
    grad_hidden_two = jnp.einsum(
        "tf,df->td", grad_gate_act, gate_w, preferred_element_type=jnp.float32
    ) + jnp.einsum("tf,df->td", grad_up_act, up_w, preferred_element_type=jnp.float32)
    grad_gain_two = jnp.sum(grad_hidden_two * normed_two, axis=0)
    grad_middle = grad_result + norm_back(
        grad_hidden_two, normed_two, gain_two.astype(jnp.float32), scale_two
    )
    group_sums = (
        lax.psum_scatter(
            grad_gain_two.astype(jnp.bfloat16), "shard", scatter_dimension=0, tiled=True
        ).astype(jnp.float32),
        lax.psum_scatter(
            grad_gate.astype(jnp.bfloat16), "shard", scatter_dimension=0, tiled=True
        ).astype(jnp.float32),
        lax.psum_scatter(
            grad_up.astype(jnp.bfloat16), "shard", scatter_dimension=0, tiled=True
        ).astype(jnp.float32),
        lax.psum_scatter(
            grad_down.astype(jnp.bfloat16), "shard", scatter_dimension=0, tiled=True
        ).astype(jnp.float32),
    )
    ffn_sums = (
        lax.psum(group_sums[0].astype(jnp.bfloat16), "rep").astype(jnp.float32),
        lax.psum(group_sums[1].astype(jnp.bfloat16), "rep").astype(jnp.float32),
        lax.psum(group_sums[2].astype(jnp.bfloat16), "rep").astype(jnp.float32),
        lax.psum(group_sums[3].astype(jnp.bfloat16), "rep").astype(jnp.float32),
    )
    gain_one, query_w, key_w, value_w, out_w = (
        lax.all_gather(attn_gain.astype(jnp.bfloat16), "shard", axis=0, tiled=True),
        lax.all_gather(w_query.astype(jnp.bfloat16), "shard", axis=0, tiled=True),
        lax.all_gather(w_key.astype(jnp.bfloat16), "shard", axis=0, tiled=True),
        lax.all_gather(w_value.astype(jnp.bfloat16), "shard", axis=0, tiled=True),
        lax.all_gather(w_out.astype(jnp.bfloat16), "shard", axis=0, tiled=True),
    )
    grad_attn = (BRANCH_SCALE * grad_middle).astype(jnp.bfloat16)
    grad_out = jnp.einsum("te,td->ed", mixed, grad_attn, preferred_element_type=jnp.float32)
    grad_mixed = (
        jnp.einsum("td,ed->te", grad_attn, out_w, preferred_element_type=jnp.float32)
        .astype(jnp.bfloat16)
        .reshape(row_count, head_count, HD)
    )
    again_scores = score_block(query, keys, allowed)
    again_probs = jnp.exp(again_scores - log_total)
    again_low = again_probs.astype(jnp.bfloat16)
    grad_values = jnp.einsum(
        "hqk,qhd->khd", again_low, grad_mixed, preferred_element_type=jnp.float32
    ).astype(jnp.bfloat16)
    grad_probs = jnp.einsum("qhd,khd->hqk", grad_mixed, values, preferred_element_type=jnp.float32)
    grad_scores = (
        again_probs * (grad_probs - jnp.sum(again_probs * grad_probs, axis=-1, keepdims=True))
    ).astype(jnp.bfloat16)
    grad_query = jnp.einsum(
        "hqk,khd->qhd", grad_scores, keys, preferred_element_type=jnp.float32
    ) * HD ** (-0.5)
    grad_keys = jnp.einsum(
        "hqk,qhd->khd", grad_scores, query, preferred_element_type=jnp.float32
    ) * HD ** (-0.5)
    grad_query_raw = (
        unrotate(grad_query, cosine, sine).astype(jnp.bfloat16).reshape(row_count, width_all)
    )
    grad_keys_raw = (
        unrotate(grad_keys, cosine, sine).astype(jnp.bfloat16).reshape(row_count, width_all)
    )
    grad_values_flat = grad_values.reshape(row_count, width_all)
    grad_query_w = jnp.einsum(
        "te,tf->ef", hidden_one, grad_query_raw, preferred_element_type=jnp.float32
    )
    grad_key_w = jnp.einsum(
        "te,tf->ef", hidden_one, grad_keys_raw, preferred_element_type=jnp.float32
    )
    grad_value_w = jnp.einsum(
        "te,tf->ef", hidden_one, grad_values_flat, preferred_element_type=jnp.float32
    )
    grad_hidden_one = jnp.einsum(
        "tf,ef->te", grad_query_raw, query_w, preferred_element_type=jnp.float32
    )
    grad_hidden_one = grad_hidden_one + jnp.einsum(
        "tf,ef->te", grad_keys_raw, key_w, preferred_element_type=jnp.float32
    )
    grad_hidden_one = grad_hidden_one + jnp.einsum(
        "tf,ef->te", grad_values_flat, value_w, preferred_element_type=jnp.float32
    )
    grad_gain_one = jnp.sum(grad_hidden_one * normed_one, axis=0)
    input_grad = grad_middle + norm_back(
        grad_hidden_one, normed_one, gain_one.astype(jnp.float32), scale_one
    )
    attn_group = (
        lax.psum_scatter(
            grad_gain_one.astype(jnp.bfloat16), "shard", scatter_dimension=0, tiled=True
        ).astype(jnp.float32),
        lax.psum_scatter(
            grad_query_w.astype(jnp.bfloat16), "shard", scatter_dimension=0, tiled=True
        ).astype(jnp.float32),
        lax.psum_scatter(
            grad_key_w.astype(jnp.bfloat16), "shard", scatter_dimension=0, tiled=True
        ).astype(jnp.float32),
        lax.psum_scatter(
            grad_value_w.astype(jnp.bfloat16), "shard", scatter_dimension=0, tiled=True
        ).astype(jnp.float32),
        lax.psum_scatter(
            grad_out.astype(jnp.bfloat16), "shard", scatter_dimension=0, tiled=True
        ).astype(jnp.float32),
    )
    attn_sums = (
        lax.psum(attn_group[0].astype(jnp.bfloat16), "rep").astype(jnp.float32),
        lax.psum(attn_group[1].astype(jnp.bfloat16), "rep").astype(jnp.float32),
        lax.psum(attn_group[2].astype(jnp.bfloat16), "rep").astype(jnp.float32),
        lax.psum(attn_group[3].astype(jnp.bfloat16), "rep").astype(jnp.float32),
        lax.psum(attn_group[4].astype(jnp.bfloat16), "rep").astype(jnp.float32),
    )
    return (
        out_tokens,
        input_grad,
        attn_sums[0],
        attn_sums[1],
        attn_sums[2],
        attn_sums[3],
        attn_sums[4],
        ffn_sums[0],
        ffn_sums[1],
        ffn_sums[2],
        ffn_sums[3],
    )


def solution(mesh):
    return jax.shard_map(
        local,
        mesh=mesh,
        in_specs=(
            P(("rep", "shard"), None),
            P(("rep", "shard"), None),
            P(("rep", "shard"), None),
            P("shard"),
            P("shard", None),
            P("shard", None),
            P("shard", None),
            P("shard", None),
            P("shard"),
            P("shard", None),
            P("shard", None),
            P("shard", None),
            P(("rep", "shard"), None),
        ),
        out_specs=(
            P(("rep", "shard"), None),
            P(("rep", "shard"), None),
            P("shard"),
            P("shard", None),
            P("shard", None),
            P("shard", None),
            P("shard", None),
            P("shard"),
            P("shard", None),
            P("shard", None),
            P("shard", None),
        ),
        check_vma=False,
    )
```

profile of v0, /device:TPU:0, one launch (start us, length us, event | category | flops | bytes accessed | tf_op | source)
XLA Modules:
  0.0 4505.5 jit_solution(12764787513258305463)
XLA Ops:
  7.2 3.1 convert_element_type.206
  10.4 1.2 convert_element_type.209
  11.7 3.1 convert_element_type.211
  14.9 1.2 convert_element_type.216
  16.1 4.9 convert_element_type.220
  21.2 5.7 convert_element_type.221
  26.9 4.9 convert_element_type.223
  34.3 39.5 all-reduce.5
  76.1 90.3 %all-gather.8.cloned.1.call-done = bf16[2304,2304]{1,0:T(8,128)(2,1)} async-done(((bf16[288,2304]{1,0:T(8,128)(2,1)}), bf16[2304,2304]{1,0:T(8,128)(2,1)}) %all-gather.8.cloned.1.call-update) | async-done | bytes 10616848 | tf_op jit(solution)/shard_map/all_gather | solution.py:100
  166.5 5.6 convolution_convert_fusion.8
  172.1 1.1 copy.52
  173.1 146.8 %all-gather.10.cloned.1.call-done = bf16[2304,2304]{1,0:T(8,128)(2,1)} async-done(((bf16[288,2304]{1,0:T(8,128)(2,1)}), bf16[2304,2304]{1,0:T(8,128)(2,1)}) %all-gather.10.cloned.1.call-update) | async-done | bytes 10616848 | tf_op jit(solution)/shard_map/all_gather | solution.py:98
  319.9 7.0 fusion.40
  326.9 146.5 %all-gather.12.cloned.1.call-done = bf16[2304,2304]{1,0:T(8,128)(2,1)} async-done(((bf16[288,2304]{1,0:T(8,128)(2,1)}), bf16[2304,2304]{1,0:T(8,128)(2,1)}) %all-gather.12.cloned.1.call-update) | async-done | bytes 10616848 | tf_op jit(solution)/shard_map/all_gather | solution.py:99
  473.3 7.3 fusion.38
  483.7 142.9 %all-gather.14.cloned.1.call-done = bf16[2304,2304]{1,0:T(8,128)(2,1)} async-done(((bf16[288,2304]{1,0:T(8,128)(2,1)}), bf16[2304,2304]{1,0:T(8,128)(2,1)}) %all-gather.14.cloned.1.call-update) | async-done | bytes 10616848 | tf_op jit(solution)/shard_map/all_gather | solution.py:101
  626.6 5.8 multiply_reduce_fusion.3
  633.6 499.4 %all-gather.16.cloned.1.call-done = bf16[2304,5760]{1,0:T(8,128)(2,1)} async-done(((bf16[288,5760]{1,0:T(8,128)(2,1)}), bf16[2304,5760]{1,0:T(8,128)(2,1)}) %all-gather.16.cloned.1.call-update) | async-done | bytes 26542096 | tf_op jit(solution)/shard_map/all_gather | solution.py:133
  1133.0 14.0 fusion.45
  1147.0 494.2 %all-gather.18.cloned.1.call-done = bf16[2304,5760]{1,0:T(8,128)(2,1)} async-done(((bf16[288,5760]{1,0:T(8,128)(2,1)}), bf16[2304,5760]{1,0:T(8,128)(2,1)}) %all-gather.18.cloned.1.call-update) | async-done | bytes 26542096 | tf_op jit(solution)/shard_map/all_gather | solution.py:134
  1641.2 14.0 fusion.46
  1655.2 494.4 %all-gather.20.cloned.1.call-done = bf16[5760,2304]{1,0:T(8,128)(2,1)} async-done(((bf16[720,2304]{1,0:T(8,128)(2,1)}), bf16[5760,2304]{1,0:T(8,128)(2,1)}) %all-gather.20.cloned.1.call-update) | async-done | bytes 26542096 | tf_op jit(solution)/shard_map/all_gather | solution.py:135
  2149.6 17.0 multiply_convert_fusion
  2166.6 13.6 fusion.47
  2180.3 14.8 multiply_reduce_fusion.1
  2195.8 2.2 convert_add_fusion
  2199.0 5.5 convolution_convert_fusion.3
  2204.6 1.4 log_add_fusion
  2206.0 8.7 convolution_convert_fusion.7
  2214.7 2.1 copy.57
  2216.8 2.0 convolution_convert_fusion.9
  2219.6 5.9 convolution_convert_fusion.4
  2225.7 2.0 multiply_reduce_fusion
  2231.0 5.8 convolution_convert_fusion.5
  2236.8 5.8 convolution_convert_fusion.6
  2242.7 1.3 copy-done.6
  2244.0 12.9 convolution_convert_fusion.2
  2257.0 1.3 copy-done.8
  2258.3 12.6 convolution_convert_fusion
  2271.0 1.3 copy-done.5
  2272.3 12.5 convolution_convert_fusion.1
  2285.1 99.6 %reduce-scatter.14.cloned.1.call-done = bf16[288,2304]{1,0:T(8,128)(2,1)} async-done(((bf16[2304,2304]{1,0:T(8,128)(2,1)}), bf16[288,2304]{1,0:T(8,128)(2,1)}) %reduce-scatter.14.cloned.1.call-update) | async-done | bytes 1327120 | tf_op jit(solution)/shard_map/reduce_scatter | solution.py:264
  2384.6 183.1 %reduce-scatter.12.cloned.1.call-done = bf16[288,2304]{1,0:T(8,128)(2,1)} async-done(((bf16[2304,2304]{1,0:T(8,128)(2,1)}), bf16[288,2304]{1,0:T(8,128)(2,1)}) %reduce-scatter.12.cloned.1.call-update) | async-done | bytes 1327120 | tf_op jit(solution)/shard_map/reduce_scatter | solution.py:261
  2567.7 182.5 %reduce-scatter.10.cloned.1.call-done = bf16[288,2304]{1,0:T(8,128)(2,1)} async-done(((bf16[2304,2304]{1,0:T(8,128)(2,1)}), bf16[288,2304]{1,0:T(8,128)(2,1)}) %reduce-scatter.10.cloned.1.call-update) | async-done | bytes 1327120 | tf_op jit(solution)/shard_map/reduce_scatter | solution.py:258
  2750.2 183.1 %reduce-scatter.8.cloned.1.call-done = bf16[288,2304]{1,0:T(8,128)(2,1)} async-done(((bf16[2304,2304]{1,0:T(8,128)(2,1)}), bf16[288,2304]{1,0:T(8,128)(2,1)}) %reduce-scatter.8.cloned.1.call-update) | async-done | bytes 1327120 | tf_op jit(solution)/shard_map/reduce_scatter | solution.py:255
  2933.3 425.6 %reduce-scatter.20.cloned.1.call-done = bf16[720,2304]{1,0:T(8,128)(2,1)} async-done(((bf16[5760,2304]{1,0:T(8,128)(2,1)}), bf16[720,2304]{1,0:T(8,128)(2,1)}) %reduce-scatter.20.cloned.1.call-update) | async-done | bytes 3317776 | tf_op jit(solution)/shard_map/reduce_scatter | solution.py:182
  3358.9 425.8 %reduce-scatter.18.cloned.1.call-done = bf16[288,5760]{1,0:T(8,128)(2,1)} async-done(((bf16[2304,5760]{1,0:T(8,128)(2,1)}), bf16[288,5760]{1,0:T(8,128)(2,1)}) %reduce-scatter.18.cloned.1.call-update) | async-done | bytes 3317776 | tf_op jit(solution)/shard_map/reduce_scatter | solution.py:179
  3784.7 425.6 %reduce-scatter.16.cloned.1.call-done = bf16[288,5760]{1,0:T(8,128)(2,1)} async-done(((bf16[2304,5760]{1,0:T(8,128)(2,1)}), bf16[288,5760]{1,0:T(8,128)(2,1)}) %reduce-scatter.16.cloned.1.call-update) | async-done | bytes 3317776 | tf_op jit(solution)/shard_map/reduce_scatter | solution.py:176
  4211.4 7.7 fusion.48
  4219.2 7.9 convolution_add_fusion.1
  4227.1 3.8 fusion.18
  4231.0 36.4 all-reduce.4
  4267.5 6.8 all-reduce.6
  4275.6 1.4 fusion.17
  4277.7 14.4 fusion.2
  4292.2 186.7 %all-reduce.10.cloned.1.call-done = (bf16[288,2304]{1,0:T(8,128)(2,1)}, bf16[288,2304]{1,0:T(8,128)(2,1)}, bf16[288,2304]{1,0:T(8,128)(2,1)}, bf16[288,2304]{1,0...) async-done(((bf16[288,2304]{1,0:T(8,128)(2,1)}, bf16[288,2304]{1,0:T(8,128)(2,1)}, bf16[288,2304]{1,0:T(8,128)(2,1)}, ...) | async-done | bytes 15261712 | tf_op jit(solution)/shard_map/psum | solution.py:270
  4478.9 3.1 convert_element_type.240
  4482.0 1.7 convert_element_type.242
  4483.8 1.7 convert_element_type.244
  4485.7 1.7 convert_element_type.246
  4487.4 1.2 copy-done.17
  4488.6 3.3 convert_element_type.250
  4491.9 3.3 convert_element_type.252
  4495.2 3.3 convert_element_type.254
  (168 shorter events, 17.8 us)
Async XLA Ops:
  7.2 159.3 %all-gather.8.cloned.1.call-start = ((), (), s32[]{:S(2)}) async-start(), calls=%async_computation.7 | async-start | bytes 11943936 | tf_op jit(solution)/shard_map/all_gather | solution.py:100
  7.2 3.2 copy-start.18
  10.4 309.5 %all-gather.10.cloned.1.call-start = ((), (), s32[]{:S(2)}) async-start(), calls=%async_computation.8 | async-start | bytes 11943936 | tf_op jit(solution)/shard_map/all_gather | solution.py:98
  11.6 461.7 %all-gather.12.cloned.1.call-start = ((), (), s32[]{:S(2)}) async-start(), calls=%async_computation.9 | async-start | bytes 11943936 | tf_op jit(solution)/shard_map/all_gather | solution.py:99
  11.7 3.2 copy-start.19
  14.8 611.8 %all-gather.14.cloned.1.call-start = ((), (), s32[]{:S(2)}) async-start(), calls=%async_computation.10 | async-start | bytes 11943936 | tf_op jit(solution)/shard_map/all_gather | solution.py:101
  16.1 1116.9 %all-gather.16.cloned.1.call-start = ((), (), s32[]{:S(2)}) async-start(), calls=%async_computation.11 | async-start | bytes 29859840 | tf_op jit(solution)/shard_map/all_gather | solution.py:133
  21.1 1620.1 %all-gather.18.cloned.1.call-start = ((), (), s32[]{:S(2)}) async-start(), calls=%async_computation.12 | async-start | bytes 29859840 | tf_op jit(solution)/shard_map/all_gather | solution.py:134
  26.9 2122.7 %all-gather.20.cloned.1.call-start = ((), (), s32[]{:S(2)}) async-start(), calls=%async_computation.13 | async-start | bytes 29859840 | tf_op jit(solution)/shard_map/all_gather | solution.py:135
  31.9 0.7 copy-start.44
  31.9 0.7 copy-start.45
  31.9 0.7 copy-start.43
  31.9 42.6 copy-start.47
  31.9 42.8 copy-start.46
  31.9 43.9 copy-start
  31.9 2352.7 %reduce-scatter.14.cloned.1.call-start = ((), (), s32[]{:S(2)}) async-start(), calls=%async_computation.17 | async-start | bytes 11943936 | tf_op jit(solution)/shard_map/reduce_scatter | solution.py:264
  76.1 404.5 %copy-start.34 = (f32[128,32]{0,1:T(8,128)}, f32[128,32]{0,1:T(8,128)S(1)}, u32[]{:S(2)}) copy-start(f32[128,32]{0,1:T(8,128)S(1)} %get-tuple-element.45) | copy-start | bytes 49156
  76.1 404.5 %copy-start.36 = (f32[128,32]{0,1:T(8,128)}, f32[128,32]{0,1:T(8,128)S(1)}, u32[]{:S(2)}) copy-start(f32[128,32]{0,1:T(8,128)S(1)} %get-tuple-element.46) | copy-start | bytes 49156
  480.6 0.7 copy-start.41
  481.0 1.0 copy-start.24
  481.0 1.0 copy-start.26
  481.0 1.0 copy-start.28
  481.0 1.1 copy-start.30
  482.0 1.2 copy-start.20
  483.7 148.7 %copy-start.13 = (bf16[36,64,128]{2,1,0:T(8,128)(2,1)}, bf16[36,64,128]{2,1,0:T(8,128)(2,1)S(1)}, u32[]{:S(2)}) copy-start(bf16[36,64,128]{2,1,0:T(8,128)(2,1)S(1)} %convolution_convert_fusion.10) | copy-start | bytes 1769476
  626.6 6.8 copy-start.33
  632.4 1.0 copy-start.1
  632.4 1.0 copy-start.42
  2195.8 3.3 copy-start.14
  2198.0 1.0 copy-start.3
  2204.6 363.2 %reduce-scatter.12.cloned.1.call-start = ((), (), s32[]{:S(2)}) async-start(), calls=%async_computation.16 | async-start | bytes 11943936 | tf_op jit(solution)/shard_map/reduce_scatter | solution.py:261
  2218.8 0.8 copy-start.9
  2225.6 524.6 %reduce-scatter.10.cloned.1.call-start = ((), (), s32[]{:S(2)}) async-start(), calls=%async_computation.15 | async-start | bytes 11943936 | tf_op jit(solution)/shard_map/reduce_scatter | solution.py:258
  2225.6 2.0 copy-start.32
  2227.6 1.0 copy-start.29
  2227.7 1.0 copy-start.31
  2228.7 1.0 copy-start.25
  2228.7 1.0 copy-start.27
  2229.8 0.7 copy-start.35
  2229.8 0.7 copy-start.37
  2230.9 5.8 copy-start.11
  2236.7 696.6 %reduce-scatter.8.cloned.1.call-start = ((), (), s32[]{:S(2)}) async-start(), calls=%async_computation.14 | async-start | bytes 11943936 | tf_op jit(solution)/shard_map/reduce_scatter | solution.py:255
  2242.6 1.4 copy-start.6
  2242.6 1116.3 %reduce-scatter.20.cloned.1.call-start = ((), (), s32[]{:S(2)}) async-start(), calls=%async_computation.20 | async-start | bytes 29859840 | tf_op jit(solution)/shard_map/reduce_scatter | solution.py:182
  2256.9 1.4 copy-start.8
  2256.9 1527.8 %reduce-scatter.18.cloned.1.call-start = ((), (), s32[]{:S(2)}) async-start(), calls=%async_computation.19 | async-start | bytes 29859840 | tf_op jit(solution)/shard_map/reduce_scatter | solution.py:179
  2270.9 1.4 copy-start.5
  2270.9 1939.4 %reduce-scatter.16.cloned.1.call-start = ((), (), s32[]{:S(2)}) async-start(), calls=%async_computation.18 | async-start | bytes 29859840 | tf_op jit(solution)/shard_map/reduce_scatter | solution.py:176
  2284.8 2194.1 %all-reduce.10.cloned.1.call-start = ((), (), s32[]{:S(2)}) async-start(), calls=%async_computation.21 | async-start | bytes 30523392 | tf_op jit(solution)/shard_map/psum | solution.py:270
  4210.3 1.1 copy-start.12
  4211.4 15.6 slice-start
  4211.4 15.7 slice-start.1
  4219.1 7.9 slice-start.2
  4219.1 7.9 copy-start.10
  4227.1 3.9 copy-start.40
  4227.1 48.4 %copy-start.4 = (f32[128,2304]{1,0:T(8,128)S(1)}, f32[128,2304]{1,0:T(8,128)}, u32[]{:S(2)}) copy-start(f32[128,2304]{1,0:T(8,128)} %copy-done.3) | copy-start | bytes 3538948
  4275.5 1.4 copy-start.2
  4275.6 2.2 copy-start.7
  4478.9 3.1 copy-start.23
  4482.0 1.8 copy-start.22
  4483.8 1.8 copy-start.21
  4485.7 2.9 copy-start.17
  4488.6 3.3 copy-start.16
  4491.9 3.3 copy-start.15
  (2 other events, 1.2 us)
Sparse Core Ops, SparseCore 0:
  10.8 155.6 all-gather.7
  169.2 150.6 all-gather.9
  322.7 150.6 all-gather.11
  475.9 150.6 all-gather.13
  628.6 504.4 all-gather.15
  1135.0 506.2 all-gather.17
  1643.3 506.1 all-gather.19
  2204.7 179.9 reduce-scatter.13
  2388.7 179.0 reduce-scatter.11
  2571.2 179.0 reduce-scatter.9
  2754.2 179.0 reduce-scatter.7
  2937.1 421.7 reduce-scatter.19
  3362.9 421.7 reduce-scatter.17
  3788.5 421.7 reduce-scatter.15
  4213.4 265.4 all-reduce.9
where the time goes:
time: 4510 us
  waiting for transfers between devices  4130 us (92%)
  matrix products  209 us (5%)
  blocking collectives  82.8 us (2%)
  other arithmetic  52.6 us (1%)
    all_gather x1, waiting for transfers between devices, local(): lax.all_gather(w_gate.astype(jnp.bfloat16), 'shard', axis=0, tiled=True)  499 us
    all_gather x1, waiting for transfers between devices, local(): lax.all_gather(w_down.astype(jnp.bfloat16), 'shard', axis=0, tiled=True)  494 us
    all_gather x1, waiting for transfers between devices, local(): lax.all_gather(w_up.astype(jnp.bfloat16), 'shard', axis=0, tiled=True)  494 us
    reduce_scatter x1, waiting for transfers between devices, local(): lax.psum_scatter(grad_up.astype(jnp.bfloat16), 'shard', scatter_dimension...  426 us
    reduce_scatter x1, waiting for transfers between devices, local(): lax.psum_scatter(grad_down.astype(jnp.bfloat16), 'shard', scatter_dimensi...  426 us
    reduce_scatter x1, waiting for transfers between devices, local(): lax.psum_scatter(grad_gate.astype(jnp.bfloat16), 'shard', scatter_dimensi...  426 us
    psum x1, waiting for transfers between devices, local(): lax.psum(attn_group[1].astype(jnp.bfloat16), 'rep').astype(jnp.float32)  187 us
    reduce_scatter x1, waiting for transfers between devices, local(): lax.psum_scatter(grad_value_w.astype(jnp.bfloat16), 'shard', scatter_dime...  183 us
  transfers between devices with their start and end apart: 15, of which 15 were waited for; matrix products, arithmetic and copies ran while one was open for 4% of the time, Pallas kernels for 0%

commit v1 on v0

v1 whole, which is shorter than its diff:
```python
import math

import jax
import jax.numpy as jnp
from jax import lax
from jax.sharding import PartitionSpec as P

HD = 64
PIC = 64

EPSILON = 1e-05
BRANCH_SCALE = 1.4 / math.sqrt(40.0)
MASKED = -1e30
F32 = jnp.float32
BF16 = jnp.bfloat16


def mm(left, right, contract):
    return lax.dot_general(left, right, ((contract[0], contract[1]), ((), ())), preferred_element_type=F32)


def layout(lengths, starts, row_count):
    places = jnp.arange(row_count, dtype=jnp.int32)
    bounds = jnp.cumsum(lengths)
    firsts = bounds - lengths
    member = (places[:, None] >= firsts[None, :]) & (places[:, None] < bounds[None, :])
    doc_of = jnp.sum(
        jnp.where(member, jnp.arange(lengths.shape[0], dtype=jnp.int32)[None, :], 0), axis=1
    )
    starting = jnp.sum(jnp.where(member, firsts[None, :], 0), axis=1)
    inside = (places[None, :] >= starts[:, None]) & (places[None, :] < starts[:, None] + PIC)
    shared = jnp.any(inside[:, :, None] & inside[:, None, :], axis=0)
    causal = places[None, :] <= places[:, None]
    allowed = (doc_of[:, None] == doc_of[None, :]) & (causal | shared)
    return (places - starting, allowed)


def angles(offsets, head_size):
    half_size = head_size // 2
    freq_table = jnp.exp(
        jnp.arange(half_size, dtype=F32) * (-2.0 * math.log(10000.0) / head_size)
    )
    turned = offsets.astype(F32)[..., None] * freq_table
    return jnp.cos(turned)[:, :, None, :], jnp.sin(turned)[:, :, None, :]


def rotate(values, cosine, sine):
    half_size = values.shape[-1] // 2
    first_half = values[..., :half_size]
    second_half = values[..., half_size:]
    return jnp.concatenate(
        [first_half * cosine - second_half * sine, second_half * cosine + first_half * sine],
        axis=-1,
    )


def build(rep, shard):
    n = shard

    def gather_shard(piece):
        return lax.all_gather(piece, "shard", axis=0, tiled=True)

    def scatter_shard(whole):
        return lax.psum_scatter(whole, "shard", scatter_dimension=0, tiled=True)

    def exchange(blocks):
        return lax.all_to_all(blocks, "shard", split_axis=0, concat_axis=0, tiled=True)

    def gather_rep(piece):
        return lax.all_gather(piece, "rep", axis=0, tiled=False)

    def scatter_rep(whole):
        return lax.psum_scatter(whole, "rep", scatter_dimension=0, tiled=False)

    def local(
        tokens,
        doc_lengths,
        pic_starts,
        attn_gain,
        w_query,
        w_key,
        w_value,
        w_out,
        ffn_gain,
        w_gate,
        w_up,
        w_down,
        cotangent,
    ):
        rows, width = tokens.shape
        heads = width // HD
        slots = -(-heads // n)
        block = slots * HD
        spare = n * block - width
        depth = w_query.shape[0]
        part = depth // rep
        ff = w_gate.shape[1]
        cols = ff // n
        all_rows = n * rows
        me = lax.axis_index("shard")
        mine = lax.axis_index("rep")
        gain_one = attn_gain.astype(BF16).astype(F32)[:, None]
        gain_two = ffn_gain.astype(BF16).astype(F32)[:, None]

        def quarter(array):
            return lax.dynamic_slice_in_dim(array, mine * part, part, 0)

        def scaled(weight, gain):
            return (quarter(weight).astype(BF16).astype(F32) * quarter(gain)).astype(BF16)

        def head_blocks(weight):
            return jnp.pad(weight, ((0, 0), (0, spare))).reshape(weight.shape[0], n, block)

        qkv_part = jnp.concatenate(
            [head_blocks(scaled(w, gain_one)) for w in (w_query, w_key, w_value)], axis=2
        ).transpose(1, 0, 2)
        qkv_w = gather_rep(exchange(qkv_part)).transpose(1, 0, 2, 3).reshape(width, 3 * block)
        out_part = gather_shard(quarter(w_out).astype(BF16)).reshape(n, part, width)
        out_w = gather_rep(out_part).transpose(1, 0, 2, 3).reshape(width, width)
        out_w = jnp.pad(out_w, ((0, spare), (0, 0)))
        ffn_part = jnp.concatenate(
            [scaled(w, gain_two).reshape(part, n, cols) for w in (w_gate, w_up)], axis=2
        ).transpose(1, 0, 2)
        ffn_w = gather_rep(exchange(ffn_part)).transpose(1, 0, 2, 3).reshape(width, 2 * cols)
        down_w = w_down.astype(BF16)

        inputs = gather_shard(tokens).astype(F32)
        lengths = lax.all_gather(doc_lengths, "shard", axis=0, tiled=True)
        starts = lax.all_gather(pic_starts, "shard", axis=0, tiled=True)
        offsets, allowed = jax.vmap(lambda a, b: layout(a, b, rows))(lengths, starts)
        cosine, sine = angles(offsets, HD)
        scale_one = lax.rsqrt(jnp.mean(inputs * inputs, axis=-1, keepdims=True) + EPSILON)
        normed_one = (inputs * scale_one).astype(BF16)
        qkv = mm(normed_one, qkv_w, ((1,), (0,)))

        def split_heads(values):
            return values.reshape(n, rows, slots, HD)

        query = rotate(split_heads(qkv[:, :block]), cosine, sine).astype(BF16)
        keys = rotate(split_heads(qkv[:, block : 2 * block]), cosine, sine).astype(BF16)
        values = split_heads(qkv[:, 2 * block :].astype(BF16))
        scores = jnp.einsum("rqhd,rkhd->rhqk", query, keys, preferred_element_type=F32) * HD**-0.5
        scores = jnp.where(allowed[:, None], scores, MASKED)
        expo = jnp.exp(scores - jnp.max(scores, axis=-1, keepdims=True))
        probs = expo / jnp.sum(expo, axis=-1, keepdims=True)
        probs_low = probs.astype(BF16)
        mixed = jnp.einsum("rhqk,rkhd->rqhd", probs_low, values, preferred_element_type=F32)
        mixed = mixed.astype(BF16).reshape(all_rows, block)
        mixed_all = lax.all_gather(mixed, "shard", axis=0, tiled=False)
        mixed_all = mixed_all.transpose(1, 0, 2).reshape(all_rows, n * block)
        middle = inputs + BRANCH_SCALE * mm(mixed_all, out_w, ((1,), (0,)))

        scale_two = lax.rsqrt(jnp.mean(middle * middle, axis=-1, keepdims=True) + EPSILON)
        normed_two = (middle * scale_two).astype(BF16)
        both = mm(normed_two, ffn_w, ((1,), (0,)))
        gate_act = both[:, :cols]
        up_act = both[:, cols:]
        sigmoid_gate = jax.nn.sigmoid(gate_act)
        silu_gate = gate_act * sigmoid_gate
        inner = (silu_gate * up_act).astype(BF16)
        grad_result = cotangent.astype(F32)
        grad_branch = gather_shard((BRANCH_SCALE * grad_result).astype(BF16))
        grad_inner = mm(grad_branch, down_w, ((1,), (1,)))
        grad_gate_act = (
            grad_inner * up_act * sigmoid_gate * (1.0 + gate_act * (1.0 - sigmoid_gate))
        ).astype(BF16)
        grad_up_act = (grad_inner * silu_gate).astype(BF16)
        grad_both = jnp.concatenate([grad_gate_act, grad_up_act], axis=1)
        grad_normed_two = scatter_shard(mm(grad_both, ffn_w, ((1,), (1,))).astype(BF16)).astype(F32)
        my_middle = lax.dynamic_slice_in_dim(middle, me * rows, rows, 0)
        my_scale_two = lax.dynamic_slice_in_dim(scale_two, me * rows, rows, 0)
        my_normed_two = my_middle * my_scale_two
        inner_mean = jnp.mean(grad_normed_two * my_normed_two, axis=-1, keepdims=True)
        grad_middle = grad_result + my_scale_two * (grad_normed_two - my_normed_two * inner_mean)
        branch = scatter_shard(mm(inner, down_w, ((1,), (0,))).astype(BF16)).astype(F32)
        out_tokens = (my_middle + BRANCH_SCALE * branch).astype(BF16)

        def down_sum(grad):
            return lax.psum(grad.astype(BF16), "rep").astype(F32)

        def to_rows(grad):
            piece = grad.astype(BF16).reshape(n, rep, part, grad.shape[1]).transpose(1, 0, 2, 3)
            piece = gather_rep(exchange(scatter_rep(piece)))
            return piece.transpose(0, 2, 1, 3).reshape(depth, n, grad.shape[1]).astype(F32)

        grad_down = down_sum(mm(inner, grad_branch, ((0,), (0,))))
        grad_ffn = to_rows(mm(normed_two, grad_both, ((0,), (0,))))
        raw_gate = grad_ffn[:, :, :cols].reshape(depth, ff)
        raw_up = grad_ffn[:, :, cols:].reshape(depth, ff)

        def low(weight):
            return weight.astype(BF16).astype(F32)

        grad_gain_two = jnp.sum(low(w_gate) * raw_gate + low(w_up) * raw_up, axis=1)
        grad_gate = raw_gate * gain_two
        grad_up = raw_up * gain_two

        grad_attn = (BRANCH_SCALE * grad_middle).astype(BF16)
        grad_mixed = mm(grad_attn, out_w, ((1,), (1,))).astype(BF16)
        grad_mixed = exchange(grad_mixed.reshape(rows, n, block).transpose(1, 0, 2))
        grad_mixed = grad_mixed.reshape(n, rows, slots, HD)
        grad_attn_cols = exchange(grad_attn.reshape(rows, n, depth).transpose(1, 0, 2))
        grad_out = to_rows(
            mm(mixed_all[:, :width], grad_attn_cols.reshape(all_rows, depth), ((0,), (0,)))
        ).reshape(depth, width)
        grad_values = jnp.einsum("rhqk,rqhd->rkhd", probs_low, grad_mixed, preferred_element_type=F32)
        grad_probs = jnp.einsum("rqhd,rkhd->rhqk", grad_mixed, values, preferred_element_type=F32)
        grad_scores = (
            probs * (grad_probs - jnp.sum(probs * grad_probs, axis=-1, keepdims=True))
        ).astype(BF16)
        grad_query = jnp.einsum("rhqk,rkhd->rqhd", grad_scores, keys, preferred_element_type=F32)
        grad_keys = jnp.einsum("rhqk,rqhd->rkhd", grad_scores, query, preferred_element_type=F32)
        grad_query = rotate(grad_query * HD**-0.5, cosine, -sine)
        grad_keys = rotate(grad_keys * HD**-0.5, cosine, -sine)
        grad_qkv = jnp.concatenate(
            [g.astype(BF16).reshape(all_rows, block) for g in (grad_query, grad_keys, grad_values)],
            axis=1,
        )
        grad_normed_one = scatter_shard(mm(grad_qkv, qkv_w, ((1,), (1,))).astype(BF16)).astype(F32)
        my_inputs = tokens.astype(F32)
        my_scale_one = lax.rsqrt(jnp.mean(my_inputs * my_inputs, axis=-1, keepdims=True) + EPSILON)
        my_normed_one = my_inputs * my_scale_one
        inner_mean = jnp.mean(grad_normed_one * my_normed_one, axis=-1, keepdims=True)
        input_grad = grad_middle + my_scale_one * (grad_normed_one - my_normed_one * inner_mean)
        grad_attn_w = to_rows(mm(normed_one, grad_qkv, ((0,), (0,))))
        raw_query, raw_key, raw_value = (
            grad_attn_w[:, :, k * block : (k + 1) * block].reshape(depth, n * block)[:, :width]
            for k in range(3)
        )
        grad_gain_one = jnp.sum(
            low(w_query) * raw_query + low(w_key) * raw_key + low(w_value) * raw_value, axis=1
        )
        return (
            out_tokens,
            input_grad,
            grad_gain_one,
            raw_query * gain_one,
            raw_key * gain_one,
            raw_value * gain_one,
            grad_out,
            grad_gain_two,
            grad_gate,
            grad_up,
            grad_down,
        )

    return local


def solution(mesh):
    tokens = P(("rep", "shard"), None)
    weight = P("shard", None)
    gain = P("shard")
    return jax.shard_map(
        build(mesh.shape["rep"], mesh.shape["shard"]),
        mesh=mesh,
        in_specs=(
            tokens,
            tokens,
            tokens,
            gain,
            weight,
            weight,
            weight,
            weight,
            gain,
            weight,
            weight,
            weight,
            tokens,
        ),
        out_specs=(
            tokens,
            tokens,
            gain,
            weight,
            weight,
            weight,
            weight,
            gain,
            weight,
            weight,
            weight,
        ),
        check_vma=False,
    )
```

time: 4510 us -> 1480 us (0.33)
  waiting for transfers between devices: 4130 us -> 791 us
  blocking collectives: 82.8 us -> 296 us
  local copies, waits for them, and re-layouts: 17 us -> 157 us
  matrix products: 209 us -> 126 us
    reduce_scatter x7 -> x3, waiting for transfers between devices: 1930 us -> 186 us  [scatter_shard(): return lax.psum_scatter(whole, 'shard', scatter_dimension=0, tiled=True)]
    all_gather x7 -> x10, waiting for transfers between devices: 2010 us -> 334 us  [the longest x6 174 us: gather_rep(): return lax.all_gather(piece, 'rep', axis=0, tiled=False)]
    unnamed x15, waiting for transfers between devices: 0.25 us -> 271 us
    all_to_all x0 -> x5, blocking collectives: none -> 261 us  [exchange(): lax.all_to_all(blocks, 'shard', split_axis=0, concat_axis=0, tiled=True)]
    psum x1 -> x0, waiting for transfers between devices: 187 us -> none  [local(): lax.psum(attn_group[1].astype(jnp.bfloat16), 'rep').astype(jnp.float32)]
    dot_general x27 -> x17, matrix products: 209 us -> 124 us  [the longest x12 116 us: mm(): lax.dot_general(left, right, ((contract[0], contract[1]), ((), ())), pref...]
    unnamed x2 -> x0, blocking collectives: 76 us -> none
    convert_element_type x2 -> x12, local copies, waits for them, and re-layouts: 3.17 us -> 59.9 us  [the longest x4 35.6 us: to_rows(): piece.transpose(0, 2, 1, 3).reshape(depth, n, grad.shape[1]).astype(F32)]
  transfers between devices with their start and end apart: 15 -> 16, of which waited for: 15 -> 12; matrix products, arithmetic and copies ran while one was open for 4% -> 15% of each run, Pallas kernels for 0% -> 0%
where the time goes in v1:
time: 1480 us; the launch traced here: 1470 us
  waiting for transfers between devices  791 us (53%)
  blocking collectives  296 us (20%)
  local copies, waits for them, and re-layouts  157 us (11%)
  matrix products  126 us (9%)
  other arithmetic  70.6 us (5%)
  between operations  14.8 us (1%)
    unnamed x15, waiting for transfers between devices  271 us
    all_to_all x5, blocking collectives, exchange(): lax.all_to_all(blocks, 'shard', split_axis=0, concat_axis=0, tiled=True)  261 us
    reduce_scatter x3, waiting for transfers between devices, scatter_shard(): return lax.psum_scatter(whole, 'shard', scatter_dimension=0, tiled=True)  186 us
    all_gather x6, waiting for transfers between devices, gather_rep(): return lax.all_gather(piece, 'rep', axis=0, tiled=False)  174 us
    dot_general x12, matrix products, mm(): lax.dot_general(left, right, ((contract[0], contract[1]), ((), ())), pref...  116 us
    all_gather x1, waiting for transfers between devices, local(): mixed_all = lax.all_gather(mixed, 'shard', axis=0, tiled=False)  82.2 us
    all_gather x3, waiting for transfers between devices, gather_shard(): return lax.all_gather(piece, 'shard', axis=0, tiled=True)  77.6 us
    convert_element_type x4, local copies, waits for them, and re-layouts, to_rows(): piece.transpose(0, 2, 1, 3).reshape(depth, n, grad.shape[1]).astype(F32)  35.6 us
  transfers between devices with their start and end apart: 16, of which 12 were waited for; matrix products, arithmetic and copies ran while one was open for 15% of the time, Pallas kernels for 0%

profile of v1, /device:TPU:0, one launch (start us, length us, event | category | flops | bytes accessed | tf_op | source)
XLA Modules:
  0.0 1467.3 jit_solution(3400168331127787797)
XLA Ops:
  9.3 2.5 multiply_convert_fusion.10
  17.0 2.1 reshape.227
  21.2 48.4 %all_to_all.35 = bf16[8,72,960]{2,1,0:T(8,128)(2,1)} all-to-all(bf16[8,72,960]{2,1,0:T(8,128)(2,1)S(1)} %copy.232), channel_id=1, replica_groups=mesh['rep'=4,'shard'=8] {'shard'}, dimensions={0} | all-to-all | bytes 2211840 | tf_op jit(solution)/shard_map/all_to_all | solution.py:67
  71.2 2.2 multiply_convert_fusion.6
  77.5 69.0 %all_to_all.36 = bf16[8,72,1440]{2,1,0:T(8,128)(2,1)} all-to-all(bf16[8,72,1440]{2,1,0:T(8,128)(2,1)S(1)} %copy.246), channel_id=1, replica_groups=mesh['rep'=4,'shard'=8] {'shard'}, dimensions={0} | all-to-all | bytes 3317760 | tf_op jit(solution)/shard_map/all_to_all | solution.py:67
  146.6 18.5 %all-gather.6 = s32[8,1,2]{2,1,0:T(1,128)S(1)} all-gather(s32[1,1,2]{2,1,0:T(1,128)S(1)} %bitcast.171), channel_id=1, replica_groups=mesh['rep'=4,'shard'=8] {'shard'}, dimensions={0}, use_global_device_ids=true | all-gather | bytes 72 | tf_op jit(solution)/shard_map/all_gather | solution.py:129
  165.1 16.7 %all-gather.5 = s32[8,1,2]{2,1,0:T(1,128)S(1)} all-gather(s32[1,1,2]{2,1,0:T(1,128)S(1)} %bitcast.172), channel_id=1, replica_groups=mesh['rep'=4,'shard'=8] {'shard'}, dimensions={0}, use_global_device_ids=true | all-gather | bytes 72 | tf_op jit(solution)/shard_map/all_gather | solution.py:128
  185.0 3.4 fusion.5
  188.4 3.2 copy.233
  192.2 5.2 fusion.20
  201.6 2.4 fusion.67
  204.1 2.0 fusion.31
  207.4 2.1 all_gather_reshape.6
  209.8 26.6 %all-gather.22.cloned.1.call-done = bf16[576,2304]{1,0:T(8,128)(2,1)} async-done(((bf16[72,2304]{1,0:T(8,128)(2,1)}), bf16[576,2304]{1,0:T(8,128)(2,1)}) %all-gather.22.cloned.1.call-update) | async-done | bytes 2654224 | tf_op jit(solution)/shard_map/all_gather | solution.py:61
  237.4 49.8 %all-gather.30.cloned.1.call-done = bf16[32,72,1440]{2,1,0:T(8,128)(2,1)} async-done(((bf16[8,72,1440]{2,1,0:T(8,128)(2,1)}), bf16[32,72,1440]{2,1,0:T(8,128)(2,1)}) %all-gather.30.cloned.1.call-update) | async-done | bytes 6635536 | tf_op jit(solution)/shard_map/all_gather | solution.py:70
  287.2 6.7 copy.247
  293.9 82.2 %all-gather.20.cloned.1.call-done = bf16[8,1024,320]{1,2,0:T(8,128)(2,1)} async-done(((bf16[1,1024,320]{1,2,0:T(8,128)(2,1)}), bf16[8,1024,320]{1,2,0:T(8,128)(2,1)}) %all-gather.20.cloned.1.call-update) | async-done | bytes 5242896 | tf_op jit(solution)/shard_map/all_gather | solution.py:149
  376.1 70.6 %all-gather.24.cloned.1.call-done = bf16[4,8,72,2304]{3,2,0,1:T(8,128)(2,1)} async-done(((bf16[1,8,72,2304]{3,2,0,1:T(8,128)(2,1)}), bf16[4,8,72,2304]{3,2,0,1:T(8,128)(2,1)}) %all-gather.24.cloned.1.call-update) | async-done | bytes 10616848 | tf_op jit(solution)/shard_map/all_gather | solution.py:70
  446.7 19.7 %multiply_reduce_fusion = (f32[1024]{0:T(1024)S(1)}, f32[1024,2304]{1,0:T(8,128)}) fusion(bf16[1024,2560]{0,1:T(8,128)(2,1)} %bitcast.173, bf16[2304,2304]{1,0:T(8,128)(2,1)} %bitcast.145, bf16[1024,2304]{1,0:T(8,128)(2,1)} %all-gather.18.cloned.1.call-done), kind=kOutput, calls=%fused_computation.14 | convolution fusion | flops 12091390976 | bytes 30019584 | tf_op jit(solution)/shard_map/dot_general | solution.py:19
  466.4 12.0 fusion.62
  478.4 51.0 %all-gather.26.cloned.1.call-done = bf16[1024,2304]{1,0:T(8,128)(2,1)} async-done(((bf16[128,2304]{1,0:T(8,128)(2,1)}), bf16[1024,2304]{1,0:T(8,128)(2,1)}) %all-gather.26.cloned.1.call-update) | async-done | bytes 4718608 | tf_op jit(solution)/shard_map/all_gather | solution.py:61
  529.4 11.8 multiply_convert_fusion.2
  542.3 9.2 convolution_convert_fusion.3
  551.6 93.6 %reduce-scatter.9.cloned.1.call-done = bf16[128,2304]{1,0:T(8,128)(2,1)} async-done(((bf16[1024,2304]{1,0:T(8,128)(2,1)}), bf16[128,2304]{1,0:T(8,128)(2,1)}) %reduce-scatter.9.cloned.1.call-update) | async-done | bytes 589840 | tf_op jit(solution)/shard_map/reduce_scatter | solution.py:64
  649.9 4.8 all-to-all-start.4
  654.7 13.2 convolution_convert_fusion
  667.9 10.2 copy.262
  678.1 7.7 fusion.14
  686.9 6.0 all-to-all-start.2
  692.9 8.2 convolution_convert_fusion.5
  701.1 5.0 fusion.11
  706.1 2.9 copy.260
  709.9 2.1 multiply_reduce_fusion.1
  714.7 2.1 fusion.32
  720.3 6.6 convolution_convert_fusion.4
  727.0 6.5 copy.256
  735.1 9.2 convolution_convert_fusion.2
  745.6 8.6 convolution_convert_fusion.1
  755.4 270.2 %all-reduce.10.cloned.1.call-done = (bf16[4,8,72,960]{3,2,0,1:T(8,128)(2,1)}, bf16[4,8,72,288]{3,2,0,1:T(8,128)(2,1)}, bf16[4,8,72,1440]{3,2,0,1:T(8,128)(2,1)}, bf16[720,2304]{1,0:T(8,128)(2,1)}) async-done(((bf16[4,8,72,960]{3,2,0,1:T(8,128)(2,1)}, bf16[4,8,72,288]{3,2,0,1:T(8,128)(2,1)}, bf16[4,8,72,1440]{3,2,0,1:T(8,128)(2,1)}, bf16[720,2304]{1,0:T(8,128)(2,1)}), (bf16[4,8,72,960]{3,2,0,1:T(8,128)(2,1)}, ...) | async-done | bytes 15704080
  1027.3 27.2 %all_to_all.37 = bf16[8,72,288]{2,1,0:T(8,128)(2,1)} all-to-all(bf16[8,72,288]{2,1,0:T(8,128)(2,1)S(1)} %dynamic-slice_bitcast_fusion.2), channel_id=1, replica_groups=mesh['rep'=4,'shard'=8] {'shard'}, dimensions={0} | all-to-all | bytes 663552 | tf_op jit(solution)/shard_map/all_to_all | solution.py:67
  1056.6 52.5 %all_to_all.38 = bf16[8,72,960]{2,1,0:T(8,128)(2,1)} all-to-all(bf16[8,72,960]{2,1,0:T(8,128)(2,1)S(1)} %dynamic-slice_bitcast_fusion.1), channel_id=1, replica_groups=mesh['rep'=4,'shard'=8] {'shard'}, dimensions={0} | all-to-all | bytes 2211840 | tf_op jit(solution)/shard_map/all_to_all | solution.py:67
  1109.2 2.2 dynamic-slice_bitcast_fusion
  1111.5 63.5 %all_to_all.39 = bf16[8,72,1440]{2,1,0:T(8,128)(2,1)} all-to-all(bf16[8,72,1440]{2,1,0:T(8,128)(2,1)S(1)} %dynamic-slice_bitcast_fusion), channel_id=1, replica_groups=mesh['rep'=4,'shard'=8] {'shard'}, dimensions={0} | all-to-all | bytes 3317760 | tf_op jit(solution)/shard_map/all_to_all | solution.py:67
  1175.2 5.3 convert_element_type.305
  1182.0 91.9 %reduce-scatter.7.cloned.1.call-done = bf16[128,2304]{1,0:T(8,128)(2,1)} async-done(((bf16[1024,2304]{1,0:T(8,128)(2,1)}), bf16[128,2304]{1,0:T(8,128)(2,1)}) %reduce-scatter.7.cloned.1.call-update) | async-done | bytes 589840 | tf_op jit(solution)/shard_map/reduce_scatter | solution.py:64
  1273.9 3.3 fusion.39
  1277.3 18.6 %all-gather.34.cloned.1.call-done = bf16[32,72,288]{2,1,0:T(8,128)(2,1)} async-done(((bf16[8,72,288]{2,1,0:T(8,128)(2,1)}), bf16[32,72,288]{2,1,0:T(8,128)(2,1)}) %all-gather.34.cloned.1.call-update) | async-done | bytes 1327120 | tf_op jit(solution)/shard_map/all_gather | solution.py:70
  1297.6 2.4 copy.261
  1300.0 4.8 reshape.253
  1304.8 30.1 %all-gather.32.cloned.1.call-done = bf16[32,72,960]{2,1,0:T(8,128)(2,1)} async-done(((bf16[8,72,960]{2,1,0:T(8,128)(2,1)}), bf16[32,72,960]{2,1,0:T(8,128)(2,1)}) %all-gather.32.cloned.1.call-update) | async-done | bytes 4423696 | tf_op jit(solution)/shard_map/all_gather | solution.py:70
  1334.9 3.5 convert_bitcast_fusion.1
  1338.4 10.2 copy.257
  1348.6 9.7 fusion.64
  1358.3 4.7 reshape.245
  1363.1 4.7 reshape.244
  1367.8 5.0 reshape.243
  1372.9 9.6 slice_multiply_fusion
  1382.5 4.8 all-gather.36.cloned.1.call-done
  1387.2 10.0 convert_bitcast_fusion
  1397.3 18.3 %copy.263 = f32[4,72,8,1440]{3,2,1,0:T(8,128)} copy(f32[4,72,8,1440]{3,1,2,0:T(8,128)} %convert_bitcast_fusion) | data formatting | bytes 26542080 | tf_op jit(solution)/shard_map/convert_element_type | solution.py:184
  1415.5 12.5 fusion.63
  1428.0 8.5 reshape.251
  1436.5 8.5 reshape.250
  1445.0 15.6 %broadcast_multiply_fusion = (f32[288,5760]{1,0:T(8,128)}, f32[288]{0:T(512)}, f32[288,5760]{1,0:T(8,128)}) fusion(f32[288,5760]{1,0:T(8,128)} %reshape.251, f32[288]{0:T(512)S(1)} %copy-done.25, f32[288,5760]{1,0:T(8,128)} %param.23, f32[288,5760]{1,0:T(8,128)} %reshape.250, f32[288,5760]{1,0:T(8,128)} %param.22), kind=kLoop, calls=%fused_computation.26 | loop fusion | flops 16588512 | bytes 39815424 | tf_op jit(solution)/shard_map/mul | solution.py:196
  (178 shorter events, 50.8 us)
Async XLA Ops:
  7.2 62.5 %copy-start = (f32[288,2304]{1,0:T(8,128)S(1)}, f32[288,2304]{1,0:T(8,128)}, u32[]{:S(2)}) copy-start(f32[288,2304]{1,0:T(8,128)} %param.20) | copy-start | bytes 7962628
  7.2 177.8 %all-gather.18.cloned.1.call-start = ((), (), s32[]{:S(2)}) async-start(), calls=%async_computation.10 | async-start | bytes 5308416 | tf_op jit(solution)/shard_map/all_gather | solution.py:61
  7.9 180.5 %all-gather.28.cloned.1.call-start = ((), (), s32[]{:S(2)}) async-start(), calls=%async_computation.18 | async-start | bytes 5898240 | tf_op jit(solution)/shard_map/all_gather | solution.py:70
  8.7 0.6 copy-start.22
  21.2 49.3 %copy-start.26 = (f32[288]{0:T(512)S(1)}, f32[288]{0:T(512)}, u32[]{:S(2)}) copy-start(f32[288]{0:T(512)} %param.21) | copy-start | bytes 3460
  69.6 166.8 %all-gather.22.cloned.1.call-start = ((), (), s32[]{:S(2)}) async-start(), calls=%async_computation.12 | async-start | bytes 2985984 | tf_op jit(solution)/shard_map/all_gather | solution.py:61
  70.4 216.8 %all-gather.30.cloned.1.call-start = ((), (), s32[]{:S(2)}) async-start(), calls=%async_computation.19 | async-start | bytes 8847360 | tf_op jit(solution)/shard_map/all_gather | solution.py:70
  70.5 0.6 copy-start.24
  77.5 69.1 %copy-start.27 = (s32[1,2]{1,0:T(1,128)S(1)}, s32[1,2]{1,0:T(1,128)}, u32[]{:S(2)}) copy-start(s32[1,2]{1,0:T(1,128)} %param.15) | copy-start | bytes 28
  77.5 87.6 %copy-start.28 = (s32[1,2]{1,0:T(1,128)S(1)}, s32[1,2]{1,0:T(1,128)}, u32[]{:S(2)}) copy-start(s32[1,2]{1,0:T(1,128)} %param.14) | copy-start | bytes 28
  146.5 229.6 %all-gather.20.cloned.1.call-start = ((), (), s32[]{:S(2)}) async-start(), calls=%async_computation.11 | async-start | bytes 5898240 | tf_op jit(solution)/shard_map/all_gather | solution.py:149
  185.0 6.7 slice-start
  188.4 3.8 slice-start.1
  191.7 5.8 copy-start.7
  199.3 0.9 copy-start.19
  201.6 2.4 copy-start.12
  201.6 2.4 copy-start.14
  204.1 2.1 copy-start.9
  206.1 30.3 %copy-start.6 = (bf16[128,2304]{1,0:T(8,128)(2,1)S(1)}, bf16[128,2304]{1,0:T(8,128)(2,1)}, u32[]{:S(2)}) copy-start(bf16[128,2304]{1,0:T(8,128)(2,1)} %param.25) | copy-start | bytes 1769476
  209.5 237.2 %all-gather.24.cloned.1.call-start = ((), (), s32[]{:S(2)}) async-start(), calls=%async_computation.13 | async-start | bytes 13271040 | tf_op jit(solution)/shard_map/all_gather | solution.py:70
  236.4 293.0 %all-gather.26.cloned.1.call-start = ((), (), s32[]{:S(2)}) async-start(), calls=%async_computation.15 | async-start | bytes 5308416 | tf_op jit(solution)/shard_map/all_gather | solution.py:61
  237.4 407.9 %reduce-scatter.9.cloned.1.call-start = ((), (), s32[]{:S(2)}) async-start(), calls=%async_computation.16 | async-start | bytes 5308416 | tf_op jit(solution)/shard_map/reduce_scatter | solution.py:64
  446.7 19.7 %copy-start.3 = (bf16[8,4,72,1440]{3,2,1,0:T(8,128)(2,1)S(1)}, bf16[8,4,72,1440]{3,2,1,0:T(8,128)(2,1)}, u32[]{:S(2)}) copy-start(bf16[8,4,72,1440]{3,2,1,0:T(8,128)(2,1)} %copy.247) | copy-start | bytes 19906564
  529.4 12.9 copy-start.4
  541.2 1.1 copy-start.32
  541.2 10.3 copy-start.31
  649.9 37.0 %all-to-all-start.4 = ((bf16[8,128,288]{1,2,0:T(8,128)(2,1)}), bf16[8,128,288]{1,2,0:T(8,128)(2,1)S(1)}, u32[]{:S(2)}, u32[]{:S(2)}) async-start(bf16[8,128,288]{1,2,0:T(8,128)(2,1)} %bitcast.32), calls=%async_computation.7 | async-start | bytes 1179648 | tf_op jit(solution)/shard_map/all_to_all | solution.py:67
  686.9 23.1 %all-to-all-start.2 = ((bf16[8,128,320]{1,2,0:T(8,128)(2,1)}), bf16[8,128,320]{1,2,0:T(8,128)(2,1)}, u32[]{:S(2)}, u32[]{:S(2)}) async-start(bf16[8,128,320]{1,2,0:T(8,128)(2,1)} %bitcast.19), calls=%async_computation.4 | async-start | bytes 1310720 | tf_op jit(solution)/shard_map/all_to_all | solution.py:67
  692.9 332.8 %all-reduce.10.cloned.1.call-start = ((), (), s32[]{:S(2)}) async-start(), calls=%async_computation.23 | async-start | bytes 33767424
  706.1 3.9 copy-start.10
  709.9 2.1 copy-start.11
  712.1 1.0 copy-start.16
  712.1 1.1 copy-start.17
  713.2 1.0 copy-start.13
  713.2 1.1 copy-start.15
  714.7 2.1 copy-start.18
  716.9 3.5 slice-start.2
  717.8 2.5 slice-start.3
  719.1 1.3 copy-start.20
  733.5 1.5 copy-start.21
  733.5 447.0 %reduce-scatter.11.cloned.1.call-start = ((), (), s32[]{:S(2)}) async-start(), calls=%async_computation.17 | async-start | bytes 5308416 | tf_op jit(solution)/shard_map/reduce_scatter | solution.py:64
  744.2 1.4 copy-start.30
  744.2 529.7 %reduce-scatter.7.cloned.1.call-start = ((), (), s32[]{:S(2)}) async-start(), calls=%async_computation.14 | async-start | bytes 5308416 | tf_op jit(solution)/shard_map/reduce_scatter | solution.py:64
  754.1 0.7 copy-start.29
  754.2 541.7 %all-gather.34.cloned.1.call-start = ((), (), s32[]{:S(2)}) async-start(), calls=%async_computation.21 | async-start | bytes 2211840 | tf_op jit(solution)/shard_map/all_gather | solution.py:70
  1054.6 280.4 %all-gather.32.cloned.1.call-start = ((), (), s32[]{:S(2)}) async-start(), calls=%async_computation.20 | async-start | bytes 5898240 | tf_op jit(solution)/shard_map/all_gather | solution.py:70
  1109.2 278.0 %all-gather.36.cloned.1.call-start = ((), (), s32[]{:S(2)}) async-start(), calls=%async_computation.22 | async-start | bytes 8847360 | tf_op jit(solution)/shard_map/all_gather | solution.py:70
  1111.5 63.5 %copy-start.2 = (bf16[128,2304]{1,0:T(8,128)(2,1)S(1)}, bf16[128,2304]{1,0:T(8,128)(2,1)}, u32[]{:S(2)}) copy-start(bf16[128,2304]{1,0:T(8,128)(2,1)} %param.13) | copy-start | bytes 1769476
  1175.2 98.7 %copy-start.5 = (bf16[128,2304]{1,0:T(8,128)(2,1)S(1)}, bf16[128,2304]{1,0:T(8,128)(2,1)}, u32[]{:S(2)}) copy-start(bf16[128,2304]{1,0:T(8,128)(2,1)} %reduce-scatter.9.cloned.1.call-done) | copy-start | bytes 1769476
  1367.8 5.1 copy-start.8
  1367.8 5.1 copy-start.23
  1436.5 8.5 copy-start.25
  1445.0 15.6 %copy-start.1 = (f32[288,2304]{1,0:T(8,128)S(1)}, f32[288,2304]{1,0:T(8,128)}, u32[]{:S(2)}) copy-start(f32[288,2304]{1,0:T(8,128)} %param.20) | copy-start | bytes 7962628
Sparse Core Ops, SparseCore 0:
  10.2 129.7 all-gather.17
  141.5 36.9 all-gather.27
  181.3 55.0 all-gather.21
  237.8 49.4 all-gather.29
  289.8 86.2 all-gather.19
  377.5 69.1 all-gather.23
  449.5 79.8 all-gather.25
  551.7 93.5 reduce-scatter.8
  733.7 291.9 all-reduce.9
  1029.7 146.1 reduce-scatter.10
  1180.1 93.7 reduce-scatter.6
  1275.3 20.5 all-gather.33
  1297.4 37.4 all-gather.31
  1336.3 50.8 all-gather.35

commit v2 on v1

v2 whole, which is shorter than its diff:
```python
import functools
import math

import jax
import jax.numpy as jnp
from jax import lax
from jax.experimental import pallas as pl
from jax.experimental.pallas import tpu as pltpu
from jax.sharding import PartitionSpec as P

HD = 64
HALF = HD // 2
PIC = 64

EPSILON = 1e-05
BRANCH_SCALE = 1.4 / math.sqrt(40.0)
MASKED = -1e30
F32 = jnp.float32
BF16 = jnp.bfloat16


def mm(left, right, left_dim, right_dim):
    return lax.dot_general(
        left, right, (((left_dim,), (right_dim,)), ((), ())), preferred_element_type=F32
    )


def layout(lengths, starts, row_count):
    places = jnp.arange(row_count, dtype=jnp.int32)
    bounds = jnp.cumsum(lengths)
    firsts = bounds - lengths
    member = (places[:, None] >= firsts[None, :]) & (places[:, None] < bounds[None, :])
    doc_of = jnp.sum(
        jnp.where(member, jnp.arange(lengths.shape[0], dtype=jnp.int32)[None, :], 0), axis=1
    )
    starting = jnp.sum(jnp.where(member, firsts[None, :], 0), axis=1)
    inside = (places[None, :] >= starts[:, None]) & (places[None, :] < starts[:, None] + PIC)
    shared = jnp.any(inside[:, :, None] & inside[:, None, :], axis=0)
    causal = places[None, :] >= places[:, None]
    allowed = (doc_of[:, None] == doc_of[None, :]) & (causal | shared)
    return (places - starting, allowed)


def turn(values, cosine, sine):
    first, second = values[:HALF], values[HALF:]
    return jnp.concatenate([first * cosine - second * sine, second * cosine + first * sine], axis=0)


def probabilities(keys, query, bias):
    scores = mm(keys, query, 0, 0) * HD**-0.5 + bias
    expo = jnp.exp(scores - jnp.max(scores, axis=0, keepdims=True))
    return expo / jnp.sum(expo, axis=0, keepdims=True)


def attend_kernel(slots, qkv_ref, scale_ref, cos_ref, sin_ref, bias_ref, qkv_out_ref, mixed_ref):
    block = slots * HD
    scale = scale_ref[...]
    cosine, sine, bias = cos_ref[...], sin_ref[...], bias_ref[0]
    for head in range(slots):
        low, high = head * HD, (head + 1) * HD
        query = turn(qkv_ref[low:high, :] * scale, cosine, sine).astype(BF16)
        keys = turn(qkv_ref[block + low : block + high, :] * scale, cosine, sine).astype(BF16)
        values = (qkv_ref[2 * block + low : 2 * block + high, :] * scale).astype(BF16)
        qkv_out_ref[low:high, :] = query
        qkv_out_ref[block + low : block + high, :] = keys
        qkv_out_ref[2 * block + low : 2 * block + high, :] = values
        probs = probabilities(keys, query, bias).astype(BF16)
        mixed_ref[low:high, :] = mm(values, probs, 1, 0).astype(BF16)


def attend_back_kernel(slots, qkv_ref, grad_ref, scale_ref, cos_ref, sin_ref, bias_ref, out_ref):
    block = slots * HD
    scale = scale_ref[...]
    cosine, sine, bias = cos_ref[...], sin_ref[...], bias_ref[0]
    back = scale * HD**-0.5
    for head in range(slots):
        low, high = head * HD, (head + 1) * HD
        query = qkv_ref[low:high, :]
        keys = qkv_ref[block + low : block + high, :]
        values = qkv_ref[2 * block + low : 2 * block + high, :]
        grad = grad_ref[low:high, :]
        probs = probabilities(keys, query, bias)
        grad_values = mm(grad, probs.astype(BF16), 1, 1)
        grad_probs = mm(values, grad, 0, 0)
        inner = jnp.sum(probs * grad_probs, axis=0, keepdims=True)
        grad_scores = (probs * (grad_probs - inner)).astype(BF16)
        grad_query = turn(mm(keys, grad_scores, 1, 0) * back, cosine, -sine)
        grad_keys = turn(mm(query, grad_scores, 1, 1) * back, cosine, -sine)
        out_ref[low:high, :] = grad_query.astype(BF16)
        out_ref[block + low : block + high, :] = grad_keys.astype(BF16)
        out_ref[2 * block + low : 2 * block + high, :] = (grad_values * scale).astype(BF16)


def columns(height, rows):
    return pl.BlockSpec((height, rows), lambda r: (0, r))


def attention_specs(rows):
    return [
        columns(1, rows),
        columns(HALF, rows),
        columns(HALF, rows),
        pl.BlockSpec((1, rows, rows), lambda r: (r, 0, 0)),
    ]


def attend(slots, n, rows, qkv, scale, cosine, sine, bias):
    block = slots * HD
    tokens = n * rows
    flops = 4 * n * slots * rows * rows * HD
    return pl.pallas_call(
        functools.partial(attend_kernel, slots),
        grid=(n,),
        in_specs=[columns(3 * block, rows)] + attention_specs(rows),
        out_specs=[columns(3 * block, rows), columns(block, rows)],
        out_shape=[
            jax.ShapeDtypeStruct((3 * block, tokens), BF16),
            jax.ShapeDtypeStruct((block, tokens), BF16),
        ],
        cost_estimate=pl.CostEstimate(
            flops=flops, bytes_accessed=20 * block * tokens, transcendentals=n * slots * rows * rows
        ),
        name="attend",
    )(qkv, scale, cosine, sine, bias)


def attend_back(slots, n, rows, qkv, grad, scale, cosine, sine, bias):
    block = slots * HD
    tokens = n * rows
    flops = 10 * n * slots * rows * rows * HD
    return pl.pallas_call(
        functools.partial(attend_back_kernel, slots),
        grid=(n,),
        in_specs=[columns(3 * block, rows), columns(block, rows)] + attention_specs(rows),
        out_specs=columns(3 * block, rows),
        out_shape=jax.ShapeDtypeStruct((3 * block, tokens), BF16),
        cost_estimate=pl.CostEstimate(
            flops=flops, bytes_accessed=14 * block * tokens, transcendentals=n * slots * rows * rows
        ),
        name="attend_back",
    )(qkv, grad, scale, cosine, sine, bias)


def build(rep, n):
    cycle = list(range(0, n, 2)) + list(range(n - 1, 0, -2)) if n % 2 == 0 else list(range(n))
    place = [cycle.index(device) for device in range(n)]
    to_right = [(cycle[i], cycle[(i + 1) % n]) for i in range(n)]
    to_left = [(b, a) for a, b in to_right]
    steps_right = n // 2
    steps_left = n - 1 - steps_right
    outer = rep // 2
    core_pairs = [(i, i ^ 1) for i in range(rep)]
    chip_pairs = [(i, (i + 2) % rep) for i in range(rep)]

    def right(x):
        return lax.ppermute(x, "shard", to_right)

    def left(x):
        return lax.ppermute(x, "shard", to_left)

    def core_swap(x):
        return lax.ppermute(x, "rep", core_pairs)

    def chip_swap(x):
        return lax.ppermute(x, "rep", chip_pairs)

    def ring_device(offset):
        at = jnp.asarray(place, jnp.int32)[lax.axis_index("shard")]
        return jnp.asarray(cycle, jnp.int32)[(at + offset) % n]

    def ring_gather(piece):
        pieces = [(ring_device(0), piece)]
        going_right = going_left = piece
        for step in range(1, steps_right + 1):
            going_right = right(going_right)
            pieces.append((ring_device(-step), going_right))
            if step <= steps_left:
                going_left = left(going_left)
                pieces.append((ring_device(step), going_left))
        return pieces

    def gather_shard(piece):
        whole = jnp.zeros((n,) + piece.shape, piece.dtype)
        for device, part in ring_gather(piece):
            whole = lax.dynamic_update_index_in_dim(whole, part, device, 0)
        return whole

    def scatter_shard(parts):
        def term(offset):
            return lax.dynamic_index_in_dim(parts, ring_device(offset), 0, keepdims=False).astype(F32)

        going_right = term(steps_right).astype(BF16)
        going_left = term(-steps_left).astype(BF16)
        for step in range(1, steps_right + 1):
            going_right = right(going_right)
            if step < steps_right:
                going_right = (going_right.astype(F32) + term(steps_right - step)).astype(BF16)
            if step <= steps_left:
                going_left = left(going_left)
                if step < steps_left:
                    going_left = (going_left.astype(F32) + term(step - steps_left)).astype(BF16)
        return going_right.astype(F32) + going_left.astype(F32) + term(0)

    def exchange(blocks):
        return lax.all_to_all(blocks, "shard", split_axis=0, concat_axis=0, tiled=True)

    def pick(array, index, axis):
        return lax.dynamic_index_in_dim(array, index, axis, keepdims=False)

    def add(a, b):
        return (a.astype(F32) + b.astype(F32)).astype(BF16)

    def gather_rep(piece):
        mine = lax.axis_index("rep")
        other_chip = chip_swap(piece)
        other_core = core_swap(piece)
        last = core_swap(other_chip)
        whole = jnp.zeros((rep,) + piece.shape, piece.dtype)
        far = (mine + 2) % rep
        for index, part in ((mine, piece), (far, other_chip), (mine ^ 1, other_core), (far ^ 1, last)):
            whole = lax.dynamic_update_index_in_dim(whole, part, index, 0)
        return whole

    def scatter_rep(blocks):
        mine = lax.axis_index("rep")
        chip, core = mine // 2, mine % 2
        blocks = blocks.reshape((blocks.shape[0], outer, 2) + blocks.shape[2:])
        half = add(pick(blocks, core, 2), core_swap(pick(blocks, 1 - core, 2)))
        return add(pick(half, chip, 1), chip_swap(pick(half, 1 - chip, 1)))

    def local(
        tokens,
        doc_lengths,
        pic_starts,
        attn_gain,
        w_query,
        w_key,
        w_value,
        w_out,
        ffn_gain,
        w_gate,
        w_up,
        w_down,
        cotangent,
    ):
        rows, width = tokens.shape
        heads = width // HD
        base = heads // n
        slots = -(-heads // n)
        block = slots * HD
        main = base * HD
        mains = n * main
        depth = w_query.shape[0]
        part = depth // rep
        ff = w_gate.shape[1]
        cols = ff // n
        all_rows = n * rows
        me = lax.axis_index("shard")
        mine = lax.axis_index("rep")
        gain_one = attn_gain.astype(BF16).astype(F32)[:, None]
        gain_two = ffn_gain.astype(BF16).astype(F32)[:, None]
        docs = doc_lengths.shape[1]
        pics = pic_starts.shape[1]

        def quarter(array):
            return lax.dynamic_slice_in_dim(array, mine * part, part, 0)

        def scaled(weight, gain):
            return (quarter(weight).astype(BF16).astype(F32) * quarter(gain)).astype(BF16)

        def by_heads(array, axis):
            if slots == base:
                return jnp.moveaxis(
                    array.reshape(array.shape[:axis] + (n, main) + array.shape[axis + 1 :]), axis, 0
                )
            first = lax.slice_in_dim(array, 0, mains, axis=axis)
            rest = lax.slice_in_dim(array, mains, width, axis=axis)
            pad = [(0, 0)] * array.ndim
            pad[axis] = (0, n * HD - (width - mains))
            rest = jnp.pad(rest, pad)
            split = [
                jnp.moveaxis(a.reshape(a.shape[:axis] + (n, size) + a.shape[axis + 1 :]), axis, 0)
                for a, size in ((first, main), (rest, HD))
            ]
            return jnp.concatenate(split, axis=axis + 1)

        def from_heads(array):
            first = array[:, :, :main].transpose(1, 0, 2).reshape(array.shape[1], mains)
            if slots == base:
                return first
            over = (width - mains) // HD
            rest = array[:over, :, main:].transpose(1, 0, 2).reshape(array.shape[1], width - mains)
            return jnp.concatenate([first, rest], axis=1)

        info = jnp.concatenate([doc_lengths[0], pic_starts[0]]).astype(BF16)
        info = jnp.zeros((n, 8, 3 * block), BF16).at[:, 0, : docs + pics].set(info)
        qkv_part = jnp.concatenate(
            [by_heads(scaled(w, gain_one), 1) for w in (w_query, w_key, w_value)], axis=2
        )
        qkv_part = exchange(jnp.concatenate([qkv_part, info], axis=1))
        info = qkv_part[:, part, : docs + pics].astype(jnp.int32)
        qkv_w = gather_rep(qkv_part[:, :part]).transpose(1, 0, 2, 3).reshape(width, 3 * block)
        out_part = gather_shard(quarter(w_out).astype(BF16))
        out_w = gather_rep(out_part).transpose(1, 0, 2, 3).reshape(width, width)
        ffn_part = jnp.concatenate(
            [scaled(w, gain_two).reshape(part, n, cols).transpose(1, 0, 2) for w in (w_gate, w_up)],
            axis=1,
        )
        ffn_w = gather_rep(exchange(ffn_part)).reshape(rep, n, 2, part, cols)
        ffn_w = ffn_w.transpose(2, 1, 0, 3, 4).reshape(2, width, cols)
        gate_w, up_w = ffn_w[0], ffn_w[1]
        down_w = w_down.astype(BF16)

        inputs = gather_shard(tokens).reshape(all_rows, width)
        offsets, allowed = jax.vmap(lambda a, b: layout(a, b, rows))(info[:, :docs], info[:, docs:])
        bias = jnp.where(allowed, 0.0, MASKED).astype(F32)
        freq_table = jnp.exp(jnp.arange(HALF, dtype=F32) * (-2.0 * math.log(10000.0) / HD))
        turned = freq_table[:, None] * offsets.reshape(1, all_rows).astype(F32)
        cosine, sine = jnp.cos(turned), jnp.sin(turned)
        squares = jnp.mean(jnp.square(inputs.astype(F32)), axis=-1)
        scale_one = lax.rsqrt(squares + EPSILON)[None, :]
        qkv = mm(qkv_w, inputs, 0, 1)
        qkv, mixed = attend(slots, n, rows, qkv, scale_one, cosine, sine, bias)
        mixed_all = jnp.zeros((n * block, all_rows), BF16)
        for device, piece in ring_gather(mixed):
            mixed_all = lax.dynamic_update_slice_in_dim(mixed_all, piece[:main], device * main, 0)
            if slots > base:
                mixed_all = lax.dynamic_update_slice_in_dim(
                    mixed_all, piece[main:], mains + device * HD, 0
                )
        mixed_all = mixed_all[:width]
        middle = inputs.astype(F32) + BRANCH_SCALE * mm(mixed_all, out_w, 0, 0)

        scale_two = lax.rsqrt(jnp.mean(middle * middle, axis=-1, keepdims=True) + EPSILON)
        middle_low = middle.astype(BF16)
        gate_act = mm(middle_low, gate_w, 1, 0) * scale_two
        up_act = mm(middle_low, up_w, 1, 0) * scale_two
        sigmoid_gate = jax.nn.sigmoid(gate_act)
        silu_gate = gate_act * sigmoid_gate
        inner = (silu_gate * up_act).astype(BF16)
        grad_result = cotangent.astype(F32)
        grad_branch = gather_shard((BRANCH_SCALE * grad_result).astype(BF16)).reshape(all_rows, width)
        grad_inner = mm(grad_branch, down_w, 1, 1)
        grad_gate_act = (
            grad_inner
            * up_act
            * sigmoid_gate
            * (1.0 + gate_act * (1.0 - sigmoid_gate))
            * scale_two
        ).astype(BF16)
        grad_up_act = (grad_inner * silu_gate * scale_two).astype(BF16)
        partial = mm(grad_gate_act, gate_w, 1, 1) + mm(grad_up_act, up_w, 1, 1)
        back_two = scatter_shard(partial.astype(BF16).reshape(n, rows, width))
        my_middle = lax.dynamic_slice_in_dim(middle, me * rows, rows, 0)
        my_normed_two = my_middle * lax.dynamic_slice_in_dim(scale_two, me * rows, rows, 0)
        inner_mean = jnp.mean(back_two * my_normed_two, axis=-1, keepdims=True)
        grad_middle = grad_result + back_two - my_normed_two * inner_mean

        grad_attn = (BRANCH_SCALE * grad_middle).astype(BF16)
        grad_mixed = exchange(by_heads(mm(out_w, grad_attn, 1, 1).astype(BF16), 0))
        grad_mixed = grad_mixed.transpose(1, 0, 2).reshape(block, all_rows)
        grad_attn_cols = exchange(grad_attn.T.reshape(n, depth, rows))
        grad_attn_cols = grad_attn_cols.transpose(1, 0, 2).reshape(depth, all_rows)
        grad_qkv = attend_back(
            slots, n, rows, qkv, grad_mixed, scale_one, cosine, sine, bias
        )
        partial = mm(grad_qkv, qkv_w, 0, 1)
        back_one = scatter_shard(partial.astype(BF16).reshape(n, rows, width))
        my_inputs = tokens.astype(F32)
        my_scale_one = lax.rsqrt(jnp.mean(my_inputs * my_inputs, axis=-1, keepdims=True) + EPSILON)
        my_normed_one = my_inputs * my_scale_one
        inner_mean = jnp.mean(back_one * my_normed_one, axis=-1, keepdims=True)
        input_grad = grad_middle + back_one - my_normed_one * inner_mean

        branch = scatter_shard(mm(inner, down_w, 1, 0).astype(BF16).reshape(n, rows, width))
        out_tokens = (my_middle + BRANCH_SCALE * branch).astype(BF16)

        def rep_rows(grad):
            return grad.astype(BF16).reshape(n, rep, part, grad.shape[1])

        def low(weight):
            return weight.astype(BF16).astype(F32)

        grad_down = mm(inner, grad_branch, 0, 0).astype(BF16).reshape(1, rep, -1, width)
        grad_down = gather_rep(scatter_rep(grad_down)[0]).reshape(-1, width).astype(F32)

        grad_ffn = [rep_rows(mm(middle_low, g, 0, 0)) for g in (grad_gate_act, grad_up_act)]
        grad_ffn = exchange(scatter_rep(jnp.concatenate(grad_ffn, axis=2).reshape(n, rep, -1, cols)))
        grad_ffn = grad_ffn.reshape(n, 2, part, cols).transpose(1, 2, 0, 3).reshape(2, part, ff)
        grad_ffn = gather_rep(grad_ffn).transpose(1, 0, 2, 3).reshape(2, depth, ff).astype(F32)
        grad_gain_two = jnp.sum(low(w_gate) * grad_ffn[0] + low(w_up) * grad_ffn[1], axis=1)

        grad_out = exchange(scatter_rep(rep_rows(mm(mixed_all, grad_attn_cols, 1, 1))))
        grad_out = grad_out.transpose(1, 0, 2).reshape(part, width)
        grad_out = gather_rep(grad_out).reshape(depth, width).astype(F32)

        grad_w = exchange(scatter_rep(rep_rows(mm(inputs, grad_qkv, 0, 1))))
        grad_w = jnp.stack([from_heads(grad_w[:, :, k * block : (k + 1) * block]) for k in range(3)])
        grad_w = gather_rep(grad_w).transpose(1, 0, 2, 3).reshape(3, depth, width).astype(F32)
        grad_gain_one = jnp.sum(
            low(w_query) * grad_w[0] + low(w_key) * grad_w[1] + low(w_value) * grad_w[2], axis=1
        )
        return (
            out_tokens,
            input_grad,
            grad_gain_one,
            grad_w[0] * gain_one,
            grad_w[1] * gain_one,
            grad_w[2] * gain_one,
            grad_out,
            grad_gain_two,
            grad_ffn[0] * gain_two,
            grad_ffn[1] * gain_two,
            grad_down,
        )

    return local


def solution(mesh):
    tokens = P(("rep", "shard"), None)
    weight = P("shard", None)
    gain = P("shard")
    return jax.shard_map(
        build(mesh.shape["rep"], mesh.shape["shard"]),
        mesh=mesh,
        in_specs=(
            tokens,
            tokens,
            tokens,
            gain,
            weight,
            weight,
            weight,
            weight,
            gain,
            weight,
            weight,
            weight,
            tokens,
        ),
        out_specs=(
            tokens,
            tokens,
            gain,
            weight,
            weight,
            weight,
            weight,
            gain,
            weight,
            weight,
            weight,
        ),
        check_vma=False,
    )
```

time: 1480 us -> 917 us (0.62)
  waiting for transfers between devices: 791 us -> 276 us
  blocking collectives: 296 us -> 0 us
  starting transfers between devices: 11.5 us -> 113 us
  local copies, waits for them, and re-layouts: 157 us -> 218 us
  other arithmetic: 70.6 us -> 119 us
  Pallas kernels: 0 us -> 21.9 us
  between operations: 14.8 us -> 36.6 us
    all_gather x10 -> x0, waiting for transfers between devices: 334 us -> none  [the longest x6 174 us: gather_rep(): return lax.all_gather(piece, 'rep', axis=0, tiled=False)]
    unnamed x15 -> x0, waiting for transfers between devices: 271 us -> none
    all_to_all x5 -> x0, blocking collectives: 261 us -> none  [exchange(): lax.all_to_all(blocks, 'shard', split_axis=0, concat_axis=0, tiled=True)]
    ppermute x0 -> x78, waiting for transfers between devices: none -> 226 us  [the longest x28 127 us: right(): return lax.ppermute(x, 'shard', to_right)]
    reduce_scatter x3 -> x0, waiting for transfers between devices: 186 us -> none  [scatter_shard(): return lax.psum_scatter(whole, 'shard', scatter_dimension=0, tiled=True)]
    dynamic_update_slice x0 -> x66, local copies, waits for them, and re-layouts: none -> 77.4 us  [the longest x27 49.8 us: gather_rep(): whole = lax.dynamic_update_index_in_dim(whole, part, index, 0)]
    ppermute x0 -> x78, starting transfers between devices: none -> 69.9 us  [the longest x28 34.8 us: right(): return lax.ppermute(x, 'shard', to_right)]
    all_to_all x2 -> x7, waiting for transfers between devices: 0.93 us -> 49.8 us  [exchange(): lax.all_to_all(blocks, 'shard', split_axis=0, concat_axis=0, tiled=True)]
  transfers between devices with their start and end apart: 16 -> 85, of which waited for: 12 -> 32; matrix products, arithmetic and copies ran while one was open for 15% -> 35% of each run, Pallas kernels for 0% -> 2%
where the time goes in v2:
time: 917 us; the launch traced here: 904 us
  waiting for transfers between devices  276 us (30%)
  local copies, waits for them, and re-layouts  218 us (24%)
  matrix products  120 us (13%)
  other arithmetic  119 us (13%)
  starting transfers between devices  113 us (12%)
  between operations  36.6 us (4%)
  Pallas kernels  21.9 us (2%)
    ppermute x28, waiting for transfers between devices, right(): return lax.ppermute(x, 'shard', to_right)  127 us
    dot_general x15, matrix products, mm(): lax.dot_general(left, right, (((left_dim,), (right_dim,)), ((), ())), pre...  120 us
    dynamic_update_slice x27, local copies, waits for them, and re-layouts, gather_rep(): whole = lax.dynamic_update_index_in_dim(whole, part, index, 0)  49.8 us
    all_to_all x7, waiting for transfers between devices, exchange(): lax.all_to_all(blocks, 'shard', split_axis=0, concat_axis=0, tiled=True)  49.8 us
    ppermute x11, waiting for transfers between devices, chip_swap(): return lax.ppermute(x, 'rep', chip_pairs)  48.8 us
    ppermute x21, waiting for transfers between devices, left(): return lax.ppermute(x, 'shard', to_left)  48.8 us
    all_to_all x7, starting transfers between devices, exchange(): lax.all_to_all(blocks, 'shard', split_axis=0, concat_axis=0, tiled=True)  43 us
    ppermute x28, starting transfers between devices, right(): return lax.ppermute(x, 'shard', to_right)  34.8 us
  transfers between devices with their start and end apart: 85, of which 32 were waited for; matrix products, arithmetic and copies ran while one was open for 35% of the time, Pallas kernels for 2%

profile of v2, /device:TPU:0, one launch (start us, length us, event | category | flops | bytes accessed | tf_op | source)
XLA Modules:
  0.0 903.9 jit_solution(5146164670475817906)
XLA Ops:
  49.6 6.3 all-to-all-start
  118.5 4.5 collective-permute-done.38
  125.8 4.2 collective-permute-done.20
  131.5 16.2 %collective-permute-done.21 = bf16[72,2304]{1,0:T(8,128)(2,1)S(1)} collective-permute-done((bf16[72,2304]{1,0:T(8,128)(2,1)S(1)}, bf16[72,2304]{1,0:T(8,128)(2,1)S(1)}, u32[]{:S(2)}, u32[]{:S(2)}) %collective-permute-start.21) | collective-permute-done | bytes 331808 | tf_op jit(solution)/shard_map/ppermute | solution.py:156
  149.5 9.8 %collective-permute-done.22 = bf16[72,2304]{1,0:T(8,128)(2,1)S(1)} collective-permute-done((bf16[72,2304]{1,0:T(8,128)(2,1)S(1)}, bf16[72,2304]{1,0:T(8,128)(2,1)S(1)}, u32[]{:S(2)}, u32[]{:S(2)}) %collective-permute-start.22) | collective-permute-done | bytes 331808 | tf_op jit(solution)/shard_map/ppermute | solution.py:159
  171.6 4.6 broadcast_in_dim.264
  177.9 4.7 collective-permute-done.4
  183.5 9.0 collective-permute-done.41
  199.1 4.7 all-to-all-start.1
  225.3 19.3 %all-to-all-done.1 = bf16[8,144,720]{2,1,0:T(8,128)(2,1)} async-done(((bf16[8,144,720]{2,1,0:T(8,128)(2,1)}), bf16[8,144,720]{2,1,0:T(8,128)(2,1)}, u32[]{:S(2)}, u32[]{:S(2)}) %all-to-all-start.1) | async-done | bytes 1658912 | tf_op jit(solution)/shard_map/all_to_all | solution.py:205
  248.2 7.2 collective-permute-done.7
  260.7 3.5 bitcast_dynamic-update-slice_fusion.1
  268.8 10.9 %fusion.67.qkv_ref = f32[960,1024]{1,0:T(8,128)} fusion(bf16[2304,960]{1,0:T(8,128)(2,1)} %bitcast.40, bf16[1024,2304]{1,0:T(8,128)(2,1)} %bitcast.24), kind=kOutput, calls=%fused_computation.259 | convolution fusion | flops 4529848320 | bytes 13074432 | tf_op jit(solution)/shard_map/dot_general | solution.py:23
  279.7 7.6 attend.1
  287.3 4.2 collective-permute-start.10
  299.0 8.5 collective-permute-done.10
  309.7 13.8 %collective-permute-done.12 = bf16[320,1024]{1,0:T(8,128)(2,1)} collective-permute-done((bf16[320,1024]{1,0:T(8,128)(2,1)S(1)}, bf16[320,1024]{1,0:T(8,128)(2,1)}, u32[]{:S(2)}, u32[]{:S(2)}) %collective-permute-start.12) | collective-permute-done | bytes 655392 | tf_op jit(solution)/shard_map/ppermute | solution.py:156
  329.1 3.6 fusion.64
  333.2 5.6 collective-permute-done.14
  344.8 8.4 collective-permute-done.16
  353.2 19.7 %multiply_reduce_fusion = (f32[1024]{0:T(1024)S(1)}, bf16[1024,2304]{1,0:T(8,128)(2,1)}, f32[1024,2304]{1,0:T(8,128)}) fusion(bf16[2304,2304]{1,0:T(8,128)(2,1)} %bitcast.85, bf16[2560,1024]{1,0:T(8,128)(2,1)S(1)} %slice_dynamic-update-slice_fusion.8, bf16[1024,2304]{1,0:T(8,128)(2,1)} %bitcast.24), kind=kOutput, calls=%fused_computation.2 | convolution fusion | flops 10885790720 | bytes 34213888 | tf_op jit(solution)/shard_map/dot_general | solution.py:23
  372.9 7.8 fusion.68
  380.8 5.5 fusion.69
  386.2 9.3 %multiply_convert_fusion = (bf16[1024,720]{0,1:T(8,128)(2,1)}, bf16[1024,720]{0,1:T(8,128)(2,1)S(1)}, bf16[1024,720]{0,1:T(8,128)(2,1)S(1)}) fusion(f32[1024]{0:T(1024)S(1)} %add_rsqrt_fusion, f32[1024,720]{0,1:T(8,128)} %fusion.68, f32[1024,720]{0,1:T(8,128)} %fusion.69, bf16[1024,2304]{1,0:T(8,128)(2,1)} %bitcast.116, f32[720,2304]{1,0:T(8,128)S(1)} %bitcast.480), kind=kOutput, calls=%fused_computation.38 | convolution fusion | flops 3413053440 | bytes 21680128 | tf_op jit(solution)/shard_map/dot_general | solution.py:23
  395.6 6.4 fusion.70
  402.0 5.0 convolution_convert_fusion.4
  407.0 4.3 convolution_convert_fusion
  411.3 9.1 %convolution_convert_fusion.5 = bf16[720,2304]{1,0:T(8,128)(2,1)} fusion(bf16[1024,720]{0,1:T(8,128)(2,1)S(1)} %get-tuple-element.49, bf16[1024,2304]{1,0:T(8,128)(2,1)} %bitcast.116), kind=kOutput, calls=%fused_computation.22 | convolution fusion | flops 3399045120 | bytes 9510912 | tf_op jit(solution)/shard_map/dot_general | solution.py:23
  420.5 5.0 convolution_convert_fusion.3
  425.5 7.0 add_convert_fusion
  439.1 4.5 copy.455
  443.5 5.7 copy.456
  449.3 3.6 fusion.9
  464.4 13.1 %collective-permute-done.45 = bf16[128,2304]{1,0:T(8,128)(2,1)S(1)} collective-permute-done((bf16[128,2304]{1,0:T(8,128)(2,1)S(1)}, bf16[128,2304]{1,0:T(8,128)(2,1)S(1)}, u32[]{:S(2)}, u32[]{:S(2)}) %collective-permute-start.45) | collective-permute-done | bytes 589856 | tf_op jit(solution)/shard_map/ppermute | solution.py:156
  481.4 8.7 collective-permute-done.31
  494.2 8.5 collective-permute-done.46
  505.2 10.2 %collective-permute-done.32 = bf16[128,2304]{1,0:T(8,128)(2,1)S(1)} collective-permute-done((bf16[128,2304]{1,0:T(8,128)(2,1)S(1)}, bf16[128,2304]{1,0:T(8,128)(2,1)S(1)}, u32[]{:S(2)}, u32[]{:S(2)}) %collective-permute-start.32) | collective-permute-done | bytes 589856 | tf_op jit(solution)/shard_map/ppermute | solution.py:156
  521.9 6.1 collective-permute-done.47
  530.8 8.9 collective-permute-done.33
  542.9 7.4 convolution_convert_fusion.6
  553.9 4.6 all-to-all-start.4
  576.5 9.5 %collective-permute-done.75 = bf16[180,2304]{1,0:T(8,128)(2,1)} collective-permute-done((bf16[180,2304]{1,0:T(8,128)(2,1)}, bf16[180,2304]{1,0:T(8,128)(2,1)}, u32[]{:S(2)}, u32[]{:S(2)}) %collective-permute-start.75) | collective-permute-done | bytes 829472 | tf_op jit(solution)/shard_map/ppermute | solution.py:165
  588.2 6.2 all-to-all-start.2
  596.6 5.1 fusion.5
  604.9 7.5 all-to-all-done.2
  613.3 14.3 %attend_back.1 = bf16[960,1024]{1,0:T(8,128)(2,1)} custom-call(bf16[960,1024]{1,0:T(8,128)(2,1)} %get-tuple-element.26.qkv_ref, bf16[320,1024]{1,0:T(8,128)(2,1)} %copy_bitcast_fusion.grad_ref, f32[1,1024]{1,0:T(1,128)} %bitcast.478, f32[32,1024]{1,0:T(8,128)} %get-tuple-element.80.cos_ref, f32[32,1024]{1,0:T(8,128)} %get-tuple-element.79.sin_ref, ...), custom_call_target="tpu_custom_call" | custom-call | flops 419430400 | bytes 4587520 | tf_op jit(solution)/shard_map/attend_back/pallas_call | solution.py:131
  627.6 8.2 convolution_convert_fusion.1
  637.4 9.0 %convolution_convert_fusion.2 = bf16[2304,960]{0,1:T(8,128)(2,1)} fusion(bf16[960,1024]{1,0:T(8,128)(2,1)S(1)} %copy-done.19, bf16[1024,2304]{1,0:T(8,128)(2,1)} %bitcast.24), kind=kOutput, calls=%fused_computation.19 | convolution fusion | flops 4532060160 | bytes 11108352 | tf_op jit(solution)/shard_map/dot_general | solution.py:23
  647.8 6.5 copy.440
  664.8 4.6 reshape.623
  671.6 4.1 all-to-all-start.5
  682.7 7.1 all-to-all-done.5
  703.7 3.6 all-to-all-start.6
  715.5 3.5 fusion.1
  722.6 29.1 %collective-permute-done.57 = bf16[128,2304]{1,0:T(8,128)(2,1)S(1)} collective-permute-done((bf16[128,2304]{1,0:T(8,128)(2,1)S(1)}, bf16[128,2304]{1,0:T(8,128)(2,1)S(1)}, u32[]{:S(2)}, u32[]{:S(2)}) %collective-permute-start.57) | collective-permute-done | bytes 589856 | tf_op jit(solution)/shard_map/ppermute | solution.py:159
  756.3 13.5 %all-to-all-start.3 = ((bf16[8,72,960]{2,1,0:T(8,128)(2,1)}), bf16[8,72,960]{2,1,0:T(8,128)(2,1)}, u32[]{:S(2)}, u32[]{:S(2)}) async-start(bf16[8,72,960]{2,1,0:T(8,128)(2,1)} %fusion.16), calls=%async_computation.3 | async-start | bytes 2359296 | tf_op jit(solution)/shard_map/all_to_all | solution.py:205
  782.8 15.9 %all-to-all-done.3 = bf16[8,72,960]{2,1,0:T(8,128)(2,1)} async-done(((bf16[8,72,960]{2,1,0:T(8,128)(2,1)}), bf16[8,72,960]{2,1,0:T(8,128)(2,1)}, u32[]{:S(2)}, u32[]{:S(2)}) %all-to-all-start.3) | async-done | bytes 1105952 | tf_op jit(solution)/shard_map/all_to_all | solution.py:205
  802.6 14.8 %collective-permute-done.70 = bf16[2,72,5760]{2,1,0:T(8,128)(2,1)} collective-permute-done((bf16[2,72,5760]{2,1,0:T(8,128)(2,1)}, bf16[2,72,5760]{2,1,0:T(8,128)(2,1)}, u32[]{:S(2)}, u32[]{:S(2)}) %collective-permute-start.70) | collective-permute-done | bytes 1658912 | tf_op jit(solution)/shard_map/ppermute | solution.py:165
  821.4 16.0 %collective-permute-done.60 = bf16[3,72,2304]{2,1,0:T(8,128)(2,1)S(1)} collective-permute-done((bf16[3,72,2304]{2,1,0:T(8,128)(2,1)S(1)}, bf16[3,72,2304]{2,1,0:T(8,128)(2,1)S(1)}, u32[]{:S(2)}, u32[]{:S(2)}) %collective-permute-start.60) | collective-permute-done | bytes 995360 | tf_op jit(solution)/shard_map/ppermute | solution.py:165
  844.2 10.2 %bitcast_multiply_fusion.4 = (f32[288,2304]{1,0:T(8,128)}, f32[288,2304]{1,0:T(8,128)S(1)}, f32[288,2304]{1,0:T(8,128)}, f32[288,2304]{1,0:T(8,128)}, f32[288,2304]{1,0:T(8,128)}) fusion(f32[1,4,72,2304]{3,2,1,0:T(8,128)} %get-tuple-element.38, f32[288]{0:T(512)S(1)} %copy-done.22, f32[288,2304]{1,0:T(8,128)} %param.133, ...), kind=kLoop, calls=%fused_computation.46 | loop fusion | flops 8626176 | bytes 29197440 | tf_op jit(solution)/shard_map/mul | solution.py:409
  859.8 8.6 convert_bitcast_fusion
  868.4 10.5 %fusion.62 = (f32[1,4,72,5760]{3,2,1,0:T(8,128)}, f32[1,4,72,5760]{3,2,1,0:T(8,128)}) fusion(f32[2,4,72,5760]{3,2,1,0:T(8,128)} %convert_bitcast_fusion), kind=kLoop, calls=%fused_computation.254 | loop fusion | bytes 26542080 | tf_op jit(solution)/shard_map/slice | solution.py:391
  878.9 18.6 %bitcast_multiply_fusion = (f32[288,5760]{1,0:T(8,128)}, f32[288,5760]{1,0:T(8,128)}, f32[288,5760]{1,0:T(8,128)}, f32[288,5760]{1,0:T(8,128)}) fusion(f32[1,4,72,5760]{3,2,1,0:T(8,128)} %get-tuple-element.33, f32[288]{0:T(512)S(1)} %copy-done.24, f32[288,5760]{1,0:T(8,128)} %param.137, f32[1,4,72,5760]{3,2,1,0:T(8,128)} %get-tuple-element.34, ...), kind=kLoop, calls=%fused_computation.12 | loop fusion | flops 13271040 | bytes 53085312 | tf_op jit(solution)/shard_map/mul | solution.py:413
  897.4 6.0 add_reduce_fusion
  (424 shorter events, 317.7 us)
Async XLA Ops:
  15.0 91.5 %collective-permute-start.17 = (bf16[72,2304]{1,0:T(8,128)(2,1)}, bf16[72,2304]{1,0:T(8,128)(2,1)}, u32[]{:S(2)}, u32[]{:S(2)}) collective-permute-start(bf16[72,2304]{1,0:T(8,128)(2,1)} %get-tuple-element.32), channel_id=1, source_target_pairs={{0,2},{2,4},{4,6},{6,7},{7,5},{5,3},{3,1},{1,0},{8,10},{10,12},{12... | collective-permute-start | bytes 995336 | tf_op jit(solution)/shard_map/ppermute | solution.py:156
  18.0 89.5 %collective-permute-start.18 = (bf16[72,2304]{1,0:T(8,128)(2,1)}, bf16[72,2304]{1,0:T(8,128)(2,1)}, u32[]{:S(2)}, u32[]{:S(2)}) collective-permute-start(bf16[72,2304]{1,0:T(8,128)(2,1)} %get-tuple-element.32), channel_id=1, source_target_pairs={{2,0},{4,2},{6,4},{7,6},{5,7},{3,5},{1,3},{0,1},{10,8},{12,10},{14... | collective-permute-start | bytes 995336 | tf_op jit(solution)/shard_map/ppermute | solution.py:159
  18.0 92.6 %collective-permute-start = (bf16[128,2304]{1,0:T(8,128)(2,1)S(1)}, bf16[128,2304]{1,0:T(8,128)(2,1)}, u32[]{:S(2)}, u32[]{:S(2)}) collective-permute-start(bf16[128,2304]{1,0:T(8,128)(2,1)S(1)} %copy-done.7), channel_id=1, source_target_pairs={{0,2},{2,4},{4,6},{6,7},{7,5},{5,3},{3,1},{1,0},{8,10},{10,12},{12... | collective-permute-start | bytes 1769480 | tf_op jit(solution)/shard_map/ppermute | solution.py:156
  20.0 92.5 %collective-permute-start.1 = (bf16[128,2304]{1,0:T(8,128)(2,1)S(1)}, bf16[128,2304]{1,0:T(8,128)(2,1)}, u32[]{:S(2)}, u32[]{:S(2)}) collective-permute-start(bf16[128,2304]{1,0:T(8,128)(2,1)S(1)} %copy-done.7), channel_id=1, source_target_pairs={{2,0},{4,2},{6,4},{7,6},{5,7},{3,5},{1,3},{0,1},{10,8},{12,10},{14... | collective-permute-start | bytes 1769480 | tf_op jit(solution)/shard_map/ppermute | solution.py:159
  49.6 149.5 %all-to-all-start = ((bf16[8,80,960]{2,1,0:T(8,128)(2,1)}), bf16[8,80,960]{2,1,0:T(8,128)(2,1)}, u32[]{:S(2)}, u32[]{:S(2)}) async-start(bf16[8,80,960]{2,1,0:T(8,128)(2,1)} %pad_maximum_fusion.1), calls=%async_computation | async-start | bytes 2621440 | tf_op jit(solution)/shard_map/all_to_all | solution.py:205
  57.9 58.6 %collective-permute-start.37 = (bf16[128,2304]{1,0:T(8,128)(2,1)}, bf16[128,2304]{1,0:T(8,128)(2,1)}, u32[]{:S(2)}, u32[]{:S(2)}) collective-permute-start(bf16[128,2304]{1,0:T(8,128)(2,1)} %fusion.26), channel_id=1, source_target_pairs={{0,2},{2,4},{4,6},{6,7},{7,5},{5,3},{3,1},{1,0},{8,10},{10,12},{12... | collective-permute-start | bytes 1769480 | tf_op jit(solution)/shard_map/ppermute | solution.py:156
  110.6 19.5 %collective-permute-start.20 = (bf16[72,2304]{1,0:T(8,128)(2,1)}, bf16[72,2304]{1,0:T(8,128)(2,1)S(1)}, u32[]{:S(2)}, u32[]{:S(2)}) collective-permute-start(bf16[72,2304]{1,0:T(8,128)(2,1)} %collective-permute-done.18), channel_id=1, source_target_pairs={{2,0},{4,2},{6,4},{7,6},{5,7},{3,5},{1,3},{0,1},{10,8},{12,10},{14... | collective-permute-start | bytes 995336 | tf_op jit(solution)/shard_map/ppermute | solution.py:159
  112.6 48.2 %collective-permute-start.2 = (bf16[128,2304]{1,0:T(8,128)(2,1)}, bf16[128,2304]{1,0:T(8,128)(2,1)S(1)}, u32[]{:S(2)}, u32[]{:S(2)}) collective-permute-start(bf16[128,2304]{1,0:T(8,128)(2,1)} %collective-permute-done), channel_id=1, source_target_pairs={{0,2},{2,4},{4,6},{6,7},{7,5},{5,3},{3,1},{1,0},{8,10},{10,12},{12... | collective-permute-start | bytes 1769480 | tf_op jit(solution)/shard_map/ppermute | solution.py:156
  116.5 46.7 %collective-permute-start.3 = (bf16[128,2304]{1,0:T(8,128)(2,1)}, bf16[128,2304]{1,0:T(8,128)(2,1)S(1)}, u32[]{:S(2)}, u32[]{:S(2)}) collective-permute-start(bf16[128,2304]{1,0:T(8,128)(2,1)} %collective-permute-done.1), channel_id=1, source_target_pairs={{2,0},{4,2},{6,4},{7,6},{5,7},{3,5},{1,3},{0,1},{10,8},{12,10},{14... | collective-permute-start | bytes 1769480 | tf_op jit(solution)/shard_map/ppermute | solution.py:159
  122.9 41.6 %collective-permute-start.39 = (bf16[128,2304]{1,0:T(8,128)(2,1)}, bf16[128,2304]{1,0:T(8,128)(2,1)S(1)}, u32[]{:S(2)}, u32[]{:S(2)}) collective-permute-start(bf16[128,2304]{1,0:T(8,128)(2,1)} %collective-permute-done.37), channel_id=1, source_target_pairs={{0,2},{2,4},{4,6},{6,7},{7,5},{5,3},{3,1},{1,0},{8,10},{10,12},{12... | collective-permute-start | bytes 1769480 | tf_op jit(solution)/shard_map/ppermute | solution.py:156
  125.2 41.7 %collective-permute-start.40 = (bf16[128,2304]{1,0:T(8,128)(2,1)S(1)}, bf16[128,2304]{1,0:T(8,128)(2,1)S(1)}, u32[]{:S(2)}, u32[]{:S(2)}) collective-permute-start(bf16[128,2304]{1,0:T(8,128)(2,1)S(1)} %collective-permute-done.38), channel_id=1, source_target_pairs={{2,0},{4,2},{6,4},{7,6},{5,7},{3,5},{1,3},{0,1},{10,8},{12,10},{14... | collective-permute-start | bytes 1769480 | tf_op jit(solution)/shard_map/ppermute | solution.py:159
  160.8 21.9 %collective-permute-start.4 = (bf16[128,2304]{1,0:T(8,128)(2,1)S(1)}, bf16[128,2304]{1,0:T(8,128)(2,1)S(1)}, u32[]{:S(2)}, u32[]{:S(2)}) collective-permute-start(bf16[128,2304]{1,0:T(8,128)(2,1)S(1)} %collective-permute-done.2), channel_id=1, source_target_pairs={{0,2},{2,4},{4,6},{6,7},{7,5},{5,3},{3,1},{1,0},{8,10},{10,12},{12... | collective-permute-start | bytes 1769480 | tf_op jit(solution)/shard_map/ppermute | solution.py:156
  163.2 32.7 %collective-permute-start.5 = (bf16[128,2304]{1,0:T(8,128)(2,1)S(1)}, bf16[128,2304]{1,0:T(8,128)(2,1)S(1)}, u32[]{:S(2)}, u32[]{:S(2)}) collective-permute-start(bf16[128,2304]{1,0:T(8,128)(2,1)S(1)} %collective-permute-done.3), channel_id=1, source_target_pairs={{2,0},{4,2},{6,4},{7,6},{5,7},{3,5},{1,3},{0,1},{10,8},{12,10},{14... | collective-permute-start | bytes 1769480 | tf_op jit(solution)/shard_map/ppermute | solution.py:159
  164.6 28.0 %collective-permute-start.41 = (bf16[128,2304]{1,0:T(8,128)(2,1)S(1)}, bf16[128,2304]{1,0:T(8,128)(2,1)}, u32[]{:S(2)}, u32[]{:S(2)}) collective-permute-start(bf16[128,2304]{1,0:T(8,128)(2,1)S(1)} %collective-permute-done.39), channel_id=1, source_target_pairs={{0,2},{2,4},{4,6},{6,7},{7,5},{5,3},{3,1},{1,0},{8,10},{10,12},{12... | collective-permute-start | bytes 1769480 | tf_op jit(solution)/shard_map/ppermute | solution.py:156
  166.9 31.3 %collective-permute-start.42 = (bf16[128,2304]{1,0:T(8,128)(2,1)S(1)}, bf16[128,2304]{1,0:T(8,128)(2,1)S(1)}, u32[]{:S(2)}, u32[]{:S(2)}) collective-permute-start(bf16[128,2304]{1,0:T(8,128)(2,1)S(1)} %collective-permute-done.40), channel_id=1, source_target_pairs={{2,0},{4,2},{6,4},{7,6},{5,7},{3,5},{1,3},{0,1},{10,8},{12,10},{14... | collective-permute-start | bytes 1769480 | tf_op jit(solution)/shard_map/ppermute | solution.py:159
  170.0 90.6 %collective-permute-start.24 = (bf16[8,72,2304]{2,1,0:T(8,128)(2,1)S(1)}, bf16[8,72,2304]{2,1,0:T(8,128)(2,1)}, u32[]{:S(2)}, u32[]{:S(2)}) collective-permute-start(bf16[8,72,2304]{2,1,0:T(8,128)(2,1)S(1)} %bitcast_dynamic-update-slice_fusion.42), channel_id=1, source_target_pairs={{0,16},{8,24},{16,0},{24,8},{1,17},{9,25},{17,1},{25,9},{2,18},{10... | collective-permute-start | bytes 7962632 | tf_op jit(solution)/shard_map/ppermute | solution.py:165
  182.6 81.6 %collective-permute-start.25 = (bf16[8,72,2304]{2,1,0:T(8,128)(2,1)S(1)}, bf16[8,72,2304]{2,1,0:T(8,128)(2,1)}, u32[]{:S(2)}, u32[]{:S(2)}) collective-permute-start(bf16[8,72,2304]{2,1,0:T(8,128)(2,1)S(1)} %bitcast_dynamic-update-slice_fusion.42), channel_id=1, source_target_pairs={{0,8},{8,0},{16,24},{24,16},{1,9},{9,1},{17,25},{25,17},{2,10},{10... | collective-permute-start | bytes 7962632 | tf_op jit(solution)/shard_map/ppermute | solution.py:162
  192.5 24.1 %collective-permute-start.6 = (bf16[128,2304]{1,0:T(8,128)(2,1)S(1)}, bf16[128,2304]{1,0:T(8,128)(2,1)}, u32[]{:S(2)}, u32[]{:S(2)}) collective-permute-start(bf16[128,2304]{1,0:T(8,128)(2,1)S(1)} %collective-permute-done.4), channel_id=1, source_target_pairs={{0,2},{2,4},{4,6},{6,7},{7,5},{5,3},{3,1},{1,0},{8,10},{10,12},{12... | collective-permute-start | bytes 1769480 | tf_op jit(solution)/shard_map/ppermute | solution.py:156
  195.9 27.4 %collective-permute-start.43 = (bf16[128,2304]{1,0:T(8,128)(2,1)}, bf16[128,2304]{1,0:T(8,128)(2,1)}, u32[]{:S(2)}, u32[]{:S(2)}) collective-permute-start(bf16[128,2304]{1,0:T(8,128)(2,1)} %collective-permute-done.41), channel_id=1, source_target_pairs={{0,2},{2,4},{4,6},{6,7},{7,5},{5,3},{3,1},{1,0},{8,10},{10,12},{12... | collective-permute-start | bytes 1769480 | tf_op jit(solution)/shard_map/ppermute | solution.py:156
  199.1 45.4 %all-to-all-start.1 = ((bf16[8,144,720]{2,1,0:T(8,128)(2,1)}), bf16[8,144,720]{2,1,0:T(8,128)(2,1)}, u32[]{:S(2)}, u32[]{:S(2)}) async-start(bf16[8,144,720]{2,1,0:T(8,128)(2,1)} %copy.436), calls=%async_computation.1 | async-start | bytes 3538944 | tf_op jit(solution)/shard_map/all_to_all | solution.py:205
  206.2 49.2 %collective-permute-start.7 = (bf16[8,72,960]{2,1,0:T(8,128)(2,1)}, bf16[8,72,960]{2,1,0:T(8,128)(2,1)}, u32[]{:S(2)}, u32[]{:S(2)}) collective-permute-start(bf16[8,72,960]{2,1,0:T(8,128)(2,1)} %slice.218), channel_id=1, source_target_pairs={{0,16},{8,24},{16,0},{24,8},{1,17},{9,25},{17,1},{25,9},{2,18},{10... | collective-permute-start | bytes 3317768 | tf_op jit(solution)/shard_map/ppermute | solution.py:165
  216.7 41.1 %collective-permute-start.8 = (bf16[8,72,960]{2,1,0:T(8,128)(2,1)}, bf16[8,72,960]{2,1,0:T(8,128)(2,1)}, u32[]{:S(2)}, u32[]{:S(2)}) collective-permute-start(bf16[8,72,960]{2,1,0:T(8,128)(2,1)} %slice.218), channel_id=1, source_target_pairs={{0,8},{8,0},{16,24},{24,16},{1,9},{9,1},{17,25},{25,17},{2,10},{10... | collective-permute-start | bytes 3317768 | tf_op jit(solution)/shard_map/ppermute | solution.py:162
  244.5 48.8 %collective-permute-start.27 = (bf16[8,144,720]{2,1,0:T(8,128)(2,1)}, bf16[8,144,720]{2,1,0:T(8,128)(2,1)}, u32[]{:S(2)}, u32[]{:S(2)}) collective-permute-start(bf16[8,144,720]{2,1,0:T(8,128)(2,1)} %all-to-all-done.1), channel_id=1, source_target_pairs={{0,16},{8,24},{16,0},{24,8},{1,17},{9,25},{17,1},{25,9},{2,18},{10... | collective-permute-start | bytes 4976648 | tf_op jit(solution)/shard_map/ppermute | solution.py:165
  255.4 40.8 %collective-permute-start.28 = (bf16[8,144,720]{2,1,0:T(8,128)(2,1)}, bf16[8,144,720]{2,1,0:T(8,128)(2,1)}, u32[]{:S(2)}, u32[]{:S(2)}) collective-permute-start(bf16[8,144,720]{2,1,0:T(8,128)(2,1)} %all-to-all-done.1), channel_id=1, source_target_pairs={{0,8},{8,0},{16,24},{24,16},{1,9},{9,1},{17,25},{25,17},{2,10},{10... | collective-permute-start | bytes 4976648 | tf_op jit(solution)/shard_map/ppermute | solution.py:162
  260.7 80.7 %collective-permute-start.26 = (bf16[8,72,2304]{2,1,0:T(8,128)(2,1)}, bf16[8,72,2304]{2,1,0:T(8,128)(2,1)}, u32[]{:S(2)}, u32[]{:S(2)}) collective-permute-start(bf16[8,72,2304]{2,1,0:T(8,128)(2,1)} %collective-permute-done.24), channel_id=1, source_target_pairs={{0,8},{8,0},{16,24},{24,16},{1,9},{9,1},{17,25},{25,17},{2,10},{10... | collective-permute-start | bytes 7962632 | tf_op jit(solution)/shard_map/ppermute | solution.py:162
  287.3 20.2 %collective-permute-start.10 = (bf16[320,1024]{1,0:T(8,128)(2,1)}, bf16[320,1024]{1,0:T(8,128)(2,1)S(1)}, u32[]{:S(2)}, u32[]{:S(2)}) collective-permute-start(bf16[320,1024]{1,0:T(8,128)(2,1)} %get-tuple-element.25), channel_id=1, source_target_pairs={{0,2},{2,4},{4,6},{6,7},{7,5},{5,3},{3,1},{1,0},{8,10},{10,12},{12... | collective-permute-start | bytes 1966088 | tf_op jit(solution)/shard_map/ppermute | solution.py:156
  293.3 34.4 %collective-permute-start.29 = (bf16[8,144,720]{2,1,0:T(8,128)(2,1)}, bf16[8,144,720]{2,1,0:T(8,128)(2,1)S(1)}, u32[]{:S(2)}, u32[]{:S(2)}) collective-permute-start(bf16[8,144,720]{2,1,0:T(8,128)(2,1)} %collective-permute-done.27), channel_id=1, source_target_pairs={{0,8},{8,0},{16,24},{24,16},{1,9},{9,1},{17,25},{25,17},{2,10},{10... | collective-permute-start | bytes 4976648 | tf_op jit(solution)/shard_map/ppermute | solution.py:162
  433.8 25.4 %collective-permute-start.44 = (bf16[128,2304]{1,0:T(8,128)(2,1)}, bf16[128,2304]{1,0:T(8,128)(2,1)}, u32[]{:S(2)}, u32[]{:S(2)}) collective-permute-start(bf16[128,2304]{1,0:T(8,128)(2,1)} %get-tuple-element.60), channel_id=1, source_target_pairs={{0,2},{2,4},{4,6},{6,7},{7,5},{5,3},{3,1},{1,0},{8,10},{10,12},{12... | collective-permute-start | bytes 1769480 | tf_op jit(solution)/shard_map/ppermute | solution.py:156
  434.1 28.8 %collective-permute-start.48 = (bf16[128,2304]{1,0:T(8,128)(2,1)}, bf16[128,2304]{1,0:T(8,128)(2,1)}, u32[]{:S(2)}, u32[]{:S(2)}) collective-permute-start(bf16[128,2304]{1,0:T(8,128)(2,1)} %get-tuple-element.61), channel_id=1, source_target_pairs={{2,0},{4,2},{6,4},{7,6},{5,7},{3,5},{1,3},{0,1},{10,8},{12,10},{14... | collective-permute-start | bytes 1769480 | tf_op jit(solution)/shard_map/ppermute | solution.py:159
  437.0 24.2 %collective-permute-start.30 = (bf16[128,2304]{1,0:T(8,128)(2,1)}, bf16[128,2304]{1,0:T(8,128)(2,1)}, u32[]{:S(2)}, u32[]{:S(2)}) collective-permute-start(bf16[128,2304]{1,0:T(8,128)(2,1)} %get-tuple-element.66), channel_id=1, source_target_pairs={{0,2},{2,4},{4,6},{6,7},{7,5},{5,3},{3,1},{1,0},{8,10},{10,12},{12... | collective-permute-start | bytes 1769480 | tf_op jit(solution)/shard_map/ppermute | solution.py:156
  437.3 42.3 %collective-permute-start.34 = (bf16[128,2304]{1,0:T(8,128)(2,1)}, bf16[128,2304]{1,0:T(8,128)(2,1)}, u32[]{:S(2)}, u32[]{:S(2)}) collective-permute-start(bf16[128,2304]{1,0:T(8,128)(2,1)} %get-tuple-element.67), channel_id=1, source_target_pairs={{2,0},{4,2},{6,4},{7,6},{5,7},{3,5},{1,3},{0,1},{10,8},{12,10},{14... | collective-permute-start | bytes 1769480 | tf_op jit(solution)/shard_map/ppermute | solution.py:159
  452.9 117.1 %collective-permute-start.68 = (bf16[8,2,144,720]{3,2,1,0:T(8,128)(2,1)}, bf16[8,2,144,720]{3,2,1,0:T(8,128)(2,1)}, u32[]{:S(2)}, u32[]{:S(2)}) collective-permute-start(bf16[8,2,144,720]{3,2,1,0:T(8,128)(2,1)} %fusion.9), channel_id=1, source_target_pairs={{0,8},{8,0},{16,24},{24,16},{1,9},{9,1},{17,25},{25,17},{2,10},{10... | collective-permute-start | bytes 9953288 | tf_op jit(solution)/shard_map/ppermute | solution.py:162
  459.3 32.9 %collective-permute-start.73 = (bf16[1,2,180,2304]{3,1,2,0:T(2,128)(2,1)S(1)}, bf16[1,2,180,2304]{3,1,2,0:T(2,128)(2,1)S(1)}, u32[]{:S(2)}, u32[]{:S(2)}) collective-permute-start(bf16[1,2,180,2304]{3,1,2,0:T(2,128)(2,1)S(1)} %copy.463), channel_id=1, source_target_pairs={{0,8},{8,0},{16,24},{24,16},{1,9},{9,1},{17,25},{25,17},{2,10},{10... | collective-permute-start | bytes 4976648 | tf_op jit(solution)/shard_map/ppermute | solution.py:162
  462.9 27.2 %collective-permute-start.31 = (bf16[128,2304]{1,0:T(8,128)(2,1)S(1)}, bf16[128,2304]{1,0:T(8,128)(2,1)S(1)}, u32[]{:S(2)}, u32[]{:S(2)}) collective-permute-start(bf16[128,2304]{1,0:T(8,128)(2,1)S(1)} %fusion.46), channel_id=1, source_target_pairs={{0,2},{2,4},{4,6},{6,7},{7,5},{5,3},{3,1},{1,0},{8,10},{10,12},{12... | collective-permute-start | bytes 1769480 | tf_op jit(solution)/shard_map/ppermute | solution.py:156
  479.3 23.4 %collective-permute-start.46 = (bf16[128,2304]{1,0:T(8,128)(2,1)S(1)}, bf16[128,2304]{1,0:T(8,128)(2,1)S(1)}, u32[]{:S(2)}, u32[]{:S(2)}) collective-permute-start(bf16[128,2304]{1,0:T(8,128)(2,1)S(1)} %get-tuple-element.58), channel_id=1, source_target_pairs={{0,2},{2,4},{4,6},{6,7},{7,5},{5,3},{3,1},{1,0},{8,10},{10,12},{12... | collective-permute-start | bytes 1769480 | tf_op jit(solution)/shard_map/ppermute | solution.py:156
  479.6 23.1 %collective-permute-start.49 = (bf16[128,2304]{1,0:T(8,128)(2,1)S(1)}, bf16[128,2304]{1,0:T(8,128)(2,1)S(1)}, u32[]{:S(2)}, u32[]{:S(2)}) collective-permute-start(bf16[128,2304]{1,0:T(8,128)(2,1)S(1)} %get-tuple-element.59), channel_id=1, source_target_pairs={{2,0},{4,2},{6,4},{7,6},{5,7},{3,5},{1,3},{0,1},{10,8},{12,10},{14... | collective-permute-start | bytes 1769480 | tf_op jit(solution)/shard_map/ppermute | solution.py:159
  491.8 23.6 %collective-permute-start.32 = (bf16[128,2304]{1,0:T(8,128)(2,1)S(1)}, bf16[128,2304]{1,0:T(8,128)(2,1)S(1)}, u32[]{:S(2)}, u32[]{:S(2)}) collective-permute-start(bf16[128,2304]{1,0:T(8,128)(2,1)S(1)} %get-tuple-element.64), channel_id=1, source_target_pairs={{0,2},{2,4},{4,6},{6,7},{7,5},{5,3},{3,1},{1,0},{8,10},{10,12},{12... | collective-permute-start | bytes 1769480 | tf_op jit(solution)/shard_map/ppermute | solution.py:156
  492.1 23.3 %collective-permute-start.35 = (bf16[128,2304]{1,0:T(8,128)(2,1)S(1)}, bf16[128,2304]{1,0:T(8,128)(2,1)S(1)}, u32[]{:S(2)}, u32[]{:S(2)}) collective-permute-start(bf16[128,2304]{1,0:T(8,128)(2,1)S(1)} %get-tuple-element.65), channel_id=1, source_target_pairs={{2,0},{4,2},{6,4},{7,6},{5,7},{3,5},{1,3},{0,1},{10,8},{12,10},{14... | collective-permute-start | bytes 1769480 | tf_op jit(solution)/shard_map/ppermute | solution.py:159
  503.9 24.1 %collective-permute-start.47 = (bf16[128,2304]{1,0:T(8,128)(2,1)S(1)}, bf16[128,2304]{1,0:T(8,128)(2,1)S(1)}, u32[]{:S(2)}, u32[]{:S(2)}) collective-permute-start(bf16[128,2304]{1,0:T(8,128)(2,1)S(1)} %get-tuple-element.56), channel_id=1, source_target_pairs={{0,2},{2,4},{4,6},{6,7},{7,5},{5,3},{3,1},{1,0},{8,10},{10,12},{12... | collective-permute-start | bytes 1769480 | tf_op jit(solution)/shard_map/ppermute | solution.py:156
  517.7 22.0 %collective-permute-start.33 = (bf16[128,2304]{1,0:T(8,128)(2,1)S(1)}, bf16[128,2304]{1,0:T(8,128)(2,1)S(1)}, u32[]{:S(2)}, u32[]{:S(2)}) collective-permute-start(bf16[128,2304]{1,0:T(8,128)(2,1)S(1)} %get-tuple-element.62), channel_id=1, source_target_pairs={{0,2},{2,4},{4,6},{6,7},{7,5},{5,3},{3,1},{1,0},{8,10},{10,12},{12... | collective-permute-start | bytes 1769480 | tf_op jit(solution)/shard_map/ppermute | solution.py:156
  520.1 41.3 %collective-permute-start.74 = (bf16[1,180,2304]{2,1,0:T(8,128)(2,1)}, bf16[1,180,2304]{2,1,0:T(8,128)(2,1)}, u32[]{:S(2)}, u32[]{:S(2)}) collective-permute-start(bf16[1,180,2304]{2,1,0:T(8,128)(2,1)} %dynamic-slice_bitcast_fusion.5), channel_id=1, source_target_pairs={{0,16},{8,24},{16,0},{24,8},{1,17},{9,25},{17,1},{25,9},{2,18},{10... | collective-permute-start | bytes 2488328 | tf_op jit(solution)/shard_map/ppermute | solution.py:165
  553.9 34.3 %all-to-all-start.4 = ((bf16[8,288,128]{2,1,0:T(8,128)(2,1)}), bf16[8,288,128]{2,1,0:T(8,128)(2,1)}, u32[]{:S(2)}, u32[]{:S(2)}) async-start(bf16[8,288,128]{2,1,0:T(8,128)(2,1)} %bitcast.462), calls=%async_computation.4 | async-start | bytes 1179648 | tf_op jit(solution)/shard_map/all_to_all | solution.py:205
  563.9 22.1 %collective-permute-start.75 = (bf16[180,2304]{1,0:T(8,128)(2,1)}, bf16[180,2304]{1,0:T(8,128)(2,1)}, u32[]{:S(2)}, u32[]{:S(2)}) collective-permute-start(bf16[180,2304]{1,0:T(8,128)(2,1)} %fusion.51), channel_id=1, source_target_pairs={{0,16},{8,24},{16,0},{24,8},{1,17},{9,25},{17,1},{25,9},{2,18},{10... | collective-permute-start | bytes 2488328 | tf_op jit(solution)/shard_map/ppermute | solution.py:165
  565.7 28.7 %collective-permute-start.76 = (bf16[180,2304]{1,0:T(8,128)(2,1)}, bf16[180,2304]{1,0:T(8,128)(2,1)}, u32[]{:S(2)}, u32[]{:S(2)}) collective-permute-start(bf16[180,2304]{1,0:T(8,128)(2,1)} %fusion.51), channel_id=1, source_target_pairs={{0,8},{8,0},{16,24},{24,16},{1,9},{9,1},{17,25},{25,17},{2,10},{10... | collective-permute-start | bytes 2488328 | tf_op jit(solution)/shard_map/ppermute | solution.py:162
  576.2 124.4 %collective-permute-start.69 = (bf16[8,144,720]{2,1,0:T(8,128)(2,1)}, bf16[8,144,720]{2,1,0:T(8,128)(2,1)}, u32[]{:S(2)}, u32[]{:S(2)}) collective-permute-start(bf16[8,144,720]{2,1,0:T(8,128)(2,1)} %dynamic-slice_bitcast_fusion.1), channel_id=1, source_target_pairs={{0,16},{8,24},{16,0},{24,8},{1,17},{9,25},{17,1},{25,9},{2,18},{10... | collective-permute-start | bytes 4976648 | tf_op jit(solution)/shard_map/ppermute | solution.py:165
  586.0 76.0 %collective-permute-start.77 = (bf16[180,2304]{1,0:T(8,128)(2,1)}, bf16[180,2304]{1,0:T(8,128)(2,1)}, u32[]{:S(2)}, u32[]{:S(2)}) collective-permute-start(bf16[180,2304]{1,0:T(8,128)(2,1)} %collective-permute-done.75), channel_id=1, source_target_pairs={{0,8},{8,0},{16,24},{24,16},{1,9},{9,1},{17,25},{25,17},{2,10},{10... | collective-permute-start | bytes 2488328 | tf_op jit(solution)/shard_map/ppermute | solution.py:162
  588.2 24.2 %all-to-all-start.2 = ((bf16[8,320,128]{2,1,0:T(8,128)(2,1)}), bf16[8,320,128]{2,1,0:T(8,128)(2,1)S(1)}, u32[]{:S(2)}, u32[]{:S(2)}) async-start(bf16[8,320,128]{2,1,0:T(8,128)(2,1)} %pad_maximum_fusion.3), calls=%async_computation.2 | async-start | bytes 1310720 | tf_op jit(solution)/shard_map/all_to_all | solution.py:205
  604.6 53.1 %collective-permute-start.63 = (bf16[8,2,72,288]{3,2,1,0:T(8,128)(2,1)}, bf16[8,2,72,288]{3,2,1,0:T(8,128)(2,1)S(1)}, u32[]{:S(2)}, u32[]{:S(2)}) collective-permute-start(bf16[8,2,72,288]{3,2,1,0:T(8,128)(2,1)} %dynamic-slice_bitcast_fusion.4), channel_id=1, source_target_pairs={{0,8},{8,0},{16,24},{24,16},{1,9},{9,1},{17,25},{25,17},{2,10},{10... | collective-permute-start | bytes 1990664 | tf_op jit(solution)/shard_map/ppermute | solution.py:162
  637.0 21.0 %collective-permute-start.51 = (bf16[128,2304]{1,0:T(8,128)(2,1)}, bf16[128,2304]{1,0:T(8,128)(2,1)}, u32[]{:S(2)}, u32[]{:S(2)}) collective-permute-start(bf16[128,2304]{1,0:T(8,128)(2,1)} %get-tuple-element.54), channel_id=1, source_target_pairs={{0,2},{2,4},{4,6},{6,7},{7,5},{5,3},{3,1},{1,0},{8,10},{10,12},{12... | collective-permute-start | bytes 1769480 | tf_op jit(solution)/shard_map/ppermute | solution.py:156
  646.4 29.3 %collective-permute-start.55 = (bf16[128,2304]{1,0:T(8,128)(2,1)}, bf16[128,2304]{1,0:T(8,128)(2,1)}, u32[]{:S(2)}, u32[]{:S(2)}) collective-permute-start(bf16[128,2304]{1,0:T(8,128)(2,1)} %get-tuple-element.55), channel_id=1, source_target_pairs={{2,0},{4,2},{6,4},{7,6},{5,7},{3,5},{1,3},{0,1},{10,8},{12,10},{14... | collective-permute-start | bytes 1769480 | tf_op jit(solution)/shard_map/ppermute | solution.py:159
  657.7 57.8 %collective-permute-start.58 = (bf16[8,2,72,960]{3,2,1,0:T(8,128)(2,1)}, bf16[8,2,72,960]{3,2,1,0:T(8,128)(2,1)}, u32[]{:S(2)}, u32[]{:S(2)}) collective-permute-start(bf16[8,2,72,960]{3,2,1,0:T(8,128)(2,1)} %dynamic-slice_bitcast_fusion), channel_id=1, source_target_pairs={{0,8},{8,0},{16,24},{24,16},{1,9},{9,1},{17,25},{25,17},{2,10},{10... | collective-permute-start | bytes 6635528 | tf_op jit(solution)/shard_map/ppermute | solution.py:162
  671.6 18.3 %all-to-all-start.5 = ((bf16[8,72,288]{2,1,0:T(8,128)(2,1)}), bf16[8,72,288]{2,1,0:T(8,128)(2,1)}, u32[]{:S(2)}, u32[]{:S(2)}) async-start(bf16[8,72,288]{2,1,0:T(8,128)(2,1)} %fusion.47), calls=%async_computation.5 | async-start | bytes 884736 | tf_op jit(solution)/shard_map/all_to_all | solution.py:205
  680.7 26.6 %collective-permute-start.53 = (bf16[128,2304]{1,0:T(8,128)(2,1)}, bf16[128,2304]{1,0:T(8,128)(2,1)}, u32[]{:S(2)}, u32[]{:S(2)}) collective-permute-start(bf16[128,2304]{1,0:T(8,128)(2,1)} %get-tuple-element.52), channel_id=1, source_target_pairs={{0,2},{2,4},{4,6},{6,7},{7,5},{5,3},{3,1},{1,0},{8,10},{10,12},{12... | collective-permute-start | bytes 1769480 | tf_op jit(solution)/shard_map/ppermute | solution.py:156
  681.5 25.8 %collective-permute-start.56 = (bf16[128,2304]{1,0:T(8,128)(2,1)}, bf16[128,2304]{1,0:T(8,128)(2,1)}, u32[]{:S(2)}, u32[]{:S(2)}) collective-permute-start(bf16[128,2304]{1,0:T(8,128)(2,1)} %get-tuple-element.53), channel_id=1, source_target_pairs={{2,0},{4,2},{6,4},{7,6},{5,7},{3,5},{1,3},{0,1},{10,8},{12,10},{14... | collective-permute-start | bytes 1769480 | tf_op jit(solution)/shard_map/ppermute | solution.py:159
  703.7 52.6 %all-to-all-start.6 = ((bf16[8,144,720]{2,1,0:T(8,128)(2,1)}), bf16[8,144,720]{2,1,0:T(8,128)(2,1)S(1)}, u32[]{:S(2)}, u32[]{:S(2)}) async-start(bf16[8,144,720]{2,1,0:T(8,128)(2,1)} %fusion.12), calls=%async_computation.6 | async-start | bytes 3538944 | tf_op jit(solution)/shard_map/all_to_all | solution.py:205
  709.2 42.4 %collective-permute-start.57 = (bf16[128,2304]{1,0:T(8,128)(2,1)S(1)}, bf16[128,2304]{1,0:T(8,128)(2,1)S(1)}, u32[]{:S(2)}, u32[]{:S(2)}) collective-permute-start(bf16[128,2304]{1,0:T(8,128)(2,1)S(1)} %get-tuple-element.51), channel_id=1, source_target_pairs={{2,0},{4,2},{6,4},{7,6},{5,7},{3,5},{1,3},{0,1},{10,8},{12,10},{14... | collective-permute-start | bytes 1769480 | tf_op jit(solution)/shard_map/ppermute | solution.py:159
  711.2 40.5 %collective-permute-start.54 = (bf16[128,2304]{1,0:T(8,128)(2,1)S(1)}, bf16[128,2304]{1,0:T(8,128)(2,1)S(1)}, u32[]{:S(2)}, u32[]{:S(2)}) collective-permute-start(bf16[128,2304]{1,0:T(8,128)(2,1)S(1)} %get-tuple-element.50), channel_id=1, source_target_pairs={{0,2},{2,4},{4,6},{6,7},{7,5},{5,3},{3,1},{1,0},{8,10},{10,12},{12... | collective-permute-start | bytes 1769480 | tf_op jit(solution)/shard_map/ppermute | solution.py:156
  719.2 35.6 %collective-permute-start.59 = (bf16[8,72,960]{2,1,0:T(8,128)(2,1)S(1)}, bf16[8,72,960]{2,1,0:T(8,128)(2,1)S(1)}, u32[]{:S(2)}, u32[]{:S(2)}) collective-permute-start(bf16[8,72,960]{2,1,0:T(8,128)(2,1)S(1)} %dynamic-slice_bitcast_fusion.3), channel_id=1, source_target_pairs={{0,16},{8,24},{16,0},{24,8},{1,17},{9,25},{17,1},{25,9},{2,18},{10... | collective-permute-start | bytes 3317768 | tf_op jit(solution)/shard_map/ppermute | solution.py:165
  756.3 42.4 %all-to-all-start.3 = ((bf16[8,72,960]{2,1,0:T(8,128)(2,1)}), bf16[8,72,960]{2,1,0:T(8,128)(2,1)}, u32[]{:S(2)}, u32[]{:S(2)}) async-start(bf16[8,72,960]{2,1,0:T(8,128)(2,1)} %fusion.16), calls=%async_computation.3 | async-start | bytes 2359296 | tf_op jit(solution)/shard_map/all_to_all | solution.py:205
  777.9 39.4 %collective-permute-start.70 = (bf16[2,72,5760]{2,1,0:T(8,128)(2,1)}, bf16[2,72,5760]{2,1,0:T(8,128)(2,1)}, u32[]{:S(2)}, u32[]{:S(2)}) collective-permute-start(bf16[2,72,5760]{2,1,0:T(8,128)(2,1)} %reshape.594), channel_id=1, source_target_pairs={{0,16},{8,24},{16,0},{24,8},{1,17},{9,25},{17,1},{25,9},{2,18},{10... | collective-permute-start | bytes 4976648 | tf_op jit(solution)/shard_map/ppermute | solution.py:165
  778.2 41.8 %collective-permute-start.71 = (bf16[2,72,5760]{2,1,0:T(8,128)(2,1)}, bf16[2,72,5760]{2,1,0:T(8,128)(2,1)S(1)}, u32[]{:S(2)}, u32[]{:S(2)}) collective-permute-start(bf16[2,72,5760]{2,1,0:T(8,128)(2,1)} %reshape.594), channel_id=1, source_target_pairs={{0,8},{8,0},{16,24},{24,16},{1,9},{9,1},{17,25},{25,17},{2,10},{10... | collective-permute-start | bytes 4976648 | tf_op jit(solution)/shard_map/ppermute | solution.py:162
  801.8 35.6 %collective-permute-start.60 = (bf16[3,72,2304]{2,1,0:T(8,128)(2,1)S(1)}, bf16[3,72,2304]{2,1,0:T(8,128)(2,1)S(1)}, u32[]{:S(2)}, u32[]{:S(2)}) collective-permute-start(bf16[3,72,2304]{2,1,0:T(8,128)(2,1)S(1)} %pad_maximum_fusion.2), channel_id=1, source_target_pairs={{0,16},{8,24},{16,0},{24,8},{1,17},{9,25},{17,1},{25,9},{2,18},{10... | collective-permute-start | bytes 2985992 | tf_op jit(solution)/shard_map/ppermute | solution.py:165
  802.2 35.5 %collective-permute-start.61 = (bf16[3,72,2304]{2,1,0:T(8,128)(2,1)S(1)}, bf16[3,72,2304]{2,1,0:T(8,128)(2,1)S(1)}, u32[]{:S(2)}, u32[]{:S(2)}) collective-permute-start(bf16[3,72,2304]{2,1,0:T(8,128)(2,1)S(1)} %pad_maximum_fusion.2), channel_id=1, source_target_pairs={{0,8},{8,0},{16,24},{24,16},{1,9},{9,1},{17,25},{25,17},{2,10},{10... | collective-permute-start | bytes 2985992 | tf_op jit(solution)/shard_map/ppermute | solution.py:162
  817.3 39.7 %collective-permute-start.72 = (bf16[2,72,5760]{2,1,0:T(8,128)(2,1)}, bf16[2,72,5760]{2,1,0:T(8,128)(2,1)}, u32[]{:S(2)}, u32[]{:S(2)}) collective-permute-start(bf16[2,72,5760]{2,1,0:T(8,128)(2,1)} %collective-permute-done.70), channel_id=1, source_target_pairs={{0,8},{8,0},{16,24},{24,16},{1,9},{9,1},{17,25},{25,17},{2,10},{10... | collective-permute-start | bytes 4976648 | tf_op jit(solution)/shard_map/ppermute | solution.py:162
  (59 other events, 800.2 us)

commit v3 on v2

v3 whole, which is shorter than its diff:
```python
import functools
import math

import jax
import jax.numpy as jnp
from jax import lax
from jax.experimental import pallas as pl
from jax.experimental.layout import Layout, with_layout_constraint
from jax.experimental.pallas import tpu as pltpu
from jax.sharding import PartitionSpec as P

HD = 64
HALF = HD // 2
PIC = 64

EPSILON = 1e-05
BRANCH_SCALE = 1.4 / math.sqrt(40.0)
MASKED = -1e30
F32 = jnp.float32
BF16 = jnp.bfloat16


def mm(left, right, left_dim, right_dim):
    return lax.dot_general(
        left, right, (((left_dim,), (right_dim,)), ((), ())), preferred_element_type=F32
    )


def layout(lengths, starts, row_count):
    places = jnp.arange(row_count, dtype=jnp.int32)
    bounds = jnp.cumsum(lengths)
    firsts = bounds - lengths
    member = (places[:, None] >= firsts[None, :]) & (places[:, None] < bounds[None, :])
    doc_of = jnp.sum(
        jnp.where(member, jnp.arange(lengths.shape[0], dtype=jnp.int32)[None, :], 0), axis=1
    )
    starting = jnp.sum(jnp.where(member, firsts[None, :], 0), axis=1)
    inside = (places[None, :] >= starts[:, None]) & (places[None, :] < starts[:, None] + PIC)
    shared = jnp.any(inside[:, :, None] & inside[:, None, :], axis=0)
    causal = places[None, :] >= places[:, None]
    allowed = (doc_of[:, None] == doc_of[None, :]) & (causal | shared)
    return (places - starting, allowed)


def turn(values, cosine, sine):
    first, second = values[:HALF], values[HALF:]
    return jnp.concatenate([first * cosine - second * sine, second * cosine + first * sine], axis=0)


def probabilities(keys, query, bias):
    scores = mm(keys, query, 0, 0) * HD**-0.5 + bias
    expo = jnp.exp(scores - jnp.max(scores, axis=0, keepdims=True))
    return expo / jnp.sum(expo, axis=0, keepdims=True)


def feature_rows(base, slots, kind, head):
    if head < base:
        return (kind * base + head) * HD
    return (3 * base + kind * (slots - base) + head - base) * HD


def attend_kernel(base, slots, qkv_ref, scale_ref, cos_ref, sin_ref, bias_ref, qkv_out_ref, mixed_ref):
    scale = scale_ref[...]
    cosine, sine, bias = cos_ref[...], sin_ref[...], bias_ref[0]
    for head in range(slots):
        at = [pl.ds(feature_rows(base, slots, kind, head), HD) for kind in range(3)]
        query = turn(qkv_ref[at[0], :] * scale, cosine, sine).astype(BF16)
        keys = turn(qkv_ref[at[1], :] * scale, cosine, sine).astype(BF16)
        values = (qkv_ref[at[2], :] * scale).astype(BF16)
        qkv_out_ref[at[0], :] = query
        qkv_out_ref[at[1], :] = keys
        qkv_out_ref[at[2], :] = values
        probs = probabilities(keys, query, bias).astype(BF16)
        mixed_ref[pl.ds(head * HD, HD), :] = mm(values, probs, 1, 0).astype(BF16)


def attend_back_kernel(base, slots, qkv_ref, grad_ref, scale_ref, cos_ref, sin_ref, bias_ref, out_ref):
    scale = scale_ref[...]
    cosine, sine, bias = cos_ref[...], sin_ref[...], bias_ref[0]
    back = scale * HD**-0.5
    for head in range(slots):
        at = [pl.ds(feature_rows(base, slots, kind, head), HD) for kind in range(3)]
        query = qkv_ref[at[0], :]
        keys = qkv_ref[at[1], :]
        values = qkv_ref[at[2], :]
        grad = grad_ref[pl.ds(head * HD, HD), :]
        probs = probabilities(keys, query, bias)
        grad_values = mm(grad, probs.astype(BF16), 1, 1)
        grad_probs = mm(values, grad, 0, 0)
        inner = jnp.sum(probs * grad_probs, axis=0, keepdims=True)
        grad_scores = (probs * (grad_probs - inner)).astype(BF16)
        grad_query = turn(mm(keys, grad_scores, 1, 0) * back, cosine, -sine)
        grad_keys = turn(mm(query, grad_scores, 1, 1) * back, cosine, -sine)
        out_ref[at[0], :] = grad_query.astype(BF16)
        out_ref[at[1], :] = grad_keys.astype(BF16)
        out_ref[at[2], :] = (grad_values * scale).astype(BF16)


def columns(height, rows):
    return pl.BlockSpec((height, rows), lambda r: (0, r))


def attention_specs(rows):
    return [
        columns(1, rows),
        columns(HALF, rows),
        columns(HALF, rows),
        pl.BlockSpec((1, rows, rows), lambda r: (r, 0, 0)),
    ]


def attend(base, slots, n, rows, qkv, scale, cosine, sine, bias):
    block = slots * HD
    tokens = n * rows
    flops = 4 * n * slots * rows * rows * HD
    return pl.pallas_call(
        functools.partial(attend_kernel, base, slots),
        grid=(n,),
        in_specs=[columns(3 * block, rows)] + attention_specs(rows),
        out_specs=[columns(3 * block, rows), columns(block, rows)],
        out_shape=[
            jax.ShapeDtypeStruct((3 * block, tokens), BF16),
            jax.ShapeDtypeStruct((block, tokens), BF16),
        ],
        cost_estimate=pl.CostEstimate(
            flops=flops, bytes_accessed=20 * block * tokens, transcendentals=n * slots * rows * rows
        ),
        compiler_params=pltpu.CompilerParams(vmem_limit_bytes=12 * 2**20),
        name="attend",
    )(qkv, scale, cosine, sine, bias)


def attend_back(base, slots, n, rows, qkv, grad, scale, cosine, sine, bias):
    block = slots * HD
    tokens = n * rows
    flops = 10 * n * slots * rows * rows * HD
    return pl.pallas_call(
        functools.partial(attend_back_kernel, base, slots),
        grid=(n,),
        in_specs=[columns(3 * block, rows), columns(block, rows)] + attention_specs(rows),
        out_specs=columns(3 * block, rows),
        out_shape=jax.ShapeDtypeStruct((3 * block, tokens), BF16),
        cost_estimate=pl.CostEstimate(
            flops=flops, bytes_accessed=14 * block * tokens, transcendentals=n * slots * rows * rows
        ),
        compiler_params=pltpu.CompilerParams(vmem_limit_bytes=16 * 2**20),
        name="attend_back",
    )(qkv, grad, scale, cosine, sine, bias)


def row_major(array):
    return with_layout_constraint(array, Layout(tuple(range(array.ndim))))


def empty(shape, dtype):
    return pl.pallas_call(
        lambda out_ref: None,
        out_specs=pl.BlockSpec(memory_space=pl.ANY),
        out_shape=jax.ShapeDtypeStruct(shape, dtype),
        compiler_params=pltpu.CompilerParams(vmem_limit_bytes=1 * 2**20),
        name="empty",
    )()


def low(weight):
    return weight.astype(BF16).astype(F32)


def prepare_kernel(n, base, slots, heads, own_ref, query_ref, key_ref, value_ref, gain_ref, info_ref, out_ref):
    part = query_ref.shape[1]
    main = base * HD
    for kind, ref in enumerate((query_ref, key_ref, value_ref)):
        weight = (low(ref[0]) * gain_ref[0]).astype(BF16)
        for j in range(n):
            out_ref[j, :part, kind * main : (kind + 1) * main] = weight[:, j * main : (j + 1) * main]
            if slots > base:
                first = 3 * main + kind * HD
                head = n * base + j
                if head < heads:
                    extra = weight[:, head * HD : (head + 1) * HD]
                else:
                    extra = jnp.zeros((part, HD), BF16)
                out_ref[j, :part, first : first + HD] = extra
    for j in range(n):
        out_ref[j, part:, :] = info_ref[...]


def prepare_ffn_kernel(n, own_ref, gate_ref, up_ref, gain_ref, out_ref):
    part, cols = gate_ref.shape[1], out_ref.shape[2]
    for kind, ref in enumerate((gate_ref, up_ref)):
        weight = (low(ref[0]) * gain_ref[0]).astype(BF16)
        for j in range(n):
            out_ref[j, kind * part : (kind + 1) * part, :] = weight[:, j * cols : (j + 1) * cols]


def own_part(part, width):
    return pl.BlockSpec((1, part, width), lambda i, own: (own[0], 0, 0))


def prepare(kernel, own, weights, gain, more, out_shape, name):
    part = weights[0].shape[1]
    return pl.pallas_call(
        kernel,
        grid_spec=pltpu.PrefetchScalarGridSpec(
            num_scalar_prefetch=1,
            grid=(1,),
            in_specs=[own_part(part, w.shape[2]) for w in weights]
            + [own_part(part, 1)]
            + [pl.BlockSpec(m.shape, lambda i, own: (0, 0)) for m in more],
            out_specs=pl.BlockSpec(out_shape, lambda i, own: (0, 0, 0)),
        ),
        out_shape=jax.ShapeDtypeStruct(out_shape, BF16),
        name=name,
    )(own, *weights, gain, *more)


def finish_kernel(count, gained, at_ref, piece_ref, *refs):
    weights = refs[:gained]
    outs = refs[-(count + (gained > 0)) :]
    total = 0.0
    for k in range(count):
        raw = piece_ref[k].astype(F32)
        if k < gained:
            total = total + jnp.sum(low(weights[k][0]) * raw, axis=1, keepdims=True)
            raw = raw * refs[gained][0]
        outs[k][0] = raw
    if gained:
        first = pl.program_id(0) == 0
        outs[count][0] = jnp.where(first, 0.0, outs[count][0]) + total


def finish(piece, at, rep, weights, gain, previous):
    count, part, width = piece.shape
    gained = len(weights)
    chunk = max(c for c in range(128, 1153, 128) if width % c == 0)

    def placed(size, moving):
        return pl.BlockSpec((1, part, size), lambda i, at: (at[0], 0, i if moving else 0))

    in_specs = [pl.BlockSpec((count, part, chunk), lambda i, at: (0, 0, i))]
    operands = [piece]
    out_specs = [placed(chunk, True)] * count
    out_shape = [jax.ShapeDtypeStruct((rep, part, width), F32)] * count
    if gained:
        in_specs += [placed(chunk, True)] * gained + [placed(1, False)]
        operands += list(weights) + [gain]
        out_specs.append(placed(1, False))
        out_shape.append(jax.ShapeDtypeStruct((rep, part, 1), F32))
    aliases = {}
    if previous is not None:
        aliases = {1 + len(operands) + k: k for k in range(len(out_shape))}
        operands += list(previous)
        in_specs += [pl.BlockSpec(memory_space=pl.ANY)] * len(out_shape)
    return pl.pallas_call(
        functools.partial(finish_kernel, count, gained),
        grid_spec=pltpu.PrefetchScalarGridSpec(
            num_scalar_prefetch=1, grid=(width // chunk,), in_specs=in_specs, out_specs=out_specs
        ),
        out_shape=out_shape,
        input_output_aliases=aliases,
        cost_estimate=pl.CostEstimate(
            flops=4 * count * part * width,
            bytes_accessed=(6 * count + 4 * gained) * part * width,
            transcendentals=0,
        ),
        name="finish",
    )(at, *operands)


def build(rep, n):
    cycle = list(range(0, n, 2)) + list(range(n - 1, 0, -2)) if n % 2 == 0 else list(range(n))
    to_right = [(cycle[i], cycle[(i + 1) % n]) for i in range(n)]
    to_left = [(b, a) for a, b in to_right]
    steps_right = n // 2
    steps_left = n - 1 - steps_right
    outer = rep // 2
    core_pairs = [(i, i ^ 1) for i in range(rep)]
    chip_pairs = [(i, (i + 2) % rep) for i in range(rep)]

    def right(x):
        return lax.ppermute(x, "shard", to_right)

    def left(x):
        return lax.ppermute(x, "shard", to_left)

    def core_swap(x):
        return lax.ppermute(x, "rep", core_pairs)

    def chip_swap(x):
        return lax.ppermute(x, "rep", chip_pairs)

    def ring_device(offset):
        device = lax.axis_index("shard")
        if n % 2:
            return (device + offset + n) % n
        place = jnp.where(device % 2 == 0, device // 2, n - 1 - device // 2)
        place = (place + offset + n) % n
        return jnp.where(place < n // 2, 2 * place, 2 * (n - 1 - place) + 1)

    def ring_gather(piece):
        pieces = [(ring_device(0), piece)]
        going_right = going_left = piece
        for step in range(1, steps_right + 1):
            going_right = right(going_right)
            pieces.append((ring_device(-step), going_right))
            if step <= steps_left:
                going_left = left(going_left)
                pieces.append((ring_device(step), going_left))
        return pieces

    def gather_shard(piece):
        pieces = ring_gather(piece)
        whole = empty((n,) + piece.shape, piece.dtype)
        for device, part in pieces:
            whole = lax.dynamic_update_index_in_dim(whole, part, device, 0)
        return whole.reshape((-1,) + piece.shape[1:]), pieces[-1][1]

    def scatter_shard(parts):
        def term(offset):
            return lax.dynamic_index_in_dim(parts, ring_device(offset), 0, keepdims=False).astype(F32)

        going_right = term(steps_right).astype(BF16)
        going_left = term(-steps_left).astype(BF16)
        for step in range(1, steps_right + 1):
            going_right = right(going_right)
            if step < steps_right:
                going_right = (going_right.astype(F32) + term(steps_right - step)).astype(BF16)
            if step <= steps_left:
                going_left = left(going_left)
                if step < steps_left:
                    going_left = (going_left.astype(F32) + term(step - steps_left)).astype(BF16)
        return going_right.astype(F32) + going_left.astype(F32) + term(0)

    def exchange(blocks):
        return lax.all_to_all(blocks, "shard", split_axis=0, concat_axis=0, tiled=True)

    def pick(array, index, axis):
        return lax.dynamic_index_in_dim(array, index, axis, keepdims=False)

    def add(a, b):
        return (a.astype(F32) + b.astype(F32)).astype(BF16)

    def after(value, *others):
        return lax.optimization_barrier((value, others))[0]

    def rep_pieces(piece):
        mine = lax.axis_index("rep")
        far = (mine + 2) % rep
        other_chip = chip_swap(piece)
        other_core = core_swap(piece)
        last = core_swap(other_chip)
        return [(mine, piece), (mine ^ 1, other_core), (far, other_chip), (far ^ 1, last)]

    def gather_rep(piece, axis):
        whole = empty(piece.shape[:axis] + (rep,) + piece.shape[axis:], piece.dtype)
        for index, part in rep_pieces(piece):
            whole = lax.dynamic_update_index_in_dim(whole, part, index, axis)
        return whole

    def scatter_rep(blocks):
        mine = lax.axis_index("rep")
        chip, core = mine // 2, mine % 2
        blocks = blocks.reshape((blocks.shape[0], outer, 2) + blocks.shape[2:])
        half = add(pick(blocks, core, 2), core_swap(pick(blocks, 1 - core, 2)))
        return add(pick(half, chip, 1), chip_swap(pick(half, 1 - chip, 1)))

    def local(
        tokens,
        doc_lengths,
        pic_starts,
        attn_gain,
        w_query,
        w_key,
        w_value,
        w_out,
        ffn_gain,
        w_gate,
        w_up,
        w_down,
        cotangent,
    ):
        rows, width = tokens.shape
        heads = width // HD
        base = heads // n
        slots = -(-heads // n)
        block = slots * HD
        main = base * HD
        mains = n * main
        over = heads - n * base
        depth = w_query.shape[0]
        part = depth // rep
        ff = w_gate.shape[1]
        cols = ff // n
        all_rows = n * rows
        me = lax.axis_index("shard")
        mine = lax.axis_index("rep")
        own = mine.reshape(1)
        docs = doc_lengths.shape[1]
        pics = pic_starts.shape[1]

        def by_rep(array):
            return array.reshape(rep, -1, array.shape[1])

        gain_one = by_rep(low(attn_gain)[:, None])
        gain_two = by_rep(low(ffn_gain)[:, None])

        def by_heads(array):
            first = array[:mains].reshape(n, main, -1)
            if slots == base:
                return first
            rest = jnp.pad(array[mains:], ((0, n * HD - (width - mains)), (0, 0)))
            return jnp.concatenate([first, rest.reshape(n, HD, -1)], axis=1)

        def from_heads(array, kind):
            first = array[:, :, kind * main : (kind + 1) * main].transpose(1, 0, 2)
            first = first.reshape(array.shape[1], mains)
            if slots == base:
                return first
            start = 3 * main + kind * HD
            rest = array[:over, :, start : start + HD].transpose(1, 0, 2)
            return jnp.concatenate([first, rest.reshape(array.shape[1], width - mains)], axis=1)

        inputs, last_input = gather_shard(tokens)
        info = jnp.concatenate([doc_lengths[0], pic_starts[0]]).astype(BF16)
        info = jnp.zeros((8, 3 * block), BF16).at[0, : docs + pics].set(info)
        qkv_part = prepare(
            functools.partial(prepare_kernel, n, base, slots, heads),
            own,
            [by_rep(w) for w in (w_query, w_key, w_value)],
            gain_one,
            [info],
            (n, part + 8, 3 * block),
            "prepare_qkv",
        )
        qkv_part = exchange(qkv_part)
        info = qkv_part[:, part, : docs + pics].astype(jnp.int32)
        qkv_w = gather_rep(qkv_part[:, :part], 1).reshape(width, 3 * block)
        out_part = after(pick(by_rep(w_out), mine, 0), last_input).astype(BF16)
        out_w = lax.all_gather(out_part, ("shard", "rep"), axis=0, tiled=True)
        ffn_part = prepare(
            functools.partial(prepare_ffn_kernel, n),
            own,
            [by_rep(w) for w in (w_gate, w_up)],
            gain_two,
            [],
            (n, 2 * part, cols),
            "prepare_ffn",
        )
        ffn_part = exchange(after(ffn_part, qkv_part, last_input))
        down_w = w_down.astype(BF16)
        grad_result = cotangent.astype(F32)

        offsets, allowed = jax.vmap(lambda a, b: layout(a, b, rows))(info[:, :docs], info[:, docs:])
        bias = jnp.where(allowed, 0.0, MASKED).astype(F32)
        freq_table = jnp.exp(jnp.arange(HALF, dtype=F32) * (-2.0 * math.log(10000.0) / HD))
        turned = freq_table[:, None] * offsets.reshape(1, all_rows).astype(F32)
        cosine, sine = jnp.cos(turned), jnp.sin(turned)
        squares = jnp.mean(jnp.square(inputs.astype(F32)), axis=-1)
        scale_one = lax.rsqrt(squares + EPSILON)[None, :]
        qkv = mm(qkv_w, inputs, 0, 1)
        qkv, mixed = attend(base, slots, n, rows, qkv, scale_one, cosine, sine, bias)
        ffn_part = after(ffn_part, mixed)
        ffn_w = gather_rep(ffn_part.reshape(n, 2, part, cols).transpose(1, 0, 2, 3), 2)
        gate_w = ffn_w[0].reshape(width, cols)
        up_w = ffn_w[1].reshape(width, cols)
        mixed_all = empty((n * block, all_rows), BF16)
        mixed_pieces = ring_gather(mixed)
        for device, piece in mixed_pieces:
            mixed_all = lax.dynamic_update_slice_in_dim(mixed_all, piece[:main], device * main, 0)
            if slots > base:
                mixed_all = lax.dynamic_update_slice_in_dim(
                    mixed_all, piece[main:], mains + device * HD, 0
                )
        mixed_all = mixed_all[:width]
        middle = inputs.astype(F32) + BRANCH_SCALE * mm(mixed_all, out_w, 0, 0)

        grad_branch = after((BRANCH_SCALE * grad_result).astype(BF16), mixed_pieces[-1][1])
        grad_branch, _ = gather_shard(grad_branch)
        scale_two = lax.rsqrt(jnp.mean(middle * middle, axis=-1, keepdims=True) + EPSILON)
        middle_low = middle.astype(BF16)
        gate_act = mm(middle_low, gate_w, 1, 0) * scale_two
        up_act = mm(middle_low, up_w, 1, 0) * scale_two
        sigmoid_gate = jax.nn.sigmoid(gate_act)
        silu_gate = gate_act * sigmoid_gate
        inner = (silu_gate * up_act).astype(BF16)
        grad_inner = mm(grad_branch, down_w, 1, 1)
        grad_gate_act = (
            grad_inner
            * up_act
            * sigmoid_gate
            * (1.0 + gate_act * (1.0 - sigmoid_gate))
            * scale_two
        ).astype(BF16)
        grad_up_act = (grad_inner * silu_gate * scale_two).astype(BF16)
        partial = mm(grad_gate_act, gate_w, 1, 1) + mm(grad_up_act, up_w, 1, 1)
        partial = partial.astype(BF16).reshape(n, rows, width)
        back_two = scatter_shard(partial)
        my_middle = lax.dynamic_slice_in_dim(middle, me * rows, rows, 0)
        my_normed_two = my_middle * lax.dynamic_slice_in_dim(scale_two, me * rows, rows, 0)
        inner_mean = jnp.mean(back_two * my_normed_two, axis=-1, keepdims=True)
        grad_middle = grad_result + back_two - my_normed_two * inner_mean

        def rep_rows(grad):
            return row_major(grad.astype(BF16)).reshape(n, rep, part, grad.shape[1])

        def finish_all(piece, weights, gain):
            done = None
            for index, arrived in rep_pieces(piece):
                done = finish(
                    arrived, index.reshape(1), rep, [by_rep(w) for w in weights], gain, done
                )
            return [a.reshape(-1, a.shape[2]) for a in done]

        inner, grad_gate_act, grad_up_act, _ = lax.optimization_barrier(
            (inner, grad_gate_act, grad_up_act, partial)
        )
        grad_down = mm(inner, grad_branch, 0, 0).astype(BF16).reshape(1, rep, -1, width)
        (grad_down,) = finish_all(scatter_rep(grad_down), (), None)
        grad_ffn = [rep_rows(mm(middle_low, g, 0, 0)) for g in (grad_gate_act, grad_up_act)]
        grad_ffn = scatter_rep(jnp.concatenate(grad_ffn, axis=2))
        grad_attn = (BRANCH_SCALE * grad_middle).astype(BF16)
        grad_mixed = exchange(by_heads(mm(out_w, grad_attn, 1, 1).astype(BF16)))
        grad_attn_cols = after(grad_attn.T.reshape(n, depth, rows), grad_mixed)
        grad_attn_cols = exchange(grad_attn_cols).transpose(1, 0, 2).reshape(depth, all_rows)
        grad_mixed = grad_mixed.transpose(1, 0, 2).reshape(block, all_rows)
        grad_qkv = attend_back(
            base, slots, n, rows, qkv, grad_mixed, scale_one, cosine, sine, bias
        )
        grad_ffn = exchange(after(grad_ffn, grad_mixed))
        grad_ffn = grad_ffn.reshape(n, 2, part, cols).transpose(1, 2, 0, 3).reshape(2, part, ff)
        grad_gate, grad_up, grad_gain_two = finish_all(grad_ffn, (w_gate, w_up), gain_two)
        grad_w = jnp.concatenate(
            [
                row_major(mm(inputs, grad_qkv, 0, 1).astype(BF16)),
                row_major(mm(mixed_all, grad_attn_cols, 1, 1).astype(BF16)),
            ],
            axis=1,
        )
        partial = mm(after(grad_qkv, grad_w), qkv_w, 0, 1)
        back_one = scatter_shard(partial.astype(BF16).reshape(n, rows, width))
        my_inputs = tokens.astype(F32)
        my_scale_one = lax.rsqrt(jnp.mean(my_inputs * my_inputs, axis=-1, keepdims=True) + EPSILON)
        my_normed_one = my_inputs * my_scale_one
        inner_mean = jnp.mean(back_one * my_normed_one, axis=-1, keepdims=True)
        input_grad = grad_middle + back_one - my_normed_one * inner_mean

        branch = mm(after(inner, back_two), down_w, 1, 0).astype(BF16).reshape(n, rows, width)
        branch = scatter_shard(after(branch, back_one))
        out_tokens = (my_middle + BRANCH_SCALE * branch).astype(BF16)

        grad_w = exchange(scatter_rep(grad_w.reshape(n, rep, part, -1)))
        grad_w = jnp.stack(
            [from_heads(grad_w, kind) for kind in range(3)]
            + [grad_w[:, :, 3 * block :].transpose(1, 0, 2).reshape(part, width)]
        )
        grad_query, grad_key, grad_value, grad_out, grad_gain_one = finish_all(
            grad_w, (w_query, w_key, w_value), gain_one
        )
        return (
            out_tokens,
            input_grad,
            grad_gain_one.reshape(depth),
            grad_query,
            grad_key,
            grad_value,
            grad_out,
            grad_gain_two.reshape(depth),
            grad_gate,
            grad_up,
            grad_down,
        )

    return local


def solution(mesh):
    tokens = P(("rep", "shard"), None)
    weight = P("shard", None)
    gain = P("shard")
    return jax.shard_map(
        build(mesh.shape["rep"], mesh.shape["shard"]),
        mesh=mesh,
        in_specs=(
            tokens,
            tokens,
            tokens,
            gain,
            weight,
            weight,
            weight,
            weight,
            gain,
            weight,
            weight,
            weight,
            tokens,
        ),
        out_specs=(
            tokens,
            tokens,
            gain,
            weight,
            weight,
            weight,
            weight,
            gain,
            weight,
            weight,
            weight,
        ),
        check_vma=False,
    )
```

time: 917 us -> 792 us (0.86)
  local copies, waits for them, and re-layouts: 218 us -> 107 us
  other arithmetic: 119 us -> 65.1 us
  Pallas kernels: 21.9 us -> 71.6 us
  between operations: 36.6 us -> 15.1 us
  starting transfers between devices: 113 us -> 131 us
  matrix products: 120 us -> 109 us
  waiting for transfers between devices: 276 us -> 286 us
    all_to_all x7 -> x6, waiting for transfers between devices: 49.8 us -> 0.02 us  [exchange(): lax.all_to_all(blocks, 'shard', split_axis=0, concat_axis=0, tiled=True)]
    pallas_call x2 -> x21, Pallas kernels: 21.9 us -> 71.6 us  [the longest x12 46.6 us: finish(): pl.pallas_call(functools.partial(finish_kernel, count, gained), grid_spec...]
    dynamic_update_slice x27 -> x8, local copies, waits for them, and re-layouts: 49.8 us -> 8.51 us  [gather_rep(): whole = lax.dynamic_update_index_in_dim(whole, part, index, axis)]
    ppermute x21 -> x18, waiting for transfers between devices: 48.8 us -> 89.5 us  [left(): return lax.ppermute(x, 'shard', to_left)]
    ppermute x28 -> x24, starting transfers between devices: 34.8 us -> 75.4 us  [right(): return lax.ppermute(x, 'shard', to_right)]
    mul x2 -> x0, other arithmetic: 28.8 us -> none  [the longest x1 18.6 us: local(): grad_ffn[1] * gain_two]
    convert_element_type x5 -> x1, local copies, waits for them, and re-layouts: 23.2 us -> 0.08 us  [local(): info = qkv_part[:, part, :docs + pics].astype(jnp.int32)]
    slice x15 -> x4, local copies, waits for them, and re-layouts: 25.3 us -> 5.75 us  [the longest x1 3.34 us: local(): gate_w = ffn_w[0].reshape(width, cols)]
  transfers between devices with their start and end apart: 85 -> 70, of which waited for: 32 -> 32; matrix products, arithmetic and copies ran while one was open for 35% -> 26% of each run, Pallas kernels for 2% -> 9%
where the time goes in v3:
time: 792 us; the launch traced here: 784 us
  waiting for transfers between devices  286 us (36%)
  starting transfers between devices  131 us (17%)
  matrix products  109 us (14%)
  local copies, waits for them, and re-layouts  107 us (14%)
  Pallas kernels  71.6 us (9%)
  other arithmetic  65.1 us (8%)
  between operations  15.1 us (2%)
    ppermute x24, waiting for transfers between devices, right(): return lax.ppermute(x, 'shard', to_right)  143 us
    dot_general x15, matrix products, mm(): lax.dot_general(left, right, (((left_dim,), (right_dim,)), ((), ())), pre...  109 us
    ppermute x18, waiting for transfers between devices, left(): return lax.ppermute(x, 'shard', to_left)  89.5 us
    ppermute x24, starting transfers between devices, right(): return lax.ppermute(x, 'shard', to_right)  75.4 us
    ppermute x8, waiting for transfers between devices, chip_swap(): return lax.ppermute(x, 'rep', chip_pairs)  53.7 us
    pallas_call x12, Pallas kernels, finish(): pl.pallas_call(functools.partial(finish_kernel, count, gained), grid_spec...  46.6 us
    all_to_all x6, starting transfers between devices, exchange(): lax.all_to_all(blocks, 'shard', split_axis=0, concat_axis=0, tiled=True)  33.9 us
    dynamic_update_slice x16, local copies, waits for them, and re-layouts, gather_shard(): whole = lax.dynamic_update_index_in_dim(whole, part, device, 0)  18.3 us
  transfers between devices with their start and end apart: 70, of which 32 were waited for; matrix products, arithmetic and copies ran while one was open for 26% of the time, Pallas kernels for 9%

profile of v3, /device:TPU:0, one launch (start us, length us, event | category | flops | bytes accessed | tf_op | source)
XLA Modules:
  0.0 784.2 jit_solution(7410211098365750068)
XLA Ops:
  16.8 6.3 all-to-all-start
  31.2 3.9 prepare_ffn.1
  35.9 21.4 %collective-permute-done.2 = bf16[128,2304]{1,0:T(8,128)(2,1)} collective-permute-done((bf16[128,2304]{1,0:T(8,128)(2,1)}, bf16[128,2304]{1,0:T(8,128)(2,1)}, u32[]{:S(2)}, u32[]{:S(2)}) %collective-permute-start.2) | collective-permute-done | bytes 589856 | tf_op jit(solution)/shard_map/ppermute | solution.py:281
  57.3 8.5 %collective-permute-start.4 = (bf16[128,2304]{1,0:T(8,128)(2,1)}, bf16[128,2304]{1,0:T(8,128)(2,1)S(1)}, u32[]{:S(2)}, u32[]{:S(2)}) collective-permute-start(bf16[128,2304]{1,0:T(8,128)(2,1)} %collective-permute-done.2), channel_id=1, source_target_pairs={{0,2},{2,4},{4,6},{6,7},{7,5},{5,3},{3,1},{1,0},{8,10},{10,12},{12... | collective-permute-start | bytes 1769480 | tf_op jit(solution)/shard_map/ppermute | solution.py:281
  66.7 12.1 %collective-permute-done.4 = bf16[128,2304]{1,0:T(8,128)(2,1)S(1)} collective-permute-done((bf16[128,2304]{1,0:T(8,128)(2,1)}, bf16[128,2304]{1,0:T(8,128)(2,1)S(1)}, u32[]{:S(2)}, u32[]{:S(2)}) %collective-permute-start.4) | collective-permute-done | bytes 589856 | tf_op jit(solution)/shard_map/ppermute | solution.py:281
  83.2 10.1 %collective-permute-done.6 = bf16[128,2304]{1,0:T(8,128)(2,1)S(1)} collective-permute-done((bf16[128,2304]{1,0:T(8,128)(2,1)S(1)}, bf16[128,2304]{1,0:T(8,128)(2,1)S(1)}, u32[]{:S(2)}, u32[]{:S(2)}) %collective-permute-start.6) | collective-permute-done | bytes 589856 | tf_op jit(solution)/shard_map/ppermute | solution.py:281
  100.9 12.0 %collective-permute-done.5 = bf16[128,2304]{1,0:T(8,128)(2,1)S(1)} collective-permute-done((bf16[128,2304]{1,0:T(8,128)(2,1)S(1)}, bf16[128,2304]{1,0:T(8,128)(2,1)S(1)}, u32[]{:S(2)}, u32[]{:S(2)}) %collective-permute-start.5) | collective-permute-done | bytes 589856 | tf_op jit(solution)/shard_map/ppermute | solution.py:284
  122.2 9.1 %all-to-all-start.1 = ((bf16[8,144,720]{2,1,0:T(8,128)(2,1)}), bf16[8,144,720]{2,1,0:T(8,128)(2,1)}, u32[]{:S(2)}, u32[]{:S(2)}) async-start(bf16[8,144,720]{2,1,0:T(8,128)(2,1)} %prepare_ffn.1), calls=%async_computation.1 | async-start | bytes 3538944 | tf_op jit(solution)/shard_map/all_to_all | solution.py:335
  133.4 20.7 %collective-permute-done.8 = bf16[8,72,960]{2,1,0:T(8,128)(2,1)S(1)} collective-permute-done((bf16[8,72,960]{2,1,0:T(8,128)(2,1)}, bf16[8,72,960]{2,1,0:T(8,128)(2,1)S(1)}, u32[]{:S(2)}, u32[]{:S(2)}) %collective-permute-start.8) | collective-permute-done | bytes 1105952 | tf_op jit(solution)/shard_map/ppermute | solution.py:290
  154.1 3.3 multiply_reduce_fusion.1
  157.9 3.6 copy-done.5
  161.5 5.3 fusion.55.qkv_ref
  166.9 4.6 attend.1
  184.0 37.9 %collective-permute-done.11 = bf16[320,1024]{1,0:T(8,128)(2,1)} collective-permute-done((bf16[320,1024]{1,0:T(8,128)(2,1)S(1)}, bf16[320,1024]{1,0:T(8,128)(2,1)}, u32[]{:S(2)}, u32[]{:S(2)}) %collective-permute-start.11) | collective-permute-done | bytes 655392 | tf_op jit(solution)/shard_map/ppermute | solution.py:284
  245.8 9.2 %collective-permute-done.14 = bf16[320,1024]{1,0:T(8,128)(2,1)S(1)} collective-permute-done((bf16[320,1024]{1,0:T(8,128)(2,1)S(1)}, bf16[320,1024]{1,0:T(8,128)(2,1)S(1)}, u32[]{:S(2)}, u32[]{:S(2)}) %collective-permute-start.14) | collective-permute-done | bytes 655392 | tf_op jit(solution)/shard_map/ppermute | solution.py:281
  259.5 14.1 %collective-permute-done.18 = bf16[2,8,72,720]{3,2,1,0:T(8,128)(2,1)S(1)} collective-permute-done((bf16[2,8,72,720]{3,2,1,0:T(8,128)(2,1)S(1)}, bf16[2,8,72,720]{3,2,1,0:T(8,128)(2,1)S(1)}, u32[]{:S(2)}, u32[]{:S(2)}) %collective-permute-start.18) | collective-permute-done | bytes 1658912 | tf_op jit(solution)/shard_map/ppermute | solution.py:290
  280.7 11.4 %collective-permute-done.21 = bf16[128,2304]{1,0:T(8,128)(2,1)S(1)} collective-permute-done((bf16[128,2304]{1,0:T(8,128)(2,1)S(1)}, bf16[128,2304]{1,0:T(8,128)(2,1)S(1)}, u32[]{:S(2)}, u32[]{:S(2)}) %collective-permute-start.21) | collective-permute-done | bytes 589856 | tf_op jit(solution)/shard_map/ppermute | solution.py:284
  295.8 11.3 %collective-permute-done.23 = bf16[128,2304]{1,0:T(8,128)(2,1)S(1)} collective-permute-done((bf16[128,2304]{1,0:T(8,128)(2,1)S(1)}, bf16[128,2304]{1,0:T(8,128)(2,1)S(1)}, u32[]{:S(2)}, u32[]{:S(2)}) %collective-permute-start.23) | collective-permute-done | bytes 589856 | tf_op jit(solution)/shard_map/ppermute | solution.py:284
  311.1 3.3 fusion.53
  314.4 7.0 collective-permute-done.24
  324.9 9.7 %collective-permute-done.26 = bf16[128,2304]{1,0:T(8,128)(2,1)S(1)} collective-permute-done((bf16[128,2304]{1,0:T(8,128)(2,1)S(1)}, bf16[128,2304]{1,0:T(8,128)(2,1)S(1)}, u32[]{:S(2)}, u32[]{:S(2)}) %collective-permute-start.26) | collective-permute-done | bytes 589856 | tf_op jit(solution)/shard_map/ppermute | solution.py:281
  335.5 18.4 %multiply_reduce_fusion = (f32[1024]{0:T(1024)S(1)}, bf16[1024,2304]{1,0:T(8,128)(2,1)S(1)}, f32[1024,2304]{1,0:T(8,128)}) fusion(bf16[2304,2304]{1,0:T(8,128)(2,1)} %all-gather.2.cloned.1.call-done, bf16[2560,1024]{1,0:T(8,128)(2,1)} %slice_dynamic-update-slice_fusion.8, bf16[1024,2304]{1,0:T(8,128)(2,1)} %bitcast.280), kind=kOutput, calls=%fused_computation.1 | convolution fusion | flops 10885790720 | bytes 34213888 | tf_op jit(solution)/shard_map/dot_general | solution.py:24
  353.9 5.4 fusion.57
  359.4 5.4 fusion.56
  364.8 9.5 %multiply_convert_fusion = (bf16[1024,720]{0,1:T(8,128)(2,1)S(1)}, bf16[1024,720]{0,1:T(8,128)(2,1)S(1)}, bf16[1024,720]{0,1:T(8,128)(2,1)}) fusion(f32[1024]{0:T(1024)S(1)} %add_rsqrt_fusion, f32[1024,720]{0,1:T(8,128)} %fusion.56, f32[1024,720]{0,1:T(8,128)} %fusion.57, bf16[1024,2304]{1,0:T(8,128)(2,1)} %bitcast.48, f32[720,2304]{1,0:T(8,128)S(1)} %bitcast.356), kind=kOutput, calls=%fused_computation.35 | convolution fusion | flops 3413053440 | bytes 21680128 | tf_op jit(solution)/shard_map/dot_general | solution.py:24
  374.3 6.5 fusion.58
  380.8 6.7 add_convert_fusion
  390.4 10.2 %collective-permute-done.27 = bf16[128,2304]{1,0:T(8,128)(2,1)S(1)} collective-permute-done((bf16[128,2304]{1,0:T(8,128)(2,1)S(1)}, bf16[128,2304]{1,0:T(8,128)(2,1)S(1)}, u32[]{:S(2)}, u32[]{:S(2)}) %collective-permute-start.27) | collective-permute-done | bytes 589856 | tf_op jit(solution)/shard_map/ppermute | solution.py:281
  403.3 10.0 %collective-permute-done.28 = bf16[128,2304]{1,0:T(8,128)(2,1)} collective-permute-done((bf16[128,2304]{1,0:T(8,128)(2,1)}, bf16[128,2304]{1,0:T(8,128)(2,1)}, u32[]{:S(2)}, u32[]{:S(2)}) %collective-permute-start.28) | collective-permute-done | bytes 589856 | tf_op jit(solution)/shard_map/ppermute | solution.py:281
  417.4 6.7 convolution_convert_fusion.4
  431.5 4.4 convolution_convert_fusion.3
  448.8 3.5 all-to-all-start.2
  452.4 8.1 %convolution_convert_fusion.5 = bf16[720,2304]{1,0:T(8,128)(2,1)} fusion(bf16[1024,720]{0,1:T(8,128)(2,1)} %get-tuple-element.75, bf16[1024,2304]{1,0:T(8,128)(2,1)} %bitcast.48), kind=kOutput, calls=%fused_computation.18 | convolution fusion | flops 3399045120 | bytes 9510912 | tf_op jit(solution)/shard_map/dot_general | solution.py:24
  460.5 3.5 reshape_reshape.15
  470.2 5.8 fusion
  476.8 6.2 all-to-all-start.3
  484.2 13.4 %attend_back.1 = bf16[960,1024]{1,0:T(8,128)(2,1)S(1)} custom-call(bf16[960,1024]{1,0:T(8,128)(2,1)S(1)} %get-tuple-element.76.qkv_ref, bf16[320,1024]{1,0:T(8,128)(2,1)S(1)} %copy_bitcast_fusion.3.grad_ref, f32[1,1024]{1,0:T(1,128)S(1)} %bitcast.286, f32[32,1024]{1,0:T(8,128)S(1)} %get-tuple-element.157.cos_ref, f32[32,1024]{1,0:T(8,128)S(1)} %get-tuple-element.156.sin_ref, ...), custom_call_target="tpu_custom_call" | custom-call | flops 419430400 | bytes 4587520 | tf_op jit(solution)/shard_map/attend_back/pallas_call | solution.py:137
  498.9 9.1 %convolution_convert_fusion.2 = bf16[2304,960]{1,0:T(8,128)(2,1)} fusion(bf16[1024,2304]{1,0:T(8,128)(2,1)} %bitcast.281, bf16[960,1024]{1,0:T(8,128)(2,1)S(1)} %attend_back.1), kind=kOutput, calls=%fused_computation.15 | convolution fusion | flops 4532060160 | bytes 11108352 | tf_op jit(solution)/shard_map/dot_general | solution.py:24
  508.0 5.1 convolution_convert_fusion.6
  513.2 3.8 pad_maximum_fusion
  517.0 7.9 %convolution_convert_fusion.1 = bf16[1024,2304]{1,0:T(8,128)(2,1)S(1)} fusion(bf16[960,1024]{1,0:T(8,128)(2,1)S(1)} %copy-done.11, bf16[2304,960]{1,0:T(8,128)(2,1)} %bitcast.284), kind=kOutput, calls=%fused_computation.14 | convolution fusion | flops 4532207616 | bytes 11108352 | tf_op jit(solution)/shard_map/dot_general | solution.py:24
  532.3 8.2 %collective-permute-done.34 = bf16[128,2304]{1,0:T(8,128)(2,1)S(1)} collective-permute-done((bf16[128,2304]{1,0:T(8,128)(2,1)S(1)}, bf16[128,2304]{1,0:T(8,128)(2,1)S(1)}, u32[]{:S(2)}, u32[]{:S(2)}) %collective-permute-start.34) | collective-permute-done | bytes 589856 | tf_op jit(solution)/shard_map/ppermute | solution.py:281
  544.7 11.1 %collective-permute-done.35 = bf16[128,2304]{1,0:T(8,128)(2,1)S(1)} collective-permute-done((bf16[128,2304]{1,0:T(8,128)(2,1)S(1)}, bf16[128,2304]{1,0:T(8,128)(2,1)S(1)}, u32[]{:S(2)}, u32[]{:S(2)}) %collective-permute-start.35) | collective-permute-done | bytes 589856 | tf_op jit(solution)/shard_map/ppermute | solution.py:281
  560.4 8.4 %collective-permute-done.54 = bf16[8,144,720]{2,1,0:T(8,128)(2,1)S(1)} collective-permute-done((bf16[8,144,720]{2,1,0:T(8,128)(2,1)S(1)}, bf16[8,144,720]{2,1,0:T(8,128)(2,1)S(1)}, u32[]{:S(2)}, u32[]{:S(2)}) %collective-permute-start.54) | collective-permute-done | bytes 1658912 | tf_op jit(solution)/shard_map/ppermute | solution.py:290
  570.4 4.5 all-to-all-start.5
  583.4 7.1 convolution_convert_fusion
  590.5 23.6 %collective-permute-done.37 = bf16[128,2304]{1,0:T(8,128)(2,1)S(1)} collective-permute-done((bf16[128,2304]{1,0:T(8,128)(2,1)S(1)}, bf16[128,2304]{1,0:T(8,128)(2,1)S(1)}, u32[]{:S(2)}, u32[]{:S(2)}) %collective-permute-start.37) | collective-permute-done | bytes 589856 | tf_op jit(solution)/shard_map/ppermute | solution.py:281
  618.3 12.6 %collective-permute-start.41 = (bf16[128,2304]{1,0:T(8,128)(2,1)}, bf16[128,2304]{1,0:T(8,128)(2,1)}, u32[]{:S(2)}, u32[]{:S(2)}) collective-permute-start(bf16[128,2304]{1,0:T(8,128)(2,1)} %get-tuple-element.136), channel_id=1, source_target_pairs={{0,2},{2,4},{4,6},{6,7},{7,5},{5,3},{3,1},{1,0},{8,10},{10,12},{12... | collective-permute-start | bytes 1769480 | tf_op jit(solution)/shard_map/ppermute | solution.py:281
  632.4 4.3 all-to-all-start.4
  641.5 3.5 collective-permute-done.41
  647.2 5.9 collective-permute-start.42
  653.1 4.8 collective-permute-done.60.piece_ref
  659.6 3.4 reshape.439.piece_ref
  664.3 10.2 %collective-permute-done.45 = bf16[128,2304]{1,0:T(8,128)(2,1)} collective-permute-done((bf16[128,2304]{1,0:T(8,128)(2,1)}, bf16[128,2304]{1,0:T(8,128)(2,1)}, u32[]{:S(2)}, u32[]{:S(2)}) %collective-permute-start.45) | collective-permute-done | bytes 589856 | tf_op jit(solution)/shard_map/ppermute | solution.py:284
  680.0 9.9 %collective-permute-start.43 = (bf16[128,2304]{1,0:T(8,128)(2,1)}, bf16[128,2304]{1,0:T(8,128)(2,1)}, u32[]{:S(2)}, u32[]{:S(2)}) collective-permute-start(bf16[128,2304]{1,0:T(8,128)(2,1)} %get-tuple-element.134), channel_id=1, source_target_pairs={{0,2},{2,4},{4,6},{6,7},{7,5},{5,3},{3,1},{1,0},{8,10},{10,12},{12... | collective-permute-start | bytes 1769480 | tf_op jit(solution)/shard_map/ppermute | solution.py:281
  717.6 5.2 reshape.442
  724.5 5.7 collective-permute-done.50.piece_ref
  733.4 6.0 finish.16
  742.3 6.1 finish.17
  748.4 6.1 finish.18
  754.5 6.1 finish.19
  765.5 3.3 finish.13
  768.8 3.3 finish.14
  772.0 3.4 finish.15
  (352 shorter events, 231.7 us)
Async XLA Ops:
  7.2 16.7 %collective-permute-start = (bf16[128,2304]{1,0:T(8,128)(2,1)}, bf16[128,2304]{1,0:T(8,128)(2,1)}, u32[]{:S(2)}, u32[]{:S(2)}) collective-permute-start(bf16[128,2304]{1,0:T(8,128)(2,1)} %param.15), channel_id=1, source_target_pairs={{0,2},{2,4},{4,6},{6,7},{7,5},{5,3},{3,1},{1,0},{8,10},{10,12},{12... | collective-permute-start | bytes 1769480 | tf_op jit(solution)/shard_map/ppermute | solution.py:281
  10.3 56.4 %collective-permute-start.1 = (bf16[128,2304]{1,0:T(8,128)(2,1)}, bf16[128,2304]{1,0:T(8,128)(2,1)}, u32[]{:S(2)}, u32[]{:S(2)}) collective-permute-start(bf16[128,2304]{1,0:T(8,128)(2,1)} %param.15), channel_id=1, source_target_pairs={{2,0},{4,2},{6,4},{7,6},{5,7},{3,5},{1,3},{0,1},{10,8},{12,10},{14... | collective-permute-start | bytes 1769480 | tf_op jit(solution)/shard_map/ppermute | solution.py:284
  16.8 96.8 %all-to-all-start = ((bf16[8,80,960]{2,1,0:T(8,128)(2,1)}), bf16[8,80,960]{2,1,0:T(8,128)(2,1)}, u32[]{:S(2)}, u32[]{:S(2)}) async-start(bf16[8,80,960]{2,1,0:T(8,128)(2,1)} %prepare_qkv.1), calls=%async_computation | async-start | bytes 2621440 | tf_op jit(solution)/shard_map/all_to_all | solution.py:335
  23.1 312.3 %all-gather.2.cloned.1.call-start = ((), (), s32[]{:S(2)}) async-start(), calls=%async_computation.6 | async-start | bytes 10948608 | tf_op jit(solution)/shard_map/all_gather | solution.py:439
  23.9 33.5 %collective-permute-start.2 = (bf16[128,2304]{1,0:T(8,128)(2,1)}, bf16[128,2304]{1,0:T(8,128)(2,1)}, u32[]{:S(2)}, u32[]{:S(2)}) collective-permute-start(bf16[128,2304]{1,0:T(8,128)(2,1)} %collective-permute-done), channel_id=1, source_target_pairs={{0,2},{2,4},{4,6},{6,7},{7,5},{5,3},{3,1},{1,0},{8,10},{10,12},{12... | collective-permute-start | bytes 1769480 | tf_op jit(solution)/shard_map/ppermute | solution.py:281
  57.3 21.5 %collective-permute-start.4 = (bf16[128,2304]{1,0:T(8,128)(2,1)}, bf16[128,2304]{1,0:T(8,128)(2,1)S(1)}, u32[]{:S(2)}, u32[]{:S(2)}) collective-permute-start(bf16[128,2304]{1,0:T(8,128)(2,1)} %collective-permute-done.2), channel_id=1, source_target_pairs={{0,2},{2,4},{4,6},{6,7},{7,5},{5,3},{3,1},{1,0},{8,10},{10,12},{12... | collective-permute-start | bytes 1769480 | tf_op jit(solution)/shard_map/ppermute | solution.py:281
  66.7 28.8 %collective-permute-start.3 = (bf16[128,2304]{1,0:T(8,128)(2,1)}, bf16[128,2304]{1,0:T(8,128)(2,1)S(1)}, u32[]{:S(2)}, u32[]{:S(2)}) collective-permute-start(bf16[128,2304]{1,0:T(8,128)(2,1)} %collective-permute-done.1), channel_id=1, source_target_pairs={{2,0},{4,2},{6,4},{7,6},{5,7},{3,5},{1,3},{0,1},{10,8},{12,10},{14... | collective-permute-start | bytes 1769480 | tf_op jit(solution)/shard_map/ppermute | solution.py:284
  78.8 14.5 %collective-permute-start.6 = (bf16[128,2304]{1,0:T(8,128)(2,1)S(1)}, bf16[128,2304]{1,0:T(8,128)(2,1)S(1)}, u32[]{:S(2)}, u32[]{:S(2)}) collective-permute-start(bf16[128,2304]{1,0:T(8,128)(2,1)S(1)} %collective-permute-done.4), channel_id=1, source_target_pairs={{0,2},{2,4},{4,6},{6,7},{7,5},{5,3},{3,1},{1,0},{8,10},{10,12},{12... | collective-permute-start | bytes 1769480 | tf_op jit(solution)/shard_map/ppermute | solution.py:281
  95.5 17.3 %collective-permute-start.5 = (bf16[128,2304]{1,0:T(8,128)(2,1)S(1)}, bf16[128,2304]{1,0:T(8,128)(2,1)S(1)}, u32[]{:S(2)}, u32[]{:S(2)}) collective-permute-start(bf16[128,2304]{1,0:T(8,128)(2,1)S(1)} %collective-permute-done.3), channel_id=1, source_target_pairs={{2,0},{4,2},{6,4},{7,6},{5,7},{3,5},{1,3},{0,1},{10,8},{12,10},{14... | collective-permute-start | bytes 1769480 | tf_op jit(solution)/shard_map/ppermute | solution.py:284
  116.1 41.4 %collective-permute-start.7 = (bf16[8,72,960]{2,1,0:T(8,128)(2,1)}, bf16[8,72,960]{2,1,0:T(8,128)(2,1)S(1)}, u32[]{:S(2)}, u32[]{:S(2)}) collective-permute-start(bf16[8,72,960]{2,1,0:T(8,128)(2,1)} %slice.144), channel_id=1, source_target_pairs={{0,8},{8,0},{16,24},{24,16},{1,9},{9,1},{17,25},{25,17},{2,10},{10... | collective-permute-start | bytes 3317768 | tf_op jit(solution)/shard_map/ppermute | solution.py:287
  116.1 38.1 %collective-permute-start.8 = (bf16[8,72,960]{2,1,0:T(8,128)(2,1)}, bf16[8,72,960]{2,1,0:T(8,128)(2,1)S(1)}, u32[]{:S(2)}, u32[]{:S(2)}) collective-permute-start(bf16[8,72,960]{2,1,0:T(8,128)(2,1)} %slice.144), channel_id=1, source_target_pairs={{0,16},{8,24},{16,0},{24,8},{1,17},{9,25},{17,1},{25,9},{2,18},{10... | collective-permute-start | bytes 3317768 | tf_op jit(solution)/shard_map/ppermute | solution.py:290
  122.2 108.6 %all-to-all-start.1 = ((bf16[8,144,720]{2,1,0:T(8,128)(2,1)}), bf16[8,144,720]{2,1,0:T(8,128)(2,1)}, u32[]{:S(2)}, u32[]{:S(2)}) async-start(bf16[8,144,720]{2,1,0:T(8,128)(2,1)} %prepare_ffn.1), calls=%async_computation.1 | async-start | bytes 3538944 | tf_op jit(solution)/shard_map/all_to_all | solution.py:335
  171.5 50.4 %collective-permute-start.11 = (bf16[320,1024]{1,0:T(8,128)(2,1)S(1)}, bf16[320,1024]{1,0:T(8,128)(2,1)}, u32[]{:S(2)}, u32[]{:S(2)}) collective-permute-start(bf16[320,1024]{1,0:T(8,128)(2,1)S(1)} %get-tuple-element.69), channel_id=1, source_target_pairs={{2,0},{4,2},{6,4},{7,6},{5,7},{3,5},{1,3},{0,1},{10,8},{12,10},{14... | collective-permute-start | bytes 1966088 | tf_op jit(solution)/shard_map/ppermute | solution.py:284
  173.4 48.5 %collective-permute-start.10 = (bf16[320,1024]{1,0:T(8,128)(2,1)S(1)}, bf16[320,1024]{1,0:T(8,128)(2,1)}, u32[]{:S(2)}, u32[]{:S(2)}) collective-permute-start(bf16[320,1024]{1,0:T(8,128)(2,1)S(1)} %get-tuple-element.69), channel_id=1, source_target_pairs={{0,2},{2,4},{4,6},{6,7},{7,5},{5,3},{3,1},{1,0},{8,10},{10,12},{12... | collective-permute-start | bytes 1966088 | tf_op jit(solution)/shard_map/ppermute | solution.py:281
  221.9 17.0 %collective-permute-start.13 = (bf16[320,1024]{1,0:T(8,128)(2,1)}, bf16[320,1024]{1,0:T(8,128)(2,1)}, u32[]{:S(2)}, u32[]{:S(2)}) collective-permute-start(bf16[320,1024]{1,0:T(8,128)(2,1)} %collective-permute-done.11), channel_id=1, source_target_pairs={{2,0},{4,2},{6,4},{7,6},{5,7},{3,5},{1,3},{0,1},{10,8},{12,10},{14... | collective-permute-start | bytes 1966088 | tf_op jit(solution)/shard_map/ppermute | solution.py:284
  221.9 17.3 %collective-permute-start.12 = (bf16[320,1024]{1,0:T(8,128)(2,1)}, bf16[320,1024]{1,0:T(8,128)(2,1)S(1)}, u32[]{:S(2)}, u32[]{:S(2)}) collective-permute-start(bf16[320,1024]{1,0:T(8,128)(2,1)} %collective-permute-done.10), channel_id=1, source_target_pairs={{0,2},{2,4},{4,6},{6,7},{7,5},{5,3},{3,1},{1,0},{8,10},{10,12},{12... | collective-permute-start | bytes 1966088 | tf_op jit(solution)/shard_map/ppermute | solution.py:281
  232.4 41.1 %collective-permute-start.17 = (bf16[2,8,72,720]{3,2,1,0:T(8,128)(2,1)S(1)}, bf16[2,8,72,720]{3,2,1,0:T(8,128)(2,1)S(1)}, u32[]{:S(2)}, u32[]{:S(2)}) collective-permute-start(bf16[2,8,72,720]{3,2,1,0:T(8,128)(2,1)S(1)} %bitcast.345), channel_id=1, source_target_pairs={{0,8},{8,0},{16,24},{24,16},{1,9},{9,1},{17,25},{25,17},{2,10},{10... | collective-permute-start | bytes 4976648 | tf_op jit(solution)/shard_map/ppermute | solution.py:287
  232.5 41.0 %collective-permute-start.18 = (bf16[2,8,72,720]{3,2,1,0:T(8,128)(2,1)S(1)}, bf16[2,8,72,720]{3,2,1,0:T(8,128)(2,1)S(1)}, u32[]{:S(2)}, u32[]{:S(2)}) collective-permute-start(bf16[2,8,72,720]{3,2,1,0:T(8,128)(2,1)S(1)} %bitcast.346), channel_id=1, source_target_pairs={{0,16},{8,24},{16,0},{24,8},{1,17},{9,25},{17,1},{25,9},{2,18},{10... | collective-permute-start | bytes 4976648 | tf_op jit(solution)/shard_map/ppermute | solution.py:290
  238.9 19.1 %collective-permute-start.15 = (bf16[320,1024]{1,0:T(8,128)(2,1)}, bf16[320,1024]{1,0:T(8,128)(2,1)S(1)}, u32[]{:S(2)}, u32[]{:S(2)}) collective-permute-start(bf16[320,1024]{1,0:T(8,128)(2,1)} %collective-permute-done.13), channel_id=1, source_target_pairs={{2,0},{4,2},{6,4},{7,6},{5,7},{3,5},{1,3},{0,1},{10,8},{12,10},{14... | collective-permute-start | bytes 1966088 | tf_op jit(solution)/shard_map/ppermute | solution.py:284
  239.2 15.9 %collective-permute-start.14 = (bf16[320,1024]{1,0:T(8,128)(2,1)S(1)}, bf16[320,1024]{1,0:T(8,128)(2,1)S(1)}, u32[]{:S(2)}, u32[]{:S(2)}) collective-permute-start(bf16[320,1024]{1,0:T(8,128)(2,1)S(1)} %collective-permute-done.12), channel_id=1, source_target_pairs={{0,2},{2,4},{4,6},{6,7},{7,5},{5,3},{3,1},{1,0},{8,10},{10,12},{12... | collective-permute-start | bytes 1966088 | tf_op jit(solution)/shard_map/ppermute | solution.py:281
  255.1 21.2 %collective-permute-start.16 = (bf16[320,1024]{1,0:T(8,128)(2,1)S(1)}, bf16[320,1024]{1,0:T(8,128)(2,1)S(1)}, u32[]{:S(2)}, u32[]{:S(2)}) collective-permute-start(bf16[320,1024]{1,0:T(8,128)(2,1)S(1)} %collective-permute-done.14), channel_id=1, source_target_pairs={{0,2},{2,4},{4,6},{6,7},{7,5},{5,3},{3,1},{1,0},{8,10},{10,12},{12... | collective-permute-start | bytes 1966088 | tf_op jit(solution)/shard_map/ppermute | solution.py:281
  273.5 37.3 %collective-permute-start.19 = (bf16[2,8,72,720]{3,2,1,0:T(8,128)(2,1)S(1)}, bf16[2,8,72,720]{3,2,1,0:T(8,128)(2,1)S(1)}, u32[]{:S(2)}, u32[]{:S(2)}) collective-permute-start(bf16[2,8,72,720]{3,2,1,0:T(8,128)(2,1)S(1)} %collective-permute-done.18), channel_id=1, source_target_pairs={{0,8},{8,0},{16,24},{24,16},{1,9},{9,1},{17,25},{25,17},{2,10},{10... | collective-permute-start | bytes 4976648 | tf_op jit(solution)/shard_map/ppermute | solution.py:287
  276.3 15.8 %collective-permute-start.21 = (bf16[128,2304]{1,0:T(8,128)(2,1)S(1)}, bf16[128,2304]{1,0:T(8,128)(2,1)S(1)}, u32[]{:S(2)}, u32[]{:S(2)}) collective-permute-start(bf16[128,2304]{1,0:T(8,128)(2,1)S(1)} %copy-done.30), channel_id=1, source_target_pairs={{2,0},{4,2},{6,4},{7,6},{5,7},{3,5},{1,3},{0,1},{10,8},{12,10},{14... | collective-permute-start | bytes 1769480 | tf_op jit(solution)/shard_map/ppermute | solution.py:284
  276.3 16.0 %collective-permute-start.20 = (bf16[128,2304]{1,0:T(8,128)(2,1)S(1)}, bf16[128,2304]{1,0:T(8,128)(2,1)S(1)}, u32[]{:S(2)}, u32[]{:S(2)}) collective-permute-start(bf16[128,2304]{1,0:T(8,128)(2,1)S(1)} %copy-done.30), channel_id=1, source_target_pairs={{0,2},{2,4},{4,6},{6,7},{7,5},{5,3},{3,1},{1,0},{8,10},{10,12},{12... | collective-permute-start | bytes 1769480 | tf_op jit(solution)/shard_map/ppermute | solution.py:281
  292.1 15.0 %collective-permute-start.23 = (bf16[128,2304]{1,0:T(8,128)(2,1)S(1)}, bf16[128,2304]{1,0:T(8,128)(2,1)S(1)}, u32[]{:S(2)}, u32[]{:S(2)}) collective-permute-start(bf16[128,2304]{1,0:T(8,128)(2,1)S(1)} %collective-permute-done.21), channel_id=1, source_target_pairs={{2,0},{4,2},{6,4},{7,6},{5,7},{3,5},{1,3},{0,1},{10,8},{12,10},{14... | collective-permute-start | bytes 1769480 | tf_op jit(solution)/shard_map/ppermute | solution.py:284
  292.3 15.1 %collective-permute-start.22 = (bf16[128,2304]{1,0:T(8,128)(2,1)S(1)}, bf16[128,2304]{1,0:T(8,128)(2,1)S(1)}, u32[]{:S(2)}, u32[]{:S(2)}) collective-permute-start(bf16[128,2304]{1,0:T(8,128)(2,1)S(1)} %collective-permute-done.20), channel_id=1, source_target_pairs={{0,2},{2,4},{4,6},{6,7},{7,5},{5,3},{3,1},{1,0},{8,10},{10,12},{12... | collective-permute-start | bytes 1769480 | tf_op jit(solution)/shard_map/ppermute | solution.py:281
  307.1 16.9 %collective-permute-start.25 = (bf16[128,2304]{1,0:T(8,128)(2,1)S(1)}, bf16[128,2304]{1,0:T(8,128)(2,1)S(1)}, u32[]{:S(2)}, u32[]{:S(2)}) collective-permute-start(bf16[128,2304]{1,0:T(8,128)(2,1)S(1)} %collective-permute-done.23), channel_id=1, source_target_pairs={{2,0},{4,2},{6,4},{7,6},{5,7},{3,5},{1,3},{0,1},{10,8},{12,10},{14... | collective-permute-start | bytes 1769480 | tf_op jit(solution)/shard_map/ppermute | solution.py:284
  307.4 14.0 %collective-permute-start.24 = (bf16[128,2304]{1,0:T(8,128)(2,1)S(1)}, bf16[128,2304]{1,0:T(8,128)(2,1)S(1)}, u32[]{:S(2)}, u32[]{:S(2)}) collective-permute-start(bf16[128,2304]{1,0:T(8,128)(2,1)S(1)} %collective-permute-done.22), channel_id=1, source_target_pairs={{0,2},{2,4},{4,6},{6,7},{7,5},{5,3},{3,1},{1,0},{8,10},{10,12},{12... | collective-permute-start | bytes 1769480 | tf_op jit(solution)/shard_map/ppermute | solution.py:281
  321.4 13.2 %collective-permute-start.26 = (bf16[128,2304]{1,0:T(8,128)(2,1)S(1)}, bf16[128,2304]{1,0:T(8,128)(2,1)S(1)}, u32[]{:S(2)}, u32[]{:S(2)}) collective-permute-start(bf16[128,2304]{1,0:T(8,128)(2,1)S(1)} %collective-permute-done.24), channel_id=1, source_target_pairs={{0,2},{2,4},{4,6},{6,7},{7,5},{5,3},{3,1},{1,0},{8,10},{10,12},{12... | collective-permute-start | bytes 1769480 | tf_op jit(solution)/shard_map/ppermute | solution.py:281
  388.4 12.2 %collective-permute-start.27 = (bf16[128,2304]{1,0:T(8,128)(2,1)S(1)}, bf16[128,2304]{1,0:T(8,128)(2,1)S(1)}, u32[]{:S(2)}, u32[]{:S(2)}) collective-permute-start(bf16[128,2304]{1,0:T(8,128)(2,1)S(1)} %get-tuple-element.148), channel_id=1, source_target_pairs={{0,2},{2,4},{4,6},{6,7},{7,5},{5,3},{3,1},{1,0},{8,10},{10,12},{12... | collective-permute-start | bytes 1769480 | tf_op jit(solution)/shard_map/ppermute | solution.py:281
  389.9 13.4 %collective-permute-start.31 = (bf16[128,2304]{1,0:T(8,128)(2,1)}, bf16[128,2304]{1,0:T(8,128)(2,1)}, u32[]{:S(2)}, u32[]{:S(2)}) collective-permute-start(bf16[128,2304]{1,0:T(8,128)(2,1)} %get-tuple-element.149), channel_id=1, source_target_pairs={{2,0},{4,2},{6,4},{7,6},{5,7},{3,5},{1,3},{0,1},{10,8},{12,10},{14... | collective-permute-start | bytes 1769480 | tf_op jit(solution)/shard_map/ppermute | solution.py:284
  439.0 31.1 %collective-permute-start.53 = (bf16[8,2,144,720]{3,2,1,0:T(8,128)(2,1)}, bf16[8,2,144,720]{3,2,1,0:T(8,128)(2,1)}, u32[]{:S(2)}, u32[]{:S(2)}) collective-permute-start(bf16[8,2,144,720]{3,2,1,0:T(8,128)(2,1)} %fusion.5), channel_id=1, source_target_pairs={{0,8},{8,0},{16,24},{24,16},{1,9},{9,1},{17,25},{25,17},{2,10},{10... | collective-permute-start | bytes 9953288 | tf_op jit(solution)/shard_map/ppermute | solution.py:287
  448.8 27.1 %all-to-all-start.2 = ((bf16[8,320,128]{2,1,0:T(8,128)(2,1)}), bf16[8,320,128]{2,1,0:T(8,128)(2,1)S(1)}, u32[]{:S(2)}, u32[]{:S(2)}) async-start(bf16[8,320,128]{2,1,0:T(8,128)(2,1)} %pad_maximum_fusion.2), calls=%async_computation.2 | async-start | bytes 1310720 | tf_op jit(solution)/shard_map/all_to_all | solution.py:335
  468.0 74.8 %collective-permute-start.58 = (bf16[1,2,180,2304]{3,1,2,0:T(2,128)(2,1)}, bf16[1,2,180,2304]{3,1,2,0:T(2,128)(2,1)}, u32[]{:S(2)}, u32[]{:S(2)}) collective-permute-start(bf16[1,2,180,2304]{3,1,2,0:T(2,128)(2,1)} %copy.249), channel_id=1, source_target_pairs={{0,8},{8,0},{16,24},{24,16},{1,9},{9,1},{17,25},{25,17},{2,10},{10... | collective-permute-start | bytes 4976648 | tf_op jit(solution)/shard_map/ppermute | solution.py:287
  476.8 31.2 %all-to-all-start.3 = ((bf16[8,288,128]{2,1,0:T(8,128)(2,1)}), bf16[8,288,128]{2,1,0:T(8,128)(2,1)}, u32[]{:S(2)}, u32[]{:S(2)}) async-start(bf16[8,288,128]{2,1,0:T(8,128)(2,1)} %bitcast.343), calls=%async_computation.3 | async-start | bytes 1179648 | tf_op jit(solution)/shard_map/all_to_all | solution.py:335
  525.0 15.5 %collective-permute-start.34 = (bf16[128,2304]{1,0:T(8,128)(2,1)S(1)}, bf16[128,2304]{1,0:T(8,128)(2,1)S(1)}, u32[]{:S(2)}, u32[]{:S(2)}) collective-permute-start(bf16[128,2304]{1,0:T(8,128)(2,1)S(1)} %get-tuple-element.142), channel_id=1, source_target_pairs={{0,2},{2,4},{4,6},{6,7},{7,5},{5,3},{3,1},{1,0},{8,10},{10,12},{12... | collective-permute-start | bytes 1769480 | tf_op jit(solution)/shard_map/ppermute | solution.py:281
  527.2 41.6 %collective-permute-start.54 = (bf16[8,144,720]{2,1,0:T(8,128)(2,1)S(1)}, bf16[8,144,720]{2,1,0:T(8,128)(2,1)S(1)}, u32[]{:S(2)}, u32[]{:S(2)}) collective-permute-start(bf16[8,144,720]{2,1,0:T(8,128)(2,1)S(1)} %dynamic-slice_bitcast_fusion), channel_id=1, source_target_pairs={{0,16},{8,24},{16,0},{24,8},{1,17},{9,25},{17,1},{25,9},{2,18},{10... | collective-permute-start | bytes 4976648 | tf_op jit(solution)/shard_map/ppermute | solution.py:290
  528.5 16.2 %collective-permute-start.38 = (bf16[128,2304]{1,0:T(8,128)(2,1)S(1)}, bf16[128,2304]{1,0:T(8,128)(2,1)S(1)}, u32[]{:S(2)}, u32[]{:S(2)}) collective-permute-start(bf16[128,2304]{1,0:T(8,128)(2,1)S(1)} %get-tuple-element.143), channel_id=1, source_target_pairs={{2,0},{4,2},{6,4},{7,6},{5,7},{3,5},{1,3},{0,1},{10,8},{12,10},{14... | collective-permute-start | bytes 1769480 | tf_op jit(solution)/shard_map/ppermute | solution.py:284
  532.3 46.9 %collective-permute-start.48 = (bf16[8,2,72,1248]{3,2,0,1:T(8,128)(2,1)}, bf16[8,2,72,1248]{3,2,0,1:T(8,128)(2,1)}, u32[]{:S(2)}, u32[]{:S(2)}) collective-permute-start(bf16[8,2,72,1248]{3,2,0,1:T(8,128)(2,1)} %bitcast.277), channel_id=1, source_target_pairs={{0,8},{8,0},{16,24},{24,16},{1,9},{9,1},{17,25},{25,17},{2,10},{10... | collective-permute-start | bytes 8626184 | tf_op jit(solution)/shard_map/ppermute | solution.py:287
  540.7 15.1 %collective-permute-start.35 = (bf16[128,2304]{1,0:T(8,128)(2,1)S(1)}, bf16[128,2304]{1,0:T(8,128)(2,1)S(1)}, u32[]{:S(2)}, u32[]{:S(2)}) collective-permute-start(bf16[128,2304]{1,0:T(8,128)(2,1)S(1)} %fusion.35), channel_id=1, source_target_pairs={{0,2},{2,4},{4,6},{6,7},{7,5},{5,3},{3,1},{1,0},{8,10},{10,12},{12... | collective-permute-start | bytes 1769480 | tf_op jit(solution)/shard_map/ppermute | solution.py:281
  557.1 17.9 %collective-permute-start.36 = (bf16[128,2304]{1,0:T(8,128)(2,1)}, bf16[128,2304]{1,0:T(8,128)(2,1)}, u32[]{:S(2)}, u32[]{:S(2)}) collective-permute-start(bf16[128,2304]{1,0:T(8,128)(2,1)} %get-tuple-element.140), channel_id=1, source_target_pairs={{0,2},{2,4},{4,6},{6,7},{7,5},{5,3},{3,1},{1,0},{8,10},{10,12},{12... | collective-permute-start | bytes 1769480 | tf_op jit(solution)/shard_map/ppermute | solution.py:281
  558.5 16.5 %collective-permute-start.39 = (bf16[128,2304]{1,0:T(8,128)(2,1)}, bf16[128,2304]{1,0:T(8,128)(2,1)}, u32[]{:S(2)}, u32[]{:S(2)}) collective-permute-start(bf16[128,2304]{1,0:T(8,128)(2,1)} %get-tuple-element.141), channel_id=1, source_target_pairs={{2,0},{4,2},{6,4},{7,6},{5,7},{3,5},{1,3},{0,1},{10,8},{12,10},{14... | collective-permute-start | bytes 1769480 | tf_op jit(solution)/shard_map/ppermute | solution.py:284
  559.2 77.6 %collective-permute-start.59 = (bf16[1,180,2304]{2,1,0:T(8,128)(2,1)S(1)}, bf16[1,180,2304]{2,1,0:T(8,128)(2,1)}, u32[]{:S(2)}, u32[]{:S(2)}) collective-permute-start(bf16[1,180,2304]{2,1,0:T(8,128)(2,1)S(1)} %dynamic-slice_bitcast_fusion.3), channel_id=1, source_target_pairs={{0,16},{8,24},{16,0},{24,8},{1,17},{9,25},{17,1},{25,9},{2,18},{10... | collective-permute-start | bytes 2488328 | tf_op jit(solution)/shard_map/ppermute | solution.py:290
  570.4 62.0 %all-to-all-start.5 = ((bf16[8,144,720]{2,1,0:T(8,128)(2,1)}), bf16[8,144,720]{2,1,0:T(8,128)(2,1)S(1)}, u32[]{:S(2)}, u32[]{:S(2)}) async-start(bf16[8,144,720]{2,1,0:T(8,128)(2,1)} %fusion.8), calls=%async_computation.5 | async-start | bytes 3538944 | tf_op jit(solution)/shard_map/all_to_all | solution.py:335
  577.0 37.1 %collective-permute-start.37 = (bf16[128,2304]{1,0:T(8,128)(2,1)S(1)}, bf16[128,2304]{1,0:T(8,128)(2,1)S(1)}, u32[]{:S(2)}, u32[]{:S(2)}) collective-permute-start(bf16[128,2304]{1,0:T(8,128)(2,1)S(1)} %get-tuple-element.138), channel_id=1, source_target_pairs={{0,2},{2,4},{4,6},{6,7},{7,5},{5,3},{3,1},{1,0},{8,10},{10,12},{12... | collective-permute-start | bytes 1769480 | tf_op jit(solution)/shard_map/ppermute | solution.py:281
  579.1 35.6 %collective-permute-start.40 = (bf16[128,2304]{1,0:T(8,128)(2,1)S(1)}, bf16[128,2304]{1,0:T(8,128)(2,1)S(1)}, u32[]{:S(2)}, u32[]{:S(2)}) collective-permute-start(bf16[128,2304]{1,0:T(8,128)(2,1)S(1)} %get-tuple-element.139), channel_id=1, source_target_pairs={{2,0},{4,2},{6,4},{7,6},{5,7},{3,5},{1,3},{0,1},{10,8},{12,10},{14... | collective-permute-start | bytes 1769480 | tf_op jit(solution)/shard_map/ppermute | solution.py:284
  582.1 48.8 %collective-permute-start.49 = (bf16[8,72,1248]{2,1,0:T(8,128)(2,1)S(1)}, bf16[8,72,1248]{2,1,0:T(8,128)(2,1)S(1)}, u32[]{:S(2)}, u32[]{:S(2)}) collective-permute-start(bf16[8,72,1248]{2,1,0:T(8,128)(2,1)S(1)} %dynamic-slice_bitcast_fusion.2), channel_id=1, source_target_pairs={{0,16},{8,24},{16,0},{24,8},{1,17},{9,25},{17,1},{25,9},{2,18},{10... | collective-permute-start | bytes 4313096 | tf_op jit(solution)/shard_map/ppermute | solution.py:290
  618.3 26.7 %collective-permute-start.41 = (bf16[128,2304]{1,0:T(8,128)(2,1)}, bf16[128,2304]{1,0:T(8,128)(2,1)}, u32[]{:S(2)}, u32[]{:S(2)}) collective-permute-start(bf16[128,2304]{1,0:T(8,128)(2,1)} %get-tuple-element.136), channel_id=1, source_target_pairs={{0,2},{2,4},{4,6},{6,7},{7,5},{5,3},{3,1},{1,0},{8,10},{10,12},{12... | collective-permute-start | bytes 1769480 | tf_op jit(solution)/shard_map/ppermute | solution.py:281
  632.4 57.6 %all-to-all-start.4 = ((bf16[8,72,1248]{2,1,0:T(8,128)(2,1)}), bf16[8,72,1248]{2,1,0:T(8,128)(2,1)}, u32[]{:S(2)}, u32[]{:S(2)}) async-start(bf16[8,72,1248]{2,1,0:T(8,128)(2,1)} %fusion.10), calls=%async_computation.4 | async-start | bytes 2949120 | tf_op jit(solution)/shard_map/all_to_all | solution.py:335
  638.4 19.5 %collective-permute-start.60 = (bf16[1,180,2304]{2,1,0:T(8,128)(2,1)S(1)}, bf16[1,180,2304]{2,1,0:T(8,128)(2,1)}, u32[]{:S(2)}, u32[]{:S(2)}) collective-permute-start(bf16[1,180,2304]{2,1,0:T(8,128)(2,1)S(1)} %fusion.12.piece_ref), channel_id=1, source_target_pairs={{0,16},{8,24},{16,0},{24,8},{1,17},{9,25},{17,1},{25,9},{2,18},{10... | collective-permute-start | bytes 2488328 | tf_op jit(solution)/shard_map/ppermute | solution.py:290
  639.7 34.9 %collective-permute-start.45 = (bf16[128,2304]{1,0:T(8,128)(2,1)}, bf16[128,2304]{1,0:T(8,128)(2,1)}, u32[]{:S(2)}, u32[]{:S(2)}) collective-permute-start(bf16[128,2304]{1,0:T(8,128)(2,1)} %get-tuple-element.137), channel_id=1, source_target_pairs={{2,0},{4,2},{6,4},{7,6},{5,7},{3,5},{1,3},{0,1},{10,8},{12,10},{14... | collective-permute-start | bytes 1769480 | tf_op jit(solution)/shard_map/ppermute | solution.py:284
  647.2 29.9 %collective-permute-start.42 = (bf16[128,2304]{1,0:T(8,128)(2,1)}, bf16[128,2304]{1,0:T(8,128)(2,1)}, u32[]{:S(2)}, u32[]{:S(2)}) collective-permute-start(bf16[128,2304]{1,0:T(8,128)(2,1)} %fusion.30), channel_id=1, source_target_pairs={{0,2},{2,4},{4,6},{6,7},{7,5},{5,3},{3,1},{1,0},{8,10},{10,12},{12... | collective-permute-start | bytes 1769480 | tf_op jit(solution)/shard_map/ppermute | solution.py:281
  653.1 57.6 %collective-permute-start.62 = (bf16[1,180,2304]{2,1,0:T(8,128)(2,1)S(1)}, bf16[1,180,2304]{2,1,0:T(8,128)(2,1)}, u32[]{:S(2)}, u32[]{:S(2)}) collective-permute-start(bf16[1,180,2304]{2,1,0:T(8,128)(2,1)S(1)} %fusion.12.piece_ref), channel_id=1, source_target_pairs={{0,8},{8,0},{16,24},{24,16},{1,9},{9,1},{17,25},{25,17},{2,10},{10... | collective-permute-start | bytes 2488328 | tf_op jit(solution)/shard_map/ppermute | solution.py:287
  657.9 57.4 %collective-permute-start.61 = (bf16[1,180,2304]{2,1,0:T(8,128)(2,1)}, bf16[1,180,2304]{2,1,0:T(8,128)(2,1)}, u32[]{:S(2)}, u32[]{:S(2)}) collective-permute-start(bf16[1,180,2304]{2,1,0:T(8,128)(2,1)} %collective-permute-done.60.piece_ref), channel_id=1, source_target_pairs={{0,8},{8,0},{16,24},{24,16},{1,9},{9,1},{17,25},{25,17},{2,10},{10... | collective-permute-start | bytes 2488328 | tf_op jit(solution)/shard_map/ppermute | solution.py:287
  663.0 59.7 %collective-permute-start.55 = (bf16[2,72,5760]{2,1,0:T(8,128)(2,1)S(1)}, bf16[2,72,5760]{2,1,0:T(8,128)(2,1)}, u32[]{:S(2)}, u32[]{:S(2)}) collective-permute-start(bf16[2,72,5760]{2,1,0:T(8,128)(2,1)S(1)} %reshape.439.piece_ref), channel_id=1, source_target_pairs={{0,16},{8,24},{16,0},{24,8},{1,17},{9,25},{17,1},{25,9},{2,18},{10... | collective-permute-start | bytes 4976648 | tf_op jit(solution)/shard_map/ppermute | solution.py:290
  680.0 20.8 %collective-permute-start.43 = (bf16[128,2304]{1,0:T(8,128)(2,1)}, bf16[128,2304]{1,0:T(8,128)(2,1)}, u32[]{:S(2)}, u32[]{:S(2)}) collective-permute-start(bf16[128,2304]{1,0:T(8,128)(2,1)} %get-tuple-element.134), channel_id=1, source_target_pairs={{0,2},{2,4},{4,6},{6,7},{7,5},{5,3},{3,1},{1,0},{8,10},{10,12},{12... | collective-permute-start | bytes 1769480 | tf_op jit(solution)/shard_map/ppermute | solution.py:281
  690.0 13.8 %collective-permute-start.46 = (bf16[128,2304]{1,0:T(8,128)(2,1)}, bf16[128,2304]{1,0:T(8,128)(2,1)}, u32[]{:S(2)}, u32[]{:S(2)}) collective-permute-start(bf16[128,2304]{1,0:T(8,128)(2,1)} %get-tuple-element.135), channel_id=1, source_target_pairs={{2,0},{4,2},{6,4},{7,6},{5,7},{3,5},{1,3},{0,1},{10,8},{12,10},{14... | collective-permute-start | bytes 1769480 | tf_op jit(solution)/shard_map/ppermute | solution.py:284
  700.8 29.5 %collective-permute-start.50 = (bf16[4,72,2304]{2,1,0:T(8,128)(2,1)}, bf16[4,72,2304]{2,1,0:T(8,128)(2,1)}, u32[]{:S(2)}, u32[]{:S(2)}) collective-permute-start(bf16[4,72,2304]{2,1,0:T(8,128)(2,1)} %pad_maximum_fusion.1.piece_ref), channel_id=1, source_target_pairs={{0,16},{8,24},{16,0},{24,8},{1,17},{9,25},{17,1},{25,9},{2,18},{10... | collective-permute-start | bytes 3981320 | tf_op jit(solution)/shard_map/ppermute | solution.py:290
  706.6 17.9 %collective-permute-start.44 = (bf16[128,2304]{1,0:T(8,128)(2,1)}, bf16[128,2304]{1,0:T(8,128)(2,1)}, u32[]{:S(2)}, u32[]{:S(2)}) collective-permute-start(bf16[128,2304]{1,0:T(8,128)(2,1)} %get-tuple-element.132), channel_id=1, source_target_pairs={{0,2},{2,4},{4,6},{6,7},{7,5},{5,3},{3,1},{1,0},{8,10},{10,12},{12... | collective-permute-start | bytes 1769480 | tf_op jit(solution)/shard_map/ppermute | solution.py:281
  722.7 19.6 %collective-permute-start.57 = (bf16[2,72,5760]{2,1,0:T(8,128)(2,1)S(1)}, bf16[2,72,5760]{2,1,0:T(8,128)(2,1)}, u32[]{:S(2)}, u32[]{:S(2)}) collective-permute-start(bf16[2,72,5760]{2,1,0:T(8,128)(2,1)S(1)} %reshape.439.piece_ref), channel_id=1, source_target_pairs={{0,8},{8,0},{16,24},{24,16},{1,9},{9,1},{17,25},{25,17},{2,10},{10... | collective-permute-start | bytes 4976648 | tf_op jit(solution)/shard_map/ppermute | solution.py:287
  722.7 31.7 %collective-permute-start.56 = (bf16[2,72,5760]{2,1,0:T(8,128)(2,1)}, bf16[2,72,5760]{2,1,0:T(8,128)(2,1)}, u32[]{:S(2)}, u32[]{:S(2)}) collective-permute-start(bf16[2,72,5760]{2,1,0:T(8,128)(2,1)} %collective-permute-done.55.piece_ref), channel_id=1, source_target_pairs={{0,8},{8,0},{16,24},{24,16},{1,9},{9,1},{17,25},{25,17},{2,10},{10... | collective-permute-start | bytes 4976648 | tf_op jit(solution)/shard_map/ppermute | solution.py:287
  723.3 16.2 %collective-permute-start.47 = (bf16[128,2304]{1,0:T(8,128)(2,1)S(1)}, bf16[128,2304]{1,0:T(8,128)(2,1)}, u32[]{:S(2)}, u32[]{:S(2)}) collective-permute-start(bf16[128,2304]{1,0:T(8,128)(2,1)S(1)} %copy-done.34), channel_id=1, source_target_pairs={{2,0},{4,2},{6,4},{7,6},{5,7},{3,5},{1,3},{0,1},{10,8},{12,10},{14... | collective-permute-start | bytes 1769480 | tf_op jit(solution)/shard_map/ppermute | solution.py:284
  724.5 40.9 %collective-permute-start.52 = (bf16[4,72,2304]{2,1,0:T(8,128)(2,1)}, bf16[4,72,2304]{2,1,0:T(8,128)(2,1)}, u32[]{:S(2)}, u32[]{:S(2)}) collective-permute-start(bf16[4,72,2304]{2,1,0:T(8,128)(2,1)} %pad_maximum_fusion.1.piece_ref), channel_id=1, source_target_pairs={{0,8},{8,0},{16,24},{24,16},{1,9},{9,1},{17,25},{25,17},{2,10},{10... | collective-permute-start | bytes 3981320 | tf_op jit(solution)/shard_map/ppermute | solution.py:287
  730.3 41.7 %collective-permute-start.51 = (bf16[4,72,2304]{2,1,0:T(8,128)(2,1)}, bf16[4,72,2304]{2,1,0:T(8,128)(2,1)}, u32[]{:S(2)}, u32[]{:S(2)}) collective-permute-start(bf16[4,72,2304]{2,1,0:T(8,128)(2,1)} %collective-permute-done.50.piece_ref), channel_id=1, source_target_pairs={{0,8},{8,0},{16,24},{24,16},{1,9},{9,1},{17,25},{25,17},{2,10},{10... | collective-permute-start | bytes 3981320 | tf_op jit(solution)/shard_map/ppermute | solution.py:287
  (55 other events, 722.7 us)
Sparse Core Ops, SparseCore 0:
  93.5 126.8 all-gather.1

commit v4 on v3

--- a/solution.py
+++ b/solution.py
@@ -148,6 +148,51 @@
     )(qkv, grad, scale, cosine, sine, bias)
 
 
+def middle_kernel(me_ref, mixed_ref, weight_ref, inputs_ref, low_ref, scale_ref, own_ref):
+    branch = mm(mixed_ref[...], weight_ref[...], 0, 0)
+    middle = inputs_ref[...].astype(F32) + BRANCH_SCALE * branch
+    scale = lax.rsqrt(jnp.mean(middle * middle, axis=1, keepdims=True) + EPSILON)
+    low_ref[...] = middle.astype(BF16)
+    scale_ref[...] = scale
+
+    @pl.when(pl.program_id(0) == me_ref[0])
+    def _():
+        own_ref[...] = middle
+
+
+def middle_rows(me, mixed, weight, inputs, rows):
+    tokens, width = inputs.shape
+    return pl.pallas_call(
+        middle_kernel,
+        grid_spec=pltpu.PrefetchScalarGridSpec(
+            num_scalar_prefetch=1,
+            grid=(tokens // rows,),
+            in_specs=[
+                pl.BlockSpec((width, rows), lambda i, me: (0, i)),
+                pl.BlockSpec((width, width), lambda i, me: (0, 0), pipeline_mode=pl.Buffered(1)),
+                pl.BlockSpec((rows, width), lambda i, me: (i, 0)),
+            ],
+            out_specs=[
+                pl.BlockSpec((rows, width), lambda i, me: (i, 0)),
+                pl.BlockSpec((rows, 1), lambda i, me: (i, 0)),
+                pl.BlockSpec((rows, width), lambda i, me: (0, 0)),
+            ],
+        ),
+        out_shape=[
+            jax.ShapeDtypeStruct((tokens, width), BF16),
+            jax.ShapeDtypeStruct((tokens, 1), F32),
+            jax.ShapeDtypeStruct((rows, width), F32),
+        ],
+        cost_estimate=pl.CostEstimate(
+            flops=2 * tokens * width * width,
+            bytes_accessed=2 * width * width + 6 * tokens * width,
+            transcendentals=tokens,
+        ),
+        compiler_params=pltpu.CompilerParams(vmem_limit_bytes=40 * 2**20),
+        name="middle_rows",
+    )(me.reshape(1), mixed, weight, inputs)
+
+
 def row_major(array):
     return with_layout_constraint(array, Layout(tuple(range(array.ndim))))
 
@@ -221,7 +266,7 @@
     for k in range(count):
         raw = piece_ref[k].astype(F32)
         if k < gained:
-            total = total + jnp.sum(low(weights[k][0]) * raw, axis=1, keepdims=True)
+            total = total + jnp.sum(weights[k][0] * raw, axis=1, keepdims=True)
             raw = raw * refs[gained][0]
         outs[k][0] = raw
     if gained:
@@ -232,7 +277,7 @@
 def finish(piece, at, rep, weights, gain, previous):
     count, part, width = piece.shape
     gained = len(weights)
-    chunk = max(c for c in range(128, 1153, 128) if width % c == 0)
+    chunk = 1152 if width == 2304 else width
 
     def placed(size, moving):
         return pl.BlockSpec((1, part, size), lambda i, at: (at[0], 0, i if moving else 0))
@@ -297,31 +342,40 @@
         place = (place + offset + n) % n
         return jnp.where(place < n // 2, 2 * place, 2 * (n - 1 - place) + 1)
 
-    def ring_gather(piece):
+    def after(value, *others):
+        return lax.optimization_barrier((value, others))[0]
+
+    def ring_gather(piece, gates=(), paired=False):
         pieces = [(ring_device(0), piece)]
         going_right = going_left = piece
         for step in range(1, steps_right + 1):
+            if step <= len(gates) and gates[step - 1] is not None:
+                going_right, going_left = after((going_right, going_left), gates[step - 1])
             going_right = right(going_right)
-            pieces.append((ring_device(-step), going_right))
             if step <= steps_left:
                 going_left = left(going_left)
+                if paired:
+                    going_right, going_left = lax.optimization_barrier((going_right, going_left))
                 pieces.append((ring_device(step), going_left))
+            pieces.append((ring_device(-step), going_right))
         return pieces
 
-    def gather_shard(piece):
-        pieces = ring_gather(piece)
-        whole = empty((n,) + piece.shape, piece.dtype)
+    def assemble(pieces):
+        shape = pieces[0][1].shape
+        whole = empty((n,) + shape, pieces[0][1].dtype)
         for device, part in pieces:
             whole = lax.dynamic_update_index_in_dim(whole, part, device, 0)
-        return whole.reshape((-1,) + piece.shape[1:]), pieces[-1][1]
-
-    def scatter_shard(parts):
+        return whole.reshape((-1,) + shape[1:])
+
+    def scatter_shard(parts, gates=()):
         def term(offset):
             return lax.dynamic_index_in_dim(parts, ring_device(offset), 0, keepdims=False).astype(F32)
 
         going_right = term(steps_right).astype(BF16)
         going_left = term(-steps_left).astype(BF16)
         for step in range(1, steps_right + 1):
+            if step <= len(gates) and gates[step - 1] is not None:
+                going_right, going_left = after((going_right, going_left), gates[step - 1])
             going_right = right(going_right)
             if step < steps_right:
                 going_right = (going_right.astype(F32) + term(steps_right - step)).astype(BF16)
@@ -340,9 +394,6 @@
     def add(a, b):
         return (a.astype(F32) + b.astype(F32)).astype(BF16)
 
-    def after(value, *others):
-        return lax.optimization_barrier((value, others))[0]
-
     def rep_pieces(piece):
         mine = lax.axis_index("rep")
         far = (mine + 2) % rep
@@ -351,9 +402,9 @@
         last = core_swap(other_chip)
         return [(mine, piece), (mine ^ 1, other_core), (far, other_chip), (far ^ 1, last)]
 
-    def gather_rep(piece, axis):
+    def gather_rep(piece, axis, pieces=None):
         whole = empty(piece.shape[:axis] + (rep,) + piece.shape[axis:], piece.dtype)
-        for index, part in rep_pieces(piece):
+        for index, part in rep_pieces(piece) if pieces is None else pieces:
             whole = lax.dynamic_update_index_in_dim(whole, part, index, axis)
         return whole
 
@@ -420,7 +471,6 @@
             rest = array[:over, :, start : start + HD].transpose(1, 0, 2)
             return jnp.concatenate([first, rest.reshape(array.shape[1], width - mains)], axis=1)
 
-        inputs, last_input = gather_shard(tokens)
         info = jnp.concatenate([doc_lengths[0], pic_starts[0]]).astype(BF16)
         info = jnp.zeros((8, 3 * block), BF16).at[0, : docs + pics].set(info)
         qkv_part = prepare(
@@ -432,11 +482,6 @@
             (n, part + 8, 3 * block),
             "prepare_qkv",
         )
-        qkv_part = exchange(qkv_part)
-        info = qkv_part[:, part, : docs + pics].astype(jnp.int32)
-        qkv_w = gather_rep(qkv_part[:, :part], 1).reshape(width, 3 * block)
-        out_part = after(pick(by_rep(w_out), mine, 0), last_input).astype(BF16)
-        out_w = lax.all_gather(out_part, ("shard", "rep"), axis=0, tiled=True)
         ffn_part = prepare(
             functools.partial(prepare_ffn_kernel, n),
             own,
@@ -446,7 +491,25 @@
             (n, 2 * part, cols),
             "prepare_ffn",
         )
-        ffn_part = exchange(after(ffn_part, qkv_part, last_input))
+        qkv_part = exchange(qkv_part)
+        x_pieces = ring_gather(tokens, (None, (qkv_part, ffn_part)), True)
+        info = qkv_part[:, part, : docs + pics].astype(jnp.int32)
+        near = x_pieces[-2][1]
+        out_part = after(pick(by_rep(w_out), mine, 0), near).astype(BF16)
+        out_w = lax.all_gather(out_part, ("shard", "rep"), axis=0, tiled=True)
+        ffn_part = exchange(after(ffn_part, near))
+        qkv_part = qkv_part[:, :part]
+        last, qkv_chip = lax.optimization_barrier((x_pieces[-1][1], chip_swap(qkv_part)))
+        x_pieces[-1] = (x_pieces[-1][0], last)
+        inputs = assemble(x_pieces)
+        far = (mine + 2) % rep
+        qkv_pieces = [
+            (mine, qkv_part),
+            (mine ^ 1, core_swap(qkv_part)),
+            (far, qkv_chip),
+            (far ^ 1, core_swap(qkv_chip)),
+        ]
+        qkv_w = gather_rep(qkv_part, 1, qkv_pieces).reshape(width, 3 * block)
         down_w = w_down.astype(BF16)
         grad_result = cotangent.astype(F32)
 
@@ -460,29 +523,32 @@
         qkv = mm(qkv_w, inputs, 0, 1)
         qkv, mixed = attend(base, slots, n, rows, qkv, scale_one, cosine, sine, bias)
         ffn_part = after(ffn_part, mixed)
-        ffn_w = gather_rep(ffn_part.reshape(n, 2, part, cols).transpose(1, 0, 2, 3), 2)
-        gate_w = ffn_w[0].reshape(width, cols)
-        up_w = ffn_w[1].reshape(width, cols)
+        ffn_pieces = rep_pieces(ffn_part)
+        gate_w, up_w = (
+            gather_rep(
+                ffn_part[:, k * part : (k + 1) * part],
+                1,
+                [(at, piece[:, k * part : (k + 1) * part]) for at, piece in ffn_pieces],
+            ).reshape(width, cols)
+            for k in range(2)
+        )
         mixed_all = empty((n * block, all_rows), BF16)
-        mixed_pieces = ring_gather(mixed)
+        mixed_pieces = ring_gather(mixed, (), True)
         for device, piece in mixed_pieces:
             mixed_all = lax.dynamic_update_slice_in_dim(mixed_all, piece[:main], device * main, 0)
             if slots > base:
                 mixed_all = lax.dynamic_update_slice_in_dim(
                     mixed_all, piece[main:], mains + device * HD, 0
                 )
-        mixed_all = mixed_all[:width]
-        middle = inputs.astype(F32) + BRANCH_SCALE * mm(mixed_all, out_w, 0, 0)
-
-        grad_branch = after((BRANCH_SCALE * grad_result).astype(BF16), mixed_pieces[-1][1])
-        grad_branch, _ = gather_shard(grad_branch)
-        scale_two = lax.rsqrt(jnp.mean(middle * middle, axis=-1, keepdims=True) + EPSILON)
-        middle_low = middle.astype(BF16)
+        middle_low, scale_two, my_middle = middle_rows(me, mixed_all, out_w, inputs, rows)
+
         gate_act = mm(middle_low, gate_w, 1, 0) * scale_two
         up_act = mm(middle_low, up_w, 1, 0) * scale_two
         sigmoid_gate = jax.nn.sigmoid(gate_act)
         silu_gate = gate_act * sigmoid_gate
         inner = (silu_gate * up_act).astype(BF16)
+        grad_branch = (BRANCH_SCALE * grad_result).astype(BF16)
+        grad_branch = assemble(ring_gather(grad_branch, (mixed_pieces[-1][1], scale_two, up_act)))
         grad_inner = mm(grad_branch, down_w, 1, 1)
         grad_gate_act = (
             grad_inner
@@ -495,7 +561,6 @@
         partial = mm(grad_gate_act, gate_w, 1, 1) + mm(grad_up_act, up_w, 1, 1)
         partial = partial.astype(BF16).reshape(n, rows, width)
         back_two = scatter_shard(partial)
-        my_middle = lax.dynamic_slice_in_dim(middle, me * rows, rows, 0)
         my_normed_two = my_middle * lax.dynamic_slice_in_dim(scale_two, me * rows, rows, 0)
         inner_mean = jnp.mean(back_two * my_normed_two, axis=-1, keepdims=True)
         grad_middle = grad_result + back_two - my_normed_two * inner_mean
@@ -503,12 +568,15 @@
         def rep_rows(grad):
             return row_major(grad.astype(BF16)).reshape(n, rep, part, grad.shape[1])
 
-        def finish_all(piece, weights, gain):
-            done = None
-            for index, arrived in rep_pieces(piece):
+        def finish_some(pieces, weights, gain, done):
+            for index, arrived in pieces:
                 done = finish(
                     arrived, index.reshape(1), rep, [by_rep(w) for w in weights], gain, done
                 )
+            return done
+
+        def finish_all(piece, weights, gain):
+            done = finish_some(rep_pieces(piece), weights, gain, None)
             return [a.reshape(-1, a.shape[2]) for a in done]
 
         inner, grad_gate_act, grad_up_act, _ = lax.optimization_barrier(
@@ -519,25 +587,39 @@
         grad_ffn = [rep_rows(mm(middle_low, g, 0, 0)) for g in (grad_gate_act, grad_up_act)]
         grad_ffn = scatter_rep(jnp.concatenate(grad_ffn, axis=2))
         grad_attn = (BRANCH_SCALE * grad_middle).astype(BF16)
-        grad_mixed = exchange(by_heads(mm(out_w, grad_attn, 1, 1).astype(BF16)))
-        grad_attn_cols = after(grad_attn.T.reshape(n, depth, rows), grad_mixed)
-        grad_attn_cols = exchange(grad_attn_cols).transpose(1, 0, 2).reshape(depth, all_rows)
-        grad_mixed = grad_mixed.transpose(1, 0, 2).reshape(block, all_rows)
+        both = exchange(
+            jnp.concatenate(
+                [
+                    by_heads(mm(out_w, grad_attn, 1, 1).astype(BF16)),
+                    grad_attn.T.reshape(n, depth, rows),
+                ],
+                axis=1,
+            )
+        )
+        grad_mixed = both[:, :block].transpose(1, 0, 2).reshape(block, all_rows)
+        grad_attn_cols = both[:, block:].transpose(1, 0, 2).reshape(depth, all_rows)
         grad_qkv = attend_back(
             base, slots, n, rows, qkv, grad_mixed, scale_one, cosine, sine, bias
         )
-        grad_ffn = exchange(after(grad_ffn, grad_mixed))
-        grad_ffn = grad_ffn.reshape(n, 2, part, cols).transpose(1, 2, 0, 3).reshape(2, part, ff)
-        grad_gate, grad_up, grad_gain_two = finish_all(grad_ffn, (w_gate, w_up), gain_two)
         grad_w = jnp.concatenate(
             [
                 row_major(mm(inputs, grad_qkv, 0, 1).astype(BF16)),
-                row_major(mm(mixed_all, grad_attn_cols, 1, 1).astype(BF16)),
+                row_major(mm(mixed_all, after(grad_attn_cols, grad_qkv), 1, 1).astype(BF16))[:width],
             ],
             axis=1,
         )
+        grad_w, grad_ffn = lax.optimization_barrier((grad_w, grad_ffn))
+        grad_ffn = exchange(grad_ffn)
         partial = mm(after(grad_qkv, grad_w), qkv_w, 0, 1)
-        back_one = scatter_shard(partial.astype(BF16).reshape(n, rows, width))
+        ffn_blocks = grad_ffn
+        grad_ffn = grad_ffn.reshape(n, 2, part, cols).transpose(1, 2, 0, 3).reshape(2, part, ff)
+        back_one = scatter_shard(
+            partial.astype(BF16).reshape(n, rows, width), (None, None, ffn_blocks)
+        )
+        ffn_pieces = rep_pieces(grad_ffn)
+        ffn_half = finish_some(ffn_pieces[:2], (w_gate, w_up), gain_two, None)
+        ffn_done = finish_some(ffn_pieces[2:], (w_gate, w_up), gain_two, ffn_half)
+        grad_gate, grad_up, grad_gain_two = (a.reshape(-1, a.shape[2]) for a in ffn_done)
         my_inputs = tokens.astype(F32)
         my_scale_one = lax.rsqrt(jnp.mean(my_inputs * my_inputs, axis=-1, keepdims=True) + EPSILON)
         my_normed_one = my_inputs * my_scale_one
@@ -545,7 +627,7 @@
         input_grad = grad_middle + back_one - my_normed_one * inner_mean
 
         branch = mm(after(inner, back_two), down_w, 1, 0).astype(BF16).reshape(n, rows, width)
-        branch = scatter_shard(after(branch, back_one))
+        branch = scatter_shard(after(branch, back_one), (None, grad_down, None, ffn_half))
         out_tokens = (my_middle + BRANCH_SCALE * branch).astype(BF16)
 
         grad_w = exchange(scatter_rep(grad_w.reshape(n, rep, part, -1)))

time: 792 us -> 767 us (0.968)
  starting transfers between devices: 131 us -> 104 us
  matrix products: 109 us -> 87.9 us
  Pallas kernels: 71.6 us -> 84 us
  waiting for transfers between devices: 286 us -> 298 us
    ppermute x18, waiting for transfers between devices: 89.5 us -> 138 us  [left(): return lax.ppermute(x, 'shard', to_left)]
    ppermute x24, waiting for transfers between devices: 143 us -> 105 us  [right(): return lax.ppermute(x, 'shard', to_right)]
    ppermute x24, starting transfers between devices: 75.4 us -> 47.8 us  [right(): return lax.ppermute(x, 'shard', to_right)]
    dot_general x15 -> x14, matrix products: 109 us -> 87.9 us  [mm(): lax.dot_general(left, right, (((left_dim,), (right_dim,)), ((), ())), pre...]
    pallas_call x0 -> x1, Pallas kernels: none -> 17.8 us  [middle_rows(): pl.pallas_call(middle_kernel, grid_spec=pltpu.PrefetchScalarGridSpec(num_...]
    ppermute x18, starting transfers between devices: 10.3 us -> 23.1 us  [left(): return lax.ppermute(x, 'shard', to_left)]
    convert_element_type x9 -> x5, other arithmetic: 15.9 us -> 7.52 us  [scatter_shard(): (going_right.astype(F32) + term(steps_right - step)).astype(BF16)]
    all_to_all x6 -> x5, starting transfers between devices: 33.9 us -> 27.4 us  [exchange(): lax.all_to_all(blocks, 'shard', split_axis=0, concat_axis=0, tiled=True)]
  transfers between devices with their start and end apart: 70 -> 69, of which waited for: 32 -> 33; matrix products, arithmetic and copies ran while one was open for 26% -> 27% of each run, Pallas kernels for 9% -> 8%
where the time goes in v4:
time: 767 us; the launch traced here: 761 us
  waiting for transfers between devices  298 us (39%)
  local copies, waits for them, and re-layouts  113 us (15%)
  starting transfers between devices  104 us (14%)
  matrix products  87.9 us (11%)
  Pallas kernels  84 us (11%)
  other arithmetic  58.7 us (8%)
  between operations  15.9 us (2%)
    ppermute x18, waiting for transfers between devices, left(): return lax.ppermute(x, 'shard', to_left)  138 us
    ppermute x24, waiting for transfers between devices, right(): return lax.ppermute(x, 'shard', to_right)  105 us
    dot_general x14, matrix products, mm(): lax.dot_general(left, right, (((left_dim,), (right_dim,)), ((), ())), pre...  87.9 us
    ppermute x8, waiting for transfers between devices, chip_swap(): return lax.ppermute(x, 'rep', chip_pairs)  48.8 us
    ppermute x24, starting transfers between devices, right(): return lax.ppermute(x, 'shard', to_right)  47.8 us
    pallas_call x12, Pallas kernels, finish(): pl.pallas_call(functools.partial(finish_kernel, count, gained), grid_spec...  41.2 us
    all_to_all x5, starting transfers between devices, exchange(): lax.all_to_all(blocks, 'shard', split_axis=0, concat_axis=0, tiled=True)  27.4 us
    ppermute x18, starting transfers between devices, left(): return lax.ppermute(x, 'shard', to_left)  23.1 us
  transfers between devices with their start and end apart: 69, of which 33 were waited for; matrix products, arithmetic and copies ran while one was open for 27% of the time, Pallas kernels for 8%

profile of v4, /device:TPU:0, one launch (start us, length us, event | category | flops | bytes accessed | tf_op | source)
XLA Modules:
  0.0 760.8 jit_solution(2711392067986076676)
XLA Ops:
  13.9 7.3 all-to-all-start
  24.2 3.8 prepare_ffn.1
  28.1 29.3 %collective-permute-done.2 = bf16[128,2304]{1,0:T(8,128)(2,1)} collective-permute-done((bf16[128,2304]{1,0:T(8,128)(2,1)S(1)}, bf16[128,2304]{1,0:T(8,128)(2,1)}, u32[]{:S(2)}, u32[]{:S(2)}) %collective-permute-start.2) | collective-permute-done | bytes 589856 | tf_op jit(solution)/shard_map/ppermute | solution.py:329
  57.4 8.5 %collective-permute-start.3 = (bf16[128,2304]{1,0:T(8,128)(2,1)}, bf16[128,2304]{1,0:T(8,128)(2,1)}, u32[]{:S(2)}, u32[]{:S(2)}) collective-permute-start(bf16[128,2304]{1,0:T(8,128)(2,1)} %collective-permute-done.1), channel_id=1, source_target_pairs={{0,2},{2,4},{4,6},{6,7},{7,5},{5,3},{3,1},{1,0},{8,10},{10,12},{12... | collective-permute-start | bytes 1769480 | tf_op jit(solution)/shard_map/ppermute | solution.py:326
  66.0 11.8 %collective-permute-done.3 = bf16[128,2304]{1,0:T(8,128)(2,1)} collective-permute-done((bf16[128,2304]{1,0:T(8,128)(2,1)}, bf16[128,2304]{1,0:T(8,128)(2,1)}, u32[]{:S(2)}, u32[]{:S(2)}) %collective-permute-start.3) | collective-permute-done | bytes 589856 | tf_op jit(solution)/shard_map/ppermute | solution.py:326
  83.0 10.9 %collective-permute-done.5 = bf16[128,2304]{1,0:T(8,128)(2,1)} collective-permute-done((bf16[128,2304]{1,0:T(8,128)(2,1)}, bf16[128,2304]{1,0:T(8,128)(2,1)}, u32[]{:S(2)}, u32[]{:S(2)}) %collective-permute-start.5) | collective-permute-done | bytes 589856 | tf_op jit(solution)/shard_map/ppermute | solution.py:326
  120.5 4.5 all-to-all-start.1
  129.0 17.9 %collective-permute-done.8 = bf16[8,72,960]{2,1,0:T(8,128)(2,1)S(1)} collective-permute-done((bf16[8,72,960]{2,1,0:T(8,128)(2,1)}, bf16[8,72,960]{2,1,0:T(8,128)(2,1)S(1)}, u32[]{:S(2)}, u32[]{:S(2)}) %collective-permute-start.8) | collective-permute-done | bytes 1105952 | tf_op jit(solution)/shard_map/ppermute | solution.py:335
  148.8 3.3 multiply_reduce_fusion
  152.4 3.7 copy-done.3
  156.2 5.3 fusion.56.qkv_ref
  161.5 4.6 attend.1
  173.1 46.9 %collective-permute-done.11 = bf16[320,1024]{1,0:T(8,128)(2,1)} collective-permute-done((bf16[320,1024]{1,0:T(8,128)(2,1)S(1)}, bf16[320,1024]{1,0:T(8,128)(2,1)}, u32[]{:S(2)}, u32[]{:S(2)}) %collective-permute-start.11) | collective-permute-done | bytes 655392 | tf_op jit(solution)/shard_map/ppermute | solution.py:329
  220.6 9.1 %collective-permute-start.12 = (bf16[320,1024]{1,0:T(8,128)(2,1)}, bf16[320,1024]{1,0:T(8,128)(2,1)}, u32[]{:S(2)}, u32[]{:S(2)}) collective-permute-start(bf16[320,1024]{1,0:T(8,128)(2,1)} %collective-permute-done.10), channel_id=1, source_target_pairs={{0,2},{2,4},{4,6},{6,7},{7,5},{5,3},{3,1},{1,0},{8,10},{10,12},{12... | collective-permute-start | bytes 1966088 | tf_op jit(solution)/shard_map/ppermute | solution.py:326
  239.9 4.3 collective-permute-done.13
  252.2 8.4 %collective-permute-done.15 = bf16[320,1024]{1,0:T(8,128)(2,1)S(1)} collective-permute-done((bf16[320,1024]{1,0:T(8,128)(2,1)S(1)}, bf16[320,1024]{1,0:T(8,128)(2,1)S(1)}, u32[]{:S(2)}, u32[]{:S(2)}) %collective-permute-start.15) | collective-permute-done | bytes 655392 | tf_op jit(solution)/shard_map/ppermute | solution.py:329
  265.5 10.7 %collective-permute-done.16 = bf16[320,1024]{1,0:T(8,128)(2,1)S(1)} collective-permute-done((bf16[320,1024]{1,0:T(8,128)(2,1)S(1)}, bf16[320,1024]{1,0:T(8,128)(2,1)S(1)}, u32[]{:S(2)}, u32[]{:S(2)}) %collective-permute-start.16) | collective-permute-done | bytes 655392 | tf_op jit(solution)/shard_map/ppermute | solution.py:326
  282.5 4.8 collective-permute-done.20
  293.2 17.8 %middle_rows.1 = (bf16[1024,2304]{1,0:T(8,128)(2,1)S(1)}, f32[1024,1]{1,0:T(8,128)S(1)}, f32[128,2304]{1,0:T(8,128)S(1)}) custom-call(s32[1]{0:T(128)} %bitcast.me_ref, bf16[2560,1024]{1,0:T(8,128)(2,1)} %slice_dynamic-update-slice_fusion.8.mixed_ref, bf16[2304,2304]{1,0:T(8,128)(2,1)} %all-gather.2.cloned.1.call-done.weight_ref, ...), custom_call_target="tpu_custom_call" | custom-call | flops 10871635968 | bytes 24772608 | tf_op jit(solution)/shard_map/middle_rows/pallas_call | solution.py:165
  315.7 6.7 convolution_multiply_fusion
  322.5 5.9 fusion.57
  332.2 11.0 %collective-permute-done.25 = bf16[128,2304]{1,0:T(8,128)(2,1)S(1)} collective-permute-done((bf16[128,2304]{1,0:T(8,128)(2,1)S(1)}, bf16[128,2304]{1,0:T(8,128)(2,1)S(1)}, u32[]{:S(2)}, u32[]{:S(2)}) %collective-permute-start.25) | collective-permute-done | bytes 589856 | tf_op jit(solution)/shard_map/ppermute | solution.py:326
  345.7 7.4 collective-permute-done.26
  354.0 8.2 %multiply_convert_fusion = (bf16[1024,720]{0,1:T(8,128)(2,1)S(1)}, bf16[1024,720]{0,1:T(8,128)(2,1)S(1)}, bf16[1024,720]{0,1:T(8,128)(2,1)}) fusion(f32[1024]{0:T(1024)S(1)} %reduce.3, f32[1024,720]{0,1:T(8,128)S(1)} %fusion.57, f32[1024,720]{0,1:T(8,128)S(1)} %convolution_multiply_fusion, bf16[1024,2304]{1,0:T(8,128)(2,1)} %bitcast.55, ...), kind=kOutput, calls=%fused_computation.31 | convolution fusion | flops 3412316160 | bytes 21680128 | tf_op jit(solution)/shard_map/dot_general | solution.py:24
  362.2 7.0 fusion.58
  369.3 6.3 add_convert_fusion
  378.7 12.5 %collective-permute-done.27 = bf16[128,2304]{1,0:T(8,128)(2,1)S(1)} collective-permute-done((bf16[128,2304]{1,0:T(8,128)(2,1)S(1)}, bf16[128,2304]{1,0:T(8,128)(2,1)S(1)}, u32[]{:S(2)}, u32[]{:S(2)}) %collective-permute-start.27) | collective-permute-done | bytes 589856 | tf_op jit(solution)/shard_map/ppermute | solution.py:326
  392.7 14.6 %collective-permute-done.28 = bf16[128,2304]{1,0:T(8,128)(2,1)} collective-permute-done((bf16[128,2304]{1,0:T(8,128)(2,1)}, bf16[128,2304]{1,0:T(8,128)(2,1)}, u32[]{:S(2)}, u32[]{:S(2)}) %collective-permute-start.28) | collective-permute-done | bytes 589856 | tf_op jit(solution)/shard_map/ppermute | solution.py:326
  411.2 6.7 convolution_convert_fusion.4
  418.0 7.2 collective-permute-done.29
  429.6 4.2 convolution_convert_fusion.3
  445.8 4.4 all-to-all-start.2
  450.5 8.2 %convolution_convert_fusion.5 = bf16[720,2304]{1,0:T(8,128)(2,1)} fusion(bf16[1024,720]{0,1:T(8,128)(2,1)} %get-tuple-element.130, bf16[1024,2304]{1,0:T(8,128)(2,1)} %bitcast.55), kind=kOutput, calls=%fused_computation.16 | convolution fusion | flops 3399045120 | bytes 9510912 | tf_op jit(solution)/shard_map/dot_general | solution.py:24
  458.6 3.5 reshape_reshape.12
  466.3 3.5 fusion
  473.4 6.3 all-to-all-done.2
  480.9 13.4 %attend_back.1 = bf16[960,1024]{1,0:T(8,128)(2,1)S(1)} custom-call(bf16[960,1024]{1,0:T(8,128)(2,1)S(1)} %copy-done.12, bf16[320,1024]{1,0:T(8,128)(2,1)S(1)} %copy_bitcast_fusion.2.grad_ref, f32[1,1024]{1,0:T(1,128)S(1)} %bitcast.311, f32[32,1024]{1,0:T(8,128)S(1)} %get-tuple-element.223.cos_ref, f32[32,1024]{1,0:T(8,128)S(1)} %get-tuple-element.222.sin_ref, ...), custom_call_target="tpu_custom_call" | custom-call | flops 419430400 | bytes 4587520 | tf_op jit(solution)/shard_map/attend_back/pallas_call | solution.py:137
  495.9 5.5 fusion.59
  501.6 5.7 convolution_convert_fusion.2
  507.3 4.0 pad_maximum_fusion
  514.2 3.1 fusion.6
  517.3 6.0 all-to-all-start.3
  523.3 7.8 %convolution_convert_fusion.1 = bf16[1024,2304]{1,0:T(8,128)(2,1)S(1)} fusion(bf16[960,1024]{1,0:T(8,128)(2,1)S(1)} %copy-done.14, bf16[2304,960]{1,0:T(8,128)(2,1)} %bitcast.309), kind=kOutput, calls=%fused_computation.12 | convolution fusion | flops 4532207616 | bytes 11108352 | tf_op jit(solution)/shard_map/dot_general | solution.py:24
  533.3 4.7 constant_dynamic-slice_fusion.1
  543.4 23.2 %collective-permute-done.38 = bf16[128,2304]{1,0:T(8,128)(2,1)S(1)} collective-permute-done((bf16[128,2304]{1,0:T(8,128)(2,1)S(1)}, bf16[128,2304]{1,0:T(8,128)(2,1)S(1)}, u32[]{:S(2)}, u32[]{:S(2)}) %collective-permute-start.38) | collective-permute-done | bytes 589856 | tf_op jit(solution)/shard_map/ppermute | solution.py:329
  568.4 9.6 %collective-permute-start.37 = (bf16[128,2304]{1,0:T(8,128)(2,1)S(1)}, bf16[128,2304]{1,0:T(8,128)(2,1)S(1)}, u32[]{:S(2)}, u32[]{:S(2)}) collective-permute-start(bf16[128,2304]{1,0:T(8,128)(2,1)S(1)} %get-tuple-element.199), channel_id=1, source_target_pairs={{0,2},{2,4},{4,6},{6,7},{7,5},{5,3},{3,1},{1,0},{8,10},{10,12},{12... | collective-permute-start | bytes 1769480 | tf_op jit(solution)/shard_map/ppermute | solution.py:326
  578.8 11.3 %collective-permute-done.39 = bf16[128,2304]{1,0:T(8,128)(2,1)S(1)} collective-permute-done((bf16[128,2304]{1,0:T(8,128)(2,1)S(1)}, bf16[128,2304]{1,0:T(8,128)(2,1)S(1)}, u32[]{:S(2)}, u32[]{:S(2)}) %collective-permute-start.39) | collective-permute-done | bytes 589856 | tf_op jit(solution)/shard_map/ppermute | solution.py:329
  593.0 3.5 fusion.1
  598.2 7.3 collective-permute-done.40
  608.1 7.3 convolution_convert_fusion
  616.0 4.5 collective-permute-done.41
  630.6 5.2 all-to-all-start.4
  650.3 5.1 reshape.413
  660.3 16.5 %collective-permute-done.61.piece_ref = bf16[2,72,5760]{2,1,0:T(8,128)(2,1)} collective-permute-done((bf16[2,72,5760]{2,1,0:T(8,128)(2,1)}, bf16[2,72,5760]{2,1,0:T(8,128)(2,1)}, u32[]{:S(2)}, u32[]{:S(2)}) %collective-permute-start.61) | collective-permute-done | bytes 1658912 | tf_op jit(solution)/shard_map/ppermute | solution.py:335
  680.6 3.7 collective-permute-start.51
  702.1 4.7 finish.16
  706.9 4.8 finish.17
  714.0 8.5 %collective-permute-done.58.piece_ref = bf16[4,72,2304]{2,1,0:T(8,128)(2,1)} collective-permute-done((bf16[4,72,2304]{2,1,0:T(8,128)(2,1)}, bf16[4,72,2304]{2,1,0:T(8,128)(2,1)}, u32[]{:S(2)}, u32[]{:S(2)}) %collective-permute-start.58) | collective-permute-done | bytes 1327136 | tf_op jit(solution)/shard_map/ppermute | solution.py:335
  725.2 4.7 finish.22
  729.9 4.7 finish.23
  736.4 3.3 finish.18
  742.0 3.2 finish.19
  745.2 3.2 finish.20
  748.4 3.3 finish.21
  (364 shorter events, 220.3 us)
Async XLA Ops:
  13.9 43.5 %all-to-all-start = ((bf16[8,80,960]{2,1,0:T(8,128)(2,1)}), bf16[8,80,960]{2,1,0:T(8,128)(2,1)}, u32[]{:S(2)}, u32[]{:S(2)}) async-start(bf16[8,80,960]{2,1,0:T(8,128)(2,1)} %prepare_qkv.1), calls=%async_computation | async-start | bytes 2621440 | tf_op jit(solution)/shard_map/all_to_all | solution.py:389
  21.2 269.7 %all-gather.2.cloned.1.call-start = ((), (), s32[]{:S(2)}) async-start(), calls=%async_computation.5 | async-start | bytes 10948608 | tf_op jit(solution)/shard_map/all_gather | solution.py:499
  21.3 36.2 %collective-permute-start.2 = (bf16[128,2304]{1,0:T(8,128)(2,1)S(1)}, bf16[128,2304]{1,0:T(8,128)(2,1)}, u32[]{:S(2)}, u32[]{:S(2)}) collective-permute-start(bf16[128,2304]{1,0:T(8,128)(2,1)S(1)} %copy-done.23), channel_id=1, source_target_pairs={{2,0},{4,2},{6,4},{7,6},{5,7},{3,5},{1,3},{0,1},{10,8},{12,10},{14... | collective-permute-start | bytes 1769480 | tf_op jit(solution)/shard_map/ppermute | solution.py:329
  23.3 34.1 %collective-permute-start.1 = (bf16[128,2304]{1,0:T(8,128)(2,1)S(1)}, bf16[128,2304]{1,0:T(8,128)(2,1)}, u32[]{:S(2)}, u32[]{:S(2)}) collective-permute-start(bf16[128,2304]{1,0:T(8,128)(2,1)S(1)} %copy-done.23), channel_id=1, source_target_pairs={{0,2},{2,4},{4,6},{6,7},{7,5},{5,3},{3,1},{1,0},{8,10},{10,12},{12... | collective-permute-start | bytes 1769480 | tf_op jit(solution)/shard_map/ppermute | solution.py:326
  57.4 20.3 %collective-permute-start.3 = (bf16[128,2304]{1,0:T(8,128)(2,1)}, bf16[128,2304]{1,0:T(8,128)(2,1)}, u32[]{:S(2)}, u32[]{:S(2)}) collective-permute-start(bf16[128,2304]{1,0:T(8,128)(2,1)} %collective-permute-done.1), channel_id=1, source_target_pairs={{0,2},{2,4},{4,6},{6,7},{7,5},{5,3},{3,1},{1,0},{8,10},{10,12},{12... | collective-permute-start | bytes 1769480 | tf_op jit(solution)/shard_map/ppermute | solution.py:326
  66.0 14.3 %collective-permute-start.4 = (bf16[128,2304]{1,0:T(8,128)(2,1)}, bf16[128,2304]{1,0:T(8,128)(2,1)}, u32[]{:S(2)}, u32[]{:S(2)}) collective-permute-start(bf16[128,2304]{1,0:T(8,128)(2,1)} %collective-permute-done.2), channel_id=1, source_target_pairs={{2,0},{4,2},{6,4},{7,6},{5,7},{3,5},{1,3},{0,1},{10,8},{12,10},{14... | collective-permute-start | bytes 1769480 | tf_op jit(solution)/shard_map/ppermute | solution.py:329
  80.2 13.7 %collective-permute-start.5 = (bf16[128,2304]{1,0:T(8,128)(2,1)}, bf16[128,2304]{1,0:T(8,128)(2,1)}, u32[]{:S(2)}, u32[]{:S(2)}) collective-permute-start(bf16[128,2304]{1,0:T(8,128)(2,1)} %collective-permute-done.3), channel_id=1, source_target_pairs={{0,2},{2,4},{4,6},{6,7},{7,5},{5,3},{3,1},{1,0},{8,10},{10,12},{12... | collective-permute-start | bytes 1769480 | tf_op jit(solution)/shard_map/ppermute | solution.py:326
  82.0 14.1 %collective-permute-start.6 = (bf16[128,2304]{1,0:T(8,128)(2,1)}, bf16[128,2304]{1,0:T(8,128)(2,1)}, u32[]{:S(2)}, u32[]{:S(2)}) collective-permute-start(bf16[128,2304]{1,0:T(8,128)(2,1)} %collective-permute-done.4), channel_id=1, source_target_pairs={{2,0},{4,2},{6,4},{7,6},{5,7},{3,5},{1,3},{0,1},{10,8},{12,10},{14... | collective-permute-start | bytes 1769480 | tf_op jit(solution)/shard_map/ppermute | solution.py:329
  108.8 38.1 %collective-permute-start.8 = (bf16[8,72,960]{2,1,0:T(8,128)(2,1)}, bf16[8,72,960]{2,1,0:T(8,128)(2,1)S(1)}, u32[]{:S(2)}, u32[]{:S(2)}) collective-permute-start(bf16[8,72,960]{2,1,0:T(8,128)(2,1)} %slice.176), channel_id=1, source_target_pairs={{0,16},{8,24},{16,0},{24,8},{1,17},{9,25},{17,1},{25,9},{2,18},{10... | collective-permute-start | bytes 3317768 | tf_op jit(solution)/shard_map/ppermute | solution.py:335
  119.9 26.9 %collective-permute-start.7 = (bf16[128,2304]{1,0:T(8,128)(2,1)}, bf16[128,2304]{1,0:T(8,128)(2,1)}, u32[]{:S(2)}, u32[]{:S(2)}) collective-permute-start(bf16[128,2304]{1,0:T(8,128)(2,1)} %collective-permute-done.5), channel_id=1, source_target_pairs={{0,2},{2,4},{4,6},{6,7},{7,5},{5,3},{3,1},{1,0},{8,10},{10,12},{12... | collective-permute-start | bytes 1769480 | tf_op jit(solution)/shard_map/ppermute | solution.py:326
  120.5 116.0 %all-to-all-start.1 = ((bf16[8,144,720]{2,1,0:T(8,128)(2,1)}), bf16[8,144,720]{2,1,0:T(8,128)(2,1)}, u32[]{:S(2)}, u32[]{:S(2)}) async-start(bf16[8,144,720]{2,1,0:T(8,128)(2,1)} %prepare_ffn.1), calls=%async_computation.1 | async-start | bytes 3538944 | tf_op jit(solution)/shard_map/all_to_all | solution.py:389
  166.2 53.7 %collective-permute-start.11 = (bf16[320,1024]{1,0:T(8,128)(2,1)S(1)}, bf16[320,1024]{1,0:T(8,128)(2,1)}, u32[]{:S(2)}, u32[]{:S(2)}) collective-permute-start(bf16[320,1024]{1,0:T(8,128)(2,1)S(1)} %get-tuple-element.110), channel_id=1, source_target_pairs={{2,0},{4,2},{6,4},{7,6},{5,7},{3,5},{1,3},{0,1},{10,8},{12,10},{14... | collective-permute-start | bytes 1966088 | tf_op jit(solution)/shard_map/ppermute | solution.py:329
  166.6 53.4 %collective-permute-start.10 = (bf16[320,1024]{1,0:T(8,128)(2,1)S(1)}, bf16[320,1024]{1,0:T(8,128)(2,1)}, u32[]{:S(2)}, u32[]{:S(2)}) collective-permute-start(bf16[320,1024]{1,0:T(8,128)(2,1)S(1)} %get-tuple-element.110), channel_id=1, source_target_pairs={{0,2},{2,4},{4,6},{6,7},{7,5},{5,3},{3,1},{1,0},{8,10},{10,12},{12... | collective-permute-start | bytes 1966088 | tf_op jit(solution)/shard_map/ppermute | solution.py:326
  219.9 24.3 %collective-permute-start.13 = (bf16[320,1024]{1,0:T(8,128)(2,1)}, bf16[320,1024]{1,0:T(8,128)(2,1)S(1)}, u32[]{:S(2)}, u32[]{:S(2)}) collective-permute-start(bf16[320,1024]{1,0:T(8,128)(2,1)} %collective-permute-done.11), channel_id=1, source_target_pairs={{2,0},{4,2},{6,4},{7,6},{5,7},{3,5},{1,3},{0,1},{10,8},{12,10},{14... | collective-permute-start | bytes 1966088 | tf_op jit(solution)/shard_map/ppermute | solution.py:329
  220.6 24.6 %collective-permute-start.12 = (bf16[320,1024]{1,0:T(8,128)(2,1)}, bf16[320,1024]{1,0:T(8,128)(2,1)}, u32[]{:S(2)}, u32[]{:S(2)}) collective-permute-start(bf16[320,1024]{1,0:T(8,128)(2,1)} %collective-permute-done.10), channel_id=1, source_target_pairs={{0,2},{2,4},{4,6},{6,7},{7,5},{5,3},{3,1},{1,0},{8,10},{10,12},{12... | collective-permute-start | bytes 1966088 | tf_op jit(solution)/shard_map/ppermute | solution.py:326
  236.6 43.2 %collective-permute-start.18 = (bf16[8,144,720]{2,1,0:T(8,128)(2,1)}, bf16[8,144,720]{2,1,0:T(8,128)(2,1)S(1)}, u32[]{:S(2)}, u32[]{:S(2)}) collective-permute-start(bf16[8,144,720]{2,1,0:T(8,128)(2,1)} %all-to-all-done.1), channel_id=1, source_target_pairs={{0,16},{8,24},{16,0},{24,8},{1,17},{9,25},{17,1},{25,9},{2,18},{10... | collective-permute-start | bytes 4976648 | tf_op jit(solution)/shard_map/ppermute | solution.py:335
  237.1 42.7 %collective-permute-start.17 = (bf16[8,144,720]{2,1,0:T(8,128)(2,1)}, bf16[8,144,720]{2,1,0:T(8,128)(2,1)S(1)}, u32[]{:S(2)}, u32[]{:S(2)}) collective-permute-start(bf16[8,144,720]{2,1,0:T(8,128)(2,1)} %all-to-all-done.1), channel_id=1, source_target_pairs={{0,8},{8,0},{16,24},{24,16},{1,9},{9,1},{17,25},{25,17},{2,10},{10... | collective-permute-start | bytes 4976648 | tf_op jit(solution)/shard_map/ppermute | solution.py:332
  245.2 15.4 %collective-permute-start.15 = (bf16[320,1024]{1,0:T(8,128)(2,1)S(1)}, bf16[320,1024]{1,0:T(8,128)(2,1)S(1)}, u32[]{:S(2)}, u32[]{:S(2)}) collective-permute-start(bf16[320,1024]{1,0:T(8,128)(2,1)S(1)} %collective-permute-done.13), channel_id=1, source_target_pairs={{2,0},{4,2},{6,4},{7,6},{5,7},{3,5},{1,3},{0,1},{10,8},{12,10},{14... | collective-permute-start | bytes 1966088 | tf_op jit(solution)/shard_map/ppermute | solution.py:329
  247.0 15.1 %collective-permute-start.14 = (bf16[320,1024]{1,0:T(8,128)(2,1)}, bf16[320,1024]{1,0:T(8,128)(2,1)S(1)}, u32[]{:S(2)}, u32[]{:S(2)}) collective-permute-start(bf16[320,1024]{1,0:T(8,128)(2,1)} %collective-permute-done.12), channel_id=1, source_target_pairs={{0,2},{2,4},{4,6},{6,7},{7,5},{5,3},{3,1},{1,0},{8,10},{10,12},{12... | collective-permute-start | bytes 1966088 | tf_op jit(solution)/shard_map/ppermute | solution.py:326
  262.1 14.1 %collective-permute-start.16 = (bf16[320,1024]{1,0:T(8,128)(2,1)S(1)}, bf16[320,1024]{1,0:T(8,128)(2,1)S(1)}, u32[]{:S(2)}, u32[]{:S(2)}) collective-permute-start(bf16[320,1024]{1,0:T(8,128)(2,1)S(1)} %collective-permute-done.14), channel_id=1, source_target_pairs={{0,2},{2,4},{4,6},{6,7},{7,5},{5,3},{3,1},{1,0},{8,10},{10,12},{12... | collective-permute-start | bytes 1966088 | tf_op jit(solution)/shard_map/ppermute | solution.py:326
  276.2 11.1 %collective-permute-start.20 = (bf16[128,2304]{1,0:T(8,128)(2,1)S(1)}, bf16[128,2304]{1,0:T(8,128)(2,1)S(1)}, u32[]{:S(2)}, u32[]{:S(2)}) collective-permute-start(bf16[128,2304]{1,0:T(8,128)(2,1)S(1)} %copy-done.36), channel_id=1, source_target_pairs={{2,0},{4,2},{6,4},{7,6},{5,7},{3,5},{1,3},{0,1},{10,8},{12,10},{14... | collective-permute-start | bytes 1769480 | tf_op jit(solution)/shard_map/ppermute | solution.py:329
  276.5 12.0 %collective-permute-start.21 = (bf16[128,2304]{1,0:T(8,128)(2,1)S(1)}, bf16[128,2304]{1,0:T(8,128)(2,1)S(1)}, u32[]{:S(2)}, u32[]{:S(2)}) collective-permute-start(bf16[128,2304]{1,0:T(8,128)(2,1)S(1)} %copy-done.36), channel_id=1, source_target_pairs={{0,2},{2,4},{4,6},{6,7},{7,5},{5,3},{3,1},{1,0},{8,10},{10,12},{12... | collective-permute-start | bytes 1769480 | tf_op jit(solution)/shard_map/ppermute | solution.py:326
  313.4 15.0 %collective-permute-start.22 = (bf16[128,2304]{1,0:T(8,128)(2,1)S(1)}, bf16[128,2304]{1,0:T(8,128)(2,1)S(1)}, u32[]{:S(2)}, u32[]{:S(2)}) collective-permute-start(bf16[128,2304]{1,0:T(8,128)(2,1)S(1)} %copy-done.38), channel_id=1, source_target_pairs={{2,0},{4,2},{6,4},{7,6},{5,7},{3,5},{1,3},{0,1},{10,8},{12,10},{14... | collective-permute-start | bytes 1769480 | tf_op jit(solution)/shard_map/ppermute | solution.py:329
  314.8 13.6 %collective-permute-start.23 = (bf16[128,2304]{1,0:T(8,128)(2,1)}, bf16[128,2304]{1,0:T(8,128)(2,1)S(1)}, u32[]{:S(2)}, u32[]{:S(2)}) collective-permute-start(bf16[128,2304]{1,0:T(8,128)(2,1)} %copy-done.39), channel_id=1, source_target_pairs={{0,2},{2,4},{4,6},{6,7},{7,5},{5,3},{3,1},{1,0},{8,10},{10,12},{12... | collective-permute-start | bytes 1769480 | tf_op jit(solution)/shard_map/ppermute | solution.py:326
  328.4 15.6 %collective-permute-start.24 = (bf16[128,2304]{1,0:T(8,128)(2,1)S(1)}, bf16[128,2304]{1,0:T(8,128)(2,1)S(1)}, u32[]{:S(2)}, u32[]{:S(2)}) collective-permute-start(bf16[128,2304]{1,0:T(8,128)(2,1)S(1)} %collective-permute-done.22), channel_id=1, source_target_pairs={{2,0},{4,2},{6,4},{7,6},{5,7},{3,5},{1,3},{0,1},{10,8},{12,10},{14... | collective-permute-start | bytes 1769480 | tf_op jit(solution)/shard_map/ppermute | solution.py:329
  329.8 13.5 %collective-permute-start.25 = (bf16[128,2304]{1,0:T(8,128)(2,1)S(1)}, bf16[128,2304]{1,0:T(8,128)(2,1)S(1)}, u32[]{:S(2)}, u32[]{:S(2)}) collective-permute-start(bf16[128,2304]{1,0:T(8,128)(2,1)S(1)} %collective-permute-done.23), channel_id=1, source_target_pairs={{0,2},{2,4},{4,6},{6,7},{7,5},{5,3},{3,1},{1,0},{8,10},{10,12},{12... | collective-permute-start | bytes 1769480 | tf_op jit(solution)/shard_map/ppermute | solution.py:326
  376.7 14.5 %collective-permute-start.27 = (bf16[128,2304]{1,0:T(8,128)(2,1)S(1)}, bf16[128,2304]{1,0:T(8,128)(2,1)S(1)}, u32[]{:S(2)}, u32[]{:S(2)}) collective-permute-start(bf16[128,2304]{1,0:T(8,128)(2,1)S(1)} %get-tuple-element.206), channel_id=1, source_target_pairs={{0,2},{2,4},{4,6},{6,7},{7,5},{5,3},{3,1},{1,0},{8,10},{10,12},{12... | collective-permute-start | bytes 1769480 | tf_op jit(solution)/shard_map/ppermute | solution.py:326
  377.4 15.2 %collective-permute-start.31 = (bf16[128,2304]{1,0:T(8,128)(2,1)}, bf16[128,2304]{1,0:T(8,128)(2,1)S(1)}, u32[]{:S(2)}, u32[]{:S(2)}) collective-permute-start(bf16[128,2304]{1,0:T(8,128)(2,1)} %get-tuple-element.207), channel_id=1, source_target_pairs={{2,0},{4,2},{6,4},{7,6},{5,7},{3,5},{1,3},{0,1},{10,8},{12,10},{14... | collective-permute-start | bytes 1769480 | tf_op jit(solution)/shard_map/ppermute | solution.py:329
  392.2 15.1 %collective-permute-start.28 = (bf16[128,2304]{1,0:T(8,128)(2,1)}, bf16[128,2304]{1,0:T(8,128)(2,1)}, u32[]{:S(2)}, u32[]{:S(2)}) collective-permute-start(bf16[128,2304]{1,0:T(8,128)(2,1)} %fusion.38), channel_id=1, source_target_pairs={{0,2},{2,4},{4,6},{6,7},{7,5},{5,3},{3,1},{1,0},{8,10},{10,12},{12... | collective-permute-start | bytes 1769480 | tf_op jit(solution)/shard_map/ppermute | solution.py:326
  409.1 16.1 %collective-permute-start.29 = (bf16[128,2304]{1,0:T(8,128)(2,1)S(1)}, bf16[128,2304]{1,0:T(8,128)(2,1)S(1)}, u32[]{:S(2)}, u32[]{:S(2)}) collective-permute-start(bf16[128,2304]{1,0:T(8,128)(2,1)S(1)} %get-tuple-element.204), channel_id=1, source_target_pairs={{0,2},{2,4},{4,6},{6,7},{7,5},{5,3},{3,1},{1,0},{8,10},{10,12},{12... | collective-permute-start | bytes 1769480 | tf_op jit(solution)/shard_map/ppermute | solution.py:326
  409.2 16.2 %collective-permute-start.32 = (bf16[128,2304]{1,0:T(8,128)(2,1)S(1)}, bf16[128,2304]{1,0:T(8,128)(2,1)S(1)}, u32[]{:S(2)}, u32[]{:S(2)}) collective-permute-start(bf16[128,2304]{1,0:T(8,128)(2,1)S(1)} %get-tuple-element.205), channel_id=1, source_target_pairs={{2,0},{4,2},{6,4},{7,6},{5,7},{3,5},{1,3},{0,1},{10,8},{12,10},{14... | collective-permute-start | bytes 1769480 | tf_op jit(solution)/shard_map/ppermute | solution.py:329
  429.1 10.3 %collective-permute-start.33 = (bf16[128,2304]{1,0:T(8,128)(2,1)S(1)}, bf16[128,2304]{1,0:T(8,128)(2,1)S(1)}, u32[]{:S(2)}, u32[]{:S(2)}) collective-permute-start(bf16[128,2304]{1,0:T(8,128)(2,1)S(1)} %get-tuple-element.203), channel_id=1, source_target_pairs={{2,0},{4,2},{6,4},{7,6},{5,7},{3,5},{1,3},{0,1},{10,8},{12,10},{14... | collective-permute-start | bytes 1769480 | tf_op jit(solution)/shard_map/ppermute | solution.py:329
  436.9 29.3 %collective-permute-start.34 = (bf16[8,2,144,720]{3,2,1,0:T(8,128)(2,1)}, bf16[8,2,144,720]{3,2,1,0:T(8,128)(2,1)}, u32[]{:S(2)}, u32[]{:S(2)}) collective-permute-start(bf16[8,2,144,720]{3,2,1,0:T(8,128)(2,1)} %fusion.3), channel_id=1, source_target_pairs={{0,8},{8,0},{16,24},{24,16},{1,9},{9,1},{17,25},{25,17},{2,10},{10... | collective-permute-start | bytes 9953288 | tf_op jit(solution)/shard_map/ppermute | solution.py:332
  445.8 33.9 %all-to-all-start.2 = ((bf16[8,608,128]{2,1,0:T(8,128)(2,1)}), bf16[8,608,128]{2,1,0:T(8,128)(2,1)}, u32[]{:S(2)}, u32[]{:S(2)}) async-start(bf16[8,608,128]{2,1,0:T(8,128)(2,1)} %pad_maximum_fusion.2), calls=%async_computation.2 | async-start | bytes 2490368 | tf_op jit(solution)/shard_map/all_to_all | solution.py:389
  466.3 73.6 %collective-permute-start.45 = (bf16[1,2,180,2304]{3,1,2,0:T(2,128)(2,1)}, bf16[1,2,180,2304]{3,1,2,0:T(2,128)(2,1)}, u32[]{:S(2)}, u32[]{:S(2)}) collective-permute-start(bf16[1,2,180,2304]{3,1,2,0:T(2,128)(2,1)} %copy.281), channel_id=1, source_target_pairs={{0,8},{8,0},{16,24},{24,16},{1,9},{9,1},{17,25},{25,17},{2,10},{10... | collective-permute-start | bytes 4976648 | tf_op jit(solution)/shard_map/ppermute | solution.py:332
  472.9 41.3 %collective-permute-start.35 = (bf16[8,144,720]{2,1,0:T(8,128)(2,1)}, bf16[8,144,720]{2,1,0:T(8,128)(2,1)}, u32[]{:S(2)}, u32[]{:S(2)}) collective-permute-start(bf16[8,144,720]{2,1,0:T(8,128)(2,1)} %dynamic-slice_bitcast_fusion), channel_id=1, source_target_pairs={{0,16},{8,24},{16,0},{24,8},{1,17},{9,25},{17,1},{25,9},{2,18},{10... | collective-permute-start | bytes 4976648 | tf_op jit(solution)/shard_map/ppermute | solution.py:335
  517.3 74.7 %all-to-all-start.3 = ((bf16[8,144,720]{2,1,0:T(8,128)(2,1)}), bf16[8,144,720]{2,1,0:T(8,128)(2,1)}, u32[]{:S(2)}, u32[]{:S(2)}) async-start(bf16[8,144,720]{2,1,0:T(8,128)(2,1)} %fusion.6), calls=%async_computation.3 | async-start | bytes 3538944 | tf_op jit(solution)/shard_map/all_to_all | solution.py:389
  531.2 35.4 %collective-permute-start.38 = (bf16[128,2304]{1,0:T(8,128)(2,1)S(1)}, bf16[128,2304]{1,0:T(8,128)(2,1)S(1)}, u32[]{:S(2)}, u32[]{:S(2)}) collective-permute-start(bf16[128,2304]{1,0:T(8,128)(2,1)S(1)} %get-tuple-element.200), channel_id=1, source_target_pairs={{2,0},{4,2},{6,4},{7,6},{5,7},{3,5},{1,3},{0,1},{10,8},{12,10},{14... | collective-permute-start | bytes 1769480 | tf_op jit(solution)/shard_map/ppermute | solution.py:329
  533.2 33.3 %collective-permute-start.36 = (bf16[128,2304]{1,0:T(8,128)(2,1)S(1)}, bf16[128,2304]{1,0:T(8,128)(2,1)S(1)}, u32[]{:S(2)}, u32[]{:S(2)}) collective-permute-start(bf16[128,2304]{1,0:T(8,128)(2,1)S(1)} %get-tuple-element.201), channel_id=1, source_target_pairs={{0,2},{2,4},{4,6},{6,7},{7,5},{5,3},{3,1},{1,0},{8,10},{10,12},{12... | collective-permute-start | bytes 1769480 | tf_op jit(solution)/shard_map/ppermute | solution.py:326
  539.8 53.2 %collective-permute-start.56 = (bf16[8,2,72,1248]{3,2,0,1:T(8,128)(2,1)}, bf16[8,2,72,1248]{3,2,0,1:T(8,128)(2,1)}, u32[]{:S(2)}, u32[]{:S(2)}) collective-permute-start(bf16[8,2,72,1248]{3,2,0,1:T(8,128)(2,1)} %bitcast.301), channel_id=1, source_target_pairs={{0,8},{8,0},{16,24},{24,16},{1,9},{9,1},{17,25},{25,17},{2,10},{10... | collective-permute-start | bytes 8626184 | tf_op jit(solution)/shard_map/ppermute | solution.py:332
  542.9 35.2 %collective-permute-start.46 = (bf16[1,180,2304]{2,1,0:T(8,128)(2,1)S(1)}, bf16[1,180,2304]{2,1,0:T(8,128)(2,1)S(1)}, u32[]{:S(2)}, u32[]{:S(2)}) collective-permute-start(bf16[1,180,2304]{2,1,0:T(8,128)(2,1)S(1)} %dynamic-slice_bitcast_fusion.3), channel_id=1, source_target_pairs={{0,16},{8,24},{16,0},{24,8},{1,17},{9,25},{17,1},{25,9},{2,18},{10... | collective-permute-start | bytes 2488328 | tf_op jit(solution)/shard_map/ppermute | solution.py:335
  566.9 23.2 %collective-permute-start.39 = (bf16[128,2304]{1,0:T(8,128)(2,1)S(1)}, bf16[128,2304]{1,0:T(8,128)(2,1)S(1)}, u32[]{:S(2)}, u32[]{:S(2)}) collective-permute-start(bf16[128,2304]{1,0:T(8,128)(2,1)S(1)} %get-tuple-element.198), channel_id=1, source_target_pairs={{2,0},{4,2},{6,4},{7,6},{5,7},{3,5},{1,3},{0,1},{10,8},{12,10},{14... | collective-permute-start | bytes 1769480 | tf_op jit(solution)/shard_map/ppermute | solution.py:329
  568.4 23.2 %collective-permute-start.37 = (bf16[128,2304]{1,0:T(8,128)(2,1)S(1)}, bf16[128,2304]{1,0:T(8,128)(2,1)S(1)}, u32[]{:S(2)}, u32[]{:S(2)}) collective-permute-start(bf16[128,2304]{1,0:T(8,128)(2,1)S(1)} %get-tuple-element.199), channel_id=1, source_target_pairs={{0,2},{2,4},{4,6},{6,7},{7,5},{5,3},{3,1},{1,0},{8,10},{10,12},{12... | collective-permute-start | bytes 1769480 | tf_op jit(solution)/shard_map/ppermute | solution.py:326
  578.2 37.3 %collective-permute-start.47 = (bf16[1,180,2304]{2,1,0:T(8,128)(2,1)S(1)}, bf16[1,180,2304]{2,1,0:T(8,128)(2,1)}, u32[]{:S(2)}, u32[]{:S(2)}) collective-permute-start(bf16[1,180,2304]{2,1,0:T(8,128)(2,1)S(1)} %fusion.10.piece_ref), channel_id=1, source_target_pairs={{0,16},{8,24},{16,0},{24,8},{1,17},{9,25},{17,1},{25,9},{2,18},{10... | collective-permute-start | bytes 2488328 | tf_op jit(solution)/shard_map/ppermute | solution.py:335
  592.0 13.5 %collective-permute-start.40 = (bf16[128,2304]{1,0:T(8,128)(2,1)S(1)}, bf16[128,2304]{1,0:T(8,128)(2,1)S(1)}, u32[]{:S(2)}, u32[]{:S(2)}) collective-permute-start(bf16[128,2304]{1,0:T(8,128)(2,1)S(1)} %get-tuple-element.138), channel_id=1, source_target_pairs={{0,2},{2,4},{4,6},{6,7},{7,5},{5,3},{3,1},{1,0},{8,10},{10,12},{12... | collective-permute-start | bytes 1769480 | tf_op jit(solution)/shard_map/ppermute | solution.py:326
  596.6 32.6 %collective-permute-start.57 = (bf16[8,72,1248]{2,1,0:T(8,128)(2,1)S(1)}, bf16[8,72,1248]{2,1,0:T(8,128)(2,1)S(1)}, u32[]{:S(2)}, u32[]{:S(2)}) collective-permute-start(bf16[8,72,1248]{2,1,0:T(8,128)(2,1)S(1)} %dynamic-slice_bitcast_fusion.2), channel_id=1, source_target_pairs={{0,16},{8,24},{16,0},{24,8},{1,17},{9,25},{17,1},{25,9},{2,18},{10... | collective-permute-start | bytes 4313096 | tf_op jit(solution)/shard_map/ppermute | solution.py:335
  597.1 18.9 %collective-permute-start.42 = (bf16[128,2304]{1,0:T(8,128)(2,1)S(1)}, bf16[128,2304]{1,0:T(8,128)(2,1)S(1)}, u32[]{:S(2)}, u32[]{:S(2)}) collective-permute-start(bf16[128,2304]{1,0:T(8,128)(2,1)S(1)} %get-tuple-element.139), channel_id=1, source_target_pairs={{2,0},{4,2},{6,4},{7,6},{5,7},{3,5},{1,3},{0,1},{10,8},{12,10},{14... | collective-permute-start | bytes 1769480 | tf_op jit(solution)/shard_map/ppermute | solution.py:329
  606.7 13.7 %collective-permute-start.41 = (bf16[128,2304]{1,0:T(8,128)(2,1)S(1)}, bf16[128,2304]{1,0:T(8,128)(2,1)S(1)}, u32[]{:S(2)}, u32[]{:S(2)}) collective-permute-start(bf16[128,2304]{1,0:T(8,128)(2,1)S(1)} %fusion.29), channel_id=1, source_target_pairs={{0,2},{2,4},{4,6},{6,7},{7,5},{5,3},{3,1},{1,0},{8,10},{10,12},{12... | collective-permute-start | bytes 1769480 | tf_op jit(solution)/shard_map/ppermute | solution.py:326
  615.4 28.0 %collective-permute-start.49 = (bf16[1,180,2304]{2,1,0:T(8,128)(2,1)S(1)}, bf16[1,180,2304]{2,1,0:T(8,128)(2,1)}, u32[]{:S(2)}, u32[]{:S(2)}) collective-permute-start(bf16[1,180,2304]{2,1,0:T(8,128)(2,1)S(1)} %fusion.10.piece_ref), channel_id=1, source_target_pairs={{0,8},{8,0},{16,24},{24,16},{1,9},{9,1},{17,25},{25,17},{2,10},{10... | collective-permute-start | bytes 2488328 | tf_op jit(solution)/shard_map/ppermute | solution.py:332
  615.5 32.5 %collective-permute-start.48 = (bf16[1,180,2304]{2,1,0:T(8,128)(2,1)}, bf16[1,180,2304]{2,1,0:T(8,128)(2,1)}, u32[]{:S(2)}, u32[]{:S(2)}) collective-permute-start(bf16[1,180,2304]{2,1,0:T(8,128)(2,1)} %collective-permute-done.47.piece_ref), channel_id=1, source_target_pairs={{0,8},{8,0},{16,24},{24,16},{1,9},{9,1},{17,25},{25,17},{2,10},{10... | collective-permute-start | bytes 2488328 | tf_op jit(solution)/shard_map/ppermute | solution.py:332
  624.0 31.4 %collective-permute-start.44 = (bf16[128,2304]{1,0:T(8,128)(2,1)}, bf16[128,2304]{1,0:T(8,128)(2,1)}, u32[]{:S(2)}, u32[]{:S(2)}) collective-permute-start(bf16[128,2304]{1,0:T(8,128)(2,1)} %get-tuple-element.194), channel_id=1, source_target_pairs={{2,0},{4,2},{6,4},{7,6},{5,7},{3,5},{1,3},{0,1},{10,8},{12,10},{14... | collective-permute-start | bytes 1769480 | tf_op jit(solution)/shard_map/ppermute | solution.py:329
  625.9 29.5 %collective-permute-start.43 = (bf16[128,2304]{1,0:T(8,128)(2,1)}, bf16[128,2304]{1,0:T(8,128)(2,1)}, u32[]{:S(2)}, u32[]{:S(2)}) collective-permute-start(bf16[128,2304]{1,0:T(8,128)(2,1)} %get-tuple-element.195), channel_id=1, source_target_pairs={{0,2},{2,4},{4,6},{6,7},{7,5},{5,3},{3,1},{1,0},{8,10},{10,12},{12... | collective-permute-start | bytes 1769480 | tf_op jit(solution)/shard_map/ppermute | solution.py:326
  630.6 53.6 %all-to-all-start.4 = ((bf16[8,72,1248]{2,1,0:T(8,128)(2,1)}), bf16[8,72,1248]{2,1,0:T(8,128)(2,1)}, u32[]{:S(2)}, u32[]{:S(2)}) async-start(bf16[8,72,1248]{2,1,0:T(8,128)(2,1)} %fusion.8), calls=%async_computation.4 | async-start | bytes 2949120 | tf_op jit(solution)/shard_map/all_to_all | solution.py:389
  640.6 36.2 %collective-permute-start.61 = (bf16[2,72,5760]{2,1,0:T(8,128)(2,1)}, bf16[2,72,5760]{2,1,0:T(8,128)(2,1)}, u32[]{:S(2)}, u32[]{:S(2)}) collective-permute-start(bf16[2,72,5760]{2,1,0:T(8,128)(2,1)} %reshape.415.piece_ref), channel_id=1, source_target_pairs={{0,16},{8,24},{16,0},{24,8},{1,17},{9,25},{17,1},{25,9},{2,18},{10... | collective-permute-start | bytes 4976648 | tf_op jit(solution)/shard_map/ppermute | solution.py:335
  658.2 20.3 %collective-permute-start.50 = (bf16[128,2304]{1,0:T(8,128)(2,1)S(1)}, bf16[128,2304]{1,0:T(8,128)(2,1)S(1)}, u32[]{:S(2)}, u32[]{:S(2)}) collective-permute-start(bf16[128,2304]{1,0:T(8,128)(2,1)S(1)} %get-tuple-element.141), channel_id=1, source_target_pairs={{0,2},{2,4},{4,6},{6,7},{7,5},{5,3},{3,1},{1,0},{8,10},{10,12},{12... | collective-permute-start | bytes 1769480 | tf_op jit(solution)/shard_map/ppermute | solution.py:326
  660.3 46.6 %collective-permute-start.54 = (bf16[2,72,5760]{2,1,0:T(8,128)(2,1)S(1)}, bf16[2,72,5760]{2,1,0:T(8,128)(2,1)}, u32[]{:S(2)}, u32[]{:S(2)}) collective-permute-start(bf16[2,72,5760]{2,1,0:T(8,128)(2,1)S(1)} %copy-done.26), channel_id=1, source_target_pairs={{0,8},{8,0},{16,24},{24,16},{1,9},{9,1},{17,25},{25,17},{2,10},{10... | collective-permute-start | bytes 4976648 | tf_op jit(solution)/shard_map/ppermute | solution.py:332
  676.8 53.1 %collective-permute-start.62 = (bf16[2,72,5760]{2,1,0:T(8,128)(2,1)}, bf16[2,72,5760]{2,1,0:T(8,128)(2,1)}, u32[]{:S(2)}, u32[]{:S(2)}) collective-permute-start(bf16[2,72,5760]{2,1,0:T(8,128)(2,1)} %collective-permute-done.61.piece_ref), channel_id=1, source_target_pairs={{0,8},{8,0},{16,24},{24,16},{1,9},{9,1},{17,25},{25,17},{2,10},{10... | collective-permute-start | bytes 4976648 | tf_op jit(solution)/shard_map/ppermute | solution.py:332
  676.8 17.0 %collective-permute-start.52 = (bf16[128,2304]{1,0:T(8,128)(2,1)}, bf16[128,2304]{1,0:T(8,128)(2,1)}, u32[]{:S(2)}, u32[]{:S(2)}) collective-permute-start(bf16[128,2304]{1,0:T(8,128)(2,1)} %get-tuple-element.142), channel_id=1, source_target_pairs={{2,0},{4,2},{6,4},{7,6},{5,7},{3,5},{1,3},{0,1},{10,8},{12,10},{14... | collective-permute-start | bytes 1769480 | tf_op jit(solution)/shard_map/ppermute | solution.py:329
  680.6 15.8 %collective-permute-start.51 = (bf16[128,2304]{1,0:T(8,128)(2,1)}, bf16[128,2304]{1,0:T(8,128)(2,1)}, u32[]{:S(2)}, u32[]{:S(2)}) collective-permute-start(bf16[128,2304]{1,0:T(8,128)(2,1)} %fusion.26), channel_id=1, source_target_pairs={{0,2},{2,4},{4,6},{6,7},{7,5},{5,3},{3,1},{1,0},{8,10},{10,12},{12... | collective-permute-start | bytes 1769480 | tf_op jit(solution)/shard_map/ppermute | solution.py:326
  693.3 29.1 %collective-permute-start.58 = (bf16[4,72,2304]{2,1,0:T(8,128)(2,1)}, bf16[4,72,2304]{2,1,0:T(8,128)(2,1)}, u32[]{:S(2)}, u32[]{:S(2)}) collective-permute-start(bf16[4,72,2304]{2,1,0:T(8,128)(2,1)} %pad_maximum_fusion.1.piece_ref), channel_id=1, source_target_pairs={{0,16},{8,24},{16,0},{24,8},{1,17},{9,25},{17,1},{25,9},{2,18},{10... | collective-permute-start | bytes 3981320 | tf_op jit(solution)/shard_map/ppermute | solution.py:335
  699.0 15.0 %collective-permute-start.53 = (bf16[128,2304]{1,0:T(8,128)(2,1)}, bf16[128,2304]{1,0:T(8,128)(2,1)}, u32[]{:S(2)}, u32[]{:S(2)}) collective-permute-start(bf16[128,2304]{1,0:T(8,128)(2,1)} %get-tuple-element.190), channel_id=1, source_target_pairs={{2,0},{4,2},{6,4},{7,6},{5,7},{3,5},{1,3},{0,1},{10,8},{12,10},{14... | collective-permute-start | bytes 1769480 | tf_op jit(solution)/shard_map/ppermute | solution.py:329
  714.0 25.7 %collective-permute-start.55 = (bf16[128,2304]{1,0:T(8,128)(2,1)S(1)}, bf16[128,2304]{1,0:T(8,128)(2,1)S(1)}, u32[]{:S(2)}, u32[]{:S(2)}) collective-permute-start(bf16[128,2304]{1,0:T(8,128)(2,1)S(1)} %get-tuple-element.149), channel_id=1, source_target_pairs={{0,2},{2,4},{4,6},{6,7},{7,5},{5,3},{3,1},{1,0},{8,10},{10,12},{12... | collective-permute-start | bytes 1769480 | tf_op jit(solution)/shard_map/ppermute | solution.py:326
  714.0 28.0 %collective-permute-start.60 = (bf16[4,72,2304]{2,1,0:T(8,128)(2,1)}, bf16[4,72,2304]{2,1,0:T(8,128)(2,1)}, u32[]{:S(2)}, u32[]{:S(2)}) collective-permute-start(bf16[4,72,2304]{2,1,0:T(8,128)(2,1)} %pad_maximum_fusion.1.piece_ref), channel_id=1, source_target_pairs={{0,8},{8,0},{16,24},{24,16},{1,9},{9,1},{17,25},{25,17},{2,10},{10... | collective-permute-start | bytes 3981320 | tf_op jit(solution)/shard_map/ppermute | solution.py:332
  722.4 26.0 %collective-permute-start.59 = (bf16[4,72,2304]{2,1,0:T(8,128)(2,1)}, bf16[4,72,2304]{2,1,0:T(8,128)(2,1)}, u32[]{:S(2)}, u32[]{:S(2)}) collective-permute-start(bf16[4,72,2304]{2,1,0:T(8,128)(2,1)} %collective-permute-done.58.piece_ref), channel_id=1, source_target_pairs={{0,8},{8,0},{16,24},{24,16},{1,9},{9,1},{17,25},{25,17},{2,10},{10... | collective-permute-start | bytes 3981320 | tf_op jit(solution)/shard_map/ppermute | solution.py:332
  (60 other events, 857.2 us)
Sparse Core Ops, SparseCore 0:
  96.2 126.0 all-gather.1

commit v5 on v4

--- a/solution.py
+++ b/solution.py
@@ -495,7 +495,7 @@
         x_pieces = ring_gather(tokens, (None, (qkv_part, ffn_part)), True)
         info = qkv_part[:, part, : docs + pics].astype(jnp.int32)
         near = x_pieces[-2][1]
-        out_part = after(pick(by_rep(w_out), mine, 0), near).astype(BF16)
+        out_part = pick(by_rep(w_out), mine, 0).astype(BF16)
         out_w = lax.all_gather(out_part, ("shard", "rep"), axis=0, tiled=True)
         ffn_part = exchange(after(ffn_part, near))
         qkv_part = qkv_part[:, :part]

time: 767 us -> 741 us (0.966)
  waiting for transfers between devices: 298 us -> 280 us
    ppermute x18, waiting for transfers between devices: 138 us -> 77.3 us  [left(): return lax.ppermute(x, 'shard', to_left)]
    all_to_all x5, waiting for transfers between devices: 6.3 us -> 42.4 us  [exchange(): lax.all_to_all(blocks, 'shard', split_axis=0, concat_axis=0, tiled=True)]
    ppermute x24, waiting for transfers between devices: 105 us -> 129 us  [right(): return lax.ppermute(x, 'shard', to_right)]
    ppermute x24, starting transfers between devices: 47.8 us -> 28.2 us  [right(): return lax.ppermute(x, 'shard', to_right)]
    ppermute x8, waiting for transfers between devices: 48.8 us -> 30.8 us  [chip_swap(): return lax.ppermute(x, 'rep', chip_pairs)]
    ppermute x18, starting transfers between devices: 23.1 us -> 37.1 us  [left(): return lax.ppermute(x, 'shard', to_left)]
  transfers between devices with their start and end apart: 69 -> 69, of which waited for: 33 -> 33; matrix products, arithmetic and copies ran while one was open for 27% -> 28% of each run, Pallas kernels for 8% -> 9%
where the time goes in v5:
time: 741 us; the launch traced here: 735 us
  waiting for transfers between devices  280 us (38%)
  local copies, waits for them, and re-layouts  109 us (15%)
  starting transfers between devices  101 us (14%)
  matrix products  87.8 us (12%)
  Pallas kernels  84.1 us (11%)
  other arithmetic  57.8 us (8%)
  between operations  15.6 us (2%)
    ppermute x24, waiting for transfers between devices, right(): return lax.ppermute(x, 'shard', to_right)  129 us
    dot_general x14, matrix products, mm(): lax.dot_general(left, right, (((left_dim,), (right_dim,)), ((), ())), pre...  87.8 us
    ppermute x18, waiting for transfers between devices, left(): return lax.ppermute(x, 'shard', to_left)  77.3 us
    all_to_all x5, waiting for transfers between devices, exchange(): lax.all_to_all(blocks, 'shard', split_axis=0, concat_axis=0, tiled=True)  42.4 us
    pallas_call x12, Pallas kernels, finish(): pl.pallas_call(functools.partial(finish_kernel, count, gained), grid_spec...  41.2 us
    ppermute x18, starting transfers between devices, left(): return lax.ppermute(x, 'shard', to_left)  37.1 us
    ppermute x8, waiting for transfers between devices, chip_swap(): return lax.ppermute(x, 'rep', chip_pairs)  30.8 us
    all_to_all x5, starting transfers between devices, exchange(): lax.all_to_all(blocks, 'shard', split_axis=0, concat_axis=0, tiled=True)  29.8 us
  transfers between devices with their start and end apart: 69, of which 33 were waited for; matrix products, arithmetic and copies ran while one was open for 28% of the time, Pallas kernels for 9%

profile of v5, /device:TPU:0, one launch (start us, length us, event | category | flops | bytes accessed | tf_op | source)
XLA Modules:
  0.0 734.5 jit_solution(17792214532368714759)
XLA Ops:
  19.5 6.2 all-to-all-start
  31.9 3.9 prepare_ffn.1
  40.5 36.0 %all-to-all-done = bf16[8,80,960]{2,1,0:T(8,128)(2,1)S(1)} async-done(((bf16[8,80,960]{2,1,0:T(8,128)(2,1)}), bf16[8,80,960]{2,1,0:T(8,128)(2,1)S(1)}, u32[]{:S(2)}, u32[]{:S(2)}) %all-to-all-start) | async-done | bytes 1228832 | tf_op jit(solution)/shard_map/all_to_all | solution.py:389
  85.1 23.6 %collective-permute-done.3 = bf16[128,2304]{1,0:T(8,128)(2,1)S(1)} collective-permute-done((bf16[128,2304]{1,0:T(8,128)(2,1)}, bf16[128,2304]{1,0:T(8,128)(2,1)S(1)}, u32[]{:S(2)}, u32[]{:S(2)}) %collective-permute-start.3) | collective-permute-done | bytes 589856 | tf_op jit(solution)/shard_map/ppermute | solution.py:326
  119.0 12.9 %collective-permute-done.5 = bf16[128,2304]{1,0:T(8,128)(2,1)S(1)} collective-permute-done((bf16[128,2304]{1,0:T(8,128)(2,1)S(1)}, bf16[128,2304]{1,0:T(8,128)(2,1)S(1)}, u32[]{:S(2)}, u32[]{:S(2)}) %collective-permute-start.5) | collective-permute-done | bytes 589856 | tf_op jit(solution)/shard_map/ppermute | solution.py:326
  131.9 6.9 collective-permute-done.6
  139.3 6.2 all-to-all-start.1
  147.2 10.9 %collective-permute-done.7 = bf16[128,2304]{1,0:T(8,128)(2,1)} collective-permute-done((bf16[128,2304]{1,0:T(8,128)(2,1)S(1)}, bf16[128,2304]{1,0:T(8,128)(2,1)}, u32[]{:S(2)}, u32[]{:S(2)}) %collective-permute-start.7) | collective-permute-done | bytes 589856 | tf_op jit(solution)/shard_map/ppermute | solution.py:326
  160.0 3.3 multiply_reduce_fusion
  163.7 3.7 copy-done.3
  167.4 5.3 fusion.57.qkv_ref
  172.8 4.6 attend.1
  185.8 12.1 %collective-permute-done.11 = bf16[320,1024]{1,0:T(8,128)(2,1)} collective-permute-done((bf16[320,1024]{1,0:T(8,128)(2,1)S(1)}, bf16[320,1024]{1,0:T(8,128)(2,1)}, u32[]{:S(2)}, u32[]{:S(2)}) %collective-permute-start.11) | collective-permute-done | bytes 655392 | tf_op jit(solution)/shard_map/ppermute | solution.py:329
  198.0 4.4 collective-permute-start.13
  212.5 4.0 collective-permute-done.13
  225.7 7.5 %collective-permute-done.15 = bf16[320,1024]{1,0:T(8,128)(2,1)S(1)} collective-permute-done((bf16[320,1024]{1,0:T(8,128)(2,1)S(1)}, bf16[320,1024]{1,0:T(8,128)(2,1)S(1)}, u32[]{:S(2)}, u32[]{:S(2)}) %collective-permute-start.15) | collective-permute-done | bytes 655392 | tf_op jit(solution)/shard_map/ppermute | solution.py:329
  239.2 11.4 %collective-permute-done.16 = bf16[320,1024]{1,0:T(8,128)(2,1)S(1)} collective-permute-done((bf16[320,1024]{1,0:T(8,128)(2,1)S(1)}, bf16[320,1024]{1,0:T(8,128)(2,1)S(1)}, u32[]{:S(2)}, u32[]{:S(2)}) %collective-permute-start.16) | collective-permute-done | bytes 655392 | tf_op jit(solution)/shard_map/ppermute | solution.py:326
  256.8 6.4 collective-permute-done.20
  269.2 17.8 %middle_rows.1 = (bf16[1024,2304]{1,0:T(8,128)(2,1)S(1)}, f32[1024,1]{1,0:T(8,128)S(1)}, f32[128,2304]{1,0:T(8,128)S(1)}) custom-call(s32[1]{0:T(128)} %bitcast.me_ref, bf16[2560,1024]{1,0:T(8,128)(2,1)} %slice_dynamic-update-slice_fusion.8.mixed_ref, bf16[2304,2304]{1,0:T(8,128)(2,1)} %bitcast.374, bf16[1024,2304]{1,0:T(8,128)(2,1)S(1)} %bitcast.304), custom_call_target="tpu_custom_call" | custom-call | flops 10871635968 | bytes 24772608 | tf_op jit(solution)/shard_map/middle_rows/pallas_call | solution.py:165
  291.7 6.7 convolution_multiply_fusion
  298.4 5.9 fusion.58
  308.2 11.0 %collective-permute-done.25 = bf16[128,2304]{1,0:T(8,128)(2,1)S(1)} collective-permute-done((bf16[128,2304]{1,0:T(8,128)(2,1)S(1)}, bf16[128,2304]{1,0:T(8,128)(2,1)S(1)}, u32[]{:S(2)}, u32[]{:S(2)}) %collective-permute-start.25) | collective-permute-done | bytes 589856 | tf_op jit(solution)/shard_map/ppermute | solution.py:326
  321.7 7.4 %collective-permute-done.26 = bf16[128,2304]{1,0:T(8,128)(2,1)S(1)} collective-permute-done((bf16[128,2304]{1,0:T(8,128)(2,1)S(1)}, bf16[128,2304]{1,0:T(8,128)(2,1)S(1)}, u32[]{:S(2)}, u32[]{:S(2)}) %collective-permute-start.26) | collective-permute-done | bytes 589856 | tf_op jit(solution)/shard_map/ppermute | solution.py:326
  329.9 8.2 %multiply_convert_fusion = (bf16[1024,720]{0,1:T(8,128)(2,1)S(1)}, bf16[1024,720]{0,1:T(8,128)(2,1)S(1)}, bf16[1024,720]{0,1:T(8,128)(2,1)}) fusion(f32[1024]{0:T(1024)S(1)} %reduce.3, f32[1024,720]{0,1:T(8,128)S(1)} %fusion.58, f32[1024,720]{0,1:T(8,128)S(1)} %convolution_multiply_fusion, bf16[1024,2304]{1,0:T(8,128)(2,1)} %bitcast.55, ...), kind=kOutput, calls=%fused_computation.31 | convolution fusion | flops 3412316160 | bytes 21680128 | tf_op jit(solution)/shard_map/dot_general | solution.py:24
  338.1 7.0 fusion.59
  345.2 6.3 add_convert_fusion
  354.6 11.8 %collective-permute-done.27 = bf16[128,2304]{1,0:T(8,128)(2,1)S(1)} collective-permute-done((bf16[128,2304]{1,0:T(8,128)(2,1)S(1)}, bf16[128,2304]{1,0:T(8,128)(2,1)S(1)}, u32[]{:S(2)}, u32[]{:S(2)}) %collective-permute-start.27) | collective-permute-done | bytes 589856 | tf_op jit(solution)/shard_map/ppermute | solution.py:326
  367.9 13.8 %collective-permute-done.28 = bf16[128,2304]{1,0:T(8,128)(2,1)} collective-permute-done((bf16[128,2304]{1,0:T(8,128)(2,1)}, bf16[128,2304]{1,0:T(8,128)(2,1)}, u32[]{:S(2)}, u32[]{:S(2)}) %collective-permute-start.28) | collective-permute-done | bytes 589856 | tf_op jit(solution)/shard_map/ppermute | solution.py:326
  385.7 6.7 convolution_convert_fusion.4
  392.4 6.9 collective-permute-done.29
  403.3 4.2 convolution_convert_fusion.3
  417.7 6.3 all-to-all-start.2
  424.2 8.2 %convolution_convert_fusion.5 = bf16[720,2304]{1,0:T(8,128)(2,1)} fusion(bf16[1024,720]{0,1:T(8,128)(2,1)} %get-tuple-element.128, bf16[1024,2304]{1,0:T(8,128)(2,1)} %bitcast.55), kind=kOutput, calls=%fused_computation.16 | convolution fusion | flops 3399045120 | bytes 9510912 | tf_op jit(solution)/shard_map/dot_general | solution.py:24
  432.3 3.5 reshape_reshape.12
  440.0 3.5 fusion
  447.1 6.4 all-to-all-done.2
  454.7 13.5 %attend_back.1 = bf16[960,1024]{1,0:T(8,128)(2,1)S(1)} custom-call(bf16[960,1024]{1,0:T(8,128)(2,1)S(1)} %copy-done.12, bf16[320,1024]{1,0:T(8,128)(2,1)S(1)} %copy_bitcast_fusion.2.grad_ref, f32[1,1024]{1,0:T(1,128)S(1)} %bitcast.311, f32[32,1024]{1,0:T(8,128)S(1)} %get-tuple-element.221.cos_ref, f32[32,1024]{1,0:T(8,128)S(1)} %get-tuple-element.220.sin_ref, ...), custom_call_target="tpu_custom_call" | custom-call | flops 419430400 | bytes 4587520 | tf_op jit(solution)/shard_map/attend_back/pallas_call | solution.py:137
  469.8 5.5 fusion.60
  475.5 5.7 convolution_convert_fusion.2
  481.1 4.0 pad_maximum_fusion
  487.9 3.1 fusion.6
  491.0 6.0 all-to-all-start.3
  497.0 7.8 %convolution_convert_fusion.1 = bf16[1024,2304]{1,0:T(8,128)(2,1)S(1)} fusion(bf16[960,1024]{1,0:T(8,128)(2,1)S(1)} %copy-done.14, bf16[2304,960]{1,0:T(8,128)(2,1)} %bitcast.309), kind=kOutput, calls=%fused_computation.12 | convolution fusion | flops 4532207616 | bytes 11108352 | tf_op jit(solution)/shard_map/dot_general | solution.py:24
  507.0 4.7 constant_dynamic-slice_fusion.1
  517.1 23.2 %collective-permute-done.38 = bf16[128,2304]{1,0:T(8,128)(2,1)S(1)} collective-permute-done((bf16[128,2304]{1,0:T(8,128)(2,1)S(1)}, bf16[128,2304]{1,0:T(8,128)(2,1)S(1)}, u32[]{:S(2)}, u32[]{:S(2)}) %collective-permute-start.38) | collective-permute-done | bytes 589856 | tf_op jit(solution)/shard_map/ppermute | solution.py:329
  542.1 9.6 %collective-permute-start.37 = (bf16[128,2304]{1,0:T(8,128)(2,1)S(1)}, bf16[128,2304]{1,0:T(8,128)(2,1)S(1)}, u32[]{:S(2)}, u32[]{:S(2)}) collective-permute-start(bf16[128,2304]{1,0:T(8,128)(2,1)S(1)} %get-tuple-element.197), channel_id=1, source_target_pairs={{0,2},{2,4},{4,6},{6,7},{7,5},{5,3},{3,1},{1,0},{8,10},{10,12},{12... | collective-permute-start | bytes 1769480 | tf_op jit(solution)/shard_map/ppermute | solution.py:326
  552.5 11.3 %collective-permute-done.39 = bf16[128,2304]{1,0:T(8,128)(2,1)S(1)} collective-permute-done((bf16[128,2304]{1,0:T(8,128)(2,1)S(1)}, bf16[128,2304]{1,0:T(8,128)(2,1)S(1)}, u32[]{:S(2)}, u32[]{:S(2)}) %collective-permute-start.39) | collective-permute-done | bytes 589856 | tf_op jit(solution)/shard_map/ppermute | solution.py:329
  566.7 3.5 fusion.1
  571.9 7.3 collective-permute-done.40
  581.8 7.3 convolution_convert_fusion
  589.7 4.5 collective-permute-done.41
  604.3 5.2 all-to-all-start.4
  624.0 5.1 reshape.414
  634.0 16.5 %collective-permute-done.61.piece_ref = bf16[2,72,5760]{2,1,0:T(8,128)(2,1)} collective-permute-done((bf16[2,72,5760]{2,1,0:T(8,128)(2,1)}, bf16[2,72,5760]{2,1,0:T(8,128)(2,1)}, u32[]{:S(2)}, u32[]{:S(2)}) %collective-permute-start.61) | collective-permute-done | bytes 1658912 | tf_op jit(solution)/shard_map/ppermute | solution.py:335
  654.3 3.7 collective-permute-start.51
  675.9 4.7 finish.16
  680.6 4.8 finish.17
  687.7 8.5 %collective-permute-done.58.piece_ref = bf16[4,72,2304]{2,1,0:T(8,128)(2,1)} collective-permute-done((bf16[4,72,2304]{2,1,0:T(8,128)(2,1)}, bf16[4,72,2304]{2,1,0:T(8,128)(2,1)}, u32[]{:S(2)}, u32[]{:S(2)}) %collective-permute-start.58) | collective-permute-done | bytes 1327136 | tf_op jit(solution)/shard_map/ppermute | solution.py:335
  698.9 4.7 finish.22
  703.6 4.7 finish.23
  710.1 3.3 finish.18
  715.8 3.2 finish.19
  718.9 3.2 finish.20
  722.2 3.3 finish.21
  (364 shorter events, 220.1 us)
Async XLA Ops:
  7.2 259.6 %all-gather.3.cloned.1.call-start = ((), (), s32[]{:S(2)}) async-start(), calls=%async_computation.5 | async-start | bytes 10948608 | tf_op jit(solution)/shard_map/all_gather | solution.py:499
  9.7 26.9 %collective-permute-start.2 = (bf16[128,2304]{1,0:T(8,128)(2,1)}, bf16[128,2304]{1,0:T(8,128)(2,1)}, u32[]{:S(2)}, u32[]{:S(2)}) collective-permute-start(bf16[128,2304]{1,0:T(8,128)(2,1)} %param.15), channel_id=1, source_target_pairs={{2,0},{4,2},{6,4},{7,6},{5,7},{3,5},{1,3},{0,1},{10,8},{12,10},{14... | collective-permute-start | bytes 1769480 | tf_op jit(solution)/shard_map/ppermute | solution.py:329
  12.7 23.9 %collective-permute-start.1 = (bf16[128,2304]{1,0:T(8,128)(2,1)}, bf16[128,2304]{1,0:T(8,128)(2,1)}, u32[]{:S(2)}, u32[]{:S(2)}) collective-permute-start(bf16[128,2304]{1,0:T(8,128)(2,1)} %param.15), channel_id=1, source_target_pairs={{0,2},{2,4},{4,6},{6,7},{7,5},{5,3},{3,1},{1,0},{8,10},{10,12},{12... | collective-permute-start | bytes 1769480 | tf_op jit(solution)/shard_map/ppermute | solution.py:326
  19.5 57.0 %all-to-all-start = ((bf16[8,80,960]{2,1,0:T(8,128)(2,1)}), bf16[8,80,960]{2,1,0:T(8,128)(2,1)S(1)}, u32[]{:S(2)}, u32[]{:S(2)}) async-start(bf16[8,80,960]{2,1,0:T(8,128)(2,1)} %prepare_qkv.1), calls=%async_computation | async-start | bytes 2621440 | tf_op jit(solution)/shard_map/all_to_all | solution.py:389
  77.6 39.1 %collective-permute-start = (bf16[8,72,960]{2,1,0:T(8,128)(2,1)}, bf16[8,72,960]{2,1,0:T(8,128)(2,1)}, u32[]{:S(2)}, u32[]{:S(2)}) collective-permute-start(bf16[8,72,960]{2,1,0:T(8,128)(2,1)} %slice.176), channel_id=1, source_target_pairs={{0,8},{8,0},{16,24},{24,16},{1,9},{9,1},{17,25},{25,17},{2,10},{10... | collective-permute-start | bytes 3317768 | tf_op jit(solution)/shard_map/ppermute | solution.py:332
  77.6 69.6 %collective-permute-start.8 = (bf16[8,72,960]{2,1,0:T(8,128)(2,1)}, bf16[8,72,960]{2,1,0:T(8,128)(2,1)S(1)}, u32[]{:S(2)}, u32[]{:S(2)}) collective-permute-start(bf16[8,72,960]{2,1,0:T(8,128)(2,1)} %slice.176), channel_id=1, source_target_pairs={{0,16},{8,24},{16,0},{24,8},{1,17},{9,25},{17,1},{25,9},{2,18},{10... | collective-permute-start | bytes 3317768 | tf_op jit(solution)/shard_map/ppermute | solution.py:335
  79.4 29.2 %collective-permute-start.3 = (bf16[128,2304]{1,0:T(8,128)(2,1)}, bf16[128,2304]{1,0:T(8,128)(2,1)S(1)}, u32[]{:S(2)}, u32[]{:S(2)}) collective-permute-start(bf16[128,2304]{1,0:T(8,128)(2,1)} %collective-permute-done.1), channel_id=1, source_target_pairs={{0,2},{2,4},{4,6},{6,7},{7,5},{5,3},{3,1},{1,0},{8,10},{10,12},{12... | collective-permute-start | bytes 1769480 | tf_op jit(solution)/shard_map/ppermute | solution.py:326
  79.8 32.0 %collective-permute-start.4 = (bf16[128,2304]{1,0:T(8,128)(2,1)}, bf16[128,2304]{1,0:T(8,128)(2,1)S(1)}, u32[]{:S(2)}, u32[]{:S(2)}) collective-permute-start(bf16[128,2304]{1,0:T(8,128)(2,1)} %collective-permute-done.2), channel_id=1, source_target_pairs={{2,0},{4,2},{6,4},{7,6},{5,7},{3,5},{1,3},{0,1},{10,8},{12,10},{14... | collective-permute-start | bytes 1769480 | tf_op jit(solution)/shard_map/ppermute | solution.py:329
  111.8 20.1 %collective-permute-start.5 = (bf16[128,2304]{1,0:T(8,128)(2,1)S(1)}, bf16[128,2304]{1,0:T(8,128)(2,1)S(1)}, u32[]{:S(2)}, u32[]{:S(2)}) collective-permute-start(bf16[128,2304]{1,0:T(8,128)(2,1)S(1)} %collective-permute-done.3), channel_id=1, source_target_pairs={{0,2},{2,4},{4,6},{6,7},{7,5},{5,3},{3,1},{1,0},{8,10},{10,12},{12... | collective-permute-start | bytes 1769480 | tf_op jit(solution)/shard_map/ppermute | solution.py:326
  112.7 26.1 %collective-permute-start.6 = (bf16[128,2304]{1,0:T(8,128)(2,1)S(1)}, bf16[128,2304]{1,0:T(8,128)(2,1)S(1)}, u32[]{:S(2)}, u32[]{:S(2)}) collective-permute-start(bf16[128,2304]{1,0:T(8,128)(2,1)S(1)} %collective-permute-done.4), channel_id=1, source_target_pairs={{2,0},{4,2},{6,4},{7,6},{5,7},{3,5},{1,3},{0,1},{10,8},{12,10},{14... | collective-permute-start | bytes 1769480 | tf_op jit(solution)/shard_map/ppermute | solution.py:329
  138.8 19.3 %collective-permute-start.7 = (bf16[128,2304]{1,0:T(8,128)(2,1)S(1)}, bf16[128,2304]{1,0:T(8,128)(2,1)}, u32[]{:S(2)}, u32[]{:S(2)}) collective-permute-start(bf16[128,2304]{1,0:T(8,128)(2,1)S(1)} %collective-permute-done.5), channel_id=1, source_target_pairs={{0,2},{2,4},{4,6},{6,7},{7,5},{5,3},{3,1},{1,0},{8,10},{10,12},{12... | collective-permute-start | bytes 1769480 | tf_op jit(solution)/shard_map/ppermute | solution.py:326
  139.3 69.9 %all-to-all-start.1 = ((bf16[8,144,720]{2,1,0:T(8,128)(2,1)}), bf16[8,144,720]{2,1,0:T(8,128)(2,1)}, u32[]{:S(2)}, u32[]{:S(2)}) async-start(bf16[8,144,720]{2,1,0:T(8,128)(2,1)} %prepare_ffn.1), calls=%async_computation.1 | async-start | bytes 3538944 | tf_op jit(solution)/shard_map/all_to_all | solution.py:389
  177.4 20.5 %collective-permute-start.11 = (bf16[320,1024]{1,0:T(8,128)(2,1)S(1)}, bf16[320,1024]{1,0:T(8,128)(2,1)}, u32[]{:S(2)}, u32[]{:S(2)}) collective-permute-start(bf16[320,1024]{1,0:T(8,128)(2,1)S(1)} %get-tuple-element.109), channel_id=1, source_target_pairs={{2,0},{4,2},{6,4},{7,6},{5,7},{3,5},{1,3},{0,1},{10,8},{12,10},{14... | collective-permute-start | bytes 1966088 | tf_op jit(solution)/shard_map/ppermute | solution.py:329
  179.7 18.2 %collective-permute-start.10 = (bf16[320,1024]{1,0:T(8,128)(2,1)S(1)}, bf16[320,1024]{1,0:T(8,128)(2,1)}, u32[]{:S(2)}, u32[]{:S(2)}) collective-permute-start(bf16[320,1024]{1,0:T(8,128)(2,1)S(1)} %get-tuple-element.109), channel_id=1, source_target_pairs={{0,2},{2,4},{4,6},{6,7},{7,5},{5,3},{3,1},{1,0},{8,10},{10,12},{12... | collective-permute-start | bytes 1966088 | tf_op jit(solution)/shard_map/ppermute | solution.py:326
  198.0 18.6 %collective-permute-start.13 = (bf16[320,1024]{1,0:T(8,128)(2,1)}, bf16[320,1024]{1,0:T(8,128)(2,1)S(1)}, u32[]{:S(2)}, u32[]{:S(2)}) collective-permute-start(bf16[320,1024]{1,0:T(8,128)(2,1)} %collective-permute-done.11), channel_id=1, source_target_pairs={{2,0},{4,2},{6,4},{7,6},{5,7},{3,5},{1,3},{0,1},{10,8},{12,10},{14... | collective-permute-start | bytes 1966088 | tf_op jit(solution)/shard_map/ppermute | solution.py:329
  202.3 16.4 %collective-permute-start.12 = (bf16[320,1024]{1,0:T(8,128)(2,1)}, bf16[320,1024]{1,0:T(8,128)(2,1)}, u32[]{:S(2)}, u32[]{:S(2)}) collective-permute-start(bf16[320,1024]{1,0:T(8,128)(2,1)} %collective-permute-done.10), channel_id=1, source_target_pairs={{0,2},{2,4},{4,6},{6,7},{7,5},{5,3},{3,1},{1,0},{8,10},{10,12},{12... | collective-permute-start | bytes 1966088 | tf_op jit(solution)/shard_map/ppermute | solution.py:326
  209.2 44.9 %collective-permute-start.18 = (bf16[8,144,720]{2,1,0:T(8,128)(2,1)}, bf16[8,144,720]{2,1,0:T(8,128)(2,1)S(1)}, u32[]{:S(2)}, u32[]{:S(2)}) collective-permute-start(bf16[8,144,720]{2,1,0:T(8,128)(2,1)} %all-to-all-done.1), channel_id=1, source_target_pairs={{0,16},{8,24},{16,0},{24,8},{1,17},{9,25},{17,1},{25,9},{2,18},{10... | collective-permute-start | bytes 4976648 | tf_op jit(solution)/shard_map/ppermute | solution.py:335
  209.7 44.4 %collective-permute-start.17 = (bf16[8,144,720]{2,1,0:T(8,128)(2,1)}, bf16[8,144,720]{2,1,0:T(8,128)(2,1)S(1)}, u32[]{:S(2)}, u32[]{:S(2)}) collective-permute-start(bf16[8,144,720]{2,1,0:T(8,128)(2,1)} %all-to-all-done.1), channel_id=1, source_target_pairs={{0,8},{8,0},{16,24},{24,16},{1,9},{9,1},{17,25},{25,17},{2,10},{10... | collective-permute-start | bytes 4976648 | tf_op jit(solution)/shard_map/ppermute | solution.py:332
  218.7 14.5 %collective-permute-start.15 = (bf16[320,1024]{1,0:T(8,128)(2,1)S(1)}, bf16[320,1024]{1,0:T(8,128)(2,1)S(1)}, u32[]{:S(2)}, u32[]{:S(2)}) collective-permute-start(bf16[320,1024]{1,0:T(8,128)(2,1)S(1)} %collective-permute-done.13), channel_id=1, source_target_pairs={{2,0},{4,2},{6,4},{7,6},{5,7},{3,5},{1,3},{0,1},{10,8},{12,10},{14... | collective-permute-start | bytes 1966088 | tf_op jit(solution)/shard_map/ppermute | solution.py:329
  219.8 14.6 %collective-permute-start.14 = (bf16[320,1024]{1,0:T(8,128)(2,1)}, bf16[320,1024]{1,0:T(8,128)(2,1)S(1)}, u32[]{:S(2)}, u32[]{:S(2)}) collective-permute-start(bf16[320,1024]{1,0:T(8,128)(2,1)} %collective-permute-done.12), channel_id=1, source_target_pairs={{0,2},{2,4},{4,6},{6,7},{7,5},{5,3},{3,1},{1,0},{8,10},{10,12},{12... | collective-permute-start | bytes 1966088 | tf_op jit(solution)/shard_map/ppermute | solution.py:326
  234.4 16.2 %collective-permute-start.16 = (bf16[320,1024]{1,0:T(8,128)(2,1)S(1)}, bf16[320,1024]{1,0:T(8,128)(2,1)S(1)}, u32[]{:S(2)}, u32[]{:S(2)}) collective-permute-start(bf16[320,1024]{1,0:T(8,128)(2,1)S(1)} %collective-permute-done.14), channel_id=1, source_target_pairs={{0,2},{2,4},{4,6},{6,7},{7,5},{5,3},{3,1},{1,0},{8,10},{10,12},{12... | collective-permute-start | bytes 1966088 | tf_op jit(solution)/shard_map/ppermute | solution.py:326
  250.6 12.7 %collective-permute-start.20 = (bf16[128,2304]{1,0:T(8,128)(2,1)S(1)}, bf16[128,2304]{1,0:T(8,128)(2,1)S(1)}, u32[]{:S(2)}, u32[]{:S(2)}) collective-permute-start(bf16[128,2304]{1,0:T(8,128)(2,1)S(1)} %copy-done.36), channel_id=1, source_target_pairs={{2,0},{4,2},{6,4},{7,6},{5,7},{3,5},{1,3},{0,1},{10,8},{12,10},{14... | collective-permute-start | bytes 1769480 | tf_op jit(solution)/shard_map/ppermute | solution.py:329
  252.3 12.1 %collective-permute-start.21 = (bf16[128,2304]{1,0:T(8,128)(2,1)S(1)}, bf16[128,2304]{1,0:T(8,128)(2,1)S(1)}, u32[]{:S(2)}, u32[]{:S(2)}) collective-permute-start(bf16[128,2304]{1,0:T(8,128)(2,1)S(1)} %copy-done.36), channel_id=1, source_target_pairs={{0,2},{2,4},{4,6},{6,7},{7,5},{5,3},{3,1},{1,0},{8,10},{10,12},{12... | collective-permute-start | bytes 1769480 | tf_op jit(solution)/shard_map/ppermute | solution.py:326
  289.4 15.0 %collective-permute-start.22 = (bf16[128,2304]{1,0:T(8,128)(2,1)S(1)}, bf16[128,2304]{1,0:T(8,128)(2,1)S(1)}, u32[]{:S(2)}, u32[]{:S(2)}) collective-permute-start(bf16[128,2304]{1,0:T(8,128)(2,1)S(1)} %copy-done.38), channel_id=1, source_target_pairs={{2,0},{4,2},{6,4},{7,6},{5,7},{3,5},{1,3},{0,1},{10,8},{12,10},{14... | collective-permute-start | bytes 1769480 | tf_op jit(solution)/shard_map/ppermute | solution.py:329
  290.7 13.7 %collective-permute-start.23 = (bf16[128,2304]{1,0:T(8,128)(2,1)}, bf16[128,2304]{1,0:T(8,128)(2,1)S(1)}, u32[]{:S(2)}, u32[]{:S(2)}) collective-permute-start(bf16[128,2304]{1,0:T(8,128)(2,1)} %copy-done.39), channel_id=1, source_target_pairs={{0,2},{2,4},{4,6},{6,7},{7,5},{5,3},{3,1},{1,0},{8,10},{10,12},{12... | collective-permute-start | bytes 1769480 | tf_op jit(solution)/shard_map/ppermute | solution.py:326
  304.4 15.6 %collective-permute-start.24 = (bf16[128,2304]{1,0:T(8,128)(2,1)S(1)}, bf16[128,2304]{1,0:T(8,128)(2,1)S(1)}, u32[]{:S(2)}, u32[]{:S(2)}) collective-permute-start(bf16[128,2304]{1,0:T(8,128)(2,1)S(1)} %collective-permute-done.22), channel_id=1, source_target_pairs={{2,0},{4,2},{6,4},{7,6},{5,7},{3,5},{1,3},{0,1},{10,8},{12,10},{14... | collective-permute-start | bytes 1769480 | tf_op jit(solution)/shard_map/ppermute | solution.py:329
  305.6 13.5 %collective-permute-start.25 = (bf16[128,2304]{1,0:T(8,128)(2,1)S(1)}, bf16[128,2304]{1,0:T(8,128)(2,1)S(1)}, u32[]{:S(2)}, u32[]{:S(2)}) collective-permute-start(bf16[128,2304]{1,0:T(8,128)(2,1)S(1)} %collective-permute-done.23), channel_id=1, source_target_pairs={{0,2},{2,4},{4,6},{6,7},{7,5},{5,3},{3,1},{1,0},{8,10},{10,12},{12... | collective-permute-start | bytes 1769480 | tf_op jit(solution)/shard_map/ppermute | solution.py:326
  352.6 13.8 %collective-permute-start.27 = (bf16[128,2304]{1,0:T(8,128)(2,1)S(1)}, bf16[128,2304]{1,0:T(8,128)(2,1)S(1)}, u32[]{:S(2)}, u32[]{:S(2)}) collective-permute-start(bf16[128,2304]{1,0:T(8,128)(2,1)S(1)} %get-tuple-element.204), channel_id=1, source_target_pairs={{0,2},{2,4},{4,6},{6,7},{7,5},{5,3},{3,1},{1,0},{8,10},{10,12},{12... | collective-permute-start | bytes 1769480 | tf_op jit(solution)/shard_map/ppermute | solution.py:326
  353.5 14.5 %collective-permute-start.31 = (bf16[128,2304]{1,0:T(8,128)(2,1)}, bf16[128,2304]{1,0:T(8,128)(2,1)S(1)}, u32[]{:S(2)}, u32[]{:S(2)}) collective-permute-start(bf16[128,2304]{1,0:T(8,128)(2,1)} %get-tuple-element.205), channel_id=1, source_target_pairs={{2,0},{4,2},{6,4},{7,6},{5,7},{3,5},{1,3},{0,1},{10,8},{12,10},{14... | collective-permute-start | bytes 1769480 | tf_op jit(solution)/shard_map/ppermute | solution.py:329
  367.4 14.4 %collective-permute-start.28 = (bf16[128,2304]{1,0:T(8,128)(2,1)}, bf16[128,2304]{1,0:T(8,128)(2,1)}, u32[]{:S(2)}, u32[]{:S(2)}) collective-permute-start(bf16[128,2304]{1,0:T(8,128)(2,1)} %fusion.38), channel_id=1, source_target_pairs={{0,2},{2,4},{4,6},{6,7},{7,5},{5,3},{3,1},{1,0},{8,10},{10,12},{12... | collective-permute-start | bytes 1769480 | tf_op jit(solution)/shard_map/ppermute | solution.py:326
  383.6 15.7 %collective-permute-start.29 = (bf16[128,2304]{1,0:T(8,128)(2,1)S(1)}, bf16[128,2304]{1,0:T(8,128)(2,1)S(1)}, u32[]{:S(2)}, u32[]{:S(2)}) collective-permute-start(bf16[128,2304]{1,0:T(8,128)(2,1)S(1)} %get-tuple-element.202), channel_id=1, source_target_pairs={{0,2},{2,4},{4,6},{6,7},{7,5},{5,3},{3,1},{1,0},{8,10},{10,12},{12... | collective-permute-start | bytes 1769480 | tf_op jit(solution)/shard_map/ppermute | solution.py:326
  383.7 15.6 %collective-permute-start.32 = (bf16[128,2304]{1,0:T(8,128)(2,1)S(1)}, bf16[128,2304]{1,0:T(8,128)(2,1)S(1)}, u32[]{:S(2)}, u32[]{:S(2)}) collective-permute-start(bf16[128,2304]{1,0:T(8,128)(2,1)S(1)} %get-tuple-element.203), channel_id=1, source_target_pairs={{2,0},{4,2},{6,4},{7,6},{5,7},{3,5},{1,3},{0,1},{10,8},{12,10},{14... | collective-permute-start | bytes 1769480 | tf_op jit(solution)/shard_map/ppermute | solution.py:329
  410.7 29.3 %collective-permute-start.34 = (bf16[8,2,144,720]{3,2,1,0:T(8,128)(2,1)}, bf16[8,2,144,720]{3,2,1,0:T(8,128)(2,1)}, u32[]{:S(2)}, u32[]{:S(2)}) collective-permute-start(bf16[8,2,144,720]{3,2,1,0:T(8,128)(2,1)} %fusion.3), channel_id=1, source_target_pairs={{0,8},{8,0},{16,24},{24,16},{1,9},{9,1},{17,25},{25,17},{2,10},{10... | collective-permute-start | bytes 9953288 | tf_op jit(solution)/shard_map/ppermute | solution.py:332
  417.7 35.8 %all-to-all-start.2 = ((bf16[8,608,128]{2,1,0:T(8,128)(2,1)}), bf16[8,608,128]{2,1,0:T(8,128)(2,1)}, u32[]{:S(2)}, u32[]{:S(2)}) async-start(bf16[8,608,128]{2,1,0:T(8,128)(2,1)} %pad_maximum_fusion.2), calls=%async_computation.2 | async-start | bytes 2490368 | tf_op jit(solution)/shard_map/all_to_all | solution.py:389
  440.0 73.6 %collective-permute-start.45 = (bf16[1,2,180,2304]{3,1,2,0:T(2,128)(2,1)}, bf16[1,2,180,2304]{3,1,2,0:T(2,128)(2,1)}, u32[]{:S(2)}, u32[]{:S(2)}) collective-permute-start(bf16[1,2,180,2304]{3,1,2,0:T(2,128)(2,1)} %copy.281), channel_id=1, source_target_pairs={{0,8},{8,0},{16,24},{24,16},{1,9},{9,1},{17,25},{25,17},{2,10},{10... | collective-permute-start | bytes 4976648 | tf_op jit(solution)/shard_map/ppermute | solution.py:332
  446.6 41.3 %collective-permute-start.35 = (bf16[8,144,720]{2,1,0:T(8,128)(2,1)}, bf16[8,144,720]{2,1,0:T(8,128)(2,1)}, u32[]{:S(2)}, u32[]{:S(2)}) collective-permute-start(bf16[8,144,720]{2,1,0:T(8,128)(2,1)} %dynamic-slice_bitcast_fusion), channel_id=1, source_target_pairs={{0,16},{8,24},{16,0},{24,8},{1,17},{9,25},{17,1},{25,9},{2,18},{10... | collective-permute-start | bytes 4976648 | tf_op jit(solution)/shard_map/ppermute | solution.py:335
  491.0 74.7 %all-to-all-start.3 = ((bf16[8,144,720]{2,1,0:T(8,128)(2,1)}), bf16[8,144,720]{2,1,0:T(8,128)(2,1)}, u32[]{:S(2)}, u32[]{:S(2)}) async-start(bf16[8,144,720]{2,1,0:T(8,128)(2,1)} %fusion.6), calls=%async_computation.3 | async-start | bytes 3538944 | tf_op jit(solution)/shard_map/all_to_all | solution.py:389
  504.9 35.4 %collective-permute-start.38 = (bf16[128,2304]{1,0:T(8,128)(2,1)S(1)}, bf16[128,2304]{1,0:T(8,128)(2,1)S(1)}, u32[]{:S(2)}, u32[]{:S(2)}) collective-permute-start(bf16[128,2304]{1,0:T(8,128)(2,1)S(1)} %get-tuple-element.198), channel_id=1, source_target_pairs={{2,0},{4,2},{6,4},{7,6},{5,7},{3,5},{1,3},{0,1},{10,8},{12,10},{14... | collective-permute-start | bytes 1769480 | tf_op jit(solution)/shard_map/ppermute | solution.py:329
  507.0 33.3 %collective-permute-start.36 = (bf16[128,2304]{1,0:T(8,128)(2,1)S(1)}, bf16[128,2304]{1,0:T(8,128)(2,1)S(1)}, u32[]{:S(2)}, u32[]{:S(2)}) collective-permute-start(bf16[128,2304]{1,0:T(8,128)(2,1)S(1)} %get-tuple-element.199), channel_id=1, source_target_pairs={{0,2},{2,4},{4,6},{6,7},{7,5},{5,3},{3,1},{1,0},{8,10},{10,12},{12... | collective-permute-start | bytes 1769480 | tf_op jit(solution)/shard_map/ppermute | solution.py:326
  513.5 53.2 %collective-permute-start.56 = (bf16[8,2,72,1248]{3,2,0,1:T(8,128)(2,1)}, bf16[8,2,72,1248]{3,2,0,1:T(8,128)(2,1)}, u32[]{:S(2)}, u32[]{:S(2)}) collective-permute-start(bf16[8,2,72,1248]{3,2,0,1:T(8,128)(2,1)} %bitcast.301), channel_id=1, source_target_pairs={{0,8},{8,0},{16,24},{24,16},{1,9},{9,1},{17,25},{25,17},{2,10},{10... | collective-permute-start | bytes 8626184 | tf_op jit(solution)/shard_map/ppermute | solution.py:332
  516.6 35.2 %collective-permute-start.46 = (bf16[1,180,2304]{2,1,0:T(8,128)(2,1)S(1)}, bf16[1,180,2304]{2,1,0:T(8,128)(2,1)S(1)}, u32[]{:S(2)}, u32[]{:S(2)}) collective-permute-start(bf16[1,180,2304]{2,1,0:T(8,128)(2,1)S(1)} %dynamic-slice_bitcast_fusion.3), channel_id=1, source_target_pairs={{0,16},{8,24},{16,0},{24,8},{1,17},{9,25},{17,1},{25,9},{2,18},{10... | collective-permute-start | bytes 2488328 | tf_op jit(solution)/shard_map/ppermute | solution.py:335
  540.6 23.2 %collective-permute-start.39 = (bf16[128,2304]{1,0:T(8,128)(2,1)S(1)}, bf16[128,2304]{1,0:T(8,128)(2,1)S(1)}, u32[]{:S(2)}, u32[]{:S(2)}) collective-permute-start(bf16[128,2304]{1,0:T(8,128)(2,1)S(1)} %get-tuple-element.196), channel_id=1, source_target_pairs={{2,0},{4,2},{6,4},{7,6},{5,7},{3,5},{1,3},{0,1},{10,8},{12,10},{14... | collective-permute-start | bytes 1769480 | tf_op jit(solution)/shard_map/ppermute | solution.py:329
  542.1 23.2 %collective-permute-start.37 = (bf16[128,2304]{1,0:T(8,128)(2,1)S(1)}, bf16[128,2304]{1,0:T(8,128)(2,1)S(1)}, u32[]{:S(2)}, u32[]{:S(2)}) collective-permute-start(bf16[128,2304]{1,0:T(8,128)(2,1)S(1)} %get-tuple-element.197), channel_id=1, source_target_pairs={{0,2},{2,4},{4,6},{6,7},{7,5},{5,3},{3,1},{1,0},{8,10},{10,12},{12... | collective-permute-start | bytes 1769480 | tf_op jit(solution)/shard_map/ppermute | solution.py:326
  552.0 37.3 %collective-permute-start.47 = (bf16[1,180,2304]{2,1,0:T(8,128)(2,1)S(1)}, bf16[1,180,2304]{2,1,0:T(8,128)(2,1)}, u32[]{:S(2)}, u32[]{:S(2)}) collective-permute-start(bf16[1,180,2304]{2,1,0:T(8,128)(2,1)S(1)} %fusion.10.piece_ref), channel_id=1, source_target_pairs={{0,16},{8,24},{16,0},{24,8},{1,17},{9,25},{17,1},{25,9},{2,18},{10... | collective-permute-start | bytes 2488328 | tf_op jit(solution)/shard_map/ppermute | solution.py:335
  565.7 13.5 %collective-permute-start.40 = (bf16[128,2304]{1,0:T(8,128)(2,1)S(1)}, bf16[128,2304]{1,0:T(8,128)(2,1)S(1)}, u32[]{:S(2)}, u32[]{:S(2)}) collective-permute-start(bf16[128,2304]{1,0:T(8,128)(2,1)S(1)} %get-tuple-element.136), channel_id=1, source_target_pairs={{0,2},{2,4},{4,6},{6,7},{7,5},{5,3},{3,1},{1,0},{8,10},{10,12},{12... | collective-permute-start | bytes 1769480 | tf_op jit(solution)/shard_map/ppermute | solution.py:326
  570.3 32.6 %collective-permute-start.57 = (bf16[8,72,1248]{2,1,0:T(8,128)(2,1)S(1)}, bf16[8,72,1248]{2,1,0:T(8,128)(2,1)S(1)}, u32[]{:S(2)}, u32[]{:S(2)}) collective-permute-start(bf16[8,72,1248]{2,1,0:T(8,128)(2,1)S(1)} %dynamic-slice_bitcast_fusion.2), channel_id=1, source_target_pairs={{0,16},{8,24},{16,0},{24,8},{1,17},{9,25},{17,1},{25,9},{2,18},{10... | collective-permute-start | bytes 4313096 | tf_op jit(solution)/shard_map/ppermute | solution.py:335
  570.8 18.9 %collective-permute-start.42 = (bf16[128,2304]{1,0:T(8,128)(2,1)S(1)}, bf16[128,2304]{1,0:T(8,128)(2,1)S(1)}, u32[]{:S(2)}, u32[]{:S(2)}) collective-permute-start(bf16[128,2304]{1,0:T(8,128)(2,1)S(1)} %get-tuple-element.137), channel_id=1, source_target_pairs={{2,0},{4,2},{6,4},{7,6},{5,7},{3,5},{1,3},{0,1},{10,8},{12,10},{14... | collective-permute-start | bytes 1769480 | tf_op jit(solution)/shard_map/ppermute | solution.py:329
  580.5 13.7 %collective-permute-start.41 = (bf16[128,2304]{1,0:T(8,128)(2,1)S(1)}, bf16[128,2304]{1,0:T(8,128)(2,1)S(1)}, u32[]{:S(2)}, u32[]{:S(2)}) collective-permute-start(bf16[128,2304]{1,0:T(8,128)(2,1)S(1)} %fusion.29), channel_id=1, source_target_pairs={{0,2},{2,4},{4,6},{6,7},{7,5},{5,3},{3,1},{1,0},{8,10},{10,12},{12... | collective-permute-start | bytes 1769480 | tf_op jit(solution)/shard_map/ppermute | solution.py:326
  589.2 28.0 %collective-permute-start.49 = (bf16[1,180,2304]{2,1,0:T(8,128)(2,1)S(1)}, bf16[1,180,2304]{2,1,0:T(8,128)(2,1)}, u32[]{:S(2)}, u32[]{:S(2)}) collective-permute-start(bf16[1,180,2304]{2,1,0:T(8,128)(2,1)S(1)} %fusion.10.piece_ref), channel_id=1, source_target_pairs={{0,8},{8,0},{16,24},{24,16},{1,9},{9,1},{17,25},{25,17},{2,10},{10... | collective-permute-start | bytes 2488328 | tf_op jit(solution)/shard_map/ppermute | solution.py:332
  589.2 32.5 %collective-permute-start.48 = (bf16[1,180,2304]{2,1,0:T(8,128)(2,1)}, bf16[1,180,2304]{2,1,0:T(8,128)(2,1)}, u32[]{:S(2)}, u32[]{:S(2)}) collective-permute-start(bf16[1,180,2304]{2,1,0:T(8,128)(2,1)} %collective-permute-done.47.piece_ref), channel_id=1, source_target_pairs={{0,8},{8,0},{16,24},{24,16},{1,9},{9,1},{17,25},{25,17},{2,10},{10... | collective-permute-start | bytes 2488328 | tf_op jit(solution)/shard_map/ppermute | solution.py:332
  597.8 31.4 %collective-permute-start.44 = (bf16[128,2304]{1,0:T(8,128)(2,1)}, bf16[128,2304]{1,0:T(8,128)(2,1)}, u32[]{:S(2)}, u32[]{:S(2)}) collective-permute-start(bf16[128,2304]{1,0:T(8,128)(2,1)} %get-tuple-element.192), channel_id=1, source_target_pairs={{2,0},{4,2},{6,4},{7,6},{5,7},{3,5},{1,3},{0,1},{10,8},{12,10},{14... | collective-permute-start | bytes 1769480 | tf_op jit(solution)/shard_map/ppermute | solution.py:329
  599.7 29.5 %collective-permute-start.43 = (bf16[128,2304]{1,0:T(8,128)(2,1)}, bf16[128,2304]{1,0:T(8,128)(2,1)}, u32[]{:S(2)}, u32[]{:S(2)}) collective-permute-start(bf16[128,2304]{1,0:T(8,128)(2,1)} %get-tuple-element.193), channel_id=1, source_target_pairs={{0,2},{2,4},{4,6},{6,7},{7,5},{5,3},{3,1},{1,0},{8,10},{10,12},{12... | collective-permute-start | bytes 1769480 | tf_op jit(solution)/shard_map/ppermute | solution.py:326
  604.3 53.6 %all-to-all-start.4 = ((bf16[8,72,1248]{2,1,0:T(8,128)(2,1)}), bf16[8,72,1248]{2,1,0:T(8,128)(2,1)}, u32[]{:S(2)}, u32[]{:S(2)}) async-start(bf16[8,72,1248]{2,1,0:T(8,128)(2,1)} %fusion.8), calls=%async_computation.4 | async-start | bytes 2949120 | tf_op jit(solution)/shard_map/all_to_all | solution.py:389
  614.4 36.2 %collective-permute-start.61 = (bf16[2,72,5760]{2,1,0:T(8,128)(2,1)}, bf16[2,72,5760]{2,1,0:T(8,128)(2,1)}, u32[]{:S(2)}, u32[]{:S(2)}) collective-permute-start(bf16[2,72,5760]{2,1,0:T(8,128)(2,1)} %reshape.416.piece_ref), channel_id=1, source_target_pairs={{0,16},{8,24},{16,0},{24,8},{1,17},{9,25},{17,1},{25,9},{2,18},{10... | collective-permute-start | bytes 4976648 | tf_op jit(solution)/shard_map/ppermute | solution.py:335
  632.0 20.3 %collective-permute-start.50 = (bf16[128,2304]{1,0:T(8,128)(2,1)S(1)}, bf16[128,2304]{1,0:T(8,128)(2,1)S(1)}, u32[]{:S(2)}, u32[]{:S(2)}) collective-permute-start(bf16[128,2304]{1,0:T(8,128)(2,1)S(1)} %get-tuple-element.139), channel_id=1, source_target_pairs={{0,2},{2,4},{4,6},{6,7},{7,5},{5,3},{3,1},{1,0},{8,10},{10,12},{12... | collective-permute-start | bytes 1769480 | tf_op jit(solution)/shard_map/ppermute | solution.py:326
  634.0 46.6 %collective-permute-start.54 = (bf16[2,72,5760]{2,1,0:T(8,128)(2,1)S(1)}, bf16[2,72,5760]{2,1,0:T(8,128)(2,1)}, u32[]{:S(2)}, u32[]{:S(2)}) collective-permute-start(bf16[2,72,5760]{2,1,0:T(8,128)(2,1)S(1)} %copy-done.26), channel_id=1, source_target_pairs={{0,8},{8,0},{16,24},{24,16},{1,9},{9,1},{17,25},{25,17},{2,10},{10... | collective-permute-start | bytes 4976648 | tf_op jit(solution)/shard_map/ppermute | solution.py:332
  650.5 53.1 %collective-permute-start.62 = (bf16[2,72,5760]{2,1,0:T(8,128)(2,1)}, bf16[2,72,5760]{2,1,0:T(8,128)(2,1)}, u32[]{:S(2)}, u32[]{:S(2)}) collective-permute-start(bf16[2,72,5760]{2,1,0:T(8,128)(2,1)} %collective-permute-done.61.piece_ref), channel_id=1, source_target_pairs={{0,8},{8,0},{16,24},{24,16},{1,9},{9,1},{17,25},{25,17},{2,10},{10... | collective-permute-start | bytes 4976648 | tf_op jit(solution)/shard_map/ppermute | solution.py:332
  650.5 17.0 %collective-permute-start.52 = (bf16[128,2304]{1,0:T(8,128)(2,1)}, bf16[128,2304]{1,0:T(8,128)(2,1)}, u32[]{:S(2)}, u32[]{:S(2)}) collective-permute-start(bf16[128,2304]{1,0:T(8,128)(2,1)} %get-tuple-element.140), channel_id=1, source_target_pairs={{2,0},{4,2},{6,4},{7,6},{5,7},{3,5},{1,3},{0,1},{10,8},{12,10},{14... | collective-permute-start | bytes 1769480 | tf_op jit(solution)/shard_map/ppermute | solution.py:329
  654.3 15.8 %collective-permute-start.51 = (bf16[128,2304]{1,0:T(8,128)(2,1)}, bf16[128,2304]{1,0:T(8,128)(2,1)}, u32[]{:S(2)}, u32[]{:S(2)}) collective-permute-start(bf16[128,2304]{1,0:T(8,128)(2,1)} %fusion.26), channel_id=1, source_target_pairs={{0,2},{2,4},{4,6},{6,7},{7,5},{5,3},{3,1},{1,0},{8,10},{10,12},{12... | collective-permute-start | bytes 1769480 | tf_op jit(solution)/shard_map/ppermute | solution.py:326
  667.1 29.1 %collective-permute-start.58 = (bf16[4,72,2304]{2,1,0:T(8,128)(2,1)}, bf16[4,72,2304]{2,1,0:T(8,128)(2,1)}, u32[]{:S(2)}, u32[]{:S(2)}) collective-permute-start(bf16[4,72,2304]{2,1,0:T(8,128)(2,1)} %pad_maximum_fusion.1.piece_ref), channel_id=1, source_target_pairs={{0,16},{8,24},{16,0},{24,8},{1,17},{9,25},{17,1},{25,9},{2,18},{10... | collective-permute-start | bytes 3981320 | tf_op jit(solution)/shard_map/ppermute | solution.py:335
  672.7 15.0 %collective-permute-start.53 = (bf16[128,2304]{1,0:T(8,128)(2,1)}, bf16[128,2304]{1,0:T(8,128)(2,1)}, u32[]{:S(2)}, u32[]{:S(2)}) collective-permute-start(bf16[128,2304]{1,0:T(8,128)(2,1)} %get-tuple-element.188), channel_id=1, source_target_pairs={{2,0},{4,2},{6,4},{7,6},{5,7},{3,5},{1,3},{0,1},{10,8},{12,10},{14... | collective-permute-start | bytes 1769480 | tf_op jit(solution)/shard_map/ppermute | solution.py:329
  687.7 25.7 %collective-permute-start.55 = (bf16[128,2304]{1,0:T(8,128)(2,1)S(1)}, bf16[128,2304]{1,0:T(8,128)(2,1)S(1)}, u32[]{:S(2)}, u32[]{:S(2)}) collective-permute-start(bf16[128,2304]{1,0:T(8,128)(2,1)S(1)} %get-tuple-element.147), channel_id=1, source_target_pairs={{0,2},{2,4},{4,6},{6,7},{7,5},{5,3},{3,1},{1,0},{8,10},{10,12},{12... | collective-permute-start | bytes 1769480 | tf_op jit(solution)/shard_map/ppermute | solution.py:326
  687.7 28.1 %collective-permute-start.60 = (bf16[4,72,2304]{2,1,0:T(8,128)(2,1)}, bf16[4,72,2304]{2,1,0:T(8,128)(2,1)}, u32[]{:S(2)}, u32[]{:S(2)}) collective-permute-start(bf16[4,72,2304]{2,1,0:T(8,128)(2,1)} %pad_maximum_fusion.1.piece_ref), channel_id=1, source_target_pairs={{0,8},{8,0},{16,24},{24,16},{1,9},{9,1},{17,25},{25,17},{2,10},{10... | collective-permute-start | bytes 3981320 | tf_op jit(solution)/shard_map/ppermute | solution.py:332
  696.2 26.0 %collective-permute-start.59 = (bf16[4,72,2304]{2,1,0:T(8,128)(2,1)}, bf16[4,72,2304]{2,1,0:T(8,128)(2,1)}, u32[]{:S(2)}, u32[]{:S(2)}) collective-permute-start(bf16[4,72,2304]{2,1,0:T(8,128)(2,1)} %collective-permute-done.58.piece_ref), channel_id=1, source_target_pairs={{0,8},{8,0},{16,24},{24,16},{1,9},{9,1},{17,25},{25,17},{2,10},{10... | collective-permute-start | bytes 3981320 | tf_op jit(solution)/shard_map/ppermute | solution.py:332
  (60 other events, 765.5 us)
Sparse Core Ops, SparseCore 0:
  11.5 129.3 all-gather.2

commit v6 on v5

--- a/solution.py
+++ b/solution.py
@@ -50,7 +50,7 @@
 def probabilities(keys, query, bias):
     scores = mm(keys, query, 0, 0) * HD**-0.5 + bias
     expo = jnp.exp(scores - jnp.max(scores, axis=0, keepdims=True))
-    return expo / jnp.sum(expo, axis=0, keepdims=True)
+    return expo * (1.0 / jnp.sum(expo, axis=0, keepdims=True))
 
 
 def feature_rows(base, slots, kind, head):

time: 741 us -> 741 us (level)
  no operation moved by 1% of the time
where the time goes in v6:
time: 741 us; the launch traced here: 735 us
  waiting for transfers between devices  280 us (38%)
  local copies, waits for them, and re-layouts  109 us (15%)
  starting transfers between devices  101 us (14%)
  matrix products  87.8 us (12%)
  Pallas kernels  84.1 us (11%)
  other arithmetic  57.8 us (8%)
  between operations  15.6 us (2%)
    ppermute x24, waiting for transfers between devices, right(): return lax.ppermute(x, 'shard', to_right)  129 us
    dot_general x14, matrix products, mm(): lax.dot_general(left, right, (((left_dim,), (right_dim,)), ((), ())), pre...  87.8 us
    ppermute x18, waiting for transfers between devices, left(): return lax.ppermute(x, 'shard', to_left)  77.3 us
    all_to_all x5, waiting for transfers between devices, exchange(): lax.all_to_all(blocks, 'shard', split_axis=0, concat_axis=0, tiled=True)  42.4 us
    pallas_call x12, Pallas kernels, finish(): pl.pallas_call(functools.partial(finish_kernel, count, gained), grid_spec...  41.2 us
    ppermute x18, starting transfers between devices, left(): return lax.ppermute(x, 'shard', to_left)  37.1 us
    ppermute x8, waiting for transfers between devices, chip_swap(): return lax.ppermute(x, 'rep', chip_pairs)  30.8 us
    all_to_all x5, starting transfers between devices, exchange(): lax.all_to_all(blocks, 'shard', split_axis=0, concat_axis=0, tiled=True)  29.8 us
  transfers between devices with their start and end apart: 69, of which 33 were waited for; matrix products, arithmetic and copies ran while one was open for 28% of the time, Pallas kernels for 9%

profile of v6, /device:TPU:0, one launch (start us, length us, event | category | flops | bytes accessed | tf_op | source)
XLA Modules:
  0.0 734.5 jit_solution(17792214532368714759)
XLA Ops:
  19.5 6.2 all-to-all-start
  31.9 3.9 prepare_ffn.1
  40.5 36.0 %all-to-all-done = bf16[8,80,960]{2,1,0:T(8,128)(2,1)S(1)} async-done(((bf16[8,80,960]{2,1,0:T(8,128)(2,1)}), bf16[8,80,960]{2,1,0:T(8,128)(2,1)S(1)}, u32[]{:S(2)}, u32[]{:S(2)}) %all-to-all-start) | async-done | bytes 1228832 | tf_op jit(solution)/shard_map/all_to_all | solution.py:389
  85.1 23.6 %collective-permute-done.3 = bf16[128,2304]{1,0:T(8,128)(2,1)S(1)} collective-permute-done((bf16[128,2304]{1,0:T(8,128)(2,1)}, bf16[128,2304]{1,0:T(8,128)(2,1)S(1)}, u32[]{:S(2)}, u32[]{:S(2)}) %collective-permute-start.3) | collective-permute-done | bytes 589856 | tf_op jit(solution)/shard_map/ppermute | solution.py:326
  119.0 12.9 %collective-permute-done.5 = bf16[128,2304]{1,0:T(8,128)(2,1)S(1)} collective-permute-done((bf16[128,2304]{1,0:T(8,128)(2,1)S(1)}, bf16[128,2304]{1,0:T(8,128)(2,1)S(1)}, u32[]{:S(2)}, u32[]{:S(2)}) %collective-permute-start.5) | collective-permute-done | bytes 589856 | tf_op jit(solution)/shard_map/ppermute | solution.py:326
  131.9 6.9 collective-permute-done.6
  139.3 6.2 all-to-all-start.1
  147.2 10.9 %collective-permute-done.7 = bf16[128,2304]{1,0:T(8,128)(2,1)} collective-permute-done((bf16[128,2304]{1,0:T(8,128)(2,1)S(1)}, bf16[128,2304]{1,0:T(8,128)(2,1)}, u32[]{:S(2)}, u32[]{:S(2)}) %collective-permute-start.7) | collective-permute-done | bytes 589856 | tf_op jit(solution)/shard_map/ppermute | solution.py:326
  160.0 3.3 multiply_reduce_fusion
  163.7 3.7 copy-done.3
  167.4 5.3 fusion.57.qkv_ref
  172.8 4.6 attend.1
  185.8 12.1 %collective-permute-done.11 = bf16[320,1024]{1,0:T(8,128)(2,1)} collective-permute-done((bf16[320,1024]{1,0:T(8,128)(2,1)S(1)}, bf16[320,1024]{1,0:T(8,128)(2,1)}, u32[]{:S(2)}, u32[]{:S(2)}) %collective-permute-start.11) | collective-permute-done | bytes 655392 | tf_op jit(solution)/shard_map/ppermute | solution.py:329
  198.0 4.4 collective-permute-start.13
  212.5 4.0 collective-permute-done.13
  225.7 7.5 %collective-permute-done.15 = bf16[320,1024]{1,0:T(8,128)(2,1)S(1)} collective-permute-done((bf16[320,1024]{1,0:T(8,128)(2,1)S(1)}, bf16[320,1024]{1,0:T(8,128)(2,1)S(1)}, u32[]{:S(2)}, u32[]{:S(2)}) %collective-permute-start.15) | collective-permute-done | bytes 655392 | tf_op jit(solution)/shard_map/ppermute | solution.py:329
  239.2 11.4 %collective-permute-done.16 = bf16[320,1024]{1,0:T(8,128)(2,1)S(1)} collective-permute-done((bf16[320,1024]{1,0:T(8,128)(2,1)S(1)}, bf16[320,1024]{1,0:T(8,128)(2,1)S(1)}, u32[]{:S(2)}, u32[]{:S(2)}) %collective-permute-start.16) | collective-permute-done | bytes 655392 | tf_op jit(solution)/shard_map/ppermute | solution.py:326
  256.8 6.4 collective-permute-done.20
  269.2 17.8 %middle_rows.1 = (bf16[1024,2304]{1,0:T(8,128)(2,1)S(1)}, f32[1024,1]{1,0:T(8,128)S(1)}, f32[128,2304]{1,0:T(8,128)S(1)}) custom-call(s32[1]{0:T(128)} %bitcast.me_ref, bf16[2560,1024]{1,0:T(8,128)(2,1)} %slice_dynamic-update-slice_fusion.8.mixed_ref, bf16[2304,2304]{1,0:T(8,128)(2,1)} %bitcast.374, bf16[1024,2304]{1,0:T(8,128)(2,1)S(1)} %bitcast.304), custom_call_target="tpu_custom_call" | custom-call | flops 10871635968 | bytes 24772608 | tf_op jit(solution)/shard_map/middle_rows/pallas_call | solution.py:165
  291.7 6.7 convolution_multiply_fusion
  298.4 5.9 fusion.58
  308.2 11.0 %collective-permute-done.25 = bf16[128,2304]{1,0:T(8,128)(2,1)S(1)} collective-permute-done((bf16[128,2304]{1,0:T(8,128)(2,1)S(1)}, bf16[128,2304]{1,0:T(8,128)(2,1)S(1)}, u32[]{:S(2)}, u32[]{:S(2)}) %collective-permute-start.25) | collective-permute-done | bytes 589856 | tf_op jit(solution)/shard_map/ppermute | solution.py:326
  321.7 7.4 %collective-permute-done.26 = bf16[128,2304]{1,0:T(8,128)(2,1)S(1)} collective-permute-done((bf16[128,2304]{1,0:T(8,128)(2,1)S(1)}, bf16[128,2304]{1,0:T(8,128)(2,1)S(1)}, u32[]{:S(2)}, u32[]{:S(2)}) %collective-permute-start.26) | collective-permute-done | bytes 589856 | tf_op jit(solution)/shard_map/ppermute | solution.py:326
  329.9 8.2 %multiply_convert_fusion = (bf16[1024,720]{0,1:T(8,128)(2,1)S(1)}, bf16[1024,720]{0,1:T(8,128)(2,1)S(1)}, bf16[1024,720]{0,1:T(8,128)(2,1)}) fusion(f32[1024]{0:T(1024)S(1)} %reduce.3, f32[1024,720]{0,1:T(8,128)S(1)} %fusion.58, f32[1024,720]{0,1:T(8,128)S(1)} %convolution_multiply_fusion, bf16[1024,2304]{1,0:T(8,128)(2,1)} %bitcast.55, ...), kind=kOutput, calls=%fused_computation.31 | convolution fusion | flops 3412316160 | bytes 21680128 | tf_op jit(solution)/shard_map/dot_general | solution.py:24
  338.1 7.0 fusion.59
  345.2 6.3 add_convert_fusion
  354.6 11.8 %collective-permute-done.27 = bf16[128,2304]{1,0:T(8,128)(2,1)S(1)} collective-permute-done((bf16[128,2304]{1,0:T(8,128)(2,1)S(1)}, bf16[128,2304]{1,0:T(8,128)(2,1)S(1)}, u32[]{:S(2)}, u32[]{:S(2)}) %collective-permute-start.27) | collective-permute-done | bytes 589856 | tf_op jit(solution)/shard_map/ppermute | solution.py:326
  367.9 13.8 %collective-permute-done.28 = bf16[128,2304]{1,0:T(8,128)(2,1)} collective-permute-done((bf16[128,2304]{1,0:T(8,128)(2,1)}, bf16[128,2304]{1,0:T(8,128)(2,1)}, u32[]{:S(2)}, u32[]{:S(2)}) %collective-permute-start.28) | collective-permute-done | bytes 589856 | tf_op jit(solution)/shard_map/ppermute | solution.py:326
  385.7 6.7 convolution_convert_fusion.4
  392.4 6.9 collective-permute-done.29
  403.3 4.2 convolution_convert_fusion.3
  417.7 6.3 all-to-all-start.2
  424.2 8.2 %convolution_convert_fusion.5 = bf16[720,2304]{1,0:T(8,128)(2,1)} fusion(bf16[1024,720]{0,1:T(8,128)(2,1)} %get-tuple-element.128, bf16[1024,2304]{1,0:T(8,128)(2,1)} %bitcast.55), kind=kOutput, calls=%fused_computation.16 | convolution fusion | flops 3399045120 | bytes 9510912 | tf_op jit(solution)/shard_map/dot_general | solution.py:24
  432.3 3.5 reshape_reshape.12
  440.0 3.5 fusion
  447.1 6.4 all-to-all-done.2
  454.7 13.5 %attend_back.1 = bf16[960,1024]{1,0:T(8,128)(2,1)S(1)} custom-call(bf16[960,1024]{1,0:T(8,128)(2,1)S(1)} %copy-done.12, bf16[320,1024]{1,0:T(8,128)(2,1)S(1)} %copy_bitcast_fusion.2.grad_ref, f32[1,1024]{1,0:T(1,128)S(1)} %bitcast.311, f32[32,1024]{1,0:T(8,128)S(1)} %get-tuple-element.221.cos_ref, f32[32,1024]{1,0:T(8,128)S(1)} %get-tuple-element.220.sin_ref, ...), custom_call_target="tpu_custom_call" | custom-call | flops 419430400 | bytes 4587520 | tf_op jit(solution)/shard_map/attend_back/pallas_call | solution.py:137
  469.8 5.5 fusion.60
  475.5 5.7 convolution_convert_fusion.2
  481.1 4.0 pad_maximum_fusion
  487.9 3.1 fusion.6
  491.0 6.0 all-to-all-start.3
  497.0 7.8 %convolution_convert_fusion.1 = bf16[1024,2304]{1,0:T(8,128)(2,1)S(1)} fusion(bf16[960,1024]{1,0:T(8,128)(2,1)S(1)} %copy-done.14, bf16[2304,960]{1,0:T(8,128)(2,1)} %bitcast.309), kind=kOutput, calls=%fused_computation.12 | convolution fusion | flops 4532207616 | bytes 11108352 | tf_op jit(solution)/shard_map/dot_general | solution.py:24
  507.0 4.7 constant_dynamic-slice_fusion.1
  517.1 23.2 %collective-permute-done.38 = bf16[128,2304]{1,0:T(8,128)(2,1)S(1)} collective-permute-done((bf16[128,2304]{1,0:T(8,128)(2,1)S(1)}, bf16[128,2304]{1,0:T(8,128)(2,1)S(1)}, u32[]{:S(2)}, u32[]{:S(2)}) %collective-permute-start.38) | collective-permute-done | bytes 589856 | tf_op jit(solution)/shard_map/ppermute | solution.py:329
  542.1 9.6 %collective-permute-start.37 = (bf16[128,2304]{1,0:T(8,128)(2,1)S(1)}, bf16[128,2304]{1,0:T(8,128)(2,1)S(1)}, u32[]{:S(2)}, u32[]{:S(2)}) collective-permute-start(bf16[128,2304]{1,0:T(8,128)(2,1)S(1)} %get-tuple-element.197), channel_id=1, source_target_pairs={{0,2},{2,4},{4,6},{6,7},{7,5},{5,3},{3,1},{1,0},{8,10},{10,12},{12... | collective-permute-start | bytes 1769480 | tf_op jit(solution)/shard_map/ppermute | solution.py:326
  552.5 11.3 %collective-permute-done.39 = bf16[128,2304]{1,0:T(8,128)(2,1)S(1)} collective-permute-done((bf16[128,2304]{1,0:T(8,128)(2,1)S(1)}, bf16[128,2304]{1,0:T(8,128)(2,1)S(1)}, u32[]{:S(2)}, u32[]{:S(2)}) %collective-permute-start.39) | collective-permute-done | bytes 589856 | tf_op jit(solution)/shard_map/ppermute | solution.py:329
  566.7 3.5 fusion.1
  571.9 7.3 collective-permute-done.40
  581.8 7.3 convolution_convert_fusion
  589.7 4.5 collective-permute-done.41
  604.3 5.2 all-to-all-start.4
  624.0 5.1 reshape.414
  634.0 16.5 %collective-permute-done.61.piece_ref = bf16[2,72,5760]{2,1,0:T(8,128)(2,1)} collective-permute-done((bf16[2,72,5760]{2,1,0:T(8,128)(2,1)}, bf16[2,72,5760]{2,1,0:T(8,128)(2,1)}, u32[]{:S(2)}, u32[]{:S(2)}) %collective-permute-start.61) | collective-permute-done | bytes 1658912 | tf_op jit(solution)/shard_map/ppermute | solution.py:335
  654.3 3.7 collective-permute-start.51
  675.9 4.7 finish.16
  680.6 4.8 finish.17
  687.7 8.5 %collective-permute-done.58.piece_ref = bf16[4,72,2304]{2,1,0:T(8,128)(2,1)} collective-permute-done((bf16[4,72,2304]{2,1,0:T(8,128)(2,1)}, bf16[4,72,2304]{2,1,0:T(8,128)(2,1)}, u32[]{:S(2)}, u32[]{:S(2)}) %collective-permute-start.58) | collective-permute-done | bytes 1327136 | tf_op jit(solution)/shard_map/ppermute | solution.py:335
  698.9 4.7 finish.22
  703.6 4.7 finish.23
  710.1 3.3 finish.18
  715.8 3.2 finish.19
  718.9 3.2 finish.20
  722.2 3.3 finish.21
  (364 shorter events, 220.1 us)
Async XLA Ops:
  7.2 259.6 %all-gather.3.cloned.1.call-start = ((), (), s32[]{:S(2)}) async-start(), calls=%async_computation.5 | async-start | bytes 10948608 | tf_op jit(solution)/shard_map/all_gather | solution.py:499
  9.7 26.9 %collective-permute-start.2 = (bf16[128,2304]{1,0:T(8,128)(2,1)}, bf16[128,2304]{1,0:T(8,128)(2,1)}, u32[]{:S(2)}, u32[]{:S(2)}) collective-permute-start(bf16[128,2304]{1,0:T(8,128)(2,1)} %param.15), channel_id=1, source_target_pairs={{2,0},{4,2},{6,4},{7,6},{5,7},{3,5},{1,3},{0,1},{10,8},{12,10},{14... | collective-permute-start | bytes 1769480 | tf_op jit(solution)/shard_map/ppermute | solution.py:329
  12.7 23.9 %collective-permute-start.1 = (bf16[128,2304]{1,0:T(8,128)(2,1)}, bf16[128,2304]{1,0:T(8,128)(2,1)}, u32[]{:S(2)}, u32[]{:S(2)}) collective-permute-start(bf16[128,2304]{1,0:T(8,128)(2,1)} %param.15), channel_id=1, source_target_pairs={{0,2},{2,4},{4,6},{6,7},{7,5},{5,3},{3,1},{1,0},{8,10},{10,12},{12... | collective-permute-start | bytes 1769480 | tf_op jit(solution)/shard_map/ppermute | solution.py:326
  19.5 57.0 %all-to-all-start = ((bf16[8,80,960]{2,1,0:T(8,128)(2,1)}), bf16[8,80,960]{2,1,0:T(8,128)(2,1)S(1)}, u32[]{:S(2)}, u32[]{:S(2)}) async-start(bf16[8,80,960]{2,1,0:T(8,128)(2,1)} %prepare_qkv.1), calls=%async_computation | async-start | bytes 2621440 | tf_op jit(solution)/shard_map/all_to_all | solution.py:389
  77.6 39.1 %collective-permute-start = (bf16[8,72,960]{2,1,0:T(8,128)(2,1)}, bf16[8,72,960]{2,1,0:T(8,128)(2,1)}, u32[]{:S(2)}, u32[]{:S(2)}) collective-permute-start(bf16[8,72,960]{2,1,0:T(8,128)(2,1)} %slice.176), channel_id=1, source_target_pairs={{0,8},{8,0},{16,24},{24,16},{1,9},{9,1},{17,25},{25,17},{2,10},{10... | collective-permute-start | bytes 3317768 | tf_op jit(solution)/shard_map/ppermute | solution.py:332
  77.6 69.6 %collective-permute-start.8 = (bf16[8,72,960]{2,1,0:T(8,128)(2,1)}, bf16[8,72,960]{2,1,0:T(8,128)(2,1)S(1)}, u32[]{:S(2)}, u32[]{:S(2)}) collective-permute-start(bf16[8,72,960]{2,1,0:T(8,128)(2,1)} %slice.176), channel_id=1, source_target_pairs={{0,16},{8,24},{16,0},{24,8},{1,17},{9,25},{17,1},{25,9},{2,18},{10... | collective-permute-start | bytes 3317768 | tf_op jit(solution)/shard_map/ppermute | solution.py:335
  79.4 29.2 %collective-permute-start.3 = (bf16[128,2304]{1,0:T(8,128)(2,1)}, bf16[128,2304]{1,0:T(8,128)(2,1)S(1)}, u32[]{:S(2)}, u32[]{:S(2)}) collective-permute-start(bf16[128,2304]{1,0:T(8,128)(2,1)} %collective-permute-done.1), channel_id=1, source_target_pairs={{0,2},{2,4},{4,6},{6,7},{7,5},{5,3},{3,1},{1,0},{8,10},{10,12},{12... | collective-permute-start | bytes 1769480 | tf_op jit(solution)/shard_map/ppermute | solution.py:326
  79.8 32.0 %collective-permute-start.4 = (bf16[128,2304]{1,0:T(8,128)(2,1)}, bf16[128,2304]{1,0:T(8,128)(2,1)S(1)}, u32[]{:S(2)}, u32[]{:S(2)}) collective-permute-start(bf16[128,2304]{1,0:T(8,128)(2,1)} %collective-permute-done.2), channel_id=1, source_target_pairs={{2,0},{4,2},{6,4},{7,6},{5,7},{3,5},{1,3},{0,1},{10,8},{12,10},{14... | collective-permute-start | bytes 1769480 | tf_op jit(solution)/shard_map/ppermute | solution.py:329
  111.8 20.1 %collective-permute-start.5 = (bf16[128,2304]{1,0:T(8,128)(2,1)S(1)}, bf16[128,2304]{1,0:T(8,128)(2,1)S(1)}, u32[]{:S(2)}, u32[]{:S(2)}) collective-permute-start(bf16[128,2304]{1,0:T(8,128)(2,1)S(1)} %collective-permute-done.3), channel_id=1, source_target_pairs={{0,2},{2,4},{4,6},{6,7},{7,5},{5,3},{3,1},{1,0},{8,10},{10,12},{12... | collective-permute-start | bytes 1769480 | tf_op jit(solution)/shard_map/ppermute | solution.py:326
  112.7 26.1 %collective-permute-start.6 = (bf16[128,2304]{1,0:T(8,128)(2,1)S(1)}, bf16[128,2304]{1,0:T(8,128)(2,1)S(1)}, u32[]{:S(2)}, u32[]{:S(2)}) collective-permute-start(bf16[128,2304]{1,0:T(8,128)(2,1)S(1)} %collective-permute-done.4), channel_id=1, source_target_pairs={{2,0},{4,2},{6,4},{7,6},{5,7},{3,5},{1,3},{0,1},{10,8},{12,10},{14... | collective-permute-start | bytes 1769480 | tf_op jit(solution)/shard_map/ppermute | solution.py:329
  138.8 19.3 %collective-permute-start.7 = (bf16[128,2304]{1,0:T(8,128)(2,1)S(1)}, bf16[128,2304]{1,0:T(8,128)(2,1)}, u32[]{:S(2)}, u32[]{:S(2)}) collective-permute-start(bf16[128,2304]{1,0:T(8,128)(2,1)S(1)} %collective-permute-done.5), channel_id=1, source_target_pairs={{0,2},{2,4},{4,6},{6,7},{7,5},{5,3},{3,1},{1,0},{8,10},{10,12},{12... | collective-permute-start | bytes 1769480 | tf_op jit(solution)/shard_map/ppermute | solution.py:326
  139.3 69.9 %all-to-all-start.1 = ((bf16[8,144,720]{2,1,0:T(8,128)(2,1)}), bf16[8,144,720]{2,1,0:T(8,128)(2,1)}, u32[]{:S(2)}, u32[]{:S(2)}) async-start(bf16[8,144,720]{2,1,0:T(8,128)(2,1)} %prepare_ffn.1), calls=%async_computation.1 | async-start | bytes 3538944 | tf_op jit(solution)/shard_map/all_to_all | solution.py:389
  177.4 20.5 %collective-permute-start.11 = (bf16[320,1024]{1,0:T(8,128)(2,1)S(1)}, bf16[320,1024]{1,0:T(8,128)(2,1)}, u32[]{:S(2)}, u32[]{:S(2)}) collective-permute-start(bf16[320,1024]{1,0:T(8,128)(2,1)S(1)} %get-tuple-element.109), channel_id=1, source_target_pairs={{2,0},{4,2},{6,4},{7,6},{5,7},{3,5},{1,3},{0,1},{10,8},{12,10},{14... | collective-permute-start | bytes 1966088 | tf_op jit(solution)/shard_map/ppermute | solution.py:329
  179.7 18.2 %collective-permute-start.10 = (bf16[320,1024]{1,0:T(8,128)(2,1)S(1)}, bf16[320,1024]{1,0:T(8,128)(2,1)}, u32[]{:S(2)}, u32[]{:S(2)}) collective-permute-start(bf16[320,1024]{1,0:T(8,128)(2,1)S(1)} %get-tuple-element.109), channel_id=1, source_target_pairs={{0,2},{2,4},{4,6},{6,7},{7,5},{5,3},{3,1},{1,0},{8,10},{10,12},{12... | collective-permute-start | bytes 1966088 | tf_op jit(solution)/shard_map/ppermute | solution.py:326
  198.0 18.6 %collective-permute-start.13 = (bf16[320,1024]{1,0:T(8,128)(2,1)}, bf16[320,1024]{1,0:T(8,128)(2,1)S(1)}, u32[]{:S(2)}, u32[]{:S(2)}) collective-permute-start(bf16[320,1024]{1,0:T(8,128)(2,1)} %collective-permute-done.11), channel_id=1, source_target_pairs={{2,0},{4,2},{6,4},{7,6},{5,7},{3,5},{1,3},{0,1},{10,8},{12,10},{14... | collective-permute-start | bytes 1966088 | tf_op jit(solution)/shard_map/ppermute | solution.py:329
  202.3 16.4 %collective-permute-start.12 = (bf16[320,1024]{1,0:T(8,128)(2,1)}, bf16[320,1024]{1,0:T(8,128)(2,1)}, u32[]{:S(2)}, u32[]{:S(2)}) collective-permute-start(bf16[320,1024]{1,0:T(8,128)(2,1)} %collective-permute-done.10), channel_id=1, source_target_pairs={{0,2},{2,4},{4,6},{6,7},{7,5},{5,3},{3,1},{1,0},{8,10},{10,12},{12... | collective-permute-start | bytes 1966088 | tf_op jit(solution)/shard_map/ppermute | solution.py:326
  209.2 44.9 %collective-permute-start.18 = (bf16[8,144,720]{2,1,0:T(8,128)(2,1)}, bf16[8,144,720]{2,1,0:T(8,128)(2,1)S(1)}, u32[]{:S(2)}, u32[]{:S(2)}) collective-permute-start(bf16[8,144,720]{2,1,0:T(8,128)(2,1)} %all-to-all-done.1), channel_id=1, source_target_pairs={{0,16},{8,24},{16,0},{24,8},{1,17},{9,25},{17,1},{25,9},{2,18},{10... | collective-permute-start | bytes 4976648 | tf_op jit(solution)/shard_map/ppermute | solution.py:335
  209.7 44.4 %collective-permute-start.17 = (bf16[8,144,720]{2,1,0:T(8,128)(2,1)}, bf16[8,144,720]{2,1,0:T(8,128)(2,1)S(1)}, u32[]{:S(2)}, u32[]{:S(2)}) collective-permute-start(bf16[8,144,720]{2,1,0:T(8,128)(2,1)} %all-to-all-done.1), channel_id=1, source_target_pairs={{0,8},{8,0},{16,24},{24,16},{1,9},{9,1},{17,25},{25,17},{2,10},{10... | collective-permute-start | bytes 4976648 | tf_op jit(solution)/shard_map/ppermute | solution.py:332
  218.7 14.5 %collective-permute-start.15 = (bf16[320,1024]{1,0:T(8,128)(2,1)S(1)}, bf16[320,1024]{1,0:T(8,128)(2,1)S(1)}, u32[]{:S(2)}, u32[]{:S(2)}) collective-permute-start(bf16[320,1024]{1,0:T(8,128)(2,1)S(1)} %collective-permute-done.13), channel_id=1, source_target_pairs={{2,0},{4,2},{6,4},{7,6},{5,7},{3,5},{1,3},{0,1},{10,8},{12,10},{14... | collective-permute-start | bytes 1966088 | tf_op jit(solution)/shard_map/ppermute | solution.py:329
  219.8 14.6 %collective-permute-start.14 = (bf16[320,1024]{1,0:T(8,128)(2,1)}, bf16[320,1024]{1,0:T(8,128)(2,1)S(1)}, u32[]{:S(2)}, u32[]{:S(2)}) collective-permute-start(bf16[320,1024]{1,0:T(8,128)(2,1)} %collective-permute-done.12), channel_id=1, source_target_pairs={{0,2},{2,4},{4,6},{6,7},{7,5},{5,3},{3,1},{1,0},{8,10},{10,12},{12... | collective-permute-start | bytes 1966088 | tf_op jit(solution)/shard_map/ppermute | solution.py:326
  234.4 16.2 %collective-permute-start.16 = (bf16[320,1024]{1,0:T(8,128)(2,1)S(1)}, bf16[320,1024]{1,0:T(8,128)(2,1)S(1)}, u32[]{:S(2)}, u32[]{:S(2)}) collective-permute-start(bf16[320,1024]{1,0:T(8,128)(2,1)S(1)} %collective-permute-done.14), channel_id=1, source_target_pairs={{0,2},{2,4},{4,6},{6,7},{7,5},{5,3},{3,1},{1,0},{8,10},{10,12},{12... | collective-permute-start | bytes 1966088 | tf_op jit(solution)/shard_map/ppermute | solution.py:326
  250.6 12.7 %collective-permute-start.20 = (bf16[128,2304]{1,0:T(8,128)(2,1)S(1)}, bf16[128,2304]{1,0:T(8,128)(2,1)S(1)}, u32[]{:S(2)}, u32[]{:S(2)}) collective-permute-start(bf16[128,2304]{1,0:T(8,128)(2,1)S(1)} %copy-done.36), channel_id=1, source_target_pairs={{2,0},{4,2},{6,4},{7,6},{5,7},{3,5},{1,3},{0,1},{10,8},{12,10},{14... | collective-permute-start | bytes 1769480 | tf_op jit(solution)/shard_map/ppermute | solution.py:329
  252.3 12.1 %collective-permute-start.21 = (bf16[128,2304]{1,0:T(8,128)(2,1)S(1)}, bf16[128,2304]{1,0:T(8,128)(2,1)S(1)}, u32[]{:S(2)}, u32[]{:S(2)}) collective-permute-start(bf16[128,2304]{1,0:T(8,128)(2,1)S(1)} %copy-done.36), channel_id=1, source_target_pairs={{0,2},{2,4},{4,6},{6,7},{7,5},{5,3},{3,1},{1,0},{8,10},{10,12},{12... | collective-permute-start | bytes 1769480 | tf_op jit(solution)/shard_map/ppermute | solution.py:326
  289.4 15.0 %collective-permute-start.22 = (bf16[128,2304]{1,0:T(8,128)(2,1)S(1)}, bf16[128,2304]{1,0:T(8,128)(2,1)S(1)}, u32[]{:S(2)}, u32[]{:S(2)}) collective-permute-start(bf16[128,2304]{1,0:T(8,128)(2,1)S(1)} %copy-done.38), channel_id=1, source_target_pairs={{2,0},{4,2},{6,4},{7,6},{5,7},{3,5},{1,3},{0,1},{10,8},{12,10},{14... | collective-permute-start | bytes 1769480 | tf_op jit(solution)/shard_map/ppermute | solution.py:329
  290.7 13.7 %collective-permute-start.23 = (bf16[128,2304]{1,0:T(8,128)(2,1)}, bf16[128,2304]{1,0:T(8,128)(2,1)S(1)}, u32[]{:S(2)}, u32[]{:S(2)}) collective-permute-start(bf16[128,2304]{1,0:T(8,128)(2,1)} %copy-done.39), channel_id=1, source_target_pairs={{0,2},{2,4},{4,6},{6,7},{7,5},{5,3},{3,1},{1,0},{8,10},{10,12},{12... | collective-permute-start | bytes 1769480 | tf_op jit(solution)/shard_map/ppermute | solution.py:326
  304.4 15.6 %collective-permute-start.24 = (bf16[128,2304]{1,0:T(8,128)(2,1)S(1)}, bf16[128,2304]{1,0:T(8,128)(2,1)S(1)}, u32[]{:S(2)}, u32[]{:S(2)}) collective-permute-start(bf16[128,2304]{1,0:T(8,128)(2,1)S(1)} %collective-permute-done.22), channel_id=1, source_target_pairs={{2,0},{4,2},{6,4},{7,6},{5,7},{3,5},{1,3},{0,1},{10,8},{12,10},{14... | collective-permute-start | bytes 1769480 | tf_op jit(solution)/shard_map/ppermute | solution.py:329
  305.6 13.5 %collective-permute-start.25 = (bf16[128,2304]{1,0:T(8,128)(2,1)S(1)}, bf16[128,2304]{1,0:T(8,128)(2,1)S(1)}, u32[]{:S(2)}, u32[]{:S(2)}) collective-permute-start(bf16[128,2304]{1,0:T(8,128)(2,1)S(1)} %collective-permute-done.23), channel_id=1, source_target_pairs={{0,2},{2,4},{4,6},{6,7},{7,5},{5,3},{3,1},{1,0},{8,10},{10,12},{12... | collective-permute-start | bytes 1769480 | tf_op jit(solution)/shard_map/ppermute | solution.py:326
  352.6 13.8 %collective-permute-start.27 = (bf16[128,2304]{1,0:T(8,128)(2,1)S(1)}, bf16[128,2304]{1,0:T(8,128)(2,1)S(1)}, u32[]{:S(2)}, u32[]{:S(2)}) collective-permute-start(bf16[128,2304]{1,0:T(8,128)(2,1)S(1)} %get-tuple-element.204), channel_id=1, source_target_pairs={{0,2},{2,4},{4,6},{6,7},{7,5},{5,3},{3,1},{1,0},{8,10},{10,12},{12... | collective-permute-start | bytes 1769480 | tf_op jit(solution)/shard_map/ppermute | solution.py:326
  353.5 14.5 %collective-permute-start.31 = (bf16[128,2304]{1,0:T(8,128)(2,1)}, bf16[128,2304]{1,0:T(8,128)(2,1)S(1)}, u32[]{:S(2)}, u32[]{:S(2)}) collective-permute-start(bf16[128,2304]{1,0:T(8,128)(2,1)} %get-tuple-element.205), channel_id=1, source_target_pairs={{2,0},{4,2},{6,4},{7,6},{5,7},{3,5},{1,3},{0,1},{10,8},{12,10},{14... | collective-permute-start | bytes 1769480 | tf_op jit(solution)/shard_map/ppermute | solution.py:329
  367.4 14.4 %collective-permute-start.28 = (bf16[128,2304]{1,0:T(8,128)(2,1)}, bf16[128,2304]{1,0:T(8,128)(2,1)}, u32[]{:S(2)}, u32[]{:S(2)}) collective-permute-start(bf16[128,2304]{1,0:T(8,128)(2,1)} %fusion.38), channel_id=1, source_target_pairs={{0,2},{2,4},{4,6},{6,7},{7,5},{5,3},{3,1},{1,0},{8,10},{10,12},{12... | collective-permute-start | bytes 1769480 | tf_op jit(solution)/shard_map/ppermute | solution.py:326
  383.6 15.7 %collective-permute-start.29 = (bf16[128,2304]{1,0:T(8,128)(2,1)S(1)}, bf16[128,2304]{1,0:T(8,128)(2,1)S(1)}, u32[]{:S(2)}, u32[]{:S(2)}) collective-permute-start(bf16[128,2304]{1,0:T(8,128)(2,1)S(1)} %get-tuple-element.202), channel_id=1, source_target_pairs={{0,2},{2,4},{4,6},{6,7},{7,5},{5,3},{3,1},{1,0},{8,10},{10,12},{12... | collective-permute-start | bytes 1769480 | tf_op jit(solution)/shard_map/ppermute | solution.py:326
  383.7 15.6 %collective-permute-start.32 = (bf16[128,2304]{1,0:T(8,128)(2,1)S(1)}, bf16[128,2304]{1,0:T(8,128)(2,1)S(1)}, u32[]{:S(2)}, u32[]{:S(2)}) collective-permute-start(bf16[128,2304]{1,0:T(8,128)(2,1)S(1)} %get-tuple-element.203), channel_id=1, source_target_pairs={{2,0},{4,2},{6,4},{7,6},{5,7},{3,5},{1,3},{0,1},{10,8},{12,10},{14... | collective-permute-start | bytes 1769480 | tf_op jit(solution)/shard_map/ppermute | solution.py:329
  410.7 29.3 %collective-permute-start.34 = (bf16[8,2,144,720]{3,2,1,0:T(8,128)(2,1)}, bf16[8,2,144,720]{3,2,1,0:T(8,128)(2,1)}, u32[]{:S(2)}, u32[]{:S(2)}) collective-permute-start(bf16[8,2,144,720]{3,2,1,0:T(8,128)(2,1)} %fusion.3), channel_id=1, source_target_pairs={{0,8},{8,0},{16,24},{24,16},{1,9},{9,1},{17,25},{25,17},{2,10},{10... | collective-permute-start | bytes 9953288 | tf_op jit(solution)/shard_map/ppermute | solution.py:332
  417.7 35.8 %all-to-all-start.2 = ((bf16[8,608,128]{2,1,0:T(8,128)(2,1)}), bf16[8,608,128]{2,1,0:T(8,128)(2,1)}, u32[]{:S(2)}, u32[]{:S(2)}) async-start(bf16[8,608,128]{2,1,0:T(8,128)(2,1)} %pad_maximum_fusion.2), calls=%async_computation.2 | async-start | bytes 2490368 | tf_op jit(solution)/shard_map/all_to_all | solution.py:389
  440.0 73.6 %collective-permute-start.45 = (bf16[1,2,180,2304]{3,1,2,0:T(2,128)(2,1)}, bf16[1,2,180,2304]{3,1,2,0:T(2,128)(2,1)}, u32[]{:S(2)}, u32[]{:S(2)}) collective-permute-start(bf16[1,2,180,2304]{3,1,2,0:T(2,128)(2,1)} %copy.281), channel_id=1, source_target_pairs={{0,8},{8,0},{16,24},{24,16},{1,9},{9,1},{17,25},{25,17},{2,10},{10... | collective-permute-start | bytes 4976648 | tf_op jit(solution)/shard_map/ppermute | solution.py:332
  446.6 41.3 %collective-permute-start.35 = (bf16[8,144,720]{2,1,0:T(8,128)(2,1)}, bf16[8,144,720]{2,1,0:T(8,128)(2,1)}, u32[]{:S(2)}, u32[]{:S(2)}) collective-permute-start(bf16[8,144,720]{2,1,0:T(8,128)(2,1)} %dynamic-slice_bitcast_fusion), channel_id=1, source_target_pairs={{0,16},{8,24},{16,0},{24,8},{1,17},{9,25},{17,1},{25,9},{2,18},{10... | collective-permute-start | bytes 4976648 | tf_op jit(solution)/shard_map/ppermute | solution.py:335
  491.0 74.7 %all-to-all-start.3 = ((bf16[8,144,720]{2,1,0:T(8,128)(2,1)}), bf16[8,144,720]{2,1,0:T(8,128)(2,1)}, u32[]{:S(2)}, u32[]{:S(2)}) async-start(bf16[8,144,720]{2,1,0:T(8,128)(2,1)} %fusion.6), calls=%async_computation.3 | async-start | bytes 3538944 | tf_op jit(solution)/shard_map/all_to_all | solution.py:389
  504.9 35.4 %collective-permute-start.38 = (bf16[128,2304]{1,0:T(8,128)(2,1)S(1)}, bf16[128,2304]{1,0:T(8,128)(2,1)S(1)}, u32[]{:S(2)}, u32[]{:S(2)}) collective-permute-start(bf16[128,2304]{1,0:T(8,128)(2,1)S(1)} %get-tuple-element.198), channel_id=1, source_target_pairs={{2,0},{4,2},{6,4},{7,6},{5,7},{3,5},{1,3},{0,1},{10,8},{12,10},{14... | collective-permute-start | bytes 1769480 | tf_op jit(solution)/shard_map/ppermute | solution.py:329
  507.0 33.3 %collective-permute-start.36 = (bf16[128,2304]{1,0:T(8,128)(2,1)S(1)}, bf16[128,2304]{1,0:T(8,128)(2,1)S(1)}, u32[]{:S(2)}, u32[]{:S(2)}) collective-permute-start(bf16[128,2304]{1,0:T(8,128)(2,1)S(1)} %get-tuple-element.199), channel_id=1, source_target_pairs={{0,2},{2,4},{4,6},{6,7},{7,5},{5,3},{3,1},{1,0},{8,10},{10,12},{12... | collective-permute-start | bytes 1769480 | tf_op jit(solution)/shard_map/ppermute | solution.py:326
  513.5 53.2 %collective-permute-start.56 = (bf16[8,2,72,1248]{3,2,0,1:T(8,128)(2,1)}, bf16[8,2,72,1248]{3,2,0,1:T(8,128)(2,1)}, u32[]{:S(2)}, u32[]{:S(2)}) collective-permute-start(bf16[8,2,72,1248]{3,2,0,1:T(8,128)(2,1)} %bitcast.301), channel_id=1, source_target_pairs={{0,8},{8,0},{16,24},{24,16},{1,9},{9,1},{17,25},{25,17},{2,10},{10... | collective-permute-start | bytes 8626184 | tf_op jit(solution)/shard_map/ppermute | solution.py:332
  516.6 35.2 %collective-permute-start.46 = (bf16[1,180,2304]{2,1,0:T(8,128)(2,1)S(1)}, bf16[1,180,2304]{2,1,0:T(8,128)(2,1)S(1)}, u32[]{:S(2)}, u32[]{:S(2)}) collective-permute-start(bf16[1,180,2304]{2,1,0:T(8,128)(2,1)S(1)} %dynamic-slice_bitcast_fusion.3), channel_id=1, source_target_pairs={{0,16},{8,24},{16,0},{24,8},{1,17},{9,25},{17,1},{25,9},{2,18},{10... | collective-permute-start | bytes 2488328 | tf_op jit(solution)/shard_map/ppermute | solution.py:335
  540.6 23.2 %collective-permute-start.39 = (bf16[128,2304]{1,0:T(8,128)(2,1)S(1)}, bf16[128,2304]{1,0:T(8,128)(2,1)S(1)}, u32[]{:S(2)}, u32[]{:S(2)}) collective-permute-start(bf16[128,2304]{1,0:T(8,128)(2,1)S(1)} %get-tuple-element.196), channel_id=1, source_target_pairs={{2,0},{4,2},{6,4},{7,6},{5,7},{3,5},{1,3},{0,1},{10,8},{12,10},{14... | collective-permute-start | bytes 1769480 | tf_op jit(solution)/shard_map/ppermute | solution.py:329
  542.1 23.2 %collective-permute-start.37 = (bf16[128,2304]{1,0:T(8,128)(2,1)S(1)}, bf16[128,2304]{1,0:T(8,128)(2,1)S(1)}, u32[]{:S(2)}, u32[]{:S(2)}) collective-permute-start(bf16[128,2304]{1,0:T(8,128)(2,1)S(1)} %get-tuple-element.197), channel_id=1, source_target_pairs={{0,2},{2,4},{4,6},{6,7},{7,5},{5,3},{3,1},{1,0},{8,10},{10,12},{12... | collective-permute-start | bytes 1769480 | tf_op jit(solution)/shard_map/ppermute | solution.py:326
  552.0 37.3 %collective-permute-start.47 = (bf16[1,180,2304]{2,1,0:T(8,128)(2,1)S(1)}, bf16[1,180,2304]{2,1,0:T(8,128)(2,1)}, u32[]{:S(2)}, u32[]{:S(2)}) collective-permute-start(bf16[1,180,2304]{2,1,0:T(8,128)(2,1)S(1)} %fusion.10.piece_ref), channel_id=1, source_target_pairs={{0,16},{8,24},{16,0},{24,8},{1,17},{9,25},{17,1},{25,9},{2,18},{10... | collective-permute-start | bytes 2488328 | tf_op jit(solution)/shard_map/ppermute | solution.py:335
  565.7 13.5 %collective-permute-start.40 = (bf16[128,2304]{1,0:T(8,128)(2,1)S(1)}, bf16[128,2304]{1,0:T(8,128)(2,1)S(1)}, u32[]{:S(2)}, u32[]{:S(2)}) collective-permute-start(bf16[128,2304]{1,0:T(8,128)(2,1)S(1)} %get-tuple-element.136), channel_id=1, source_target_pairs={{0,2},{2,4},{4,6},{6,7},{7,5},{5,3},{3,1},{1,0},{8,10},{10,12},{12... | collective-permute-start | bytes 1769480 | tf_op jit(solution)/shard_map/ppermute | solution.py:326
  570.3 32.6 %collective-permute-start.57 = (bf16[8,72,1248]{2,1,0:T(8,128)(2,1)S(1)}, bf16[8,72,1248]{2,1,0:T(8,128)(2,1)S(1)}, u32[]{:S(2)}, u32[]{:S(2)}) collective-permute-start(bf16[8,72,1248]{2,1,0:T(8,128)(2,1)S(1)} %dynamic-slice_bitcast_fusion.2), channel_id=1, source_target_pairs={{0,16},{8,24},{16,0},{24,8},{1,17},{9,25},{17,1},{25,9},{2,18},{10... | collective-permute-start | bytes 4313096 | tf_op jit(solution)/shard_map/ppermute | solution.py:335
  570.8 18.9 %collective-permute-start.42 = (bf16[128,2304]{1,0:T(8,128)(2,1)S(1)}, bf16[128,2304]{1,0:T(8,128)(2,1)S(1)}, u32[]{:S(2)}, u32[]{:S(2)}) collective-permute-start(bf16[128,2304]{1,0:T(8,128)(2,1)S(1)} %get-tuple-element.137), channel_id=1, source_target_pairs={{2,0},{4,2},{6,4},{7,6},{5,7},{3,5},{1,3},{0,1},{10,8},{12,10},{14... | collective-permute-start | bytes 1769480 | tf_op jit(solution)/shard_map/ppermute | solution.py:329
  580.5 13.7 %collective-permute-start.41 = (bf16[128,2304]{1,0:T(8,128)(2,1)S(1)}, bf16[128,2304]{1,0:T(8,128)(2,1)S(1)}, u32[]{:S(2)}, u32[]{:S(2)}) collective-permute-start(bf16[128,2304]{1,0:T(8,128)(2,1)S(1)} %fusion.29), channel_id=1, source_target_pairs={{0,2},{2,4},{4,6},{6,7},{7,5},{5,3},{3,1},{1,0},{8,10},{10,12},{12... | collective-permute-start | bytes 1769480 | tf_op jit(solution)/shard_map/ppermute | solution.py:326
  589.2 28.0 %collective-permute-start.49 = (bf16[1,180,2304]{2,1,0:T(8,128)(2,1)S(1)}, bf16[1,180,2304]{2,1,0:T(8,128)(2,1)}, u32[]{:S(2)}, u32[]{:S(2)}) collective-permute-start(bf16[1,180,2304]{2,1,0:T(8,128)(2,1)S(1)} %fusion.10.piece_ref), channel_id=1, source_target_pairs={{0,8},{8,0},{16,24},{24,16},{1,9},{9,1},{17,25},{25,17},{2,10},{10... | collective-permute-start | bytes 2488328 | tf_op jit(solution)/shard_map/ppermute | solution.py:332
  589.2 32.5 %collective-permute-start.48 = (bf16[1,180,2304]{2,1,0:T(8,128)(2,1)}, bf16[1,180,2304]{2,1,0:T(8,128)(2,1)}, u32[]{:S(2)}, u32[]{:S(2)}) collective-permute-start(bf16[1,180,2304]{2,1,0:T(8,128)(2,1)} %collective-permute-done.47.piece_ref), channel_id=1, source_target_pairs={{0,8},{8,0},{16,24},{24,16},{1,9},{9,1},{17,25},{25,17},{2,10},{10... | collective-permute-start | bytes 2488328 | tf_op jit(solution)/shard_map/ppermute | solution.py:332
  597.8 31.4 %collective-permute-start.44 = (bf16[128,2304]{1,0:T(8,128)(2,1)}, bf16[128,2304]{1,0:T(8,128)(2,1)}, u32[]{:S(2)}, u32[]{:S(2)}) collective-permute-start(bf16[128,2304]{1,0:T(8,128)(2,1)} %get-tuple-element.192), channel_id=1, source_target_pairs={{2,0},{4,2},{6,4},{7,6},{5,7},{3,5},{1,3},{0,1},{10,8},{12,10},{14... | collective-permute-start | bytes 1769480 | tf_op jit(solution)/shard_map/ppermute | solution.py:329
  599.7 29.5 %collective-permute-start.43 = (bf16[128,2304]{1,0:T(8,128)(2,1)}, bf16[128,2304]{1,0:T(8,128)(2,1)}, u32[]{:S(2)}, u32[]{:S(2)}) collective-permute-start(bf16[128,2304]{1,0:T(8,128)(2,1)} %get-tuple-element.193), channel_id=1, source_target_pairs={{0,2},{2,4},{4,6},{6,7},{7,5},{5,3},{3,1},{1,0},{8,10},{10,12},{12... | collective-permute-start | bytes 1769480 | tf_op jit(solution)/shard_map/ppermute | solution.py:326
  604.3 53.6 %all-to-all-start.4 = ((bf16[8,72,1248]{2,1,0:T(8,128)(2,1)}), bf16[8,72,1248]{2,1,0:T(8,128)(2,1)}, u32[]{:S(2)}, u32[]{:S(2)}) async-start(bf16[8,72,1248]{2,1,0:T(8,128)(2,1)} %fusion.8), calls=%async_computation.4 | async-start | bytes 2949120 | tf_op jit(solution)/shard_map/all_to_all | solution.py:389
  614.4 36.2 %collective-permute-start.61 = (bf16[2,72,5760]{2,1,0:T(8,128)(2,1)}, bf16[2,72,5760]{2,1,0:T(8,128)(2,1)}, u32[]{:S(2)}, u32[]{:S(2)}) collective-permute-start(bf16[2,72,5760]{2,1,0:T(8,128)(2,1)} %reshape.416.piece_ref), channel_id=1, source_target_pairs={{0,16},{8,24},{16,0},{24,8},{1,17},{9,25},{17,1},{25,9},{2,18},{10... | collective-permute-start | bytes 4976648 | tf_op jit(solution)/shard_map/ppermute | solution.py:335
  632.0 20.3 %collective-permute-start.50 = (bf16[128,2304]{1,0:T(8,128)(2,1)S(1)}, bf16[128,2304]{1,0:T(8,128)(2,1)S(1)}, u32[]{:S(2)}, u32[]{:S(2)}) collective-permute-start(bf16[128,2304]{1,0:T(8,128)(2,1)S(1)} %get-tuple-element.139), channel_id=1, source_target_pairs={{0,2},{2,4},{4,6},{6,7},{7,5},{5,3},{3,1},{1,0},{8,10},{10,12},{12... | collective-permute-start | bytes 1769480 | tf_op jit(solution)/shard_map/ppermute | solution.py:326
  634.0 46.6 %collective-permute-start.54 = (bf16[2,72,5760]{2,1,0:T(8,128)(2,1)S(1)}, bf16[2,72,5760]{2,1,0:T(8,128)(2,1)}, u32[]{:S(2)}, u32[]{:S(2)}) collective-permute-start(bf16[2,72,5760]{2,1,0:T(8,128)(2,1)S(1)} %copy-done.26), channel_id=1, source_target_pairs={{0,8},{8,0},{16,24},{24,16},{1,9},{9,1},{17,25},{25,17},{2,10},{10... | collective-permute-start | bytes 4976648 | tf_op jit(solution)/shard_map/ppermute | solution.py:332
  650.5 53.1 %collective-permute-start.62 = (bf16[2,72,5760]{2,1,0:T(8,128)(2,1)}, bf16[2,72,5760]{2,1,0:T(8,128)(2,1)}, u32[]{:S(2)}, u32[]{:S(2)}) collective-permute-start(bf16[2,72,5760]{2,1,0:T(8,128)(2,1)} %collective-permute-done.61.piece_ref), channel_id=1, source_target_pairs={{0,8},{8,0},{16,24},{24,16},{1,9},{9,1},{17,25},{25,17},{2,10},{10... | collective-permute-start | bytes 4976648 | tf_op jit(solution)/shard_map/ppermute | solution.py:332
  650.5 17.0 %collective-permute-start.52 = (bf16[128,2304]{1,0:T(8,128)(2,1)}, bf16[128,2304]{1,0:T(8,128)(2,1)}, u32[]{:S(2)}, u32[]{:S(2)}) collective-permute-start(bf16[128,2304]{1,0:T(8,128)(2,1)} %get-tuple-element.140), channel_id=1, source_target_pairs={{2,0},{4,2},{6,4},{7,6},{5,7},{3,5},{1,3},{0,1},{10,8},{12,10},{14... | collective-permute-start | bytes 1769480 | tf_op jit(solution)/shard_map/ppermute | solution.py:329
  654.3 15.8 %collective-permute-start.51 = (bf16[128,2304]{1,0:T(8,128)(2,1)}, bf16[128,2304]{1,0:T(8,128)(2,1)}, u32[]{:S(2)}, u32[]{:S(2)}) collective-permute-start(bf16[128,2304]{1,0:T(8,128)(2,1)} %fusion.26), channel_id=1, source_target_pairs={{0,2},{2,4},{4,6},{6,7},{7,5},{5,3},{3,1},{1,0},{8,10},{10,12},{12... | collective-permute-start | bytes 1769480 | tf_op jit(solution)/shard_map/ppermute | solution.py:326
  667.1 29.1 %collective-permute-start.58 = (bf16[4,72,2304]{2,1,0:T(8,128)(2,1)}, bf16[4,72,2304]{2,1,0:T(8,128)(2,1)}, u32[]{:S(2)}, u32[]{:S(2)}) collective-permute-start(bf16[4,72,2304]{2,1,0:T(8,128)(2,1)} %pad_maximum_fusion.1.piece_ref), channel_id=1, source_target_pairs={{0,16},{8,24},{16,0},{24,8},{1,17},{9,25},{17,1},{25,9},{2,18},{10... | collective-permute-start | bytes 3981320 | tf_op jit(solution)/shard_map/ppermute | solution.py:335
  672.7 15.0 %collective-permute-start.53 = (bf16[128,2304]{1,0:T(8,128)(2,1)}, bf16[128,2304]{1,0:T(8,128)(2,1)}, u32[]{:S(2)}, u32[]{:S(2)}) collective-permute-start(bf16[128,2304]{1,0:T(8,128)(2,1)} %get-tuple-element.188), channel_id=1, source_target_pairs={{2,0},{4,2},{6,4},{7,6},{5,7},{3,5},{1,3},{0,1},{10,8},{12,10},{14... | collective-permute-start | bytes 1769480 | tf_op jit(solution)/shard_map/ppermute | solution.py:329
  687.7 25.7 %collective-permute-start.55 = (bf16[128,2304]{1,0:T(8,128)(2,1)S(1)}, bf16[128,2304]{1,0:T(8,128)(2,1)S(1)}, u32[]{:S(2)}, u32[]{:S(2)}) collective-permute-start(bf16[128,2304]{1,0:T(8,128)(2,1)S(1)} %get-tuple-element.147), channel_id=1, source_target_pairs={{0,2},{2,4},{4,6},{6,7},{7,5},{5,3},{3,1},{1,0},{8,10},{10,12},{12... | collective-permute-start | bytes 1769480 | tf_op jit(solution)/shard_map/ppermute | solution.py:326
  687.7 28.1 %collective-permute-start.60 = (bf16[4,72,2304]{2,1,0:T(8,128)(2,1)}, bf16[4,72,2304]{2,1,0:T(8,128)(2,1)}, u32[]{:S(2)}, u32[]{:S(2)}) collective-permute-start(bf16[4,72,2304]{2,1,0:T(8,128)(2,1)} %pad_maximum_fusion.1.piece_ref), channel_id=1, source_target_pairs={{0,8},{8,0},{16,24},{24,16},{1,9},{9,1},{17,25},{25,17},{2,10},{10... | collective-permute-start | bytes 3981320 | tf_op jit(solution)/shard_map/ppermute | solution.py:332
  696.2 26.0 %collective-permute-start.59 = (bf16[4,72,2304]{2,1,0:T(8,128)(2,1)}, bf16[4,72,2304]{2,1,0:T(8,128)(2,1)}, u32[]{:S(2)}, u32[]{:S(2)}) collective-permute-start(bf16[4,72,2304]{2,1,0:T(8,128)(2,1)} %collective-permute-done.58.piece_ref), channel_id=1, source_target_pairs={{0,8},{8,0},{16,24},{24,16},{1,9},{9,1},{17,25},{25,17},{2,10},{10... | collective-permute-start | bytes 3981320 | tf_op jit(solution)/shard_map/ppermute | solution.py:332
  (60 other events, 765.5 us)
Sparse Core Ops, SparseCore 0:
  11.5 129.3 all-gather.2
